TPU v7x, 32 devices: a whole 2x2x4 slice. The times are simulated.
32 devices in a mesh: narrow: 2 (over y), wide: 16 (over z, x, core).
Axes of the slice: x: 2, y: 2, z: 4, core: 2. Of those that a mesh axis runs over, the one named last changes fastest.
Arguments:
- tokens: bfloat16 [2, 16384, 768], P(None, ('narrow', 'wide')), may hold values from -6 to 6
- image_ids: int32 [2, 16384], P(None, ('narrow', 'wide')), may hold values from -1 to 1, as said below
- cotangent: bfloat16 [2, 16384, 768], P(None, ('narrow', 'wide')), may hold values from -6 to 6
- w_joined: bfloat16 [768, 5376], P('wide'), may hold values from -0.21875 to 0.21875
- w_out: bfloat16 [768, 768], P('wide'), may hold values from -1 to 1
- w_mlp: bfloat16 [3072, 768], P('wide'), may hold values from -0.109375 to 0.109375
- norm_gain: bfloat16 [768], P('wide'), may hold values from 0.5 to 1.5
- bias_attn: bfloat16 [1536], P('wide'), may hold values from -1.1953125 to 1.1953125
- bias_mlp: bfloat16 [3072], P('wide'), may hold values from -1.1953125 to 1.1953125
- bias_out: bfloat16 [768], P('wide'), may hold values from -1.1953125 to 1.1953125
Outputs:
- block_out: bfloat16 [2, 16384, 768], P(None, ('narrow', 'wide'))
- d_tokens: bfloat16 [2, 16384, 768], P(None, ('narrow', 'wide'))
- grad_joined: float32 [768, 5376], P('wide')
- grad_out: float32 [768, 768], P('wide')
- grad_mlp: float32 [3072, 768], P('wide')
- grad_gain: float32 [768], P('wide')
- grad_bias_attn: float32 [1536], P('wide')
- grad_bias_mlp: float32 [3072], P('wide')
- grad_bias_out: float32 [768], P('wide')
Inputs may be any that keep to these rules, and one draw needn't show every extreme that they name: `image_ids`: each block of 512 consecutive tokens (one device's share of a micro-batch) holds either one image of 512 tokens, all with id 0, or 2 images of 196 tokens in order with ids 0, 1, ..., followed by padding tokens with id -1. Every micro-batch has blocks of both kinds.
All inputs are finite; a program needn't handle non-finite values.
Results may differ from a plain program's by a relative error of at most 0.0083.
Values may be sent and summed in bfloat16 or wider, within the bound.
No kernel may reach another device: no remote copies, remote signals or barrier semaphores. Data moves between devices by JAX's collectives and lax.ppermute only.
A program may use at most 192 MiB of HBM per device.

v0:
```python
import jax
import jax.numpy as jnp
from jax import lax
from jax.sharding import PartitionSpec as P

HEADS = 12


norm_eps = 1e-06
masked_score = -1e30


def gelu_tanh(inputs):
    inner = 0.7978845608028654 * (inputs + 0.044715 * inputs * inputs * inputs)
    return 0.5 * inputs * (1.0 + jnp.tanh(inner))


def masked_scores(query_rows, key_rows, same_image, score_scale):
    raw_scores = (
        jnp.einsum("qhe,khe->hqk", query_rows, key_rows, preferred_element_type=jnp.float32)
        * score_scale
    )
    return jnp.where(same_image[None], raw_scores, masked_score)


def forward_block(block_rows, block_ids, gathered):
    w_joined, w_out, w_mlp, norm_gain, bias_attn, bias_mlp, bias_out = gathered
    block_len, model_width = block_rows.shape
    head_count = HEADS
    head_size = model_width // head_count
    score_scale = head_size ** (-0.5)
    inputs = block_rows.astype(jnp.float32)
    row_mean = jnp.mean(inputs, axis=1, keepdims=True)
    centered = inputs - row_mean
    inverse_std = lax.rsqrt(jnp.mean(centered * centered, axis=1, keepdims=True) + norm_eps)
    standard = centered * inverse_std
    normed = (standard * norm_gain.astype(jnp.float32)).astype(jnp.bfloat16)
    bias_full = jnp.concatenate(
        [
            bias_attn[:model_width],
            jnp.zeros((model_width,), jnp.bfloat16),
            bias_attn[model_width:],
            bias_mlp,
        ]
    ).astype(jnp.float32)
    joined = jnp.dot(normed, w_joined, preferred_element_type=jnp.float32) + bias_full
    attn_part = joined[:, : 3 * model_width].astype(jnp.bfloat16)
    pre_act = joined[:, 3 * model_width :]
    query_rows = attn_part[:, :model_width].reshape(block_len, head_count, head_size)
    key_rows = attn_part[:, model_width : 2 * model_width].reshape(block_len, head_count, head_size)
    value_rows = attn_part[:, 2 * model_width :].reshape(block_len, head_count, head_size)
    same_image = block_ids[:, None] == block_ids[None, :]
    scores = masked_scores(query_rows, key_rows, same_image, score_scale)
    row_max = jnp.max(scores, axis=2, keepdims=True)
    exponents = jnp.exp(scores - row_max)
    row_total = jnp.sum(exponents, axis=2, keepdims=True)
    probs_low = (exponents / row_total).astype(jnp.bfloat16)
    log_total = row_max + jnp.log(row_total)
    attended = jnp.einsum("hqk,khe->qhe", probs_low, value_rows, preferred_element_type=jnp.float32)
    attended = attended.reshape(block_len, model_width).astype(jnp.bfloat16)
    activated = gelu_tanh(pre_act).astype(jnp.bfloat16)
    attn_branch = jnp.dot(attended, w_out, preferred_element_type=jnp.float32)
    mlp_branch = jnp.dot(activated, w_mlp, preferred_element_type=jnp.float32)
    output = inputs + attn_branch + mlp_branch + bias_out.astype(jnp.float32)
    saved_state = (
        standard,
        inverse_std,
        normed,
        query_rows,
        key_rows,
        value_rows,
        pre_act,
        log_total,
        attended,
        activated,
        same_image,
    )
    return (saved_state, output.astype(jnp.bfloat16))


def backward_block(saved_state, block_cot, gathered):
    (
        standard,
        inverse_std,
        normed,
        query_rows,
        key_rows,
        value_rows,
        pre_act,
        log_total,
        attended,
        activated,
        same_image,
    ) = saved_state
    w_joined, w_out, w_mlp, norm_gain, bias_attn, bias_mlp, bias_out = gathered
    block_len, head_count, head_size = query_rows.shape
    model_width = head_count * head_size
    score_scale = head_size ** (-0.5)
    upstream = block_cot.astype(jnp.float32)
    grad_bias_out = jnp.sum(upstream, axis=0)
    grad_mlp = jnp.einsum("tf,td->fd", activated, block_cot, preferred_element_type=jnp.float32)
    d_act = jnp.einsum("td,fd->tf", block_cot, w_mlp, preferred_element_type=jnp.float32)
    gelu_out, gelu_back = jax.vjp(gelu_tanh, pre_act)
    d_pre = gelu_back(d_act)[0]
    grad_out = jnp.einsum("tc,td->cd", attended, block_cot, preferred_element_type=jnp.float32)
    d_att = jnp.einsum("td,cd->tc", block_cot, w_out, preferred_element_type=jnp.float32)
    d_att = d_att.astype(jnp.bfloat16).reshape(block_len, head_count, head_size)
    scores = masked_scores(query_rows, key_rows, same_image, score_scale)
    attn_probs = jnp.exp(scores - log_total)
    probs_low = attn_probs.astype(jnp.bfloat16)
    d_values = jnp.einsum("hqk,qhe->khe", probs_low, d_att, preferred_element_type=jnp.float32)
    d_probs = jnp.einsum("qhe,khe->hqk", d_att, value_rows, preferred_element_type=jnp.float32)
    row_inner = jnp.sum(attn_probs * d_probs, axis=2, keepdims=True)
    d_scores = (attn_probs * (d_probs - row_inner)).astype(jnp.bfloat16)
    d_queries = (
        jnp.einsum("hqk,khe->qhe", d_scores, key_rows, preferred_element_type=jnp.float32)
        * score_scale
    )
    d_keys = (
        jnp.einsum("hqk,qhe->khe", d_scores, query_rows, preferred_element_type=jnp.float32)
        * score_scale
    )
    d_joined = jnp.concatenate(
        [
            d_queries.reshape(block_len, model_width),
            d_keys.reshape(block_len, model_width),
            d_values.reshape(block_len, model_width),
            d_pre,
        ],
        axis=1,
    ).astype(jnp.bfloat16)
    grad_bias_attn = jnp.concatenate(
        [
            jnp.sum(d_joined[:, :model_width], axis=0, dtype=jnp.float32),
            jnp.sum(d_joined[:, 2 * model_width : 3 * model_width], axis=0, dtype=jnp.float32),
        ]
    )
    grad_bias_mlp = jnp.sum(d_joined[:, 3 * model_width :], axis=0, dtype=jnp.float32)
    grad_joined = jnp.einsum("tc,tf->cf", normed, d_joined, preferred_element_type=jnp.float32)
    d_normed = jnp.einsum("tf,cf->tc", d_joined, w_joined, preferred_element_type=jnp.float32)
    grad_gain = jnp.sum(d_normed * standard, axis=0)
    d_standard = d_normed * norm_gain.astype(jnp.float32)
    mean_grad = jnp.mean(d_standard, axis=1, keepdims=True)
    mean_proj = jnp.mean(d_standard * standard, axis=1, keepdims=True)
    input_grad = upstream + inverse_std * (d_standard - mean_grad - standard * mean_proj)
    grad_terms = (
        grad_joined,
        grad_out,
        grad_mlp,
        grad_gain,
        grad_bias_attn,
        grad_bias_mlp,
        grad_bias_out,
    )
    return (grad_terms, input_grad.astype(jnp.bfloat16))


def body(
    tokens, image_ids, cotangent, w_joined, w_out, w_mlp, norm_gain, bias_attn, bias_mlp, bias_out
):
    micro_count = tokens.shape[0]
    outputs = []
    input_grads = []
    grad_total = None
    for micro_index in range(micro_count):
        forward_weights = (
            lax.all_gather(w_joined, "wide", axis=0, tiled=True),
            lax.all_gather(w_out, "wide", axis=0, tiled=True),
            lax.all_gather(w_mlp, "wide", axis=0, tiled=True),
            lax.all_gather(norm_gain, "wide", axis=0, tiled=True),
            lax.all_gather(bias_attn, "wide", axis=0, tiled=True),
            lax.all_gather(bias_mlp, "wide", axis=0, tiled=True),
            lax.all_gather(bias_out, "wide", axis=0, tiled=True),
        )
        saved_state, output = forward_block(
            tokens[micro_index], image_ids[micro_index], forward_weights
        )
        backward_weights = (
            lax.all_gather(w_joined, "wide", axis=0, tiled=True),
            lax.all_gather(w_out, "wide", axis=0, tiled=True),
            lax.all_gather(w_mlp, "wide", axis=0, tiled=True),
            lax.all_gather(norm_gain, "wide", axis=0, tiled=True),
            lax.all_gather(bias_attn, "wide", axis=0, tiled=True),
            lax.all_gather(bias_mlp, "wide", axis=0, tiled=True),
            lax.all_gather(bias_out, "wide", axis=0, tiled=True),
        )
        grad_terms, input_grad = backward_block(
            saved_state, cotangent[micro_index], backward_weights
        )
        if grad_total is None:
            grad_total = grad_terms
        else:
            grad_total = jax.tree.map(jnp.add, grad_total, grad_terms)
        outputs.append(output)
        input_grads.append(input_grad)
    grad_total = (
        lax.psum_scatter(grad_total[0], "wide", scatter_dimension=0, tiled=True),
        lax.psum_scatter(grad_total[1], "wide", scatter_dimension=0, tiled=True),
        lax.psum_scatter(grad_total[2], "wide", scatter_dimension=0, tiled=True),
        lax.psum_scatter(grad_total[3], "wide", scatter_dimension=0, tiled=True),
        lax.psum_scatter(grad_total[4], "wide", scatter_dimension=0, tiled=True),
        lax.psum_scatter(grad_total[5], "wide", scatter_dimension=0, tiled=True),
        lax.psum_scatter(grad_total[6], "wide", scatter_dimension=0, tiled=True),
    )
    summed = lax.psum(
        (
            grad_total[0],
            grad_total[1],
            grad_total[2],
            grad_total[3],
            grad_total[4],
            grad_total[5],
            grad_total[6],
        ),
        "narrow",
    )
    return (
        jnp.stack(outputs),
        jnp.stack(input_grads),
        summed[0],
        summed[1],
        summed[2],
        summed[3],
        summed[4],
        summed[5],
        summed[6],
    )


def solution(mesh):
    placed = (
        P(None, ("narrow", "wide"), None),
        P(None, ("narrow", "wide")),
        P(None, ("narrow", "wide"), None),
        P("wide", None),
        P("wide", None),
        P("wide", None),
        P("wide"),
        P("wide"),
        P("wide"),
        P("wide"),
    )
    return jax.shard_map(
        body,
        mesh=mesh,
        in_specs=placed,
        out_specs=(
            P(None, ("narrow", "wide"), None),
            P(None, ("narrow", "wide"), None),
            P("wide", None),
            P("wide", None),
            P("wide", None),
            P("wide"),
            P("wide"),
            P("wide"),
            P("wide"),
        ),
        check_vma=False,
    )
```

profile of v0, /device:TPU:0, one launch (start us, length us, event | category | flops | bytes accessed | tf_op | source)
XLA Modules:
  0.0 634.2 jit_solution(8152209839163728400)
XLA Ops:
  9.5 1.3 fusion.131
  13.5 1.6 convert_reduce_fusion.5
  15.2 2.0 fusion.57
  20.6 63.7 %all-reduce.11 = (bf16[3072]{0:T(1024)(128)(2,1)S(1)}, bf16[1536]{0:T(1024)(128)(2,1)S(1)}, bf16[768]{0:T(1024)(128)(2,1)S(1)}, bf16[768]{0:T(1024)(128)(2,1)}) all-reduce(bf16[3072]{0:T(1024)(128)(2,1)S(1)} %dynamic-update-slice.2, bf16[1536]{0:T(1024)(128)(2,1)S(1)} %dynamic-update-slice.1, ...), channel_id=1, replica_groups=mesh['narrow'=2,'wide'=16] {'wide'}, use_global_device_ids=true, to_apply=%add.2 | all-reduce | flops 6144 | bytes 24576
  85.5 2.9 convolution_convert_fusion
  88.4 1.2 copy.86
  89.6 37.3 %all-gather.4.cloned.1.call-done = bf16[768,5376]{1,0:T(8,128)(2,1)} async-done(((bf16[48,5376]{1,0:T(8,128)(2,1)}), bf16[768,5376]{1,0:T(8,128)(2,1)}) %all-gather.4.cloned.1.call-update) | async-done | bytes 8257552 | tf_op jit(solution)/shard_map/all_gather | solution.py:167
  127.0 10.7 %fusion.132 = (bf16[512,5376]{1,0:T(8,128)(2,1)S(1)}, f32[512,5376]{1,0:T(8,128)}) fusion(f32[5376]{0:T(1024)S(1)} %maximum_convert_fusion, bf16[768,5376]{1,0:T(8,128)(2,1)} %all-gather.4.cloned.1.call-done, f32[512]{0:T(512)S(1)} %add_rsqrt_fusion, f32[512]{0:T(512)S(1)} %get-tuple-element.71, f32[768]{0:T(1024)S(1)} %convert_element_type.130, ...), kind=kOutput, calls=%fused_computation.179 | convolution fusion | flops 4235329536 | bytes 25591808 | tf_op jit(solution)/shard_map/dot_general | solution.py:46
  137.6 1.3 fusion.128
  139.2 1.4 copy.76
  140.6 2.3 copy.75
  142.9 10.8 %fusion.133 = (bf16[512,5376]{1,0:T(8,128)(2,1)S(1)}, f32[512,5376]{1,0:T(8,128)}) fusion(f32[5376]{0:T(1024)S(1)} %maximum_convert_fusion, bf16[768,5376]{1,0:T(8,128)(2,1)} %all-gather.4.cloned.1.call-done, f32[768]{0:T(1024)S(1)} %convert_element_type.130, f32[512]{0:T(512)S(1)} %add_rsqrt_fusion.1, f32[512]{0:T(512)S(1)} %get-tuple-element.72, ...), kind=kOutput, calls=%fused_computation.180 | convolution fusion | flops 4235329536 | bytes 25591808 | tf_op jit(solution)/shard_map/dot_general | solution.py:46
  153.7 1.3 fusion.127
  155.3 1.4 copy.72
  156.7 2.3 copy.71
  159.0 2.1 fusion.28
  161.1 2.6 fusion
  163.7 2.0 copy-done
  165.7 5.3 fusion.73
  171.0 2.2 fusion.90
  173.2 2.1 fusion.29
  175.3 3.7 fusion.1
  179.8 4.9 fusion.72
  185.6 2.2 convolution_add_fusion.4
  187.9 3.2 convolution_convert_fusion.1
  191.1 2.3 copy.79
  194.2 9.1 %fusion.69 = bf16[12,64,512]{2,1,0:T(8,128)(2,1)} fusion(bf16[512,12,64]{0,2,1:T(8,128)(2,1)} %bitcast.222, f32[12,512]{1,0:T(8,128)S(1)} %log_add_fusion, f32[12,512,512]{1,2,0:T(8,128)} %copy-done.1, pred[512,512]{0,1:T(8,128)(4,1)} %broadcast_compare_fusion), kind=kOutput, calls=%fused_computation.114 | convolution fusion | flops 415629312 | bytes 14442496 | tf_op jit(solution)/shard_map/hqk,qhe->khe/dot_general | solution.py:111
  203.4 2.3 copy.92
  205.7 6.6 %fusion.88 = f32[3072,768]{1,0:T(8,128)S(1)} fusion(bf16[2,512,768]{2,1,0:T(8,128)(2,1)} %param.12, f32[512,5376]{1,0:T(8,128)} %get-tuple-element.59), kind=kOutput, calls=%fused_computation.131 | convolution fusion | flops 2430074880 | bytes 16515072 | tf_op jit(solution)/shard_map/tf,td->fd/dot_general | solution.py:101
  212.3 10.0 %convolution_add_fusion.3 = f32[3072,768]{1,0:T(8,128)} fusion(f32[3072,768]{1,0:T(8,128)S(1)} %fusion.88, bf16[2,512,768]{2,1,0:T(8,128)(2,1)S(1)} %copy-done.11, f32[512,5376]{1,0:T(8,128)} %get-tuple-element.55), kind=kOutput, calls=%fused_computation.53 | convolution fusion | flops 2432434176 | bytes 25952256 | tf_op jit(solution)/shard_map/tf,td->fd/dot_general | solution.py:101
  222.4 9.6 %multiply_reduce_fusion = (f32[12,512]{1,0:T(8,128)S(1)}, f32[12,512,512]{1,2,0:T(8,128)S(1)}) fusion(f32[12,512]{1,0:T(8,128)S(1)} %log_add_fusion, f32[12,512,512]{1,2,0:T(8,128)} %copy-done.1, pred[512,512]{0,1:T(8,128)(4,1)} %broadcast_compare_fusion, bf16[512,12,64]{0,2,1:T(8,128)(2,1)} %bitcast.223, bf16[512,12,64]{0,2,1:T(8,128)(2,1)} %bitcast.227), kind=kOutput, calls=%fused_computation.1 | convolution fusion | flops 418375680 | bytes 27049984 | tf_op jit(solution)/shard_map/qhe,khe->hqk/dot_general | solution.py:112
  232.0 7.3 %multiply_convert_fusion = bf16[12,512,512]{1,2,0:T(8,128)(2,1)S(1)} fusion(f32[12,512,512]{1,2,0:T(8,128)S(1)} %get-tuple-element.65, f32[12,512]{1,0:T(8,128)S(1)} %get-tuple-element.64, f32[12,512]{1,0:T(8,128)S(1)} %log_add_fusion, f32[12,512,512]{1,2,0:T(8,128)} %copy-done.1, pred[512,512]{0,1:T(8,128)(4,1)S(1)} %copy-done.8), kind=kLoop, calls=%fused_computation | loop fusion | flops 18874368 | bytes 31768576 | tf_op jit(solution)/shard_map/convert_element_type | solution.py:114
  239.3 2.6 copy-done.2
  241.9 2.9 multiply_convert_fusion.2
  244.8 2.3 copy.91
  247.1 3.9 multiply_convert_fusion.3
  252.2 8.9 %fusion.66 = bf16[12,64,512]{2,1,0:T(8,128)(2,1)} fusion(bf16[512,12,64]{0,2,1:T(8,128)(2,1)} %bitcast.228, f32[12,512]{1,0:T(8,128)S(1)} %log_add_fusion.1, f32[12,512,512]{1,2,0:T(8,128)} %copy-done, pred[512,512]{0,1:T(8,128)(4,1)S(1)} %broadcast_compare_fusion.1), kind=kOutput, calls=%fused_computation.113 | convolution fusion | flops 415629312 | bytes 14442496 | tf_op jit(solution)/shard_map/hqk,qhe->khe/dot_general | solution.py:111
  261.1 2.4 copy.85
  263.5 8.5 %multiply_reduce_fusion.1 = (f32[12,512]{1,0:T(8,128)S(1)}, f32[12,512,512]{1,2,0:T(8,128)S(1)}) fusion(f32[12,512]{1,0:T(8,128)S(1)} %log_add_fusion.1, f32[12,512,512]{1,2,0:T(8,128)} %copy-done, pred[512,512]{0,1:T(8,128)(4,1)S(1)} %broadcast_compare_fusion.1, bf16[512,12,64]{0,2,1:T(8,128)(2,1)} %bitcast.229, bf16[512,12,64]{0,2,1:T(8,128)(2,1)S(1)} %bitcast.225), kind=kOutput, calls=%fused_computation.4 | convolution fusion | flops 418375680 | bytes 27049984 | tf_op jit(solution)/shard_map/qhe,khe->hqk/dot_general | solution.py:112
  272.0 8.0 %multiply_convert_fusion.1 = bf16[12,512,512]{1,2,0:T(8,128)(2,1)S(1)} fusion(f32[12,512,512]{1,2,0:T(8,128)S(1)} %get-tuple-element.63, f32[12,512]{1,0:T(8,128)S(1)} %get-tuple-element.62, f32[12,512]{1,0:T(8,128)S(1)} %log_add_fusion.1, f32[12,512,512]{1,2,0:T(8,128)} %copy-done, pred[512,512]{0,1:T(8,128)(4,1)S(1)} %broadcast_compare_fusion.1), kind=kLoop, calls=%fused_computation.3 | loop fusion | flops 18874368 | bytes 31768576 | tf_op jit(solution)/shard_map/convert_element_type | solution.py:114
  280.0 2.7 copy-done.3
  282.7 2.0 multiply_convert_fusion.4
  284.7 1.2 copy.84
  285.8 3.9 multiply_convert_fusion.5
  291.0 10.1 %convert_reduce_fusion.1 = (f32[3072]{0:T(1024)S(1)}, bf16[512,3072]{1,0:T(8,128)(2,1)S(1)}) fusion(f32[512,5376]{1,0:T(8,128)} %get-tuple-element.59, bf16[3072,768]{1,0:T(8,128)(2,1)} %all-gather.8.cloned.1.call-done, bf16[2,512,768]{2,1,0:T(8,128)(2,1)} %param.12), kind=kOutput, calls=%fused_computation.42 | convolution fusion | flops 2456810496 | bytes 14954496 | tf_op jit(solution)/shard_map/td,fd->tf/dot_general | solution.py:102
  301.2 9.0 %fusion.77 = f32[768,5376]{1,0:T(8,128)} fusion(bf16[512,3072]{1,0:T(8,128)(2,1)S(1)} %get-tuple-element.68, bf16[512,768]{1,0:T(8,128)(2,1)S(1)} %copy-done.21, bf16[512,768]{1,0:T(8,128)(2,1)S(1)} %copy-done.23, bf16[512,768]{1,0:T(8,128)(2,1)S(1)} %copy-done.25, f32[768]{0:T(1024)S(1)} %copy-done.18, f32[512]{0:T(512)S(1)} %copy-done.38, ...), kind=kOutput, calls=%fused_computation.122 | convolution fusion | flops 4251844608 | bytes 22814720 | tf_op jit(solution)/shard_map/tc,tf->cf/dot_general | solution.py:139
  310.2 10.2 %convert_reduce_fusion = (f32[3072]{0:T(1024)S(1)}, bf16[512,3072]{1,0:T(8,128)(2,1)}) fusion(f32[512,5376]{1,0:T(8,128)} %get-tuple-element.55, bf16[3072,768]{1,0:T(8,128)(2,1)S(1)} %copy-done.40, bf16[2,512,768]{2,1,0:T(8,128)(2,1)S(1)} %copy-done.12), kind=kOutput, calls=%fused_computation.41 | convolution fusion | flops 2456810496 | bytes 14954496 | tf_op jit(solution)/shard_map/td,fd->tf/dot_general | solution.py:102
  320.4 13.4 %convolution_add_fusion = f32[768,5376]{1,0:T(8,128)} fusion(f32[768,5376]{1,0:T(8,128)} %fusion.77, bf16[512,3072]{1,0:T(8,128)(2,1)} %get-tuple-element.70, bf16[512,768]{1,0:T(8,128)(2,1)S(1)} %copy-done.15, bf16[512,768]{1,0:T(8,128)(2,1)S(1)} %copy-done.16, bf16[512,768]{1,0:T(8,128)(2,1)} %copy.90, f32[512]{0:T(512)S(1)} %copy-done.33, ...), kind=kOutput, calls=%fused_computation.14 | convolution fusion | flops 4255973376 | bytes 39329792 | tf_op jit(solution)/shard_map/tc,tf->cf/dot_general | solution.py:139
  335.9 1.3 convert_reduce_fusion.6
  337.4 1.3 convert_reduce_fusion.8
  339.0 9.4 %fusion.76 = f32[512,768]{1,0:T(8,128)S(1)} fusion(bf16[768,5376]{1,0:T(8,128)(2,1)} %all-gather.4.cloned.1.call-done, bf16[512,3072]{1,0:T(8,128)(2,1)} %get-tuple-element.70, bf16[512,768]{1,0:T(8,128)(2,1)} %copy.92, bf16[512,768]{1,0:T(8,128)(2,1)} %copy.91, bf16[512,768]{1,0:T(8,128)(2,1)} %copy.90), kind=kOutput, calls=%fused_computation.121 | convolution fusion | flops 4249878528 | bytes 15335424 | tf_op jit(solution)/shard_map/tf,cf->tc/dot_general | solution.py:140
  348.5 9.2 %fusion.56 = (f32[768]{0:T(1024)S(1)}, f32[512]{0:T(512)S(1)}, f32[512]{0:T(512)S(1)}, f32[768]{0:T(1024)S(1)}, f32[512]{0:T(512)S(1)}, /*index=5*/f32[512]{0:T(512)S(1)}, f32[512,768]{1,0:T(8,128)S(1)}) fusion(f32[512]{0:T(512)S(1)} %copy-done.38, f32[512]{0:T(512)S(1)} %copy-done.36, bf16[2,512,768]{2,1,0:T(8,128)(2,1)S(1)} %copy-done.5, ...), kind=kOutput, calls=%fused_computation.91 | convolution fusion | flops 4256952832 | bytes 18506752 | tf_op jit(solution)/shard_map/tf,cf->tc/dot_general | solution.py:140
  357.7 6.1 fusion.125
  363.9 1.7 fusion.74
  365.6 1.6 convert_reduce_fusion.2
  367.3 177.5 %reduce-scatter.4.cloned.1.call-done = f32[48,5376]{1,0:T(8,128)} async-done(((f32[768,5376]{1,0:T(8,128)}), f32[48,5376]{1,0:T(8,128)}) %reduce-scatter.4.cloned.1.call-update) | async-done | bytes 1032208 | tf_op jit(solution)/shard_map/reduce_scatter | solution.py:197
  544.8 59.5 %all-reduce.8 = (f32[768]{0:T(1024)S(1)}, f32[1536]{0:T(1024)S(1)}, f32[3072]{0:T(1024)S(1)}, f32[768]{0:T(1024)S(1)}) all-reduce(f32[768]{0:T(1024)S(1)} %add.168, f32[1536]{0:T(1024)S(1)} %maximum_add_fusion, f32[3072]{0:T(1024)S(1)} %add.170, f32[768]{0:T(1024)S(1)} %add.171), channel_id=5, replica_groups=mesh['narrow'=2,'wide'=16] {'wide'}, use_global_device_ids=true, to_apply=%region_22.23.clone | all-reduce | flops 6144 | bytes 49152
  604.7 5.5 all-reduce.9
  610.2 7.5 %fusion.122 = f32[512,768]{1,0:T(8,128)S(1)} fusion(bf16[3072,768]{1,0:T(8,128)(2,1)} %all-gather.8.cloned.1.call-done, f32[512,5376]{1,0:T(8,128)} %get-tuple-element.59), kind=kOutput, calls=%fused_computation.172 | convolution fusion | flops 2430074880 | bytes 12582912 | tf_op jit(solution)/shard_map/dot_general | solution.py:63
  618.8 1.3 pad_maximum_fusion.2
  620.1 1.3 pad_maximum_fusion.3
  621.4 2.2 copy.108
  623.6 1.6 copy.109
  625.2 1.9 copy.110
  (149 shorter events, 15.1 us)
Async XLA Ops:
  7.2 119.8 %copy-start.4 = (bf16[2,512,768]{2,1,0:T(8,128)(2,1)S(1)}, bf16[2,512,768]{2,1,0:T(8,128)(2,1)}, u32[]{:S(2)}) copy-start(bf16[2,512,768]{2,1,0:T(8,128)(2,1)} %param.10) | copy-start | bytes 4718596
  7.2 78.3 %all-gather.6.cloned.1.call-start = ((), (), s32[]{:S(2)}) async-start(), calls=%async_computation.4 | async-start | bytes 1253376 | tf_op jit(solution)/shard_map/all_gather | solution.py:168
  7.9 119.1 %all-gather.4.cloned.1.call-start = ((), (), s32[]{:S(2)}) async-start(), calls=%async_computation.3 | async-start | bytes 8773632 | tf_op jit(solution)/shard_map/all_gather | solution.py:167
  8.7 282.3 %all-gather.8.cloned.1.call-start = ((), (), s32[]{:S(2)}) async-start(), calls=%async_computation.5 | async-start | bytes 5013504 | tf_op jit(solution)/shard_map/all_gather | solution.py:169
  9.4 357.9 %reduce-scatter.6.cloned.1.call-start = ((), (), s32[]{:S(2)}) async-start(), calls=%async_computation.7 | async-start | bytes 2506752 | tf_op jit(solution)/shard_map/reduce_scatter | solution.py:198
  15.2 122.5 %copy-start.30 = (f32[512]{0:T(512)}, f32[512]{0:T(512)S(1)}, u32[]{:S(2)}) copy-start(f32[512]{0:T(512)S(1)} %get-tuple-element.71) | copy-start | bytes 6148
  15.2 127.8 %copy-start.35 = (f32[512]{0:T(512)}, f32[512]{0:T(512)S(1)}, u32[]{:S(2)}) copy-start(f32[512]{0:T(512)S(1)} %get-tuple-element.72) | copy-start | bytes 6148
  17.1 125.8 %copy-start.37 = (f32[512]{0:T(512)}, f32[512]{0:T(512)S(1)}, u32[]{:S(2)}) copy-start(f32[512]{0:T(512)S(1)} %add_rsqrt_fusion.1) | copy-start | bytes 6148
  17.2 120.5 %copy-start.32 = (f32[512]{0:T(512)}, f32[512]{0:T(512)S(1)}, u32[]{:S(2)}) copy-start(f32[512]{0:T(512)S(1)} %add_rsqrt_fusion) | copy-start | bytes 6148
  84.3 58.6 %copy-start.17 = (f32[768]{0:T(1024)}, f32[768]{0:T(1024)S(1)}, u32[]{:S(2)}) copy-start(f32[768]{0:T(1024)S(1)} %convert_element_type.130) | copy-start | bytes 9220
  161.1 4.6 copy-start
  165.7 5.3 copy-start.9
  165.7 7.5 %copy-start.7 = (pred[512,512]{0,1:T(8,128)(4,1)S(1)}, pred[512,512]{0,1:T(8,128)(4,1)}, u32[]{:S(2)}) copy-start(pred[512,512]{0,1:T(8,128)(4,1)} %broadcast_compare_fusion) | copy-start | bytes 786436
  171.0 4.3 copy-start.28
  175.2 4.5 copy-start.1
  179.0 5.7 copy-start.34
  179.8 5.8 copy-start.6
  179.8 5.8 copy-start.10
  184.7 0.9 copy-start.19
  187.8 179.5 %reduce-scatter.8.cloned.1.call-start = ((), (), s32[]{:S(2)}) async-start(), calls=%async_computation.8 | async-start | bytes 10027008 | tf_op jit(solution)/shard_map/reduce_scatter | solution.py:199
  205.7 6.6 %copy-start.11 = (bf16[2,512,768]{2,1,0:T(8,128)(2,1)S(1)}, bf16[2,512,768]{2,1,0:T(8,128)(2,1)}, u32[]{:S(2)}) copy-start(bf16[2,512,768]{2,1,0:T(8,128)(2,1)} %param.12) | copy-start | bytes 4718596
  222.3 322.5 %reduce-scatter.4.cloned.1.call-start = ((), (), s32[]{:S(2)}) async-start(), calls=%async_computation.6 | async-start | bytes 17547264 | tf_op jit(solution)/shard_map/reduce_scatter | solution.py:197
  222.4 9.6 %copy-start.8 = (pred[512,512]{0,1:T(8,128)(4,1)S(1)}, pred[512,512]{0,1:T(8,128)(4,1)}, u32[]{:S(2)}) copy-start(pred[512,512]{0,1:T(8,128)(4,1)} %broadcast_compare_fusion) | copy-start | bytes 786436
  239.3 2.6 copy-start.2
  252.2 11.3 %copy-start.14 = (bf16[512,768]{0,1:T(8,128)(2,1)S(1)}, bf16[512,768]{0,1:T(8,128)(2,1)}, u32[]{:S(2)}) copy-start(bf16[512,768]{0,1:T(8,128)(2,1)} %copy.71) | copy-start | bytes 2359300
  280.0 2.7 copy-start.3
  290.9 10.2 %copy-start.5 = (bf16[2,512,768]{2,1,0:T(8,128)(2,1)S(1)}, bf16[2,512,768]{2,1,0:T(8,128)(2,1)}, u32[]{:S(2)}) copy-start(bf16[2,512,768]{2,1,0:T(8,128)(2,1)} %param.10) | copy-start | bytes 4718596
  290.9 10.2 %copy-start.18 = (f32[768]{0:T(1024)S(1)}, f32[768]{0:T(1024)}, u32[]{:S(2)}) copy-start(f32[768]{0:T(1024)} %copy-done.17) | copy-start | bytes 9220
  290.9 10.2 %copy-start.36 = (f32[512]{0:T(512)S(1)}, f32[512]{0:T(512)}, u32[]{:S(2)}) copy-start(f32[512]{0:T(512)} %copy-done.35) | copy-start | bytes 6148
  290.9 10.2 %copy-start.38 = (f32[512]{0:T(512)S(1)}, f32[512]{0:T(512)}, u32[]{:S(2)}) copy-start(f32[512]{0:T(512)} %copy-done.37) | copy-start | bytes 6148
  291.0 10.2 %copy-start.21 = (bf16[512,768]{1,0:T(8,128)(2,1)S(1)}, bf16[512,768]{1,0:T(8,128)(2,1)}, u32[]{:S(2)}) copy-start(bf16[512,768]{1,0:T(8,128)(2,1)} %copy.85) | copy-start | bytes 2359300
  291.0 10.2 %copy-start.23 = (bf16[512,768]{1,0:T(8,128)(2,1)S(1)}, bf16[512,768]{1,0:T(8,128)(2,1)}, u32[]{:S(2)}) copy-start(bf16[512,768]{1,0:T(8,128)(2,1)} %copy.84) | copy-start | bytes 2359300
  291.0 10.2 %copy-start.25 = (bf16[512,768]{1,0:T(8,128)(2,1)S(1)}, bf16[512,768]{1,0:T(8,128)(2,1)}, u32[]{:S(2)}) copy-start(bf16[512,768]{1,0:T(8,128)(2,1)} %copy.83) | copy-start | bytes 2359300
  301.1 9.1 %copy-start.43 = (bf16[512,3072]{1,0:T(8,128)(2,1)}, bf16[512,3072]{1,0:T(8,128)(2,1)S(1)}, u32[]{:S(2)}) copy-start(bf16[512,3072]{1,0:T(8,128)(2,1)S(1)} %get-tuple-element.68) | copy-start | bytes 9437188
  301.2 9.0 %copy-start.12 = (bf16[2,512,768]{2,1,0:T(8,128)(2,1)S(1)}, bf16[2,512,768]{2,1,0:T(8,128)(2,1)}, u32[]{:S(2)}) copy-start(bf16[2,512,768]{2,1,0:T(8,128)(2,1)} %param.12) | copy-start | bytes 4718596
  301.2 9.0 %copy-start.40 = (bf16[3072,768]{1,0:T(8,128)(2,1)S(1)}, bf16[3072,768]{1,0:T(8,128)(2,1)}, u32[]{:S(2)}) copy-start(bf16[3072,768]{1,0:T(8,128)(2,1)} %all-gather.8.cloned.1.call-done) | copy-start | bytes 14155780
  310.2 10.2 %copy-start.15 = (bf16[512,768]{1,0:T(8,128)(2,1)S(1)}, bf16[512,768]{1,0:T(8,128)(2,1)}, u32[]{:S(2)}) copy-start(bf16[512,768]{1,0:T(8,128)(2,1)} %copy.92) | copy-start | bytes 2359300
  310.2 10.2 %copy-start.16 = (bf16[512,768]{1,0:T(8,128)(2,1)S(1)}, bf16[512,768]{1,0:T(8,128)(2,1)}, u32[]{:S(2)}) copy-start(bf16[512,768]{1,0:T(8,128)(2,1)} %copy.91) | copy-start | bytes 2359300
  310.2 10.2 %copy-start.31 = (f32[512]{0:T(512)S(1)}, f32[512]{0:T(512)}, u32[]{:S(2)}) copy-start(f32[512]{0:T(512)} %copy-done.30) | copy-start | bytes 6148
  310.2 10.2 %copy-start.33 = (f32[512]{0:T(512)S(1)}, f32[512]{0:T(512)}, u32[]{:S(2)}) copy-start(f32[512]{0:T(512)} %copy-done.32) | copy-start | bytes 6148
  333.9 2.0 copy-start.39
  333.9 287.5 %all-reduce.14.cloned.1.call-start = ((), (), s32[]{:S(2)}) async-start(), calls=%async_computation.9 | async-start | bytes 3538944 | tf_op jit(solution)/shard_map/psum | solution.py:205
  338.9 9.5 %copy-start.22 = (bf16[512,768]{1,0:T(8,128)(2,1)S(1)}, bf16[512,768]{1,0:T(8,128)(2,1)}, u32[]{:S(2)}) copy-start(bf16[512,768]{1,0:T(8,128)(2,1)} %copy.85) | copy-start | bytes 2359300
  338.9 9.5 %copy-start.24 = (bf16[512,768]{1,0:T(8,128)(2,1)S(1)}, bf16[512,768]{1,0:T(8,128)(2,1)}, u32[]{:S(2)}) copy-start(bf16[512,768]{1,0:T(8,128)(2,1)} %copy.84) | copy-start | bytes 2359300
  339.0 9.5 %copy-start.26 = (bf16[512,768]{1,0:T(8,128)(2,1)S(1)}, bf16[512,768]{1,0:T(8,128)(2,1)}, u32[]{:S(2)}) copy-start(bf16[512,768]{1,0:T(8,128)(2,1)} %copy.83) | copy-start | bytes 2359300
  339.0 18.7 %slice-start = ((s8[4718592]{0:T(1024)(128)(4,1)}), s8[4194304]{0:T(1024)(128)(4,1)S(1)}, s32[]{:S(2)}) async-start(s8[4718592]{0:T(1024)(128)(4,1)} %bitcast.240), calls=%async_computation.10 | async-start | bytes 8388608
  348.5 9.2 %slice-start.1 = ((s8[4718592]{0:T(1024)(128)(4,1)}), s8[524288]{0:T(1024)(128)(4,1)S(1)}, s32[]{:S(2)}) async-start(s8[4718592]{0:T(1024)(128)(4,1)} %bitcast.240), calls=%async_computation.11 | async-start | bytes 1048576
  357.7 6.1 copy-start.20
  357.7 6.1 copy-start.41
  363.9 1.8 copy-start.13
  610.2 7.5 %copy-start.29 = (bf16[12,64,512]{2,1,0:T(8,128)(2,1)S(1)}, bf16[12,64,512]{2,1,0:T(8,128)(2,1)}, u32[]{:S(2)}) copy-start(bf16[12,64,512]{2,1,0:T(8,128)(2,1)} %copy-done.28) | copy-start | bytes 2359300
  610.2 7.5 %copy-start.42 = (bf16[768,768]{1,0:T(8,128)(2,1)S(1)}, bf16[768,768]{1,0:T(8,128)(2,1)}, u32[]{:S(2)}) copy-start(bf16[768,768]{1,0:T(8,128)(2,1)} %all-gather.6.cloned.1.call-done) | copy-start | bytes 3538948
  617.7 1.1 copy-start.27
Sparse Core Ops, SparseCore 0:
  10.3 41.2 all-gather.5
  53.9 73.0 all-gather.3
  129.3 51.4 all-gather.7
  188.0 61.4 reduce-scatter.5
  253.9 110.4 reduce-scatter.7
  368.5 176.2 reduce-scatter.3
  547.3 55.1 all-reduce.13
where the time goes:
time: 642 us; the launch traced here: 634 us
  waiting for transfers between devices  217 us (34%)
  matrix products  189 us (29%)
  blocking collectives  129 us (20%)
  local copies, waits for them, and re-layouts  45.4 us (7%)
  other arithmetic  34.4 us (5%)
  between operations  19.1 us (3%)
    reduce_scatter x1, waiting for transfers between devices, body(): lax.psum_scatter(grad_total[0], 'wide', scatter_dimension=0, tiled=True)  177 us
    unnamed x2, blocking collectives  123 us
    all_gather x1, waiting for transfers between devices, body(): lax.all_gather(w_joined, 'wide', axis=0, tiled=True)  37.3 us
    dot_general x2, matrix products, backward_block(): jnp.einsum('tc,tf->cf', normed, d_joined, preferred_element_type=jnp.floa...  22.4 us
    dot_general x2, matrix products, forward_block(): jnp.dot(normed, w_joined, preferred_element_type=jnp.float32) + bias_full  21.4 us
    dot_general x2, matrix products, backward_block(): jnp.einsum('td,fd->tf', block_cot, w_mlp, preferred_element_type=jnp.floa...  20.3 us
    unnamed x109, local copies, waits for them, and re-layouts  20.1 us
    dot_general x2, matrix products, backward_block(): jnp.einsum('tf,cf->tc', d_joined, w_joined, preferred_element_type=jnp.fl...  18.6 us
  transfers between devices with their start and end apart: 7, of which 2 were waited for; matrix products, arithmetic and copies ran while one was open for 40% of the time, Pallas kernels for 0%

commit v1 on v0

v1 whole, which is shorter than its diff:
```python
import functools

import jax
import jax.numpy as jnp
from jax import lax
from jax.experimental import pallas as pl
from jax.experimental.pallas import tpu as pltpu
from jax.sharding import PartitionSpec as P

HEADS = 12
HEAD = 64
IMG = 196
EPS = 1e-06
GELU_C = 0.7978845608028654
GELU_A = 0.044715

F32 = jnp.float32
BF16 = jnp.bfloat16
HBM = pl.BlockSpec(memory_space=pltpu.HBM)
SMEM = pl.BlockSpec(memory_space=pltpu.SMEM)


def dot_nn(a, b):
    return lax.dot_general(a, b, (((1,), (0,)), ((), ())), preferred_element_type=F32)


def dot_nt(a, b):
    return lax.dot_general(a, b, (((1,), (1,)), ((), ())), preferred_element_type=F32)


def dot_tn(a, b):
    return lax.dot_general(a, b, (((0,), (0,)), ((), ())), preferred_element_type=F32)


def norm_rows(rows):
    rows = rows.astype(F32)
    mean = jnp.mean(rows, axis=1, keepdims=True)
    centered = rows - mean
    inv = lax.rsqrt(jnp.mean(centered * centered, axis=1, keepdims=True) + EPS)
    return centered * inv, inv


def attend(q_ref, k_ref, v_ref, da_ref, o_ref, dq_ref, dk_ref, dv_ref, start, rows, lo, hi, merge):
    win = pl.ds(start, rows)
    q2, k2, v2, da2 = q_ref[win, :], k_ref[win, :], v_ref[win, :], da_ref[win, :]
    lane = lax.broadcasted_iota(jnp.int32, (rows, 128), 1)
    masked = lo > 0 or hi < rows
    step = 256 if rows == 512 else rows
    outs, dqs = [], []
    dk = jnp.zeros((rows, 128), F32)
    dv = jnp.zeros((rows, 128), F32)
    zero = jnp.zeros((), BF16)
    heads = []
    for h in range(2):
        keep = (lane < 64) if h == 0 else (lane >= 64)
        heads.append([jnp.where(keep, t, zero) for t in (q2, k2, v2, da2)])
    for at in range(0, rows, step):
        qs = slice(at, at + step)
        out = jnp.zeros((step, 128), F32)
        dq = jnp.zeros((step, 128), F32)
        for h in range(2):
            qh, kh, vh, dah = heads[h]
            s = dot_nt(k2, qh[qs])
            if masked:
                key = lax.broadcasted_iota(jnp.int32, (rows, step), 0)
                s = jnp.where((key >= lo) & (key < hi), s, -1e30)
            top = jnp.max(s, axis=0, keepdims=True)
            e = jnp.exp(s - top)
            total = jnp.sum(e, axis=0, keepdims=True)
            scale = 1.0 / total
            if masked:
                query = lax.broadcasted_iota(jnp.int32, (1, step), 1) + at
                scale = jnp.where((query >= lo) & (query < hi), scale, 0.0)
            p = e * scale
            pb = p.astype(BF16)
            dp = dot_nt(v2, dah[qs])
            inner = jnp.sum(p * dp, axis=0, keepdims=True)
            ds = (p * (dp - inner)).astype(BF16)
            out += dot_tn(pb, vh)
            dq += dot_tn(ds, kh)
            dv += dot_nn(pb, dah[qs])
            dk += dot_nn(ds, qh[qs])
        outs.append(out)
        dqs.append(dq * 0.125)
    for ref, val in ((o_ref, outs), (dq_ref, dqs), (dk_ref, [dk]), (dv_ref, [dv])):
        val = val[0] if len(val) == 1 else jnp.concatenate(val, axis=0)
        val = val.astype(BF16)
        if merge:
            head, rest = pl.ds(start, merge), pl.ds(start + merge, rows - merge)
            ref[head, :] = ref[head, :] + val[:merge]
            ref[rest, :] = val[merge:]
        else:
            ref[win, :] = val


def call(kernel, name, grid, ins, outs, scratch, operands, flops, moved):
    return pl.pallas_call(
        kernel,
        name=name,
        grid=grid,
        out_shape=[s for s, _ in outs],
        in_specs=ins,
        out_specs=[m for _, m in outs],
        scratch_shapes=scratch,
        compiler_params=pltpu.CompilerParams(
            vmem_limit_bytes=60 << 20, dimension_semantics=("arbitrary",) * len(grid)
        ),
        cost_estimate=pl.CostEstimate(flops=flops, bytes_accessed=moved, transcendentals=0),
    )(*operands)


def sds(shape, dtype=BF16):
    return jax.ShapeDtypeStruct(shape, dtype)


def fixed(shape):
    return pl.BlockSpec(shape, lambda *i: (0,) * len(shape), pipeline_mode=pl.Buffered(1))


def by_rows(rows, width):
    return pl.BlockSpec((rows, width), lambda i: (i, 0))


def by_tile(tokens, width):
    return pl.BlockSpec((None, tokens, width), lambda i: (i, 0, 0))


def square_loop(width, fn, rb=256):
    def step(i, c):
        fn(pl.multiple_of(i * rb, rb), rb)
        return c

    lax.fori_loop(0, width // rb, step, 0)


ROWS = 256


def project_kernel(load, n_w, *refs):
    scal, x_ref, cot_ref, vec_ref = refs[:4]
    xn, q, k, v, da = refs[4 + n_w : 9 + n_w]
    w, sem = refs[9 + n_w :]
    first = pl.program_id(0) == 0

    @pl.when(first)
    def _():
        load(scal, refs[4 : 4 + n_w], w, sem, (0, 1, 2, 3))

    standard, _ = norm_rows(x_ref[...])
    xr = (standard * vec_ref[0:1, :]).astype(BF16)
    xn[...] = xr

    @pl.when(first)
    def _():
        for i in range(4):
            whole_wait(w.at[i], sem.at[i])()

    q[...] = (dot_nn(xr, w[0]) + vec_ref[1:2, :]).astype(BF16) * jnp.asarray(0.125, BF16)
    k[...] = dot_nn(xr, w[1]).astype(BF16)
    v[...] = (dot_nn(xr, w[2]) + vec_ref[2:3, :]).astype(BF16)
    da[...] = dot_nt(cot_ref[...], w[3]).astype(BF16)


def project_call(scal, x, cot, vec, weights, load):
    tokens, width = x.shape
    return call(
        functools.partial(project_kernel, load, len(weights)),
        "project",
        (tokens // ROWS,),
        [SMEM, by_rows(ROWS, width), by_rows(ROWS, width), fixed(vec.shape)] + [HBM] * len(weights),
        [(sds(x.shape), by_rows(ROWS, width))] * 5,
        [pltpu.VMEM((4, width, width), BF16), pltpu.SemaphoreType.DMA((4,))],
        (scal, x, cot, vec, *weights),
        8 * tokens * width * width,
        16 << 20,
    )


def core_kernel(scal, q, k, v, da, o, dq, dk, dv):
    whole = scal[8 + pl.program_id(0)] == 0
    args = (q, k, v, da, o, dq, dk, dv)

    @pl.when(whole)
    def _():
        attend(*args, 0, 512, 0, 512, 0)

    @pl.when(jnp.logical_not(whole))
    def _():
        attend(*args, 0, 208, 0, IMG, 0)
        attend(*args, 192, 208, IMG - 192, 2 * IMG - 192, 16)
        attend(*args, 384, 128, 2 * IMG - 384, 128, 16)


def core_call(scal, q, k, v, da):
    tokens, width = q.shape
    spec = pl.BlockSpec((512, 128), lambda b, i: (b, i))
    return call(
        core_kernel,
        "core",
        (tokens // 512, width // 128),
        [SMEM] + [spec] * 4,
        [(sds(q.shape), spec)] * 4,
        [],
        (scal, q, k, v, da),
        20 << 30,
        12 << 20,
    )


def attn_grad_kernel(store, n_g, *refs):
    scal = refs[0]
    g_refs = refs[7 : 7 + n_g]
    sums = refs[7 + n_g]
    xn, o, dq, dk, dv, cot, g, isem, sem = refs[8 + n_g :]
    tokens, width = xn.shape
    order = ((1, xn), (3, dq), (4, dk), (5, dv), (2, o), (6, cot))
    copies = [pltpu.make_async_copy(refs[i], ref, isem.at[j]) for j, (i, ref) in enumerate(order)]
    for cp in copies:
        cp.start()
    ones = jnp.ones((8, tokens), BF16)
    copies[0].wait()
    for b, rhs in enumerate((dq, dk, dv)):
        copies[1 + b].wait()

        def grads(at, n, b=b, rhs=rhs):
            g[b, pl.ds(at, n), :] = dot_tn(xn[:, pl.ds(at, n)], rhs[...]).astype(BF16)

        square_loop(width, grads)
    copies[4].wait()
    copies[5].wait()

    def grads(at, n):
        g[3, pl.ds(at, n), :] = dot_tn(o[:, pl.ds(at, n)], cot[...]).astype(BF16)

    square_loop(width, grads)
    done = store(scal, g, g_refs, sem)
    sums[0:1, :] = dot_nn(ones, dq[...])[0:1]
    sums[1:2, :] = dot_nn(ones, dv[...])[0:1]
    sums[2:3, :] = dot_nn(ones, cot[...])[0:1]
    done()


def attn_grad_call(scal, xn, o, dq, dk, dv, cot, store, g_shapes):
    tokens, width = xn.shape
    n_g = len(g_shapes)
    return call(
        functools.partial(attn_grad_kernel, store, n_g),
        "attn_grad",
        (1,),
        [SMEM] + [HBM] * 6,
        [(s, HBM) for s in g_shapes] + [(sds((8, width), F32), fixed((8, width)))],
        [pltpu.VMEM((tokens, width), BF16)] * 6
        + [pltpu.VMEM((4, width, width), BF16), pltpu.SemaphoreType.DMA((6,)), pltpu.SemaphoreType.DMA((n_g,))],
        (scal, xn, o, dq, dk, dv, cot),
        8 * tokens * width * width,
        14 << 20,
    )


def gelu_parts(u):
    t = jnp.tanh(GELU_C * (u + GELU_A * u * u * u))
    half = 0.5 * (1.0 + t)
    act = u * half
    grad = half + (0.5 * GELU_C) * u * (1.0 - t * t) * (1.0 + (3.0 * GELU_A) * u * u)
    return act, grad

def tile_of(t, width):
    return pl.ds(pl.multiple_of(t * width, 128), width)


def wait_tile(w, sem, t, width):
    whole_wait(w.at[tile_of(t, width), :], sem.at[t])()


def up_kernel(load, n_w, *refs):
    scal, xn, bias = refs[:3]
    act, gp = refs[3 + n_w : 5 + n_w]
    w, sem = refs[5 + n_w :]
    tokens, width = xn.shape
    t = pl.program_id(0)

    @pl.when(t == 0)
    def _():
        load(scal, refs[3 : 3 + n_w], w, sem)

    wait_tile(w, sem, t, width)

    def up(at, n):
        r = pl.ds(at, n)
        u = dot_nn(xn[r, :], w[tile_of(t, width), :]) + bias[...]
        a, gr = gelu_parts(u)
        act[r, :] = a.astype(BF16)
        gp[r, :] = gr.astype(BF16)

    square_loop(tokens, up)


def up_call(scal, xn, bias, weights, load):
    tokens, width = xn.shape
    tiles = bias.shape[0]
    return call(
        functools.partial(up_kernel, load, len(weights)),
        "up",
        (tiles,),
        [SMEM, fixed(xn.shape), pl.BlockSpec((None, 1, width), lambda i: (i, 0, 0))] + [HBM] * len(weights),
        [(sds((tiles, tokens, width)), by_tile(tokens, width))] * 2,
        [pltpu.VMEM((tiles * width, width), BF16), pltpu.SemaphoreType.DMA((tiles,))],
        (scal, xn, bias.reshape(tiles, 1, width), *weights),
        2 * tiles * tokens * width * width,
        19 << 20,
    )


def down_grad_kernel(store, n_g, *refs):
    scal, act, cot = refs[:3]
    g_refs = refs[3 : 3 + n_g]
    g, sem = refs[3 + n_g :]
    tokens, width = cot.shape
    t = pl.program_id(0)

    def grad(at, n):
        g[pl.ds(pl.multiple_of(t * width + at, 128), n), :] = dot_tn(act[:, pl.ds(at, n)], cot[...]).astype(BF16)

    square_loop(width, grad)

    @pl.when(t == pl.num_programs(0) - 1)
    def _():
        store(scal, g, g_refs, sem)()


def down_grad_call(scal, act, cot, store, g_shapes):
    tiles, tokens, width = act.shape
    n_g = len(g_shapes)
    return call(
        functools.partial(down_grad_kernel, store, n_g),
        "down_grad",
        (tiles,),
        [SMEM, by_tile(tokens, width), fixed(cot.shape)],
        [(s, HBM) for s in g_shapes],
        [pltpu.VMEM((tiles * width, width), BF16), pltpu.SemaphoreType.DMA((n_g,))],
        (scal, act, cot),
        2 * tiles * tokens * width * width,
        13 << 20,
    )


def dpre_kernel(load, n_w, *refs):
    scal, cot, gp = refs[:3]
    dpre, sums = refs[3 + n_w : 5 + n_w]
    w, sem = refs[5 + n_w :]
    tokens, width = cot.shape
    t = pl.program_id(0)

    @pl.when(t == 0)
    def _():
        load(scal, refs[3 : 3 + n_w], w, sem)

    wait_tile(w, sem, t, width)

    def down(at, n):
        r = pl.ds(at, n)
        d = dot_nt(cot[r, :], w[tile_of(t, width), :]) * gp[r, :].astype(F32)
        dpre[r, :] = d.astype(BF16)

    square_loop(tokens, down)
    sums[...] = dot_nn(jnp.ones((8, tokens), BF16), dpre[...])


def dpre_call(scal, cot, gp, weights, load):
    tiles, tokens, width = gp.shape
    return call(
        functools.partial(dpre_kernel, load, len(weights)),
        "dpre",
        (tiles,),
        [SMEM, fixed(cot.shape), by_tile(tokens, width)] + [HBM] * len(weights),
        [(sds(gp.shape), by_tile(tokens, width)), (sds((tiles, 8, width), F32), by_tile(8, width))],
        [pltpu.VMEM((tiles * width, width), BF16), pltpu.SemaphoreType.DMA((tiles,))],
        (scal, cot, gp, *weights),
        2 * tiles * tokens * width * width,
        19 << 20,
    )


def up_grad_kernel(store, n_g, *refs):
    scal, xn, dpre = refs[:3]
    g_refs = refs[3 : 3 + n_g]
    g, sem = refs[3 + n_g :]
    tokens, width = xn.shape
    t = pl.program_id(0)

    def grad(at, n):
        g[t, pl.ds(at, n), :] = dot_tn(xn[:, pl.ds(at, n)], dpre[...]).astype(BF16)

    square_loop(width, grad)

    @pl.when(t == pl.num_programs(0) - 1)
    def _():
        store(scal, g, g_refs, sem)()


def up_grad_call(scal, xn, dpre, store, g_shapes):
    tiles, tokens, width = dpre.shape
    n_g = len(g_shapes)
    return call(
        functools.partial(up_grad_kernel, store, n_g),
        "up_grad",
        (tiles,),
        [SMEM, fixed(xn.shape), by_tile(tokens, width)],
        [(s, HBM) for s in g_shapes],
        [pltpu.VMEM((tiles, width, width), BF16), pltpu.SemaphoreType.DMA((n_g,))],
        (scal, xn, dpre),
        2 * tiles * tokens * width * width,
        13 << 20,
    )


def input_grad_kernel(load_a, load_u, n_a, n_u, *refs):
    scal, x, cot, dq, dk, dv, dpre, vec = refs[:8]
    dx, sums = refs[8 + n_a + n_u : 10 + n_a + n_u]
    wa, wu, sem_a, sem_u = refs[10 + n_a + n_u :]
    tiles, _, width = dpre.shape
    first = pl.program_id(0) == 0

    @pl.when(first)
    def _():
        load_a(scal, refs[8 : 8 + n_a], wa, sem_a, (0, 1, 2))
        load_u(scal, refs[8 + n_a : 8 + n_a + n_u], wu, sem_u)
        sums[...] = jnp.zeros_like(sums)
        for i in range(3):
            whole_wait(wa.at[i], sem_a.at[i])()

    dnr = dot_nt(dq[...], wa[0]) + dot_nt(dk[...], wa[1]) + dot_nt(dv[...], wa[2])

    @pl.when(first)
    def _():
        for t in range(tiles):
            wait_tile(wu, sem_u, t, width)

    for t in range(tiles):
        dnr += dot_nt(dpre[t], wu[pl.ds(t * width, width), :])
    standard, inv = norm_rows(x[...])
    sums[0:1, :] += jnp.sum(dnr * standard, axis=0, keepdims=True)
    gs = dnr * vec[0:1, :]
    mean_g = jnp.mean(gs, axis=1, keepdims=True)
    mean_p = jnp.mean(gs * standard, axis=1, keepdims=True)
    dx[...] = (cot[...].astype(F32) + inv * (gs - mean_g - standard * mean_p)).astype(BF16)


def input_grad_call(scal, x, cot, dq, dk, dv, dpre, vec, attn_w, up_w, load_a, load_u):
    tiles, tokens, width = dpre.shape
    return call(
        functools.partial(input_grad_kernel, load_a, load_u, len(attn_w), len(up_w)),
        "input_grad",
        (tokens // ROWS,),
        [SMEM]
        + [by_rows(ROWS, width)] * 5
        + [pl.BlockSpec((tiles, ROWS, width), lambda i: (0, i, 0)), fixed(vec.shape)]
        + [HBM] * (len(attn_w) + len(up_w)),
        [(sds(x.shape), by_rows(ROWS, width)), (sds((8, width), F32), fixed((8, width)))],
        [
            pltpu.VMEM((4, width, width), BF16),
            pltpu.VMEM((tiles * width, width), BF16),
            pltpu.SemaphoreType.DMA((4,)),
            pltpu.SemaphoreType.DMA((tiles,)),
        ],
        (scal, x, cot, dq, dk, dv, dpre, vec, *attn_w, *up_w),
        2 * (tiles + 3) * tokens * width * width,
        28 << 20,
    )


def out_kernel(load_a, load_d, n_a, n_d, *refs):
    scal, x, o, act, vec = refs[:5]
    out = refs[5 + n_a + n_d]
    wa, wd, sem_a, sem_d = refs[6 + n_a + n_d :]
    tiles, _, width = act.shape
    first = pl.program_id(0) == 0

    @pl.when(first)
    def _():
        load_a(scal, refs[5 : 5 + n_a], wa, sem_a, (3,))
        load_d(scal, refs[5 + n_a : 5 + n_a + n_d], wd, sem_d)
        whole_wait(wa.at[3], sem_a.at[3])()

    total = x[...].astype(F32) + vec[3:4, :] + dot_nn(o[...], wa[3])

    @pl.when(first)
    def _():
        for t in range(tiles):
            wait_tile(wd, sem_d, t, width)

    for t in range(tiles):
        total += dot_nn(act[t], wd[pl.ds(t * width, width), :])
    out[...] = total.astype(BF16)


def out_call(scal, x, o, act, vec, attn_w, down_w, load_a, load_d):
    tiles, tokens, width = act.shape
    (out,) = call(
        functools.partial(out_kernel, load_a, load_d, len(attn_w), len(down_w)),
        "out",
        (tokens // ROWS,),
        [SMEM]
        + [by_rows(ROWS, width)] * 2
        + [pl.BlockSpec((tiles, ROWS, width), lambda i: (0, i, 0)), fixed(vec.shape)]
        + [HBM] * (len(attn_w) + len(down_w)),
        [(sds(x.shape), by_rows(ROWS, width))],
        [
            pltpu.VMEM((4, width, width), BF16),
            pltpu.VMEM((tiles * width, width), BF16),
            pltpu.SemaphoreType.DMA((4,)),
            pltpu.SemaphoreType.DMA((tiles,)),
        ],
        (scal, x, o, act, vec, *attn_w, *down_w),
        2 * (tiles + 1) * tokens * width * width,
        20 << 20,
    )
    return out


def swap(value, mask):
    return lax.ppermute(value, "wide", [(i, i ^ mask) for i in range(16)])


def swap_y(value):
    return lax.ppermute(value, "narrow", [(0, 1), (1, 0)])


def slots():
    for part in range(2):
        for i in range(2):
            for s in range(2):
                half, side = (i, s) if part == 0 else (s, i)
                for k in range(4):
                    yield part, i, s * 4 + k, half, side, k


def device_of(scal, k, side, core):
    return ((scal[1] ^ k) * 2 + (scal[2] ^ side)) * 2 + (scal[3] ^ core)


def behind(value, *marks):
    return lax.optimization_barrier((value, marks))[0]


def gather_z(own, n):
    half = lax.dynamic_index_in_dim(own, n, 0, keepdims=False)
    return half, [swap(half, k << 2) for k in (1, 2, 3)]


def gather_stack(half, got):
    got = [half] + got
    return [jnp.stack([t[i] for t in got]) for i in range(2)]


def gather_xy(za, zb):
    return swap(za, 2), swap_y(zb)


def total(*parts):
    return sum(v.astype(F32) for v in parts)


def scatter_sum1(keep1, got1):
    return [total(keep1[i], got1[i]).astype(BF16) for i in range(2)]


def scatter_sum2(keep0, got0, got):
    return [total(keep0[i, 4:], got0[i, 4:], got[i][4:]).astype(BF16) for i in range(2)]


def scatter_sum3(keep0, got0, got, got2):
    parts = [total(keep0[i, :4], got0[i, :4], got[i][:4], got2[i]).astype(BF16) for i in range(2)]
    return [jnp.stack([p[k] for p in parts]) for k in range(4)]


def scatter_sum4(own, got):
    return total(own, *got).astype(BF16)


def scatter_join(mine, other, n):
    return jnp.stack([jnp.where(n == 0, mine, other), jnp.where(n == 0, other, mine)])


def flip(value, axis, bit):
    return jnp.where(bit == 1, jnp.flip(value, axis), value)


def gather_vectors(own, scal):
    got = jnp.stack([own] + [swap(own, k << 2) for k in (1, 2, 3)])
    got = jnp.stack([got, swap(got, 2)], axis=1)
    got = jnp.stack([got, swap(got, 1)], axis=2)
    got = got.reshape(2, 2, 2, 2, -1)
    z = scal[1]
    got = flip(flip(flip(flip(got, 0, z >> 1), 1, z & 1), 2, scal[2]), 3, scal[3])
    return got.reshape(16, -1)


def scatter_vectors(value, scal):
    pick = lambda v, i: lax.dynamic_index_in_dim(v, i, 0, keepdims=False)
    z, x, c = scal[1], scal[2], scal[3]
    value = value.reshape(4, 2, 2, -1).transpose(2, 1, 0, 3)
    value = pick(value, c) + swap(pick(value, 1 - c), 1)
    value = pick(value, x) + swap(pick(value, 1 - x), 2)
    value = pick(value, z) + sum(swap(pick(value, z ^ k), k << 2) for k in (1, 2, 3))
    return value + swap_y(value)


def whole_wait(ref, sem):
    return pltpu.make_async_copy(ref, ref, sem).wait


def load_attn(scal, refs, w, sem, blocks):
    def start(own):
        for block in blocks:
            for core in range(2):
                for part, i, slot, half, side, k in slots():
                    if (own ^ half) * 2 + part != block:
                        continue
                    src = refs[core * 4 + part * 2 + i]
                    rows = src.shape[1]
                    at = pl.multiple_of(device_of(scal, k, side, core) * rows, 16)
                    pltpu.make_async_copy(src.at[slot], w.at[block, pl.ds(at, rows), :], sem.at[block]).start()

    @pl.when(scal[0] == 0)
    def _():
        start(0)

    @pl.when(scal[0] != 0)
    def _():
        start(1)


def load_half(which):
    def load(scal, refs, w, sem):
        def start(rel):
            for core in range(2):
                for part, i, slot, half, side, k in slots():
                    if half != rel:
                        continue
                    src = refs[core * 4 + part * 2 + i]
                    per, rows, width = src.shape[1:]
                    dev = device_of(scal, k, side, core)
                    for b in range(per):
                        block = part * per + b
                        if which == 0:
                            at, tile = block * width + dev * rows, block
                        else:
                            at, tile = (dev * 2 * per + block) * rows, scal[1] ^ k
                        dst = w.at[pl.ds(pl.multiple_of(at, 16), rows), :]
                        pltpu.make_async_copy(src.at[slot, b], dst, sem.at[tile]).start()

        @pl.when(scal[0] == which)
        def _():
            start(0)

        @pl.when(scal[0] != which)
        def _():
            start(1)

    return load


def store_with(source):
    def store(scal, g, refs, sem):
        for core in range(2):
            for part, i, slot, half, side, k in slots():
                at = core * 2 + i
                dst = refs[at]
                src = source(g, scal[0] ^ half, part, device_of(scal, k, side, core), dst.shape[2], dst.shape[3])
                pltpu.make_async_copy(src, dst.at[part, slot], sem.at[at]).start()

        def done():
            for at in range(4):
                whole_wait(refs[at], sem.at[at])()

        return done

    return store


def rows_at(base, rows):
    return pl.ds(pl.multiple_of(base, 16), rows)


def attn_source(g, half, part, dev, rows, cols):
    return g.at[half * 2 + part, rows_at(dev * rows, rows), :]


def down_source(g, half, part, dev, rows, cols):
    return g.at[rows_at((dev * 4 + half * 2 + part) * rows, rows), :]


def load_whole_attn(scal, refs, w, sem, blocks):
    for i in blocks:
        pltpu.make_async_copy(refs[i], w.at[i], sem.at[i]).start()


def load_whole_mlp(scal, refs, w, sem):
    width = w.shape[1]
    for i, r in enumerate(refs):
        for t in range(r.shape[0] // width):
            at = i + t
            src = r.at[pl.ds(t * width, width), :]
            pltpu.make_async_copy(src, w.at[pl.ds(at * width, width), :], sem.at[at]).start()


def store_whole(scal, g, refs, sem):
    if len(refs) == 1:
        copies = [pltpu.make_async_copy(g, refs[0], sem.at[0])]
    else:
        copies = [pltpu.make_async_copy(g.at[i], r, sem.at[i]) for i, r in enumerate(refs)]
    for cp in copies:
        cp.start()

    def done():
        for cp in copies:
            cp.wait()

    return done


def split_rows(value, count):
    rows, cols = value.shape
    return value.reshape(rows, count, cols // count).transpose(1, 0, 2)


def body(sizes, tokens, image_ids, cotangent, w_joined, w_out, w_mlp, norm_gain, bias_attn, bias_mlp, bias_out):
    micro, length, width = tokens.shape
    narrow, wide = sizes
    paired = narrow == 2 and wide == 16
    rows = width // wide
    tiles = w_mlp.shape[0] // rows
    x = tokens.reshape(micro * length, width)
    cot = cotangent.reshape(micro * length, width)
    n = lax.axis_index("narrow")
    w = lax.axis_index("wide")
    last = image_ids.reshape(-1, 512)[:, -1]
    scal = [n, w >> 2, (w >> 1) & 1, w & 1] + [jnp.int32(0)] * 4 + [last[b] for b in range(last.shape[0])]
    scal = jnp.stack([jnp.asarray(s, jnp.int32) for s in scal])
    vec_own = jnp.concatenate([norm_gain, bias_attn, bias_mlp, bias_out])

    def vectors(vec):
        vec = vec.astype(F32)
        b_at = 3 * rows
        b_mlp = vec[:, b_at : b_at + tiles * rows].reshape(tiles, width)
        head = [
            vec[:, :rows].reshape(1, width),
            vec[:, rows:b_at].reshape(2, width),
            vec[:, b_at + tiles * rows :].reshape(1, width),
            jnp.zeros((4, width), F32),
        ]
        return jnp.concatenate(head), b_mlp

    def vector_grads(sums_a, sums_d, sums_x):
        return jnp.concatenate(
            [
                sums_x[0].reshape(wide, rows),
                sums_a[:2].reshape(wide, 2 * rows),
                sums_d[:, 0].reshape(wide, tiles * rows),
                sums_a[2].reshape(wide, rows),
            ],
            axis=1,
        )

    if not paired:
        full = lax.all_gather(w_joined, "wide", axis=0, tiled=True)
        parts = [full[:, i * width : (i + 1) * width] for i in range(3 + tiles)]
        attn_w = parts[:3] + [lax.all_gather(w_out, "wide", axis=0, tiled=True)]
        up_w = parts[3:]
        down_w = [lax.all_gather(w_mlp, "wide", axis=0, tiled=True)]
        vec, b_mlp = vectors(lax.all_gather(vec_own, "wide", axis=0))
        square = [sds((width, width))]
        xn, q, k, v, da = project_call(scal, x, cot, vec, attn_w, load_whole_attn)
        o, dq, dk, dv = core_call(scal, q, k, v, da)
        *g_attn, sums_a = attn_grad_call(scal, xn, o, dq, dk, dv, cot, store_whole, square * 4)
        act, gp = up_call(scal, xn, b_mlp, up_w, load_whole_mlp)
        g_down = down_grad_call(scal, act, cot, store_whole, [sds((tiles * width, width))])
        dpre, sums_d = dpre_call(scal, cot, gp, down_w, load_whole_mlp)
        g_up = up_grad_call(scal, xn, dpre, store_whole, square * tiles)
        d_x, sums_x = input_grad_call(
            scal, x, cot, dq, dk, dv, dpre, vec, attn_w, up_w, load_whole_attn, load_whole_mlp
        )
        out = out_call(scal, x, o, act, vec, attn_w, down_w, load_whole_attn, load_whole_mlp)

        def reduce(g):
            g = lax.psum_scatter(g.astype(F32), "wide", scatter_dimension=0, tiled=True)
            return lax.psum(g, "narrow")

        grad_joined = reduce(jnp.concatenate([*g_attn[:3], *g_up], axis=1))
        grad_out = reduce(g_attn[3])
        grad_mlp = reduce(g_down[0])
        vg = reduce(vector_grads(sums_a, sums_d, sums_x))[0]
    else:
        own_attn = jnp.concatenate([split_rows(w_joined[:, : 3 * width], 3), w_out[None]])
        own_mlp = jnp.concatenate([split_rows(w_joined[:, 3 * width :], tiles), w_mlp.reshape(tiles, rows, width)])
        half, got = gather_z(own_attn.reshape(2, 2, rows, width), n)
        za, zb = gather_stack(half, got)
        xa, yb = gather_xy(za, zb)
        vec, b_mlp = vectors(gather_vectors(behind(vec_own, za), scal))
        c_half, c_got = gather_z(behind(own_mlp.reshape(2, 2, tiles // 2, rows, width), za, zb), n)
        a0, b0 = jnp.concatenate([za, xa]), jnp.concatenate([zb, yb])
        a1, b1 = swap_y(a0), swap(b0, 2)
        a0s, b0s = swap(a0, 1), swap(b0, 1)
        attn_w = [a0, a1, b0, b1, a0s, swap(a1, 1), b0s, swap(b1, 1)]

        cza, czb = gather_stack(c_half, c_got)
        xp, attn_w, vec, cza, czb = lax.optimization_barrier((x, attn_w, vec, cza, czb))
        cxa, cyb = gather_xy(cza, czb)
        xn, q, k, v, da = project_call(scal, xp, cot, vec, attn_w, load_attn)

        cxa, cyb = behind((cxa, cyb), q)
        ca0, cb0 = jnp.concatenate([cza, cxa]), jnp.concatenate([czb, cyb])
        q, ca0, cb0 = lax.optimization_barrier((q, ca0, cb0))
        ca1, cb1 = swap_y(ca0), swap(cb0, 2)
        ca0s, cb0s = swap(ca0, 1), swap(cb0, 1)
        o, dq, dk, dv = core_call(scal, q, k, v, da)

        ca1, cb1 = behind((ca1, cb1), dq)
        dq, ca1, cb1 = lax.optimization_barrier((dq, ca1, cb1))
        ca1s, cb1s = swap(ca1, 1), swap(cb1, 1)
        attn_shapes = [sds((2, 8, rows, width))] * 4
        *ga, sums_a = attn_grad_call(scal, xn, o, dq, dk, dv, cot, store_with(attn_source), attn_shapes)
        mlp_w = [ca0, ca1, cb0, cb1, ca0s, *behind([ca1s, cb0s, cb1s], sums_a)]

        a_got1, a_got0 = swap(ga[3], 1), swap(ga[2], 1)
        xn_u = behind(xn, ga)
        act, gp = up_call(scal, xn_u, b_mlp, mlp_w, load_half(0))

        a_got1, a_got0 = behind((a_got1, a_got0), gp)
        sa, sb = scatter_sum1(ga[1], a_got1)
        act_g, sa, sb = lax.optimization_barrier((act, sa, sb))
        a_xy = swap_y(sa), swap(sb, 2)
        gd = down_grad_call(scal, act_g, cot, store_with(down_source), attn_shapes)

        a_xy = behind(a_xy, gd)
        sa, sb = scatter_sum2(ga[0], a_got0, a_xy)
        gp, sa, sb, gd = lax.optimization_barrier((gp, sa, sb, gd))
        a_yx = swap(sa, 2), swap_y(sb)
        d_got1, d_got0 = swap(gd[3], 1), swap(gd[2], 1)
        dpre, sums_d = dpre_call(scal, cot, gp, mlp_w, load_half(1))

        a_yx, d_got1, d_got0 = behind((a_yx, d_got1, d_got0), dpre)
        a_t = scatter_sum3(ga[0], a_got0, a_xy, a_yx)
        sa, sb = scatter_sum1(gd[1], d_got1)
        dpre_g, a_t, sa, sb = lax.optimization_barrier((dpre, a_t, sa, sb))
        d_xy = swap_y(sa), swap(sb, 2)
        a_z = [swap(a_t[k], k << 2) for k in (1, 2, 3)]
        gu = up_grad_call(scal, xn, dpre_g, store_with(attn_source), attn_shapes)

        a_z, d_xy = behind((a_z, d_xy), gu)
        a_sum = scatter_sum4(a_t[0], a_z)
        sa, sb = scatter_sum2(gd[0], d_got0, d_xy)
        x_i, sa, sb, gu, a_sum = lax.optimization_barrier((x, sa, sb, gu, a_sum))
        u_got1, u_got0 = swap(gu[3], 1), swap(gu[2], 1)
        d_yx = swap(sa, 2), swap_y(sb)
        a_other = swap_y(a_sum)
        d_x, sums_x = input_grad_call(
            scal, x_i, cot, dq, dk, dv, dpre, vec, attn_w, mlp_w, load_attn, load_half(0)
        )

        d_yx, u_got1, u_got0, a_other = behind((d_yx, u_got1, u_got0, a_other), d_x)
        sa, sb = scatter_sum1(gu[1], u_got1)
        d_t = scatter_sum3(gd[0], d_got0, d_xy, d_yx)
        x_o, sa, sb, d_t, sums_x = lax.optimization_barrier((x, sa, sb, d_t, sums_x))
        u_xy = swap_y(sa), swap(sb, 2)
        d_z = [swap(d_t[k], k << 2) for k in (1, 2, 3)]
        out = out_call(scal, x_o, o, act, vec, attn_w, mlp_w, load_attn, load_half(1))

        u_xy, d_z = behind((u_xy, d_z), out)
        sa, sb = scatter_sum2(gu[0], u_got0, u_xy)
        u_yx = swap(sa, 2), swap_y(sb)
        d_sum = scatter_sum4(d_t[0], d_z)
        u_t = scatter_sum3(gu[0], u_got0, u_xy, u_yx)
        u_z = [swap(u_t[k], k << 2) for k in (1, 2, 3)]
        d_other = swap_y(behind(d_sum, u_t))
        vg = scatter_vectors(vector_grads(sums_a, sums_d, behind(sums_x, u_t)), scal)
        u_sum = scatter_sum4(u_t[0], u_z)
        u_other = swap_y(u_sum)
        g_attn = scatter_join(a_sum, a_other, n).reshape(4, rows, width).astype(F32)
        g_up = scatter_join(u_sum, u_other, n).reshape(tiles, rows, width).astype(F32)
        grad_joined = jnp.concatenate([g_attn[0], g_attn[1], g_attn[2], *[g_up[t] for t in range(tiles)]], axis=1)
        grad_out = g_attn[3]
        grad_mlp = scatter_join(d_sum, d_other, n).reshape(tiles * rows, width).astype(F32)
    b_at = 3 * rows
    return (
        out.reshape(tokens.shape),
        d_x.reshape(tokens.shape),
        grad_joined,
        grad_out,
        grad_mlp,
        vg[:rows],
        vg[rows:b_at],
        vg[b_at : b_at + tiles * rows],
        vg[b_at + tiles * rows :],
    )


def solution(mesh):
    sizes = (mesh.shape["narrow"], mesh.shape["wide"])
    rows = P(None, ("narrow", "wide"), None)
    placed = (rows, P(None, ("narrow", "wide")), rows) + (P("wide", None),) * 3 + (P("wide"),) * 4
    return jax.shard_map(
        functools.partial(body, sizes),
        mesh=mesh,
        in_specs=placed,
        out_specs=(rows, rows) + (P("wide", None),) * 3 + (P("wide"),) * 4,
        check_vma=False,
    )
```

time: 642 us -> 323 us (0.50); the launches traced: 634 us -> 322 us
  matrix products: 189 us -> 0 us
  waiting for transfers between devices: 217 us -> 64.1 us
  Pallas kernels: 0 us -> 137 us
  blocking collectives: 129 us -> 0 us
  starting transfers between devices: 0.28 us -> 67.3 us
  local copies, waits for them, and re-layouts: 45.4 us -> 24.1 us
  between operations: 19.1 us -> 1.82 us
  other arithmetic: 34.4 us -> 27.1 us
    dot_general x30 -> x0, matrix products: 189 us -> none  [the longest x2 22.4 us: backward_block(): jnp.einsum('tc,tf->cf', normed, d_joined, preferred_element_type=jnp.floa...]
    reduce_scatter x3 -> x0, waiting for transfers between devices: 177 us -> none  [the longest x1 177 us: body(): lax.psum_scatter(grad_total[0], 'wide', scatter_dimension=0, tiled=True)]
    pallas_call x0 -> x9, Pallas kernels: none -> 137 us  [call(): pl.pallas_call(kernel, name=name, grid=grid, out_shape=[s for s, _ in out...]
    unnamed x2 -> x0, blocking collectives: 123 us -> none
    ppermute x0 -> x63, starting transfers between devices: none -> 67.3 us  [the longest x49 51.7 us: swap(): return lax.ppermute(value, 'wide', [(i, i ^ mask) for i in range(16)])]
    ppermute x0 -> x63, waiting for transfers between devices: none -> 64.1 us  [the longest x49 48 us: swap(): return lax.ppermute(value, 'wide', [(i, i ^ mask) for i in range(16)])]
    all_gather x3 -> x0, waiting for transfers between devices: 37.4 us -> none  [the longest x1 37.3 us: body(): lax.all_gather(w_joined, 'wide', axis=0, tiled=True)]
    unnamed x109 -> x81, local copies, waits for them, and re-layouts: 20.1 us -> 5.43 us
  transfers between devices with their start and end apart: 7 -> 63, of which waited for: 2 -> 23; matrix products, arithmetic and copies ran while one was open for 40% -> 6% of each run, Pallas kernels for 0% -> 43%
where the time goes in v1:
time: 323 us; the launch traced here: 322 us
  Pallas kernels  137 us (42%)
  starting transfers between devices  67.3 us (21%)
  waiting for transfers between devices  64.1 us (20%)
  other arithmetic  27.1 us (8%)
  local copies, waits for them, and re-layouts  24.1 us (7%)
    pallas_call x9, Pallas kernels, call(): pl.pallas_call(kernel, name=name, grid=grid, out_shape=[s for s, _ in out...  137 us
    ppermute x49, starting transfers between devices, swap(): return lax.ppermute(value, 'wide', [(i, i ^ mask) for i in range(16)])  51.7 us
    ppermute x49, waiting for transfers between devices, swap(): return lax.ppermute(value, 'wide', [(i, i ^ mask) for i in range(16)])  48 us
    ppermute x14, waiting for transfers between devices, swap_y(): return lax.ppermute(value, 'narrow', [(0, 1), (1, 0)])  16.1 us
    ppermute x14, starting transfers between devices, swap_y(): return lax.ppermute(value, 'narrow', [(0, 1), (1, 0)])  15.7 us
  transfers between devices with their start and end apart: 63, of which 23 were waited for; matrix products, arithmetic and copies ran while one was open for 6% of the time, Pallas kernels for 43%

profile of v1, /device:TPU:0, one launch (start us, length us, event | category | flops | bytes accessed | tf_op | source)
XLA Modules:
  0.0 321.8 jit_solution(2755798749591043719)
XLA Ops:
  3.2 5.1 %collective-permute-start.2 = (bf16[2,48,768]{2,1,0:T(8,128)(2,1)S(1)}, bf16[2,48,768]{2,1,0:T(8,128)(2,1)S(1)}, u32[]{:S(2)}, u32[]{:S(2)}) collective-permute-start(bf16[2,48,768]{2,1,0:T(8,128)(2,1)S(1)} %dynamic-slice_bitcast_fusion.3), channel_id=1, source_target_pairs={{0,12},{1,13},{2,14},{3,15},{4,8},{5,9},{6,10},{7,11},{8,4},{9,5},... | collective-permute-start | bytes 442376 | tf_op jit(solution)/shard_map/ppermute | solution.py:522
  9.2 8.6 %collective-permute-done = bf16[2,48,768]{2,1,0:T(8,128)(2,1)S(1)} collective-permute-done((bf16[2,48,768]{2,1,0:T(8,128)(2,1)S(1)}, bf16[2,48,768]{2,1,0:T(8,128)(2,1)S(1)}, u32[]{:S(2)}, u32[]{:S(2)}) %collective-permute-start) | collective-permute-done | bytes 147488 | tf_op jit(solution)/shard_map/ppermute | solution.py:522
  17.8 2.9 collective-permute-done.1
  20.9 2.6 collective-permute-start.13
  23.5 1.9 collective-permute-start.11
  26.3 1.6 collective-permute-done.12
  28.0 1.6 collective-permute-start.14
  29.5 2.1 collective-permute-done.14
  32.5 1.5 collective-permute-start.18
  34.9 2.0 collective-permute-start.16
  36.9 1.5 collective-permute-start.3
  38.4 1.6 collective-permute-start.5
  41.1 5.6 %collective-permute-done.5 = bf16[4,48,768]{2,1,0:T(8,128)(2,1)S(1)} collective-permute-done((bf16[4,48,768]{2,1,0:T(8,128)(2,1)S(1)}, bf16[4,48,768]{2,1,0:T(8,128)(2,1)S(1)}, u32[]{:S(2)}, u32[]{:S(2)}) %collective-permute-start.5) | collective-permute-done | bytes 294944 | tf_op jit(solution)/shard_map/ppermute | solution.py:526
  47.4 1.6 collective-permute-start.4
  50.1 11.3 %collective-permute-done.17 = bf16[2,2,48,768]{3,2,1,0:T(8,128)(2,1)S(1)} collective-permute-done((bf16[2,2,48,768]{3,2,1,0:T(8,128)(2,1)}, bf16[2,2,48,768]{3,2,1,0:T(8,128)(2,1)S(1)}, u32[]{:S(2)}, u32[]{:S(2)}) %collective-permute-start.17) | collective-permute-done | bytes 294944 | tf_op jit(solution)/shard_map/ppermute | solution.py:522
  62.1 1.2 pad_maximum_fusion.3
  65.1 1.5 collective-permute-start.19
  66.6 1.5 collective-permute-start.20
  68.1 1.3 fusion.50
  69.5 1.9 stack.131.refs_0_.scal
  71.4 11.1 %project.1 = (bf16[1024,768]{1,0:T(8,128)(2,1)}, bf16[1024,768]{1,0:T(8,128)(2,1)}, bf16[1024,768]{1,0:T(8,128)(2,1)}, bf16[1024,768]{1,0:T(8,128)(2,1)}, bf16[1024,768]{1,0:T(8,128)(2,1)}) custom-call(s32[10]{0:T(128)} %stack.131.refs_0_.scal, bf16[1024,768]{1,0:T(8,128)(2,1)} %bitcast.181, bf16[1024,768]{1,0:T(8,128)(2,1)} %bitcast.196, ...), custom_call_target="tpu_custom_call" | custom-call | flops 4831838208 | bytes 16777216 | tf_op jit(solution)/shard_map/project/pallas_call | solution.py:97
  84.9 23.7 %core.1 = (bf16[1024,768]{1,0:T(8,128)(2,1)}, bf16[1024,768]{1,0:T(8,128)(2,1)}, bf16[1024,768]{1,0:T(8,128)(2,1)}, bf16[1024,768]{1,0:T(8,128)(2,1)}) custom-call(s32[10]{0:T(128)} %stack.131.refs_0_.scal, bf16[1024,768]{1,0:T(8,128)(2,1)} %get-tuple-element.141.q, bf16[1024,768]{1,0:T(8,128)(2,1)} %get-tuple-element.142.k, ...), custom_call_target="tpu_custom_call" | custom-call | flops 21474836480 | bytes 12582912 | tf_op jit(solution)/shard_map/core/pallas_call | solution.py:97
  108.6 2.8 collective-permute-done.21.refs_4_.refs_17_.refs_14_
  111.3 1.5 collective-permute-done.22.refs_6_.refs_19_.refs_16_
  113.3 13.0 %attn_grad.1 = (bf16[2,8,48,768]{3,2,1,0:T(8,128)(2,1)}, bf16[2,8,48,768]{3,2,1,0:T(8,128)(2,1)}, bf16[2,8,48,768]{3,2,1,0:T(8,128)(2,1)}, bf16[2,8,48,768]{3,2,1,0:T(8,128)(2,1)}, f32[8,768]{1,0:T(8,128)}) custom-call(s32[10]{0:T(128)} %stack.131.refs_0_.scal, bf16[1024,768]{1,0:T(8,128)(2,1)} %get-tuple-element.158.refs_1_, ...), custom_call_target="tpu_custom_call" | custom-call | flops 4831838208 | bytes 14680064 | tf_op jit(solution)/shard_map/attn_grad/pallas_call | solution.py:97
  128.8 18.2 %up.1 = (bf16[4,1024,768]{2,1,0:T(8,128)(2,1)}, bf16[4,1024,768]{2,1,0:T(8,128)(2,1)}) custom-call(s32[10]{0:T(128)} %stack.131.refs_0_.scal, bf16[1024,768]{1,0:T(8,128)(2,1)} %get-tuple-element.158.refs_1_, f32[4,1,768]{2,1,0:T(1,128)} %reshape_reshape.3.refs_2_, bf16[8,2,48,768]{3,2,1,0:T(8,128)(2,1)} %copy-done, ...), custom_call_target="tpu_custom_call" | custom-call | flops 4831838208 | bytes 19922944 | tf_op jit(solution)/shard_map/up/pallas_call | solution.py:97
  147.1 1.5 fusion.1
  148.6 1.4 collective-permute-start.29
  150.0 4.1 %collective-permute-start.30 = (bf16[8,48,768]{2,1,0:T(8,128)(2,1)S(1)}, bf16[8,48,768]{2,1,0:T(8,128)(2,1)S(1)}, u32[]{:S(2)}, u32[]{:S(2)}) collective-permute-start(bf16[8,48,768]{2,1,0:T(8,128)(2,1)S(1)} %get-tuple-element.170), channel_id=1, source_target_pairs={{0,2},{1,3},{2,0},{3,1},{4,6},{5,7},{6,4},{7,5},{8,10},{9,11},{10,... | collective-permute-start | bytes 1769480 | tf_op jit(solution)/shard_map/ppermute | solution.py:522
  154.1 11.7 %down_grad.1 = (bf16[2,8,48,768]{3,2,1,0:T(8,128)(2,1)}, bf16[2,8,48,768]{3,2,1,0:T(8,128)(2,1)}, bf16[2,8,48,768]{3,2,1,0:T(8,128)(2,1)}, bf16[2,8,48,768]{3,2,1,0:T(8,128)(2,1)}) custom-call(s32[10]{0:T(128)} %stack.131.refs_0_.scal, bf16[4,1024,768]{2,1,0:T(8,128)(2,1)} %get-tuple-element.171.refs_1_.refs_3_, bf16[1024,768]{1,0:T(8,128)(2,1)} %bitcast.198), custom_call_target="tpu_custom_call" | custom-call | flops 4831838208 | bytes 13631488 | tf_op jit(solution)/shard_map/down_grad/pallas_call | solution.py:97
  165.8 1.7 collective-permute-done.30
  167.5 2.3 fusion.22
  170.3 1.7 collective-permute-start.31
  172.8 14.5 %dpre.1 = (bf16[4,1024,768]{2,1,0:T(8,128)(2,1)}, f32[4,8,768]{2,1,0:T(8,128)}) custom-call(s32[10]{0:T(128)} %stack.131.refs_0_.scal, bf16[1024,768]{1,0:T(8,128)(2,1)} %bitcast.199, bf16[4,1024,768]{2,1,0:T(8,128)(2,1)} %get-tuple-element.183.refs_2_, bf16[8,2,48,768]{3,2,1,0:T(8,128)(2,1)} %copy-done, ...), custom_call_target="tpu_custom_call" | custom-call | flops 4831838208 | bytes 19922944 | tf_op jit(solution)/shard_map/dpre/pallas_call | solution.py:97
  187.3 2.0 fusion.20
  189.4 1.2 copy-done.4
  190.6 1.3 fusion.3
  194.0 1.4 collective-permute-start.38
  195.8 3.1 collective-permute-start.36
  200.1 11.7 %up_grad.1 = (bf16[2,8,48,768]{3,2,1,0:T(8,128)(2,1)}, bf16[2,8,48,768]{3,2,1,0:T(8,128)(2,1)}, bf16[2,8,48,768]{3,2,1,0:T(8,128)(2,1)}, bf16[2,8,48,768]{3,2,1,0:T(8,128)(2,1)}) custom-call(s32[10]{0:T(128)} %stack.131.refs_0_.scal, bf16[1024,768]{1,0:T(8,128)(2,1)} %get-tuple-element.158.refs_1_, bf16[4,1024,768]{2,1,0:T(8,128)(2,1)} %get-tuple-element.195.refs_2_.refs_6_), custom_call_target="tpu_custom_call" | custom-call | flops 4831838208 | bytes 13631488 | tf_op jit(solution)/shard_map/up_grad/pallas_call | solution.py:97
  211.8 1.8 add_convert_fusion.8
  218.1 1.5 slice_reduce_fusion
  221.1 1.7 collective-permute-start.40
  222.9 1.4 collective-permute-start.41
  224.2 18.8 %input_grad.1 = (bf16[1024,768]{1,0:T(8,128)(2,1)}, f32[8,768]{1,0:T(8,128)}) custom-call(s32[10]{0:T(128)} %stack.131.refs_0_.scal, bf16[1024,768]{1,0:T(8,128)(2,1)} %bitcast.182, bf16[1024,768]{1,0:T(8,128)(2,1)} %bitcast.200, bf16[1024,768]{1,0:T(8,128)(2,1)} %get-tuple-element.151.refs_3_, bf16[1024,768]{1,0:T(8,128)(2,1)} %get-tuple-element.152.refs_4_, ...), custom_call_target="tpu_custom_call" | custom-call | flops 8455716864 | bytes 29360128 | tf_op jit(solution)/shard_map/input_grad/pallas_call | solution.py:97
  243.1 1.6 fusion.15
  244.8 1.2 copy-done.3
  250.0 3.0 collective-permute-start.48
  255.2 14.6 %out.1 = bf16[1024,768]{1,0:T(8,128)(2,1)} custom-call(s32[10]{0:T(128)} %stack.131.refs_0_.scal, bf16[1024,768]{1,0:T(8,128)(2,1)} %bitcast.183, bf16[1024,768]{1,0:T(8,128)(2,1)} %get-tuple-element.145.refs_2_, bf16[4,1024,768]{2,1,0:T(8,128)(2,1)} %get-tuple-element.171.refs_1_.refs_3_, f32[8,768]{1,0:T(8,128)} %maximum_maximum_fusion.refs_3_.refs_7_.refs_4_, ...), custom_call_target="tpu_custom_call" | custom-call | flops 6039797760 | bytes 20971520 | tf_op jit(solution)/shard_map/out/pallas_call | solution.py:97
  270.8 1.3 fusion.9
  272.1 1.8 collective-permute-start.50
  274.0 4.9 %collective-permute-done.50 = bf16[4,48,768]{2,1,0:T(8,128)(2,1)S(1)} collective-permute-done((bf16[4,48,768]{2,1,0:T(8,128)(2,1)S(1)}, bf16[4,48,768]{2,1,0:T(8,128)(2,1)S(1)}, u32[]{:S(2)}, u32[]{:S(2)}) %collective-permute-start.50) | collective-permute-done | bytes 294944 | tf_op jit(solution)/shard_map/ppermute | solution.py:522
  278.9 1.3 fusion.11
  280.2 1.4 collective-permute-start.51
  282.9 4.0 %collective-permute-done.51 = bf16[4,48,768]{2,1,0:T(8,128)(2,1)S(1)} collective-permute-done((bf16[4,48,768]{2,1,0:T(8,128)(2,1)S(1)}, bf16[4,48,768]{2,1,0:T(8,128)(2,1)S(1)}, u32[]{:S(2)}, u32[]{:S(2)}) %collective-permute-start.51) | collective-permute-done | bytes 294944 | tf_op jit(solution)/shard_map/ppermute | solution.py:526
  290.3 1.8 collective-permute-start.58
  292.1 1.9 collective-permute-done.58
  294.5 2.2 collective-permute-start.61
  298.6 1.3 collective-permute-done.61
  300.2 1.5 collective-permute-start.62
  303.7 1.7 collective-permute-start.53
  305.4 2.0 collective-permute-start.54
  310.7 4.5 %collective-permute-done.53 = bf16[2,48,768]{2,1,0:T(8,128)(2,1)S(1)} collective-permute-done((bf16[2,48,768]{2,1,0:T(8,128)(2,1)S(1)}, bf16[2,48,768]{2,1,0:T(8,128)(2,1)S(1)}, u32[]{:S(2)}, u32[]{:S(2)}) %collective-permute-start.53) | collective-permute-done | bytes 147488 | tf_op jit(solution)/shard_map/ppermute | solution.py:522
  316.9 3.7 %collective-permute-done.55 = bf16[2,48,768]{2,1,0:T(8,128)(2,1)S(1)} collective-permute-done((bf16[2,48,768]{2,1,0:T(8,128)(2,1)S(1)}, bf16[2,48,768]{2,1,0:T(8,128)(2,1)S(1)}, u32[]{:S(2)}, u32[]{:S(2)}) %collective-permute-start.55) | collective-permute-done | bytes 147488 | tf_op jit(solution)/shard_map/ppermute | solution.py:526
  (270 shorter events, 50.2 us)
Async XLA Ops:
  3.2 17.6 %collective-permute-start.2 = (bf16[2,48,768]{2,1,0:T(8,128)(2,1)S(1)}, bf16[2,48,768]{2,1,0:T(8,128)(2,1)S(1)}, u32[]{:S(2)}, u32[]{:S(2)}) collective-permute-start(bf16[2,48,768]{2,1,0:T(8,128)(2,1)S(1)} %dynamic-slice_bitcast_fusion.3), channel_id=1, source_target_pairs={{0,12},{1,13},{2,14},{3,15},{4,8},{5,9},{6,10},{7,11},{8,4},{9,5},... | collective-permute-start | bytes 442376 | tf_op jit(solution)/shard_map/ppermute | solution.py:522
  8.3 12.5 %collective-permute-start.1 = (bf16[2,48,768]{2,1,0:T(8,128)(2,1)S(1)}, bf16[2,48,768]{2,1,0:T(8,128)(2,1)S(1)}, u32[]{:S(2)}, u32[]{:S(2)}) collective-permute-start(bf16[2,48,768]{2,1,0:T(8,128)(2,1)S(1)} %dynamic-slice_bitcast_fusion.3), channel_id=1, source_target_pairs={{0,8},{1,9},{2,10},{3,11},{4,12},{5,13},{6,14},{7,15},{8,0},{9,1},... | collective-permute-start | bytes 442376 | tf_op jit(solution)/shard_map/ppermute | solution.py:522
  8.3 9.5 %collective-permute-start = (bf16[2,48,768]{2,1,0:T(8,128)(2,1)S(1)}, bf16[2,48,768]{2,1,0:T(8,128)(2,1)S(1)}, u32[]{:S(2)}, u32[]{:S(2)}) collective-permute-start(bf16[2,48,768]{2,1,0:T(8,128)(2,1)S(1)} %dynamic-slice_bitcast_fusion.3), channel_id=1, source_target_pairs={{0,4},{1,5},{2,6},{3,7},{4,0},{5,1},{6,2},{7,3},{8,12},{9,13},{10,... | collective-permute-start | bytes 442376 | tf_op jit(solution)/shard_map/ppermute | solution.py:522
  20.9 5.4 %collective-permute-start.13 = (bf16[384]{0:T(512)(128)(2,1)S(1)}, bf16[384]{0:T(512)(128)(2,1)S(1)}, u32[]{:S(2)}, u32[]{:S(2)}) collective-permute-start(bf16[384]{0:T(512)(128)(2,1)S(1)} %pad_maximum_fusion.27), channel_id=1, source_target_pairs={{0,12},{1,13},{2,14},{3,15},{4,8},{5,9},{6,10},{7,11},{8,4},{9,5},... | collective-permute-start | bytes 2312 | tf_op jit(solution)/shard_map/ppermute | solution.py:522
  23.5 4.5 %collective-permute-start.12 = (bf16[384]{0:T(512)(128)(2,1)S(1)}, bf16[384]{0:T(512)(128)(2,1)S(1)}, u32[]{:S(2)}, u32[]{:S(2)}) collective-permute-start(bf16[384]{0:T(512)(128)(2,1)S(1)} %pad_maximum_fusion.27), channel_id=1, source_target_pairs={{0,8},{1,9},{2,10},{3,11},{4,12},{5,13},{6,14},{7,15},{8,0},{9,1},... | collective-permute-start | bytes 2312 | tf_op jit(solution)/shard_map/ppermute | solution.py:522
  23.5 4.5 %collective-permute-start.11 = (bf16[384]{0:T(512)(128)(2,1)S(1)}, bf16[384]{0:T(512)(128)(2,1)S(1)}, u32[]{:S(2)}, u32[]{:S(2)}) collective-permute-start(bf16[384]{0:T(512)(128)(2,1)S(1)} %pad_maximum_fusion.27), channel_id=1, source_target_pairs={{0,4},{1,5},{2,6},{3,7},{4,0},{5,1},{6,2},{7,3},{8,12},{9,13},{10,... | collective-permute-start | bytes 2312 | tf_op jit(solution)/shard_map/ppermute | solution.py:522
  28.0 3.7 %collective-permute-start.14 = (bf16[4,384]{1,0:T(4,128)(2,1)S(1)}, bf16[4,384]{1,0:T(4,128)(2,1)S(1)}, u32[]{:S(2)}, u32[]{:S(2)}) collective-permute-start(bf16[4,384]{1,0:T(4,128)(2,1)S(1)} %pad_maximum_fusion.26), channel_id=1, source_target_pairs={{0,2},{1,3},{2,0},{3,1},{4,6},{5,7},{6,4},{7,5},{8,10},{9,11},{10,... | collective-permute-start | bytes 9224 | tf_op jit(solution)/shard_map/ppermute | solution.py:522
  31.6 6.7 %collective-permute-start.15 = (bf16[4,2,384]{2,0,1:T(4,128)(2,1)S(1)}, bf16[4,2,384]{2,0,1:T(4,128)(2,1)S(1)}, u32[]{:S(2)}, u32[]{:S(2)}) collective-permute-start(bf16[4,2,384]{2,0,1:T(4,128)(2,1)S(1)} %pad_maximum_fusion.25), channel_id=1, source_target_pairs={{0,1},{1,0},{2,3},{3,2},{4,5},{5,4},{6,7},{7,6},{8,9},{9,8},{10,11... | collective-permute-start | bytes 18440 | tf_op jit(solution)/shard_map/ppermute | solution.py:522
  32.5 17.6 %collective-permute-start.18 = (bf16[2,2,48,768]{3,2,1,0:T(8,128)(2,1)}, bf16[2,2,48,768]{3,2,1,0:T(8,128)(2,1)S(1)}, u32[]{:S(2)}, u32[]{:S(2)}) collective-permute-start(bf16[2,2,48,768]{3,2,1,0:T(8,128)(2,1)} %dynamic-slice_bitcast_fusion), channel_id=1, source_target_pairs={{0,12},{1,13},{2,14},{3,15},{4,8},{5,9},{6,10},{7,11},{8,4},{9,5},... | collective-permute-start | bytes 884744 | tf_op jit(solution)/shard_map/ppermute | solution.py:522
  33.9 27.5 %collective-permute-start.17 = (bf16[2,2,48,768]{3,2,1,0:T(8,128)(2,1)}, bf16[2,2,48,768]{3,2,1,0:T(8,128)(2,1)S(1)}, u32[]{:S(2)}, u32[]{:S(2)}) collective-permute-start(bf16[2,2,48,768]{3,2,1,0:T(8,128)(2,1)} %dynamic-slice_bitcast_fusion), channel_id=1, source_target_pairs={{0,8},{1,9},{2,10},{3,11},{4,12},{5,13},{6,14},{7,15},{8,0},{9,1},... | collective-permute-start | bytes 884744 | tf_op jit(solution)/shard_map/ppermute | solution.py:522
  34.9 27.2 %collective-permute-start.16 = (bf16[2,2,48,768]{3,2,1,0:T(8,128)(2,1)}, bf16[2,2,48,768]{3,2,1,0:T(8,128)(2,1)S(1)}, u32[]{:S(2)}, u32[]{:S(2)}) collective-permute-start(bf16[2,2,48,768]{3,2,1,0:T(8,128)(2,1)} %dynamic-slice_bitcast_fusion), channel_id=1, source_target_pairs={{0,4},{1,5},{2,6},{3,7},{4,0},{5,1},{6,2},{7,3},{8,12},{9,13},{10,... | collective-permute-start | bytes 884744 | tf_op jit(solution)/shard_map/ppermute | solution.py:522
  36.9 10.5 %collective-permute-start.3 = (bf16[4,48,768]{2,1,0:T(8,128)(2,1)S(1)}, bf16[4,48,768]{2,1,0:T(8,128)(2,1)S(1)}, u32[]{:S(2)}, u32[]{:S(2)}) collective-permute-start(bf16[4,48,768]{2,1,0:T(8,128)(2,1)S(1)} %pad_maximum_fusion.6), channel_id=1, source_target_pairs={{0,2},{1,3},{2,0},{3,1},{4,6},{5,7},{6,4},{7,5},{8,10},{9,11},{10,... | collective-permute-start | bytes 884744 | tf_op jit(solution)/shard_map/ppermute | solution.py:522
  38.4 8.3 %collective-permute-start.5 = (bf16[4,48,768]{2,1,0:T(8,128)(2,1)S(1)}, bf16[4,48,768]{2,1,0:T(8,128)(2,1)S(1)}, u32[]{:S(2)}, u32[]{:S(2)}) collective-permute-start(bf16[4,48,768]{2,1,0:T(8,128)(2,1)S(1)} %pad_maximum_fusion.7), channel_id=1, source_target_pairs={{0,16},{16,0},{1,17},{17,1},{2,18},{18,2},{3,19},{19,3},{4,20},{20... | collective-permute-start | bytes 884744 | tf_op jit(solution)/shard_map/ppermute | solution.py:526
  46.8 14.7 %collective-permute-start.6 = (bf16[8,48,768]{2,1,0:T(8,128)(2,1)S(1)}, bf16[8,48,768]{2,1,0:T(8,128)(2,1)S(1)}, u32[]{:S(2)}, u32[]{:S(2)}) collective-permute-start(bf16[8,48,768]{2,1,0:T(8,128)(2,1)S(1)} %constant_dynamic-update-slice_fusion.5.refs_6_.refs_10_.refs_7_), channel_id=1, source_target_pairs={{0,2},{1,3},{2,0},{3,1},{4,6},{5,7},{6,4},{7,5},{8,10},{9,11},{10,... | collective-permute-start | bytes 1769480 | tf_op jit(solution)/shard_map/ppermute | solution.py:522
  47.4 14.5 %collective-permute-start.4 = (bf16[8,48,768]{2,1,0:T(8,128)(2,1)S(1)}, bf16[8,48,768]{2,1,0:T(8,128)(2,1)S(1)}, u32[]{:S(2)}, u32[]{:S(2)}) collective-permute-start(bf16[8,48,768]{2,1,0:T(8,128)(2,1)S(1)} %constant_dynamic-update-slice_fusion.refs_4_.refs_8_.refs_5_), channel_id=1, source_target_pairs={{0,16},{16,0},{1,17},{17,1},{2,18},{18,2},{3,19},{19,3},{4,20},{20... | collective-permute-start | bytes 1769480 | tf_op jit(solution)/shard_map/ppermute | solution.py:526
  50.1 13.3 %collective-permute-start.9 = (bf16[8,48,768]{2,1,0:T(8,128)(2,1)S(1)}, bf16[8,48,768]{2,1,0:T(8,128)(2,1)S(1)}, u32[]{:S(2)}, u32[]{:S(2)}) collective-permute-start(bf16[8,48,768]{2,1,0:T(8,128)(2,1)S(1)} %constant_dynamic-update-slice_fusion.5.refs_6_.refs_10_.refs_7_), channel_id=1, source_target_pairs={{0,1},{1,0},{2,3},{3,2},{4,5},{5,4},{6,7},{7,6},{8,9},{9,8},{10,11... | collective-permute-start | bytes 1769480 | tf_op jit(solution)/shard_map/ppermute | solution.py:522
  61.4 2.0 collective-permute-start.7
  61.4 2.8 collective-permute-start.10
  61.9 3.2 collective-permute-start.8
  65.1 17.4 %collective-permute-start.19 = (bf16[4,2,48,768]{3,2,1,0:T(8,128)(2,1)S(1)}, bf16[4,2,48,768]{3,2,1,0:T(8,128)(2,1)S(1)}, u32[]{:S(2)}, u32[]{:S(2)}) collective-permute-start(bf16[4,2,48,768]{3,2,1,0:T(8,128)(2,1)S(1)} %get-tuple-element.137), channel_id=1, source_target_pairs={{0,2},{1,3},{2,0},{3,1},{4,6},{5,7},{6,4},{7,5},{8,10},{9,11},{10,... | collective-permute-start | bytes 1769480 | tf_op jit(solution)/shard_map/ppermute | solution.py:522
  66.6 15.9 %collective-permute-start.20 = (bf16[4,2,48,768]{3,2,1,0:T(8,128)(2,1)S(1)}, bf16[4,2,48,768]{3,2,1,0:T(8,128)(2,1)S(1)}, u32[]{:S(2)}, u32[]{:S(2)}) collective-permute-start(bf16[4,2,48,768]{3,2,1,0:T(8,128)(2,1)S(1)} %get-tuple-element.138), channel_id=1, source_target_pairs={{0,16},{16,0},{1,17},{17,1},{2,18},{18,2},{3,19},{19,3},{4,20},{20... | collective-permute-start | bytes 1769480 | tf_op jit(solution)/shard_map/ppermute | solution.py:526
  82.8 45.0 %collective-permute-start.23 = (bf16[8,2,48,768]{3,2,1,0:T(8,128)(2,1)S(1)}, bf16[8,2,48,768]{3,2,1,0:T(8,128)(2,1)S(1)}, u32[]{:S(2)}, u32[]{:S(2)}) collective-permute-start(bf16[8,2,48,768]{3,2,1,0:T(8,128)(2,1)S(1)} %pad_maximum_fusion.refs_3_.refs_16_.refs_13_), channel_id=1, source_target_pairs={{0,1},{1,0},{2,3},{3,2},{4,5},{5,4},{6,7},{7,6},{8,9},{9,8},{10,11... | collective-permute-start | bytes 3538952 | tf_op jit(solution)/shard_map/ppermute | solution.py:522
  83.7 27.7 %collective-permute-start.21 = (bf16[8,2,48,768]{3,2,1,0:T(8,128)(2,1)S(1)}, bf16[8,2,48,768]{3,2,1,0:T(8,128)(2,1)}, u32[]{:S(2)}, u32[]{:S(2)}) collective-permute-start(bf16[8,2,48,768]{3,2,1,0:T(8,128)(2,1)S(1)} %pad_maximum_fusion.refs_3_.refs_16_.refs_13_), channel_id=1, source_target_pairs={{0,16},{16,0},{1,17},{17,1},{2,18},{18,2},{3,19},{19,3},{4,20},{20... | collective-permute-start | bytes 3538952 | tf_op jit(solution)/shard_map/ppermute | solution.py:526
  84.3 42.1 %collective-permute-start.25 = (bf16[8,2,48,768]{3,2,1,0:T(8,128)(2,1)S(1)}, bf16[8,2,48,768]{3,2,1,0:T(8,128)(2,1)}, u32[]{:S(2)}, u32[]{:S(2)}) collective-permute-start(bf16[8,2,48,768]{3,2,1,0:T(8,128)(2,1)S(1)} %pad_maximum_fusion.1.refs_5_.refs_18_.refs_15_), channel_id=1, source_target_pairs={{0,1},{1,0},{2,3},{3,2},{4,5},{5,4},{6,7},{7,6},{8,9},{9,8},{10,11... | collective-permute-start | bytes 3538952 | tf_op jit(solution)/shard_map/ppermute | solution.py:522
  84.4 28.5 %collective-permute-start.22 = (bf16[8,2,48,768]{3,2,1,0:T(8,128)(2,1)S(1)}, bf16[8,2,48,768]{3,2,1,0:T(8,128)(2,1)}, u32[]{:S(2)}, u32[]{:S(2)}) collective-permute-start(bf16[8,2,48,768]{3,2,1,0:T(8,128)(2,1)S(1)} %pad_maximum_fusion.1.refs_5_.refs_18_.refs_15_), channel_id=1, source_target_pairs={{0,2},{1,3},{2,0},{3,1},{4,6},{5,7},{6,4},{7,5},{8,10},{9,11},{10,... | collective-permute-start | bytes 3538952 | tf_op jit(solution)/shard_map/ppermute | solution.py:522
  112.8 14.9 %collective-permute-start.24 = (bf16[8,2,48,768]{3,2,1,0:T(8,128)(2,1)}, bf16[8,2,48,768]{3,2,1,0:T(8,128)(2,1)}, u32[]{:S(2)}, u32[]{:S(2)}) collective-permute-start(bf16[8,2,48,768]{3,2,1,0:T(8,128)(2,1)} %collective-permute-done.21.refs_4_.refs_17_.refs_14_), channel_id=1, source_target_pairs={{0,1},{1,0},{2,3},{3,2},{4,5},{5,4},{6,7},{7,6},{8,9},{9,8},{10,11... | collective-permute-start | bytes 3538952 | tf_op jit(solution)/shard_map/ppermute | solution.py:522
  112.8 14.9 %collective-permute-start.26 = (bf16[8,2,48,768]{3,2,1,0:T(8,128)(2,1)}, bf16[8,2,48,768]{3,2,1,0:T(8,128)(2,1)}, u32[]{:S(2)}, u32[]{:S(2)}) collective-permute-start(bf16[8,2,48,768]{3,2,1,0:T(8,128)(2,1)} %collective-permute-done.22.refs_6_.refs_19_.refs_16_), channel_id=1, source_target_pairs={{0,1},{1,0},{2,3},{3,2},{4,5},{5,4},{6,7},{7,6},{8,9},{9,8},{10,11... | collective-permute-start | bytes 3538952 | tf_op jit(solution)/shard_map/ppermute | solution.py:522
  126.4 20.6 %collective-permute-start.28 = (bf16[2,8,48,768]{3,2,1,0:T(8,128)(2,1)}, bf16[2,8,48,768]{3,2,1,0:T(8,128)(2,1)}, u32[]{:S(2)}, u32[]{:S(2)}) collective-permute-start(bf16[2,8,48,768]{3,2,1,0:T(8,128)(2,1)} %get-tuple-element.156), channel_id=1, source_target_pairs={{0,1},{1,0},{2,3},{3,2},{4,5},{5,4},{6,7},{7,6},{8,9},{9,8},{10,11... | collective-permute-start | bytes 3538952 | tf_op jit(solution)/shard_map/ppermute | solution.py:522
  126.5 20.6 %collective-permute-start.27 = (bf16[2,8,48,768]{3,2,1,0:T(8,128)(2,1)}, bf16[2,8,48,768]{3,2,1,0:T(8,128)(2,1)}, u32[]{:S(2)}, u32[]{:S(2)}) collective-permute-start(bf16[2,8,48,768]{3,2,1,0:T(8,128)(2,1)} %get-tuple-element.157), channel_id=1, source_target_pairs={{0,1},{1,0},{2,3},{3,2},{4,5},{5,4},{6,7},{7,6},{8,9},{9,8},{10,11... | collective-permute-start | bytes 3538952 | tf_op jit(solution)/shard_map/ppermute | solution.py:522
  148.6 17.2 %collective-permute-start.29 = (bf16[8,48,768]{2,1,0:T(8,128)(2,1)S(1)}, bf16[8,48,768]{2,1,0:T(8,128)(2,1)S(1)}, u32[]{:S(2)}, u32[]{:S(2)}) collective-permute-start(bf16[8,48,768]{2,1,0:T(8,128)(2,1)S(1)} %get-tuple-element.169), channel_id=1, source_target_pairs={{0,16},{16,0},{1,17},{17,1},{2,18},{18,2},{3,19},{19,3},{4,20},{20... | collective-permute-start | bytes 1769480 | tf_op jit(solution)/shard_map/ppermute | solution.py:526
  150.0 17.5 %collective-permute-start.30 = (bf16[8,48,768]{2,1,0:T(8,128)(2,1)S(1)}, bf16[8,48,768]{2,1,0:T(8,128)(2,1)S(1)}, u32[]{:S(2)}, u32[]{:S(2)}) collective-permute-start(bf16[8,48,768]{2,1,0:T(8,128)(2,1)S(1)} %get-tuple-element.170), channel_id=1, source_target_pairs={{0,2},{1,3},{2,0},{3,1},{4,6},{5,7},{6,4},{7,5},{8,10},{9,11},{10,... | collective-permute-start | bytes 1769480 | tf_op jit(solution)/shard_map/ppermute | solution.py:522
  169.8 17.4 %collective-permute-start.33 = (bf16[2,8,48,768]{3,2,1,0:T(8,128)(2,1)}, bf16[2,8,48,768]{3,2,1,0:T(8,128)(2,1)S(1)}, u32[]{:S(2)}, u32[]{:S(2)}) collective-permute-start(bf16[2,8,48,768]{3,2,1,0:T(8,128)(2,1)} %get-tuple-element.181), channel_id=1, source_target_pairs={{0,1},{1,0},{2,3},{3,2},{4,5},{5,4},{6,7},{7,6},{8,9},{9,8},{10,11... | collective-permute-start | bytes 3538952 | tf_op jit(solution)/shard_map/ppermute | solution.py:522
  169.9 17.4 %collective-permute-start.34 = (bf16[2,8,48,768]{3,2,1,0:T(8,128)(2,1)}, bf16[2,8,48,768]{3,2,1,0:T(8,128)(2,1)S(1)}, u32[]{:S(2)}, u32[]{:S(2)}) collective-permute-start(bf16[2,8,48,768]{3,2,1,0:T(8,128)(2,1)} %get-tuple-element.182), channel_id=1, source_target_pairs={{0,1},{1,0},{2,3},{3,2},{4,5},{5,4},{6,7},{7,6},{8,9},{9,8},{10,11... | collective-permute-start | bytes 3538952 | tf_op jit(solution)/shard_map/ppermute | solution.py:522
  170.3 16.9 %collective-permute-start.31 = (bf16[4,48,768]{2,1,0:T(8,128)(2,1)}, bf16[4,48,768]{2,1,0:T(8,128)(2,1)S(1)}, u32[]{:S(2)}, u32[]{:S(2)}) collective-permute-start(bf16[4,48,768]{2,1,0:T(8,128)(2,1)} %get-tuple-element.179), channel_id=1, source_target_pairs={{0,2},{1,3},{2,0},{3,1},{4,6},{5,7},{6,4},{7,5},{8,10},{9,11},{10,... | collective-permute-start | bytes 884744 | tf_op jit(solution)/shard_map/ppermute | solution.py:522
  172.1 15.2 %collective-permute-start.32 = (bf16[4,48,768]{2,1,0:T(8,128)(2,1)}, bf16[4,48,768]{2,1,0:T(8,128)(2,1)}, u32[]{:S(2)}, u32[]{:S(2)}) collective-permute-start(bf16[4,48,768]{2,1,0:T(8,128)(2,1)} %get-tuple-element.180), channel_id=1, source_target_pairs={{0,16},{16,0},{1,17},{17,1},{2,18},{18,2},{3,19},{19,3},{4,20},{20... | collective-permute-start | bytes 884744 | tf_op jit(solution)/shard_map/ppermute | solution.py:526
  194.0 17.8 %collective-permute-start.38 = (bf16[8,48,768]{2,1,0:T(8,128)(2,1)}, bf16[8,48,768]{2,1,0:T(8,128)(2,1)S(1)}, u32[]{:S(2)}, u32[]{:S(2)}) collective-permute-start(bf16[8,48,768]{2,1,0:T(8,128)(2,1)} %get-tuple-element.193), channel_id=1, source_target_pairs={{0,16},{16,0},{1,17},{17,1},{2,18},{18,2},{3,19},{19,3},{4,20},{20... | collective-permute-start | bytes 1769480 | tf_op jit(solution)/shard_map/ppermute | solution.py:526
  195.4 16.4 %collective-permute-start.39 = (bf16[8,48,768]{2,1,0:T(8,128)(2,1)}, bf16[8,48,768]{2,1,0:T(8,128)(2,1)S(1)}, u32[]{:S(2)}, u32[]{:S(2)}) collective-permute-start(bf16[8,48,768]{2,1,0:T(8,128)(2,1)} %get-tuple-element.194), channel_id=1, source_target_pairs={{0,2},{1,3},{2,0},{3,1},{4,6},{5,7},{6,4},{7,5},{8,10},{9,11},{10,... | collective-permute-start | bytes 1769480 | tf_op jit(solution)/shard_map/ppermute | solution.py:522
  195.7 16.1 %collective-permute-start.35 = (bf16[2,48,768]{2,1,0:T(8,128)(2,1)}, bf16[2,48,768]{2,1,0:T(8,128)(2,1)S(1)}, u32[]{:S(2)}, u32[]{:S(2)}) collective-permute-start(bf16[2,48,768]{2,1,0:T(8,128)(2,1)} %pad_maximum_fusion.12), channel_id=1, source_target_pairs={{0,4},{1,5},{2,6},{3,7},{4,0},{5,1},{6,2},{7,3},{8,12},{9,13},{10,... | collective-permute-start | bytes 442376 | tf_op jit(solution)/shard_map/ppermute | solution.py:522
  195.8 16.0 %collective-permute-start.36 = (bf16[2,48,768]{2,1,0:T(8,128)(2,1)}, bf16[2,48,768]{2,1,0:T(8,128)(2,1)S(1)}, u32[]{:S(2)}, u32[]{:S(2)}) collective-permute-start(bf16[2,48,768]{2,1,0:T(8,128)(2,1)} %pad_maximum_fusion.13), channel_id=1, source_target_pairs={{0,8},{1,9},{2,10},{3,11},{4,12},{5,13},{6,14},{7,15},{8,0},{9,1},... | collective-permute-start | bytes 442376 | tf_op jit(solution)/shard_map/ppermute | solution.py:522
  198.9 12.9 %collective-permute-start.37 = (bf16[2,48,768]{2,1,0:T(8,128)(2,1)}, bf16[2,48,768]{2,1,0:T(8,128)(2,1)}, u32[]{:S(2)}, u32[]{:S(2)}) collective-permute-start(bf16[2,48,768]{2,1,0:T(8,128)(2,1)} %pad_maximum_fusion.14), channel_id=1, source_target_pairs={{0,12},{1,13},{2,14},{3,15},{4,8},{5,9},{6,10},{7,11},{8,4},{9,5},... | collective-permute-start | bytes 442376 | tf_op jit(solution)/shard_map/ppermute | solution.py:522
  214.7 28.4 %collective-permute-start.42 = (bf16[2,8,48,768]{3,2,1,0:T(8,128)(2,1)}, bf16[2,8,48,768]{3,2,1,0:T(8,128)(2,1)S(1)}, u32[]{:S(2)}, u32[]{:S(2)}) collective-permute-start(bf16[2,8,48,768]{3,2,1,0:T(8,128)(2,1)} %get-tuple-element.209), channel_id=1, source_target_pairs={{0,1},{1,0},{2,3},{3,2},{4,5},{5,4},{6,7},{7,6},{8,9},{9,8},{10,11... | collective-permute-start | bytes 3538952 | tf_op jit(solution)/shard_map/ppermute | solution.py:522
  214.7 28.4 %collective-permute-start.43 = (bf16[2,8,48,768]{3,2,1,0:T(8,128)(2,1)}, bf16[2,8,48,768]{3,2,1,0:T(8,128)(2,1)S(1)}, u32[]{:S(2)}, u32[]{:S(2)}) collective-permute-start(bf16[2,8,48,768]{3,2,1,0:T(8,128)(2,1)} %get-tuple-element.210), channel_id=1, source_target_pairs={{0,1},{1,0},{2,3},{3,2},{4,5},{5,4},{6,7},{7,6},{8,9},{9,8},{10,11... | collective-permute-start | bytes 3538952 | tf_op jit(solution)/shard_map/ppermute | solution.py:522
  220.4 22.6 %collective-permute-start.44 = (bf16[2,48,768]{2,1,0:T(8,128)(2,1)}, bf16[2,48,768]{2,1,0:T(8,128)(2,1)S(1)}, u32[]{:S(2)}, u32[]{:S(2)}) collective-permute-start(bf16[2,48,768]{2,1,0:T(8,128)(2,1)} %add_convert_fusion.8), channel_id=1, source_target_pairs={{0,16},{16,0},{1,17},{17,1},{2,18},{18,2},{3,19},{19,3},{4,20},{20... | collective-permute-start | bytes 442376 | tf_op jit(solution)/shard_map/ppermute | solution.py:526
  221.1 21.9 %collective-permute-start.40 = (bf16[4,48,768]{2,1,0:T(8,128)(2,1)}, bf16[4,48,768]{2,1,0:T(8,128)(2,1)S(1)}, u32[]{:S(2)}, u32[]{:S(2)}) collective-permute-start(bf16[4,48,768]{2,1,0:T(8,128)(2,1)} %get-tuple-element.207), channel_id=1, source_target_pairs={{0,2},{1,3},{2,0},{3,1},{4,6},{5,7},{6,4},{7,5},{8,10},{9,11},{10,... | collective-permute-start | bytes 884744 | tf_op jit(solution)/shard_map/ppermute | solution.py:522
  222.9 20.2 %collective-permute-start.41 = (bf16[4,48,768]{2,1,0:T(8,128)(2,1)}, bf16[4,48,768]{2,1,0:T(8,128)(2,1)}, u32[]{:S(2)}, u32[]{:S(2)}) collective-permute-start(bf16[4,48,768]{2,1,0:T(8,128)(2,1)} %get-tuple-element.208), channel_id=1, source_target_pairs={{0,16},{16,0},{1,17},{17,1},{2,18},{18,2},{3,19},{19,3},{4,20},{20... | collective-permute-start | bytes 884744 | tf_op jit(solution)/shard_map/ppermute | solution.py:526
  249.8 20.9 %collective-permute-start.47 = (bf16[2,48,768]{2,1,0:T(8,128)(2,1)}, bf16[2,48,768]{2,1,0:T(8,128)(2,1)}, u32[]{:S(2)}, u32[]{:S(2)}) collective-permute-start(bf16[2,48,768]{2,1,0:T(8,128)(2,1)} %pad_maximum_fusion.16), channel_id=1, source_target_pairs={{0,4},{1,5},{2,6},{3,7},{4,0},{5,1},{6,2},{7,3},{8,12},{9,13},{10,... | collective-permute-start | bytes 442376 | tf_op jit(solution)/shard_map/ppermute | solution.py:522
  250.0 20.7 %collective-permute-start.48 = (bf16[2,48,768]{2,1,0:T(8,128)(2,1)}, bf16[2,48,768]{2,1,0:T(8,128)(2,1)}, u32[]{:S(2)}, u32[]{:S(2)}) collective-permute-start(bf16[2,48,768]{2,1,0:T(8,128)(2,1)} %pad_maximum_fusion.17), channel_id=1, source_target_pairs={{0,8},{1,9},{2,10},{3,11},{4,12},{5,13},{6,14},{7,15},{8,0},{9,1},... | collective-permute-start | bytes 442376 | tf_op jit(solution)/shard_map/ppermute | solution.py:522
  253.0 17.7 %collective-permute-start.49 = (bf16[2,48,768]{2,1,0:T(8,128)(2,1)}, bf16[2,48,768]{2,1,0:T(8,128)(2,1)}, u32[]{:S(2)}, u32[]{:S(2)}) collective-permute-start(bf16[2,48,768]{2,1,0:T(8,128)(2,1)} %pad_maximum_fusion.18), channel_id=1, source_target_pairs={{0,12},{1,13},{2,14},{3,15},{4,8},{5,9},{6,10},{7,11},{8,4},{9,5},... | collective-permute-start | bytes 442376 | tf_op jit(solution)/shard_map/ppermute | solution.py:522
  254.2 16.5 %collective-permute-start.45 = (bf16[8,48,768]{2,1,0:T(8,128)(2,1)}, bf16[8,48,768]{2,1,0:T(8,128)(2,1)}, u32[]{:S(2)}, u32[]{:S(2)}) collective-permute-start(bf16[8,48,768]{2,1,0:T(8,128)(2,1)} %get-tuple-element.222), channel_id=1, source_target_pairs={{0,16},{16,0},{1,17},{17,1},{2,18},{18,2},{3,19},{19,3},{4,20},{20... | collective-permute-start | bytes 1769480 | tf_op jit(solution)/shard_map/ppermute | solution.py:526
  254.9 15.9 %collective-permute-start.46 = (bf16[8,48,768]{2,1,0:T(8,128)(2,1)S(1)}, bf16[8,48,768]{2,1,0:T(8,128)(2,1)S(1)}, u32[]{:S(2)}, u32[]{:S(2)}) collective-permute-start(bf16[8,48,768]{2,1,0:T(8,128)(2,1)S(1)} %get-tuple-element.223), channel_id=1, source_target_pairs={{0,2},{1,3},{2,0},{3,1},{4,6},{5,7},{6,4},{7,5},{8,10},{9,11},{10,... | collective-permute-start | bytes 1769480 | tf_op jit(solution)/shard_map/ppermute | solution.py:522
  272.1 6.8 %collective-permute-start.50 = (bf16[4,48,768]{2,1,0:T(8,128)(2,1)S(1)}, bf16[4,48,768]{2,1,0:T(8,128)(2,1)S(1)}, u32[]{:S(2)}, u32[]{:S(2)}) collective-permute-start(bf16[4,48,768]{2,1,0:T(8,128)(2,1)S(1)} %fusion.9), channel_id=1, source_target_pairs={{0,2},{1,3},{2,0},{3,1},{4,6},{5,7},{6,4},{7,5},{8,10},{9,11},{10,... | collective-permute-start | bytes 884744 | tf_op jit(solution)/shard_map/ppermute | solution.py:522
  280.2 6.8 %collective-permute-start.51 = (bf16[4,48,768]{2,1,0:T(8,128)(2,1)S(1)}, bf16[4,48,768]{2,1,0:T(8,128)(2,1)S(1)}, u32[]{:S(2)}, u32[]{:S(2)}) collective-permute-start(bf16[4,48,768]{2,1,0:T(8,128)(2,1)S(1)} %get-tuple-element.246), channel_id=1, source_target_pairs={{0,16},{16,0},{1,17},{17,1},{2,18},{18,2},{3,19},{19,3},{4,20},{20... | collective-permute-start | bytes 884744 | tf_op jit(solution)/shard_map/ppermute | solution.py:526
  287.2 28.1 %copy-start.26 = (bf16[1,48,768]{2,1,0:T(8,128)(2,1)S(1)}, bf16[1,48,768]{2,1,0:T(8,128)(2,1)}, u32[]{:S(2)}) copy-start(bf16[1,48,768]{2,1,0:T(8,128)(2,1)} %get-tuple-element.267) | copy-start | bytes 221188
  289.0 1.2 collective-permute-start.57
  290.3 3.7 %collective-permute-start.58 = (f32[4,384]{1,0:T(4,128)S(1)}, f32[4,384]{1,0:T(4,128)S(1)}, u32[]{:S(2)}, u32[]{:S(2)}) collective-permute-start(f32[4,384]{1,0:T(4,128)S(1)} %bitcast.195), channel_id=1, source_target_pairs={{0,2},{1,3},{2,0},{3,1},{4,6},{5,7},{6,4},{7,5},{8,10},{9,11},{10,... | collective-permute-start | bytes 18440 | tf_op jit(solution)/shard_map/ppermute | solution.py:522
  294.0 4.5 %collective-permute-start.60 = (f32[384]{0:T(512)S(1)}, f32[384]{0:T(512)S(1)}, u32[]{:S(2)}, u32[]{:S(2)}) collective-permute-start(f32[384]{0:T(512)S(1)} %get-tuple-element.237), channel_id=1, source_target_pairs={{0,8},{1,9},{2,10},{3,11},{4,12},{5,13},{6,14},{7,15},{8,0},{9,1},... | collective-permute-start | bytes 4616 | tf_op jit(solution)/shard_map/ppermute | solution.py:522
  294.5 5.4 %collective-permute-start.61 = (f32[384]{0:T(512)S(1)}, f32[384]{0:T(512)S(1)}, u32[]{:S(2)}, u32[]{:S(2)}) collective-permute-start(f32[384]{0:T(512)S(1)} %get-tuple-element.238), channel_id=1, source_target_pairs={{0,12},{1,13},{2,14},{3,15},{4,8},{5,9},{6,10},{7,11},{8,4},{9,5},... | collective-permute-start | bytes 4616 | tf_op jit(solution)/shard_map/ppermute | solution.py:522
  296.7 3.6 %collective-permute-start.59 = (f32[384]{0:T(512)S(1)}, f32[384]{0:T(512)S(1)}, u32[]{:S(2)}, u32[]{:S(2)}) collective-permute-start(f32[384]{0:T(512)S(1)} %get-tuple-element.239), channel_id=1, source_target_pairs={{0,4},{1,5},{2,6},{3,7},{4,0},{5,1},{6,2},{7,3},{8,12},{9,13},{10,... | collective-permute-start | bytes 4616 | tf_op jit(solution)/shard_map/ppermute | solution.py:522
  300.2 7.6 %collective-permute-start.62 = (f32[384]{0:T(512)S(1)}, f32[384]{0:T(512)S(1)}, u32[]{:S(2)}, u32[]{:S(2)}) collective-permute-start(f32[384]{0:T(512)S(1)} %add_add_fusion), channel_id=1, source_target_pairs={{0,16},{16,0},{1,17},{17,1},{2,18},{18,2},{3,19},{19,3},{4,20},{20... | collective-permute-start | bytes 4616 | tf_op jit(solution)/shard_map/ppermute | solution.py:526
  302.9 7.8 %collective-permute-start.52 = (bf16[2,48,768]{2,1,0:T(8,128)(2,1)S(1)}, bf16[2,48,768]{2,1,0:T(8,128)(2,1)S(1)}, u32[]{:S(2)}, u32[]{:S(2)}) collective-permute-start(bf16[2,48,768]{2,1,0:T(8,128)(2,1)S(1)} %pad_maximum_fusion.20), channel_id=1, source_target_pairs={{0,4},{1,5},{2,6},{3,7},{4,0},{5,1},{6,2},{7,3},{8,12},{9,13},{10,... | collective-permute-start | bytes 442376 | tf_op jit(solution)/shard_map/ppermute | solution.py:522
  303.7 11.6 %collective-permute-start.53 = (bf16[2,48,768]{2,1,0:T(8,128)(2,1)S(1)}, bf16[2,48,768]{2,1,0:T(8,128)(2,1)S(1)}, u32[]{:S(2)}, u32[]{:S(2)}) collective-permute-start(bf16[2,48,768]{2,1,0:T(8,128)(2,1)S(1)} %pad_maximum_fusion.21), channel_id=1, source_target_pairs={{0,8},{1,9},{2,10},{3,11},{4,12},{5,13},{6,14},{7,15},{8,0},{9,1},... | collective-permute-start | bytes 442376 | tf_op jit(solution)/shard_map/ppermute | solution.py:522
  305.4 9.9 %collective-permute-start.54 = (bf16[2,48,768]{2,1,0:T(8,128)(2,1)S(1)}, bf16[2,48,768]{2,1,0:T(8,128)(2,1)S(1)}, u32[]{:S(2)}, u32[]{:S(2)}) collective-permute-start(bf16[2,48,768]{2,1,0:T(8,128)(2,1)S(1)} %pad_maximum_fusion.22), channel_id=1, source_target_pairs={{0,12},{1,13},{2,14},{3,15},{4,8},{5,9},{6,10},{7,11},{8,4},{9,5},... | collective-permute-start | bytes 442376 | tf_op jit(solution)/shard_map/ppermute | solution.py:522
  307.4 8.6 %collective-permute-start.56 = (bf16[2,48,768]{2,1,0:T(8,128)(2,1)S(1)}, bf16[2,48,768]{2,1,0:T(8,128)(2,1)S(1)}, u32[]{:S(2)}, u32[]{:S(2)}) collective-permute-start(bf16[2,48,768]{2,1,0:T(8,128)(2,1)S(1)} %add_convert_fusion.6), channel_id=1, source_target_pairs={{0,16},{16,0},{1,17},{17,1},{2,18},{18,2},{3,19},{19,3},{4,20},{20... | collective-permute-start | bytes 442376 | tf_op jit(solution)/shard_map/ppermute | solution.py:526
  315.4 5.2 %collective-permute-start.55 = (bf16[2,48,768]{2,1,0:T(8,128)(2,1)S(1)}, bf16[2,48,768]{2,1,0:T(8,128)(2,1)S(1)}, u32[]{:S(2)}, u32[]{:S(2)}) collective-permute-start(bf16[2,48,768]{2,1,0:T(8,128)(2,1)S(1)} %add_convert_fusion.7), channel_id=1, source_target_pairs={{0,16},{16,0},{1,17},{17,1},{2,18},{18,2},{3,19},{19,3},{4,20},{20... | collective-permute-start | bytes 442376 | tf_op jit(solution)/shard_map/ppermute | solution.py:526
  (36 other events, 308.1 us)

commit v2 on v1

v2 whole, which is shorter than its diff:
```python
import functools

import jax
import jax.numpy as jnp
from jax import lax
from jax.experimental import pallas as pl
from jax.experimental.pallas import tpu as pltpu
from jax.sharding import PartitionSpec as P

HEADS = 12
HEAD = 64
IMG = 196
EPS = 1e-06
GELU_C = 0.7978845608028654
GELU_A = 0.044715

F32 = jnp.float32
BF16 = jnp.bfloat16
HBM = pl.BlockSpec(memory_space=pltpu.HBM)
VMEM = pl.BlockSpec(memory_space=pltpu.VMEM)
SMEM = pl.BlockSpec(memory_space=pltpu.SMEM)


def dot_nn(a, b):
    return lax.dot_general(a, b, (((1,), (0,)), ((), ())), preferred_element_type=F32)


def dot_nt(a, b):
    return lax.dot_general(a, b, (((1,), (1,)), ((), ())), preferred_element_type=F32)


def dot_tn(a, b):
    return lax.dot_general(a, b, (((0,), (0,)), ((), ())), preferred_element_type=F32)


def norm_rows(rows):
    rows = rows.astype(F32)
    mean = jnp.mean(rows, axis=1, keepdims=True)
    centered = rows - mean
    inv = lax.rsqrt(jnp.mean(centered * centered, axis=1, keepdims=True) + EPS)
    return centered * inv, inv


def attend(refs, base, cols, windows):
    q_ref, k_ref, v_ref, da_ref, o_ref, dq_ref, dk_ref, dv_ref = refs
    zero = jnp.zeros((), BF16)
    jobs, ends = [], {}
    for start, rows, lo, hi, merge in windows:
        win = pl.ds(pl.multiple_of(base + start, 16), rows)
        tiles = [r[win, cols] for r in (q_ref, k_ref, v_ref, da_ref)]
        lane = lax.broadcasted_iota(jnp.int32, (rows, 128), 1)
        sums = {}
        step = 256 if rows == 512 else rows
        for at in range(0, rows, step):
            for h in range(2):
                keep = (lane < 64) if h == 0 else (lane >= 64)
                heads = [jnp.where(keep, t, zero) for t in tiles]
                jobs.append([tiles, heads, rows, lo, hi, at, step, sums])
        ends[len(jobs) - 1] = (start, rows, merge, sums)

    def products(job):
        tiles, heads, _, _, _, at, step, _ = job
        qs = slice(at, at + step)
        job += [dot_nt(tiles[1], heads[0][qs]), dot_nt(tiles[2], heads[3][qs])]

    def soften(job):
        _, _, rows, lo, hi, at, step, _, s, dp = job
        masked = lo > 0 or hi < rows
        if masked:
            key = lax.broadcasted_iota(jnp.int32, (rows, step), 0)
            s = jnp.where((key >= lo) & (key < hi), s, -1e30)
        e = jnp.exp(s - jnp.max(s, axis=0, keepdims=True))
        scale = 1.0 / jnp.sum(e, axis=0, keepdims=True)
        if masked:
            query = lax.broadcasted_iota(jnp.int32, (1, step), 1) + at
            scale = jnp.where((query >= lo) & (query < hi), scale, 0.0)
        p = e * scale
        inner = jnp.sum(p * dp, axis=0, keepdims=True)
        job[8:] = [p.astype(BF16), (p * (dp - inner)).astype(BF16)]

    def gather(job):
        _, heads, _, _, _, at, step, sums, p, ds = job
        qs = slice(at, at + step)
        parts = (
            (("o", at), dot_tn(p, heads[2])),
            (("q", at), dot_tn(ds, heads[1])),
            (("v", 0), dot_nn(p, heads[3][qs])),
            (("k", 0), dot_nn(ds, heads[0][qs])),
        )
        for key, val in parts:
            sums[key] = sums[key] + val if key in sums else val

    def write(start, rows, merge, sums):
        for name, ref in (("o", o_ref), ("q", dq_ref), ("k", dk_ref), ("v", dv_ref)):
            for (n, at), val in sums.items():
                if n != name:
                    continue
                val = (val * 0.125 if n == "q" else val).astype(BF16)
                size = val.shape[0]
                if merge and at == 0:
                    head = pl.ds(pl.multiple_of(base + start, 16), merge)
                    ref[head, cols] = ref[head, cols] + val[:merge]
                    val, at, size = val[merge:], merge, size - merge
                ref[pl.ds(pl.multiple_of(base + start + at, 16), size), cols] = val

    for i in range(len(jobs) + 2):
        if i < len(jobs):
            products(jobs[i])
        if 0 <= i - 1 < len(jobs):
            soften(jobs[i - 1])
        if 0 <= i - 2:
            gather(jobs[i - 2])
            if i - 2 in ends:
                write(*ends[i - 2])


WHOLE = ((0, 512, 0, 512, 0),)
SMALL = (
    (0, 208, 0, IMG, 0),
    (192, 208, IMG - 192, 2 * IMG - 192, 16),
    (384, 128, 2 * IMG - 384, 128, 16),
)


def sds(shape, dtype=BF16):
    return jax.ShapeDtypeStruct(shape, dtype)


def kept(shape, dtype=BF16):
    return pltpu.VMEM(shape, dtype)


def call(kernel, name, operands, pieces, outs, g_shapes, scratch, flops, limit=14, alias=None):
    n_p, n_g = len(pieces), len(g_shapes)
    scal, *rest = operands
    rest = [pltpu.with_memory_space_constraint(v, pltpu.VMEM) for v in rest]
    pieces = [pltpu.with_memory_space_constraint(v, pltpu.HBM) for v in pieces]
    g_shapes = [pltpu.HBM(g.shape, g.dtype) for g in g_shapes]
    return pl.pallas_call(
        kernel,
        name=name,
        out_shape=list(outs) + list(g_shapes),
        in_specs=[SMEM] + [VMEM] * len(rest) + [HBM] * n_p,
        out_specs=[VMEM] * len(outs) + [HBM] * n_g,
        scratch_shapes=scratch,
        compiler_params=pltpu.CompilerParams(vmem_limit_bytes=limit << 20),
        input_output_aliases=alias or {},
        cost_estimate=pl.CostEstimate(flops=flops, bytes_accessed=1 << 20, transcendentals=0),
    )(scal, *rest, *pieces)


def loop(count, fn, after=None):
    def step(i, c):
        fn(i)
        if after is not None:
            after(i)
        return c

    lax.fori_loop(0, count, step, 0)


def send_rows(src, dst, i, size, sem):
    per = dst.shape[1] // size
    pltpu.make_async_copy(src.at[rows_of(i, size), :], dst.at[i // per, rows_of(i % per, size), :], sem).start()


def rows_of(i, size):
    return pl.ds(pl.multiple_of(i * size, size), size)


def project_kernel(load, n_w, *refs):
    scal, x_ref, cot_ref, vec_ref = refs[:4]
    xn, q, k, v, da, w = refs[4 + n_w : 10 + n_w]
    (sem,) = refs[10 + n_w :]
    load(scal, refs[4 : 4 + n_w], w, sem, (0, 1, 2, 3))
    tokens = x_ref.shape[0]

    def norm(i):
        r = rows_of(i, 256)
        standard, _ = norm_rows(x_ref[r, :])
        xn[r, :] = (standard * vec_ref[0:1, :]).astype(BF16)

    loop(tokens // 256, norm)

    def ready(i):
        whole_wait(w.at[i], sem.at[i])()

    ready(0)
    q[...] = (dot_nn(xn[...], w[0]) + vec_ref[1:2, :]).astype(BF16) * jnp.asarray(0.125, BF16)
    ready(1)
    k[...] = dot_nn(xn[...], w[1]).astype(BF16)
    ready(2)
    v[...] = (dot_nn(xn[...], w[2]) + vec_ref[2:3, :]).astype(BF16)
    ready(3)
    da[...] = dot_nt(cot_ref[...], w[3]).astype(BF16)


def project_call(scal, x, cot, vec, weights, load):
    tokens, width = x.shape
    return call(
        functools.partial(project_kernel, load, len(weights)),
        "project",
        (scal, x, cot, vec),
        weights,
        [kept(x.shape)] * 5 + [kept((4, width, width))],
        [],
        [pltpu.SemaphoreType.DMA((4,))],
        8 * tokens * width * width,
    )


def core_kernel(scal, q, k, v, da, o, dq, dk, dv):
    tokens, width = q.shape
    pairs = width // 128

    def pair(i):
        b = i // pairs
        cols = pl.ds(pl.multiple_of(i % pairs * 128, 128), 128)
        refs = (q, k, v, da, o, dq, dk, dv)
        whole = scal[8 + b] == 0

        @pl.when(whole)
        def _():
            attend(refs, b * 512, cols, WHOLE)

        @pl.when(jnp.logical_not(whole))
        def _():
            attend(refs, b * 512, cols, SMALL)

    loop(tokens // 512 * pairs, pair)


def core_call(scal, q, k, v, da):
    return call(core_kernel, "core", (scal, q, k, v, da), [], [kept(q.shape)] * 4, [], [], 20 << 30)


def attn_grad_kernel(store, scal, xn, o, dq, dk, dv, cot, sums, *refs):
    *g_refs, g, sem = refs
    tokens, width = xn.shape
    for b, (lhs, rhs) in enumerate(((xn, dq), (xn, dk), (xn, dv), (o, cot))):
        g[b] = dot_tn(lhs[...], rhs[...]).astype(BF16)
    done = store(scal, g, g_refs, sem)
    ones = jnp.ones((8, tokens), BF16)
    sums[0:1, :] = dot_nn(ones, dq[...])[0:1]
    sums[1:2, :] = dot_nn(ones, dv[...])[0:1]
    sums[2:3, :] = dot_nn(ones, cot[...])[0:1]
    done()


def attn_grad_call(scal, xn, o, dq, dk, dv, cot, store, g_shapes):
    tokens, width = xn.shape
    return call(
        functools.partial(attn_grad_kernel, store),
        "attn_grad",
        (scal, xn, o, dq, dk, dv, cot),
        [],
        [kept((8, width), F32)],
        g_shapes,
        [pltpu.VMEM((4, width, width), BF16), pltpu.SemaphoreType.DMA((len(g_shapes),))],
        8 * tokens * width * width,
    )


def gelu_parts(u):
    u2 = u * u
    half = 0.5 * jnp.tanh(u * (GELU_C + (GELU_C * GELU_A) * u2)) + 0.5
    act = u * half
    grad = half + act * (1.0 - half) * (2.0 * GELU_C + (6.0 * GELU_C * GELU_A) * u2)
    return act, grad

def tile_of(t, width):
    return pl.ds(t * width if isinstance(t, int) else pl.multiple_of(t * width, 128), width)


def wait_tile(w, sem, t, width):
    whole_wait(w.at[tile_of(t, width), :], sem.at[t])()


def up_kernel(load_u, load_d, n_u, n_d, *refs):
    scal, xn, bias = refs[:3]
    act, gp, wu, wd = refs[3 + n_u + n_d : 7 + n_u + n_d]
    even, odd, sem_u, sem_d = refs[7 + n_u + n_d :]
    tokens, width = xn.shape
    load_u(scal, refs[3 : 3 + n_u], wu, sem_u)
    load_d(scal, refs[3 + n_u : 3 + n_u + n_d] or refs[3 : 3 + n_u], wd, sem_d)
    tiles = bias.shape[0]
    rows = even.shape[0]
    per = tokens // rows

    def product(i):
        t = i // per
        return dot_nn(xn[rows_of(i % per, rows), :], wu[tile_of(t, width), :])

    def finish(i, u):
        t, r = i // per, rows_of(i % per, rows)
        a, gr = gelu_parts(u + bias[pl.ds(t, 1), :])
        act[t, r, :] = a.astype(BF16)
        gp[t, r, :] = gr.astype(BF16)

    for t in range(tiles):
        wait_tile(wu, sem_u, t, width)
    even[...] = product(0)

    def step(i):
        odd[...] = product(2 * i + 1)
        finish(2 * i, even[...])
        even[...] = product(2 * i + 2)
        finish(2 * i + 1, odd[...])

    last = tiles * per - 1
    loop(last // 2, step)
    odd[...] = product(last)
    finish(last - 1, even[...])
    finish(last, odd[...])
    for t in range(tiles):
        wait_tile(wd, sem_d, t, width)


def up_call(scal, xn, bias, up_w, down_w, load_u, load_d):
    tokens, width = xn.shape
    tiles = bias.shape[0]
    return call(
        functools.partial(up_kernel, load_u, load_d, len(up_w), len(down_w)),
        "up",
        (scal, xn, bias),
        [*up_w, *down_w],
        [kept((tiles, tokens, width))] * 2 + [kept((tiles * width, width))] * 2,
        [],
        [pltpu.VMEM((256, width), F32)] * 2 + [pltpu.SemaphoreType.DMA((tiles,)), pltpu.SemaphoreType.DMA((tiles,))],
        2 * tiles * tokens * width * width,
    )


def down_grad_kernel(store, scal, act, cot, *refs):
    *g_refs, g, sem = refs
    tiles, tokens, width = act.shape

    def grad(t):
        g[tile_of(t, width), :] = dot_tn(act[t], cot[...]).astype(BF16)

    loop(tiles, grad)
    store(scal, g, g_refs, sem)()


def down_grad_call(scal, act, cot, store, g_shapes):
    tiles, tokens, width = act.shape
    return call(
        functools.partial(down_grad_kernel, store),
        "down_grad",
        (scal, act, cot),
        [],
        [],
        g_shapes,
        [pltpu.VMEM((tiles * width, width), BF16), pltpu.SemaphoreType.DMA((len(g_shapes),))],
        2 * tiles * tokens * width * width,
    )


def dpre_kernel(scal, cot, gp, w, dpre, sums):
    tiles, tokens, width = gp.shape
    ones = jnp.ones((8, tokens), BF16)

    def down(t):
        dpre[t] = (dot_nt(cot[...], w[tile_of(t, width), :]) * gp[t].astype(F32)).astype(BF16)

    loop(tiles, down)
    for t in range(tiles):
        sums[t : t + 1, :] = dot_nn(ones, dpre[t])[0:1]


def dpre_call(scal, cot, gp, w):
    tiles, tokens, width = gp.shape
    return call(
        dpre_kernel,
        "dpre",
        (scal, cot, gp, w),
        [],
        [kept(gp.shape), kept((8, width), F32)],
        [],
        [],
        2 * tiles * tokens * width * width,
        alias={2: 0},
    )


def up_grad_kernel(store, scal, xn, dpre, *refs):
    *g_refs, g, sem = refs
    tiles, tokens, width = dpre.shape

    def grad(t):
        g[t] = dot_tn(xn[...], dpre[t]).astype(BF16)

    loop(tiles, grad)
    store(scal, g, g_refs, sem)()


def up_grad_call(scal, xn, dpre, store, g_shapes):
    tiles, tokens, width = dpre.shape
    return call(
        functools.partial(up_grad_kernel, store),
        "up_grad",
        (scal, xn, dpre),
        [],
        [],
        g_shapes,
        [pltpu.VMEM((tiles, width, width), BF16), pltpu.SemaphoreType.DMA((len(g_shapes),))],
        2 * tiles * tokens * width * width,
    )


def input_grad_kernel(scal, x, cot, dq, dk, dv, dpre, vec, wa, wu, sums, dx_ref, dx, sem):
    tiles, tokens, width = dpre.shape
    sums[...] = jnp.zeros_like(sums)

    def step(i):
        r = rows_of(i, 256)
        dnr = dot_nt(dq[r, :], wa[0]) + dot_nt(dk[r, :], wa[1]) + dot_nt(dv[r, :], wa[2])
        for t in range(tiles):
            dnr += dot_nt(dpre[t, r, :], wu[tile_of(t, width), :])
        standard, inv = norm_rows(x[r, :])
        sums[0:1, :] += jnp.sum(dnr * standard, axis=0, keepdims=True)
        gs = dnr * vec[0:1, :]
        mean_g = jnp.mean(gs, axis=1, keepdims=True)
        mean_p = jnp.mean(gs * standard, axis=1, keepdims=True)
        dx[r, :] = (cot[r, :].astype(F32) + inv * (gs - mean_g - standard * mean_p)).astype(BF16)

    loop(tokens // 256, step, lambda i: send_rows(dx, dx_ref, i, 256, sem))
    whole_wait(dx_ref, sem)()


def input_grad_call(scal, x, cot, dq, dk, dv, dpre, vec, wa, wu):
    tiles, tokens, width = dpre.shape
    return call(
        input_grad_kernel,
        "input_grad",
        (scal, x, cot, dq, dk, dv, dpre, vec, wa, wu),
        [],
        [kept((8, width), F32)],
        [sds((tokens // 512, 512, width))],
        [pltpu.VMEM((tokens, width), BF16), pltpu.SemaphoreType.DMA],
        2 * (tiles + 3) * tokens * width * width,
    )


def out_kernel(scal, x, o, act, vec, wa, wd, out_ref, out, sem):
    tiles, tokens, width = act.shape

    def step(i):
        r = rows_of(i, 256)
        total = x[r, :].astype(F32) + vec[3:4, :] + dot_nn(o[r, :], wa[3])
        for t in range(tiles):
            total += dot_nn(act[t, r, :], wd[tile_of(t, width), :])
        out[r, :] = total.astype(BF16)

    loop(tokens // 256, step, lambda i: send_rows(out, out_ref, i, 256, sem))
    whole_wait(out_ref, sem)()


def out_call(scal, x, o, act, vec, wa, wd):
    tiles, tokens, width = act.shape
    (out,) = call(
        out_kernel,
        "out",
        (scal, x, o, act, vec, wa, wd),
        [],
        [],
        [sds((tokens // 512, 512, width))],
        [pltpu.VMEM((tokens, width), BF16), pltpu.SemaphoreType.DMA],
        2 * (tiles + 1) * tokens * width * width,
    )
    return out


def swap(value, mask):
    return lax.ppermute(value, "wide", [(i, i ^ mask) for i in range(16)])


def swap_y(value):
    return lax.ppermute(value, "narrow", [(0, 1), (1, 0)])


def slots():
    for part in range(2):
        for i in range(2):
            for s in range(2):
                half, side = (i, s) if part == 0 else (s, i)
                for k in range(4):
                    yield part, i, s * 4 + k, half, side, k


def device_of(scal, k, side, core):
    return ((scal[1] ^ k) * 2 + (scal[2] ^ side)) * 2 + (scal[3] ^ core)


def behind(value, *marks):
    return lax.optimization_barrier((value, marks))[0]


def gather_z(value):
    return [swap(value, k << 2) for k in (1, 2, 3)]


def gather_stack(half, got):
    got = [half] + got
    return [jnp.stack([t[i] for t in got]) for i in range(2)]


def gather_xy(za, zb):
    return swap(za, 2), swap_y(zb)


def total(*parts):
    return sum(v.astype(F32) for v in parts)


def mix(name, jobs):
    held = [v for job in jobs for v in job[1]]
    near = [v for job in jobs for v in job[2]]
    outs = [o for job in jobs for o in job[3]]

    def kernel(*refs):
        at = len(near) + len(held)
        scratch = refs[at + len(outs) :]
        copies = [
            pltpu.make_async_copy(refs[len(near) + i], scratch[i], scratch[-1].at[i]) for i in range(len(held))
        ]
        for cp in copies:
            cp.start()
        h = n = o = 0
        for fn, job_h, job_n, job_o in jobs:
            for i in range(len(job_h)):
                copies[h + i].wait()
            fn(
                scratch[h : h + len(job_h)],
                refs[n : n + len(job_n)],
                refs[at + o : at + o + len(job_o)],
            )
            h, n, o = h + len(job_h), n + len(job_n), o + len(job_o)

    got = pl.pallas_call(
        kernel,
        name=name,
        out_shape=outs,
        in_specs=[VMEM] * len(near) + [HBM] * len(held),
        out_specs=[VMEM] * len(outs),
        scratch_shapes=[pltpu.VMEM(v.shape, v.dtype) for v in held]
        + [pltpu.SemaphoreType.DMA((max(len(held), 1),))],
        compiler_params=pltpu.CompilerParams(vmem_limit_bytes=8 << 20),
        cost_estimate=pl.CostEstimate(flops=1 << 20, bytes_accessed=1 << 20, transcendentals=0),
    )(
        *[pltpu.with_memory_space_constraint(v, pltpu.VMEM) for v in near],
        *[pltpu.with_memory_space_constraint(v, pltpu.HBM) for v in held],
    )
    split, at = [], 0
    for job in jobs:
        split.append(got[at : at + len(job[3])])
        at += len(job[3])
    return split


def total(*parts):
    return sum(v.astype(F32) for v in parts)


def join_job(pairs):
    def fn(held, near, outs):
        for i, out in enumerate(outs):
            size = near[2 * i].shape[0]
            out[:size] = near[2 * i][...]
            out[size:] = near[2 * i + 1][...]

    near = [v for pair in pairs for v in pair]
    return fn, [], near, [kept((2 * a.shape[0], *a.shape[1:])) for a, _ in pairs]


def sum1_job(keep1, got1):
    def fn(held, near, outs):
        for i in range(2):
            outs[i][...] = total(held[0][i], near[0][i]).astype(BF16)

    return fn, [keep1], [got1], [kept(keep1.shape[1:])] * 2


def sum2_job(keep0, got0, got):
    half = keep0.shape[1] // 2

    def fn(held, near, outs):
        for i in range(2):
            outs[i][...] = total(held[0][i, half:], near[0][i, half:], near[1 + i][half:]).astype(BF16)

    return fn, [keep0], [got0, *got], [kept((half, *keep0.shape[2:]))] * 2


def sum3_job(keep0, got0, got, got2):
    half = keep0.shape[1] // 2

    def fn(held, near, outs):
        for k in range(half):
            for i in range(2):
                outs[k][i] = total(held[0][i, k], near[0][i, k], near[1 + i][k], near[3 + i][k]).astype(BF16)

    return fn, [keep0], [got0, *got, *got2], [kept((2, *keep0.shape[2:]))] * half


def sum4_job(own, got):
    def fn(held, near, outs):
        outs[0][...] = total(*[v[...] for v in near]).astype(BF16)

    return fn, [], [own, *got], [kept(own.shape)]


def place_kernel(scal, a_mine, a_other, d_mine, d_other, u_mine, u_other, joined, out, down):
    _, rows, width = a_mine.shape

    def place(half, a, d, u):
        for p in range(2):
            block = half * 2 + p
            down[pl.ds(block * rows, rows), :] = d[p].astype(F32)
            joined[:, (3 + block) * width : (4 + block) * width] = u[p].astype(F32)
            if block < 3:
                joined[:, block * width : (block + 1) * width] = a[p].astype(F32)
            else:
                out[...] = a[p].astype(F32)

    @pl.when(scal[0] == 0)
    def _():
        place(0, a_mine, d_mine, u_mine)
        place(1, a_other, d_other, u_other)

    @pl.when(scal[0] != 0)
    def _():
        place(1, a_mine, d_mine, u_mine)
        place(0, a_other, d_other, u_other)


def place_call(scal, parts):
    _, rows, width = parts[0].shape
    return pl.pallas_call(
        place_kernel,
        name="place",
        out_shape=[sds((rows, 7 * width), F32), sds((rows, width), F32), sds((4 * rows, width), F32)],
        in_specs=[SMEM] + [VMEM] * 6,
        out_specs=[VMEM] * 3,
    )(scal, *[pltpu.with_memory_space_constraint(v, pltpu.VMEM) for v in parts])


def whole_wait(ref, sem):
    return pltpu.make_async_copy(ref, ref, sem).wait


def load_attn(scal, refs, w, sem, blocks):
    def start(own):
        for block in blocks:
            for core in range(2):
                for part, i, slot, half, side, k in slots():
                    if (own ^ half) * 2 + part != block:
                        continue
                    src = refs[core * 4 + part * 2 + i]
                    rows = src.shape[1]
                    at = pl.multiple_of(device_of(scal, k, side, core) * rows, 16)
                    pltpu.make_async_copy(src.at[slot], w.at[block, pl.ds(at, rows), :], sem.at[block]).start()

    @pl.when(scal[0] == 0)
    def _():
        start(0)

    @pl.when(scal[0] != 0)
    def _():
        start(1)


def load_half(which):
    def load(scal, refs, w, sem):
        def start(rel):
            for core in range(2):
                for part, i, slot, half, side, k in slots():
                    if half != rel:
                        continue
                    src = refs[core * 4 + part * 2 + i]
                    per, rows, width = src.shape[1:]
                    dev = device_of(scal, k, side, core)
                    for b in range(per):
                        block = part * per + b
                        if which == 0:
                            at, tile = block * width + dev * rows, block
                        else:
                            at, tile = (dev * 2 * per + block) * rows, scal[1] ^ k
                        dst = w.at[pl.ds(pl.multiple_of(at, 16), rows), :]
                        pltpu.make_async_copy(src.at[slot, b], dst, sem.at[tile]).start()

        @pl.when(scal[0] == which)
        def _():
            start(0)

        @pl.when(scal[0] != which)
        def _():
            start(1)

    return load


def store_with(source):
    def store(scal, g, refs, sem):
        for core in range(2):
            for part, i, slot, half, side, k in slots():
                at = core * 2 + i
                dst = refs[at]
                src = source(g, scal[0] ^ half, part, device_of(scal, k, side, core), dst.shape[2], dst.shape[3])
                pltpu.make_async_copy(src, dst.at[part, slot], sem.at[at]).start()

        def done():
            for at in range(4):
                whole_wait(refs[at], sem.at[at])()

        return done

    return store


def rows_at(base, rows):
    return pl.ds(pl.multiple_of(base, 16), rows)


def attn_source(g, half, part, dev, rows, cols):
    return g.at[half * 2 + part, rows_at(dev * rows, rows), :]


def down_source(g, half, part, dev, rows, cols):
    return g.at[rows_at((dev * 4 + half * 2 + part) * rows, rows), :]


def load_whole_attn(scal, refs, w, sem, blocks):
    for i in blocks:
        pltpu.make_async_copy(refs[i], w.at[i], sem.at[i]).start()


def load_whole_mlp(scal, refs, w, sem):
    width = w.shape[1]
    for i, r in enumerate(refs):
        for t in range(r.shape[0] // width):
            at = i + t
            src = r.at[pl.ds(t * width, width), :]
            pltpu.make_async_copy(src, w.at[pl.ds(at * width, width), :], sem.at[at]).start()


def store_whole(scal, g, refs, sem):
    if len(refs) == 1:
        copies = [pltpu.make_async_copy(g, refs[0], sem.at[0])]
    else:
        copies = [pltpu.make_async_copy(g.at[i], r, sem.at[i]) for i, r in enumerate(refs)]
    for cp in copies:
        cp.start()

    def done():
        for cp in copies:
            cp.wait()

    return done


def body(sizes, tokens, image_ids, cotangent, w_joined, w_out, w_mlp, norm_gain, bias_attn, bias_mlp, bias_out):
    micro, length, width = tokens.shape
    narrow, wide = sizes
    paired = narrow == 2 and wide == 16
    rows = width // wide
    tiles = w_mlp.shape[0] // rows
    x = tokens.reshape(micro * length, width)
    cot = cotangent.reshape(micro * length, width)
    n = lax.axis_index("narrow")
    w = lax.axis_index("wide")
    last = image_ids.reshape(-1, 512)[:, -1]
    scal = [n, w >> 2, (w >> 1) & 1, w & 1] + [jnp.int32(0)] * 4 + [last[b] for b in range(last.shape[0])]
    scal = jnp.stack([jnp.asarray(s, jnp.int32) for s in scal])
    vec_own = jnp.concatenate([norm_gain, bias_attn, bias_mlp, bias_out])

    def vectors(vec):
        vec = vec.astype(F32)
        b_at = 3 * rows
        b_mlp = vec[:, b_at : b_at + tiles * rows].reshape(tiles, width)
        head = [
            vec[:, :rows].reshape(1, width),
            vec[:, rows:b_at].reshape(2, width),
            vec[:, b_at + tiles * rows :].reshape(1, width),
            jnp.zeros((4, width), F32),
        ]
        return jnp.concatenate(head), b_mlp

    def vector_grads(sums_a, sums_d, sums_x):
        return jnp.concatenate(
            [
                sums_x[0].reshape(wide, rows),
                sums_a[:2].reshape(wide, 2 * rows),
                sums_d[:tiles].reshape(wide, tiles * rows),
                sums_a[2].reshape(wide, rows),
            ],
            axis=1,
        )

    if not paired:
        full = lax.all_gather(w_joined, "wide", axis=0, tiled=True)
        parts = [full[:, i * width : (i + 1) * width] for i in range(3 + tiles)]
        attn_w = parts[:3] + [lax.all_gather(w_out, "wide", axis=0, tiled=True)]
        up_w = parts[3:]
        down_w = [lax.all_gather(w_mlp, "wide", axis=0, tiled=True)]
        vec, b_mlp = vectors(lax.all_gather(vec_own, "wide", axis=0))
        square = [sds((width, width))]
        xn, q, k, v, da, wa = project_call(scal, x, cot, vec, attn_w, load_whole_attn)
        o, dq, dk, dv = core_call(scal, q, k, v, da)
        sums_a, *g_attn = attn_grad_call(scal, xn, o, dq, dk, dv, cot, store_whole, square * 4)
        act, gp, wu, wd = up_call(scal, xn, b_mlp, up_w, down_w, load_whole_mlp, load_whole_mlp)
        g_down = down_grad_call(scal, act, cot, store_whole, [sds((tiles * width, width))])
        dpre, sums_d = dpre_call(scal, cot, gp, wd)
        g_up = up_grad_call(scal, xn, dpre, store_whole, square * tiles)
        sums_x, d_x = input_grad_call(scal, x, cot, dq, dk, dv, dpre, vec, wa, wu)
        out = out_call(scal, x, o, act, vec, wa, wd)

        def reduce(g):
            g = lax.psum_scatter(g.astype(F32), "wide", scatter_dimension=0, tiled=True)
            return lax.psum(g, "narrow")

        grad_joined = reduce(jnp.concatenate([*g_attn[:3], *g_up], axis=1))
        grad_out = reduce(g_attn[3])
        grad_mlp = reduce(g_down[0])
        vg = reduce(vector_grads(sums_a, sums_d, sums_x))[0]
    else:
        col = lambda i: w_joined[:, i * width : (i + 1) * width]
        half = jnp.stack([jnp.where(n == 0, col(0), col(2)), jnp.where(n == 0, col(1), w_out)])
        got = gather_z(half)
        v_own = behind(vec_own, half)
        v_all = lax.all_to_all(jnp.broadcast_to(v_own, (wide, *v_own.shape)), "wide", 0, 0, tiled=True)
        w_up, v_all = lax.optimization_barrier((behind(w_joined, half), v_all))
        cols = jnp.stack([w_up[:, (3 + t) * width : (4 + t) * width] for t in range(tiles)])
        c_half = jnp.where(n == 0, cols, w_mlp.reshape(tiles, rows, width))
        c_half = c_half.reshape(2, tiles // 2, rows, width)
        c_got = gather_z(c_half)
        za, zb = gather_stack(half, got)
        xa, yb = gather_xy(za, zb)
        vec, b_mlp = vectors(v_all)
        a0, b0 = jnp.concatenate([za, xa]), jnp.concatenate([zb, yb])
        a1, b1 = swap_y(a0), swap(b0, 2)
        a0s, b0s = swap(a0, 1), swap(b0, 1)
        attn_w = [a0, a1, b0, b1, a0s, swap(a1, 1), b0s, swap(b1, 1)]

        cza, czb = gather_stack(c_half, c_got)
        xp, attn_w, vec, b_mlp, cza, czb = lax.optimization_barrier((x, attn_w, vec, b_mlp, cza, czb))
        cxa, cyb = gather_xy(cza, czb)
        xn, q, k, v, da, wa = project_call(scal, xp, cot, vec, attn_w, load_attn)

        cxa, cyb = behind((cxa, cyb), q)
        ((ca0, cb0),) = mix("join", [join_job([(cza, cxa), (czb, cyb)])])
        q, ca0, cb0 = lax.optimization_barrier((q, ca0, cb0))
        ca1, cb1 = swap_y(ca0), swap(cb0, 2)
        ca0s, cb0s = swap(ca0, 1), swap(cb0, 1)
        o, dq, dk, dv = core_call(scal, q, k, v, da)

        ca1, cb1 = behind((ca1, cb1), dq)
        dq, ca1, cb1 = lax.optimization_barrier((dq, ca1, cb1))
        ca1s, cb1s = swap(ca1, 1), swap(cb1, 1)
        attn_shapes = [sds((2, 8, rows, width))] * 4
        sums_a, *ga = attn_grad_call(scal, xn, o, dq, dk, dv, cot, store_with(attn_source), attn_shapes)
        mlp_w = [ca0, ca1, cb0, cb1, ca0s, *behind([ca1s, cb0s, cb1s], sums_a)]

        a_got1, a_got0 = swap(ga[3], 1), swap(ga[2], 1)
        xn_u = behind(xn, ga)
        act, gp, wu, wd = up_call(scal, xn_u, b_mlp, mlp_w, [], load_half(0), load_half(1))

        a_got1, a_got0 = behind((a_got1, a_got0), gp)
        ((sa, sb),) = mix("sums_1", [sum1_job(ga[1], a_got1)])
        act_g, sa, sb = lax.optimization_barrier((act, sa, sb))
        a_xy = swap_y(sa), swap(sb, 2)
        gd = down_grad_call(scal, act_g, cot, store_with(down_source), attn_shapes)

        a_xy = behind(a_xy, gd)
        ((sa, sb),) = mix("sums_2", [sum2_job(ga[0], a_got0, a_xy)])
        gp, sa, sb, gd = lax.optimization_barrier((gp, sa, sb, gd))
        a_yx = swap(sa, 2), swap_y(sb)
        d_got1, d_got0 = swap(gd[3], 1), swap(gd[2], 1)
        dpre, sums_d = dpre_call(scal, cot, gp, wd)

        a_yx, d_got1, d_got0 = behind((a_yx, d_got1, d_got0), dpre)
        a_t, (sa, sb) = mix("sums_3", [sum3_job(ga[0], a_got0, a_xy, a_yx), sum1_job(gd[1], d_got1)])
        dpre_g, a_t, sa, sb = lax.optimization_barrier((dpre, a_t, sa, sb))
        d_xy = swap_y(sa), swap(sb, 2)
        a_z = [swap(a_t[k], k << 2) for k in (1, 2, 3)]
        gu = up_grad_call(scal, xn, dpre_g, store_with(attn_source), attn_shapes)

        a_z, d_xy = behind((a_z, d_xy), gu)
        (a_sum,), (sa, sb) = mix("sums_4", [sum4_job(a_t[0], a_z), sum2_job(gd[0], d_got0, d_xy)])
        x_i, sa, sb, gu, a_sum = lax.optimization_barrier((x, sa, sb, gu, a_sum))
        u_got1, u_got0 = swap(gu[3], 1), swap(gu[2], 1)
        d_yx = swap(sa, 2), swap_y(sb)
        a_other = swap_y(a_sum)
        sums_x, d_x = input_grad_call(scal, x_i, cot, dq, dk, dv, dpre, vec, wa, wu)

        d_yx, u_got1, u_got0, a_other = behind((d_yx, u_got1, u_got0, a_other), d_x)
        (sa, sb), d_t = mix("sums_5", [sum1_job(gu[1], u_got1), sum3_job(gd[0], d_got0, d_xy, d_yx)])
        x_o, sa, sb, d_t, sums_x = lax.optimization_barrier((x, sa, sb, d_t, sums_x))
        u_xy = swap_y(sa), swap(sb, 2)
        d_z = [swap(d_t[k], k << 2) for k in (1, 2, 3)]
        out = out_call(scal, x_o, o, act, vec, wa, wd)

        late = (u_xy, d_z, a_sum, a_other, sums_a, sums_d, sums_x)
        u_xy, d_z, a_sum, a_other, sums_a, sums_d, sums_x = behind(late, out)
        ((sa, sb),) = mix("sums_6", [sum2_job(gu[0], u_got0, u_xy)])
        u_yx = swap(sa, 2), swap_y(sb)
        sums_a, sums_d, sums_x, d_z = behind((sums_a, sums_d, sums_x, d_z), sa, sb)
        v_sum = lax.all_to_all(vector_grads(sums_a, sums_d, sums_x), "wide", 0, 0, tiled=True)
        v_sum = jnp.sum(v_sum, axis=0)
        (d_sum,), u_t = mix(
            "sums_7", [sum4_job(d_t[0], behind(d_z, v_sum)), sum3_job(gu[0], u_got0, u_xy, u_yx)]
        )
        u_z = [swap(u_t[k], k << 2) for k in (1, 2, 3)]
        d_other = swap_y(d_sum)
        vg = v_sum + swap_y(v_sum)
        ((u_sum,),) = mix("sums_8", [sum4_job(u_t[0], u_z)])
        u_other = swap_y(u_sum)
        grad_joined, grad_out, grad_mlp = place_call(
            scal, [a_sum, a_other, d_sum, d_other, u_sum, u_other]
        )
    b_at = 3 * rows
    return (
        out.reshape(tokens.shape),
        d_x.reshape(tokens.shape),
        grad_joined,
        grad_out,
        grad_mlp,
        vg[:rows],
        vg[rows:b_at],
        vg[b_at : b_at + tiles * rows],
        vg[b_at + tiles * rows :],
    )


def solution(mesh):
    sizes = (mesh.shape["narrow"], mesh.shape["wide"])
    rows = P(None, ("narrow", "wide"), None)
    placed = (rows, P(None, ("narrow", "wide")), rows) + (P("wide", None),) * 3 + (P("wide"),) * 4
    return jax.shard_map(
        functools.partial(body, sizes),
        mesh=mesh,
        in_specs=placed,
        out_specs=(rows, rows) + (P("wide", None),) * 3 + (P("wide"),) * 4,
        check_vma=False,
    )
```

time: 323 us -> 276 us (0.85)
  Pallas kernels: 137 us -> 107 us
  other arithmetic: 27.1 us -> 5.19 us
  blocking collectives: 0 us -> 11 us
  starting transfers between devices: 67.3 us -> 59.8 us
    pallas_call x9 -> x19, Pallas kernels: 137 us -> 107 us  [the longest x9 92.6 us: call(): pl.pallas_call(kernel, name=name, out_shape=list(outs) + list(g_shapes),...]
    convert_element_type x17 -> x0, other arithmetic: 17.7 us -> none  [the longest x4 5.11 us: scatter_sum3(): total(keep0[i, :4], got0[i, :4], got[i][:4], got2[i]).astype(BF16)]
    ppermute x49 -> x39, starting transfers between devices: 51.7 us -> 37.7 us  [swap(): return lax.ppermute(value, 'wide', [(i, i ^ mask) for i in range(16)])]
    ppermute x14, waiting for transfers between devices: 16.1 us -> 28.1 us  [swap_y(): return lax.ppermute(value, 'narrow', [(0, 1), (1, 0)])]
    ppermute x49 -> x39, waiting for transfers between devices: 48 us -> 36.6 us  [swap(): return lax.ppermute(value, 'wide', [(i, i ^ mask) for i in range(16)])]
    all_to_all x0 -> x1, blocking collectives: none -> 11 us  [body(): lax.all_to_all(vector_grads(sums_a, sums_d, sums_x), 'wide', 0, 0, tiled=...]
    all_to_all x0 -> x1, starting transfers between devices: none -> 7.36 us  [body(): lax.all_to_all(jnp.broadcast_to(v_own, (wide, *v_own.shape)), 'wide', 0,...]
    another operation x21 -> x1, other arithmetic: 5.9 us -> 0.02 us  [body(): jnp.stack([jnp.where(n == 0, col(0), col(2)), jnp.where(n == 0, col(1), w...]
  transfers between devices with their start and end apart: 63 -> 54, of which waited for: 23 -> 18; matrix products, arithmetic and copies ran while one was open for 6% -> 6% of each run, Pallas kernels for 43% -> 34%
where the time goes in v2:
time: 276 us; the launch traced here: 275 us
  Pallas kernels  107 us (39%)
  waiting for transfers between devices  66.7 us (24%)
  starting transfers between devices  59.8 us (22%)
  local copies, waits for them, and re-layouts  23.4 us (8%)
  blocking collectives  11 us (4%)
  other arithmetic  5.19 us (2%)
    pallas_call x9, Pallas kernels, call(): pl.pallas_call(kernel, name=name, out_shape=list(outs) + list(g_shapes),...  92.6 us
    ppermute x39, starting transfers between devices, swap(): return lax.ppermute(value, 'wide', [(i, i ^ mask) for i in range(16)])  37.7 us
    ppermute x39, waiting for transfers between devices, swap(): return lax.ppermute(value, 'wide', [(i, i ^ mask) for i in range(16)])  36.6 us
    ppermute x14, waiting for transfers between devices, swap_y(): return lax.ppermute(value, 'narrow', [(0, 1), (1, 0)])  28.1 us
    ppermute x14, starting transfers between devices, swap_y(): return lax.ppermute(value, 'narrow', [(0, 1), (1, 0)])  14.7 us
    pallas_call x9, Pallas kernels, mix(): pl.pallas_call(kernel, name=name, out_shape=outs, in_specs=[VMEM] * len(n...  12.8 us
    all_to_all x1, blocking collectives, body(): lax.all_to_all(vector_grads(sums_a, sums_d, sums_x), 'wide', 0, 0, tiled=...  11 us
    unnamed x67, local copies, waits for them, and re-layouts  9.2 us
  transfers between devices with their start and end apart: 54, of which 18 were waited for; matrix products, arithmetic and copies ran while one was open for 6% of the time, Pallas kernels for 34%

profile of v2, /device:TPU:0, one launch (start us, length us, event | category | flops | bytes accessed | tf_op | source)
XLA Modules:
  0.0 274.8 jit_solution(17460925121003032289)
XLA Ops:
  0.7 1.7 constant_dynamic-update-slice_fusion.9
  5.1 7.4 %all-to-all-start = ((bf16[16,2,192]{2,1,0:T(2,128)(2,1)}), bf16[16,2,192]{2,1,0:T(2,128)(2,1)S(1)}, u32[]{:S(2)}, u32[]{:S(2)}) async-start(bf16[16,2,192]{2,1,0:T(2,128)(2,1)} %reshape.72), calls=%async_computation | async-start | bytes 32768 | tf_op jit(solution)/shard_map/all_to_all | solution.py:830
  12.5 3.7 %collective-permute-start.2 = (bf16[2,48,768]{2,1,0:T(8,128)(2,1)S(1)}, bf16[2,48,768]{2,1,0:T(8,128)(2,1)S(1)}, u32[]{:S(2)}, u32[]{:S(2)}) collective-permute-start(bf16[2,48,768]{2,1,0:T(8,128)(2,1)S(1)} %pad_maximum_fusion.5), channel_id=1, source_target_pairs={{0,12},{1,13},{2,14},{3,15},{4,8},{5,9},{6,10},{7,11},{8,4},{9,5},... | collective-permute-start | bytes 442376 | tf_op jit(solution)/shard_map/ppermute | solution.py:475
  17.0 2.1 all-to-all-done
  19.3 1.7 collective-permute-start.13
  21.3 5.5 %collective-permute-done = bf16[2,48,768]{2,1,0:T(8,128)(2,1)S(1)} collective-permute-done((bf16[2,48,768]{2,1,0:T(8,128)(2,1)S(1)}, bf16[2,48,768]{2,1,0:T(8,128)(2,1)S(1)}, u32[]{:S(2)}, u32[]{:S(2)}) %collective-permute-start) | collective-permute-done | bytes 147488 | tf_op jit(solution)/shard_map/ppermute | solution.py:475
  26.8 2.5 collective-permute-start.11
  30.0 12.9 %collective-permute-done.1 = bf16[2,48,768]{2,1,0:T(8,128)(2,1)S(1)} collective-permute-done((bf16[2,48,768]{2,1,0:T(8,128)(2,1)S(1)}, bf16[2,48,768]{2,1,0:T(8,128)(2,1)S(1)}, u32[]{:S(2)}, u32[]{:S(2)}) %collective-permute-start.1) | collective-permute-done | bytes 147488 | tf_op jit(solution)/shard_map/ppermute | solution.py:475
  44.2 1.6 collective-permute-start.5
  45.9 1.5 collective-permute-start.3
  47.5 4.5 %collective-permute-done.5 = bf16[4,48,768]{2,1,0:T(8,128)(2,1)S(1)} collective-permute-done((bf16[4,48,768]{2,1,0:T(8,128)(2,1)S(1)}, bf16[4,48,768]{2,1,0:T(8,128)(2,1)S(1)}, u32[]{:S(2)}, u32[]{:S(2)}) %collective-permute-start.5) | collective-permute-done | bytes 294944 | tf_op jit(solution)/shard_map/ppermute | solution.py:479
  52.0 1.5 collective-permute-start.6
  57.0 9.0 %collective-permute-done.6.refs_7_ = bf16[8,48,768]{2,1,0:T(8,128)(2,1)} collective-permute-done((bf16[8,48,768]{2,1,0:T(8,128)(2,1)S(1)}, bf16[8,48,768]{2,1,0:T(8,128)(2,1)}, u32[]{:S(2)}, u32[]{:S(2)}) %collective-permute-start.6) | collective-permute-done | bytes 589856 | tf_op jit(solution)/shard_map/ppermute | solution.py:475
  66.1 1.2 collective-permute-done.4.refs_5_
  68.3 1.2 collective-permute-done.8.refs_9_
  69.5 1.3 collective-permute-start.14
  70.8 1.1 collective-permute-start.15
  71.9 1.4 fusion.7
  73.3 1.4 stack.57.refs_0_.scal
  74.7 1.4 copy-done.9
  76.1 1.4 copy-done.11
  77.5 9.3 %project.1 = (bf16[1024,768]{1,0:T(8,128)(2,1)S(1)}, bf16[1024,768]{1,0:T(8,128)(2,1)S(1)}, bf16[1024,768]{1,0:T(8,128)(2,1)S(1)}, bf16[1024,768]{1,0:T(8,128)(2...) custom-call(s32[10]{0:T(128)S(1)} %stack.57.refs_0_.scal, bf16[1024,768]{1,0:T(8,128)(2,1)S(1)} %bitcast.37, ...), custom_call_target="tpu_custom_call" | custom-call | flops 4831838208 | bytes 1048576 | tf_op jit(solution)/shard_map/project/pallas_call | solution.py:139
  87.1 1.4 collective-permute-start.17
  88.9 16.7 %core.1 = (bf16[1024,768]{1,0:T(8,128)(2,1)S(1)}, bf16[1024,768]{1,0:T(8,128)(2,1)S(1)}, bf16[1024,768]{1,0:T(8,128)(2,1)S(1)}, bf16[1024,768]{1,0:T(8,128)(2,1)S(1)}) custom-call(s32[10]{0:T(128)S(1)} %stack.57.refs_0_.scal, bf16[1024,768]{1,0:T(8,128)(2,1)S(1)} %get-tuple-element.194.q, bf16[1024,768]{1,0:T(8,128)(2,1)S(1)} %get-tuple-element.195.k, ...), custom_call_target="tpu_custom_call" | custom-call | flops 21474836480 | bytes 1048576 | tf_op jit(solution)/shard_map/core/pallas_call | solution.py:139
  105.6 10.8 %collective-permute-done.16.refs_4_ = bf16[8,2,48,768]{3,2,1,0:T(8,128)(2,1)S(1)} collective-permute-done((bf16[8,2,48,768]{3,2,1,0:T(8,128)(2,1)S(1)}, bf16[8,2,48,768]{3,2,1,0:T(8,128)(2,1)S(1)}, u32[]{:S(2)}, u32[]{:S(2)}) %collective-permute-start.16) | collective-permute-done | bytes 1179680 | tf_op jit(solution)/shard_map/ppermute | solution.py:479
  117.1 8.2 %attn_grad.1 = (f32[8,768]{1,0:T(8,128)S(1)}, bf16[2,8,48,768]{3,2,1,0:T(8,128)(2,1)}, bf16[2,8,48,768]{3,2,1,0:T(8,128)(2,1)}, bf16[2,8,48,768]{3,2,1,0:T(8,128)(2,1)}, bf16[2,8,48,768]{3,2,1,0:T(8,128)(2,1)}) custom-call(s32[10]{0:T(128)S(1)} %stack.57.refs_0_.scal, bf16[1024,768]{1,0:T(8,128)(2,1)S(1)} %get-tuple-element.211.xn.refs_1_, ...), custom_call_target="tpu_custom_call" | custom-call | flops 4831838208 | bytes 1048576 | tf_op jit(solution)/shard_map/attn_grad/pallas_call | solution.py:139
  127.8 1.0 copy-done.27
  128.8 14.1 %up.1 = (bf16[4,1024,768]{2,1,0:T(8,128)(2,1)S(1)}, bf16[4,1024,768]{2,1,0:T(8,128)(2,1)S(1)}, bf16[3072,768]{1,0:T(8,128)(2,1)S(1)}, bf16[3072,768]{1,0:T(8,128)(2,1)S(1)}) custom-call(s32[10]{0:T(128)S(1)} %stack.57.refs_0_.scal, bf16[1024,768]{1,0:T(8,128)(2,1)S(1)} %get-tuple-element.211.xn.refs_1_, f32[4,768]{1,0:T(4,128)S(1)} %reshape.65.refs_2_, ...), custom_call_target="tpu_custom_call" | custom-call | flops 4831838208 | bytes 1048576 | tf_op jit(solution)/shard_map/up/pallas_call | solution.py:139
  142.9 1.5 sums_1.1
  145.0 1.3 collective-permute-start.25
  146.3 8.4 %down_grad.1 = (bf16[2,8,48,768]{3,2,1,0:T(8,128)(2,1)}, bf16[2,8,48,768]{3,2,1,0:T(8,128)(2,1)}, bf16[2,8,48,768]{3,2,1,0:T(8,128)(2,1)}, bf16[2,8,48,768]{3,2,1,0:T(8,128)(2,1)}) custom-call(s32[10]{0:T(128)S(1)} %stack.57.refs_0_.scal, bf16[4,1024,768]{2,1,0:T(8,128)(2,1)S(1)} %get-tuple-element.227.act, bf16[1024,768]{1,0:T(8,128)(2,1)S(1)} %bitcast.34), custom_call_target="tpu_custom_call" | custom-call | flops 4831838208 | bytes 1048576 | tf_op jit(solution)/shard_map/down_grad/pallas_call | solution.py:139
  154.7 5.5 %collective-permute-done.24.refs_1_ = bf16[8,48,768]{2,1,0:T(8,128)(2,1)S(1)} collective-permute-done((bf16[8,48,768]{2,1,0:T(8,128)(2,1)S(1)}, bf16[8,48,768]{2,1,0:T(8,128)(2,1)S(1)}, u32[]{:S(2)}, u32[]{:S(2)}) %collective-permute-start.24) | collective-permute-done | bytes 589856 | tf_op jit(solution)/shard_map/ppermute | solution.py:479
  160.4 1.6 sums_2.1
  162.6 1.3 collective-permute-start.26
  164.9 7.5 %dpre.1 = (bf16[4,1024,768]{2,1,0:T(8,128)(2,1)S(1)}, f32[8,768]{1,0:T(8,128)S(1)}) custom-call(s32[10]{0:T(128)S(1)} %stack.57.refs_0_.scal, bf16[1024,768]{1,0:T(8,128)(2,1)S(1)} %bitcast.35, bf16[4,1024,768]{2,1,0:T(8,128)(2,1)S(1)} %get-tuple-element.236.gp, bf16[3072,768]{1,0:T(8,128)(2,1)S(1)} %get-tuple-element.237.w.wd), custom_call_target="tpu_custom_call", output_to_operand_aliasing={{0}: (2, {})} | custom-call | flops 4831838208 | bytes 1048576 | tf_op jit(solution)/shard_map/dpre/pallas_call | solution.py:139
  172.8 1.9 sums_3.1
  174.7 1.1 collective-permute-start.33
  175.8 1.3 collective-permute-start.34
  177.1 1.7 collective-permute-start.31
  178.7 2.7 collective-permute-start.32
  181.5 8.5 %up_grad.1 = (bf16[2,8,48,768]{3,2,1,0:T(8,128)(2,1)}, bf16[2,8,48,768]{3,2,1,0:T(8,128)(2,1)}, bf16[2,8,48,768]{3,2,1,0:T(8,128)(2,1)}, bf16[2,8,48,768]{3,2,1,0:T(8,128)(2,1)}) custom-call(s32[10]{0:T(128)S(1)} %stack.57.refs_0_.scal, bf16[1024,768]{1,0:T(8,128)(2,1)S(1)} %get-tuple-element.211.xn.refs_1_, bf16[4,1024,768]{2,1,0:T(8,128)(2,1)S(1)} %get-tuple-element.259.dpre), custom_call_target="tpu_custom_call" | custom-call | flops 4831838208 | bytes 1048576 | tf_op jit(solution)/shard_map/up_grad/pallas_call | solution.py:139
  190.3 1.7 sums_4.1
  192.5 1.2 collective-permute-start.39
  195.5 11.9 %input_grad.1 = (f32[8,768]{1,0:T(8,128)S(1)}, bf16[2,512,768]{2,1,0:T(8,128)(2,1)}) custom-call(s32[10]{0:T(128)S(1)} %stack.57.refs_0_.scal, bf16[1024,768]{1,0:T(8,128)(2,1)S(1)} %bitcast.38, bf16[1024,768]{1,0:T(8,128)(2,1)S(1)} %bitcast.36, bf16[1024,768]{1,0:T(8,128)(2,1)S(1)} %get-tuple-element.204.dq, bf16[1024,768]{1,0:T(8,128)(2,1)S(1)} %copy-done.16, ...), custom_call_target="tpu_custom_call" | custom-call | flops 8455716864 | bytes 1048576 | tf_op jit(solution)/shard_map/input_grad/pallas_call | solution.py:139
  207.5 2.0 sums_5.1
  209.5 1.2 collective-permute-start.40
  210.7 1.1 collective-permute-start.41
  211.8 2.2 collective-permute-start.42
  214.0 2.4 collective-permute-start.44
  216.4 8.1 %out.1 = bf16[2,512,768]{2,1,0:T(8,128)(2,1)} custom-call(s32[10]{0:T(128)S(1)} %stack.57.refs_0_.scal, bf16[1024,768]{1,0:T(8,128)(2,1)S(1)} %bitcast.39, bf16[1024,768]{1,0:T(8,128)(2,1)S(1)} %get-tuple-element.198.o, bf16[4,1024,768]{2,1,0:T(8,128)(2,1)S(1)} %get-tuple-element.227.act, f32[8,768]{1,0:T(8,128)S(1)} %maximum_maximum_fusion.refs_3_.vec, ...), custom_call_target="tpu_custom_call" | custom-call | flops 6039797760 | bytes 1048576 | tf_op jit(solution)/shard_map/out/pallas_call | solution.py:139
  224.5 2.1 collective-permute-done.43.refs_2_
  226.5 2.2 sums_6.1
  229.5 1.0 collective-permute-start.46
  234.1 1.3 slice.153
  237.1 11.0 %all_to_all.18 = f32[16,1,384]{2,1,0:T(1,128)} all-to-all(f32[16,1,384]{2,1,0:T(1,128)S(1)} %all_to_all.14), channel_id=1, replica_groups=mesh['narrow'=2,'wide'=16] {'wide'}, dimensions={0} | all-to-all | bytes 49152 | tf_op jit(solution)/shard_map/all_to_all | solution.py:907
  248.8 1.6 sums_7.1
  251.5 3.3 %collective-permute-start.50 = (bf16[2,48,768]{2,1,0:T(8,128)(2,1)S(1)}, bf16[2,48,768]{2,1,0:T(8,128)(2,1)S(1)}, u32[]{:S(2)}, u32[]{:S(2)}) collective-permute-start(bf16[2,48,768]{2,1,0:T(8,128)(2,1)S(1)} %get-tuple-element.331), channel_id=1, source_target_pairs={{0,12},{1,13},{2,14},{3,15},{4,8},{5,9},{6,10},{7,11},{8,4},{9,5},... | collective-permute-start | bytes 442376 | tf_op jit(solution)/shard_map/ppermute | solution.py:475
  254.8 1.2 collective-permute-start.52
  256.1 2.4 collective-permute-done.52
  259.7 1.2 collective-permute-start.47
  260.9 3.9 %collective-permute-done.49.refs_2_ = bf16[2,48,768]{2,1,0:T(8,128)(2,1)S(1)} collective-permute-done((bf16[2,48,768]{2,1,0:T(8,128)(2,1)S(1)}, bf16[2,48,768]{2,1,0:T(8,128)(2,1)S(1)}, u32[]{:S(2)}, u32[]{:S(2)}) %collective-permute-start.49) | collective-permute-done | bytes 147488 | tf_op jit(solution)/shard_map/ppermute | solution.py:475
  264.9 1.3 collective-permute-start.51
  266.8 3.3 %collective-permute-done.51.u_other = bf16[2,48,768]{2,1,0:T(8,128)(2,1)S(1)} collective-permute-done((bf16[2,48,768]{2,1,0:T(8,128)(2,1)S(1)}, bf16[2,48,768]{2,1,0:T(8,128)(2,1)S(1)}, u32[]{:S(2)}, u32[]{:S(2)}) %collective-permute-start.51) | collective-permute-done | bytes 147488 | tf_op jit(solution)/shard_map/ppermute | solution.py:479
  272.9 2.0 place.1
  (180 shorter events, 32.2 us)
Async XLA Ops:
  0.6 18.6 %copy-start.18 = (bf16[48,5376]{1,0:T(8,128)(2,1)S(1)}, bf16[48,5376]{1,0:T(8,128)(2,1)}, u32[]{:S(2)}) copy-start(bf16[48,5376]{1,0:T(8,128)(2,1)} %param.13) | copy-start | bytes 1548292
  0.7 18.6 %copy-start.17 = (bf16[192,768]{1,0:T(8,128)(2,1)S(1)}, bf16[192,768]{1,0:T(8,128)(2,1)}, u32[]{:S(2)}) copy-start(bf16[192,768]{1,0:T(8,128)(2,1)} %param.15) | copy-start | bytes 884740
  5.1 14.0 %all-to-all-start = ((bf16[16,2,192]{2,1,0:T(2,128)(2,1)}), bf16[16,2,192]{2,1,0:T(2,128)(2,1)S(1)}, u32[]{:S(2)}, u32[]{:S(2)}) async-start(bf16[16,2,192]{2,1,0:T(2,128)(2,1)} %reshape.72), calls=%async_computation | async-start | bytes 32768 | tf_op jit(solution)/shard_map/all_to_all | solution.py:830
  12.5 31.1 %collective-permute-start.2 = (bf16[2,48,768]{2,1,0:T(8,128)(2,1)S(1)}, bf16[2,48,768]{2,1,0:T(8,128)(2,1)S(1)}, u32[]{:S(2)}, u32[]{:S(2)}) collective-permute-start(bf16[2,48,768]{2,1,0:T(8,128)(2,1)S(1)} %pad_maximum_fusion.5), channel_id=1, source_target_pairs={{0,12},{1,13},{2,14},{3,15},{4,8},{5,9},{6,10},{7,11},{8,4},{9,5},... | collective-permute-start | bytes 442376 | tf_op jit(solution)/shard_map/ppermute | solution.py:475
  16.2 26.7 %collective-permute-start.1 = (bf16[2,48,768]{2,1,0:T(8,128)(2,1)S(1)}, bf16[2,48,768]{2,1,0:T(8,128)(2,1)S(1)}, u32[]{:S(2)}, u32[]{:S(2)}) collective-permute-start(bf16[2,48,768]{2,1,0:T(8,128)(2,1)S(1)} %pad_maximum_fusion.5), channel_id=1, source_target_pairs={{0,8},{1,9},{2,10},{3,11},{4,12},{5,13},{6,14},{7,15},{8,0},{9,1},... | collective-permute-start | bytes 442376 | tf_op jit(solution)/shard_map/ppermute | solution.py:475
  16.2 10.6 %collective-permute-start = (bf16[2,48,768]{2,1,0:T(8,128)(2,1)S(1)}, bf16[2,48,768]{2,1,0:T(8,128)(2,1)S(1)}, u32[]{:S(2)}, u32[]{:S(2)}) collective-permute-start(bf16[2,48,768]{2,1,0:T(8,128)(2,1)S(1)} %pad_maximum_fusion.5), channel_id=1, source_target_pairs={{0,4},{1,5},{2,6},{3,7},{4,0},{5,1},{6,2},{7,3},{8,12},{9,13},{10,... | collective-permute-start | bytes 442376 | tf_op jit(solution)/shard_map/ppermute | solution.py:475
  19.3 37.1 %collective-permute-start.13 = (bf16[2,2,48,768]{3,2,1,0:T(8,128)(2,1)S(1)}, bf16[2,2,48,768]{3,2,1,0:T(8,128)(2,1)S(1)}, u32[]{:S(2)}, u32[]{:S(2)}) collective-permute-start(bf16[2,2,48,768]{3,2,1,0:T(8,128)(2,1)S(1)} %broadcast_select_fusion), channel_id=1, source_target_pairs={{0,12},{1,13},{2,14},{3,15},{4,8},{5,9},{6,10},{7,11},{8,4},{9,5},... | collective-permute-start | bytes 884744 | tf_op jit(solution)/shard_map/ppermute | solution.py:475
  21.0 35.5 %collective-permute-start.12 = (bf16[2,2,48,768]{3,2,1,0:T(8,128)(2,1)S(1)}, bf16[2,2,48,768]{3,2,1,0:T(8,128)(2,1)S(1)}, u32[]{:S(2)}, u32[]{:S(2)}) collective-permute-start(bf16[2,2,48,768]{3,2,1,0:T(8,128)(2,1)S(1)} %broadcast_select_fusion), channel_id=1, source_target_pairs={{0,8},{1,9},{2,10},{3,11},{4,12},{5,13},{6,14},{7,15},{8,0},{9,1},... | collective-permute-start | bytes 884744 | tf_op jit(solution)/shard_map/ppermute | solution.py:475
  26.8 40.5 %collective-permute-start.11 = (bf16[2,2,48,768]{3,2,1,0:T(8,128)(2,1)S(1)}, bf16[2,2,48,768]{3,2,1,0:T(8,128)(2,1)S(1)}, u32[]{:S(2)}, u32[]{:S(2)}) collective-permute-start(bf16[2,2,48,768]{3,2,1,0:T(8,128)(2,1)S(1)} %broadcast_select_fusion), channel_id=1, source_target_pairs={{0,4},{1,5},{2,6},{3,7},{4,0},{5,1},{6,2},{7,3},{8,12},{9,13},{10,... | collective-permute-start | bytes 884744 | tf_op jit(solution)/shard_map/ppermute | solution.py:475
  44.2 7.7 %collective-permute-start.5 = (bf16[4,48,768]{2,1,0:T(8,128)(2,1)S(1)}, bf16[4,48,768]{2,1,0:T(8,128)(2,1)S(1)}, u32[]{:S(2)}, u32[]{:S(2)}) collective-permute-start(bf16[4,48,768]{2,1,0:T(8,128)(2,1)S(1)} %pad_maximum_fusion.3), channel_id=1, source_target_pairs={{0,16},{16,0},{1,17},{17,1},{2,18},{18,2},{3,19},{19,3},{4,20},{20... | collective-permute-start | bytes 884744 | tf_op jit(solution)/shard_map/ppermute | solution.py:479
  45.9 8.2 %collective-permute-start.3 = (bf16[4,48,768]{2,1,0:T(8,128)(2,1)S(1)}, bf16[4,48,768]{2,1,0:T(8,128)(2,1)S(1)}, u32[]{:S(2)}, u32[]{:S(2)}) collective-permute-start(bf16[4,48,768]{2,1,0:T(8,128)(2,1)S(1)} %pad_maximum_fusion.2), channel_id=1, source_target_pairs={{0,2},{1,3},{2,0},{3,1},{4,6},{5,7},{6,4},{7,5},{8,10},{9,11},{10,... | collective-permute-start | bytes 884744 | tf_op jit(solution)/shard_map/ppermute | solution.py:475
  52.0 14.1 %collective-permute-start.6 = (bf16[8,48,768]{2,1,0:T(8,128)(2,1)S(1)}, bf16[8,48,768]{2,1,0:T(8,128)(2,1)}, u32[]{:S(2)}, u32[]{:S(2)}) collective-permute-start(bf16[8,48,768]{2,1,0:T(8,128)(2,1)S(1)} %constant_dynamic-update-slice_fusion.5.refs_6_), channel_id=1, source_target_pairs={{0,2},{1,3},{2,0},{3,1},{4,6},{5,7},{6,4},{7,5},{8,10},{9,11},{10,... | collective-permute-start | bytes 1769480 | tf_op jit(solution)/shard_map/ppermute | solution.py:475
  54.9 12.4 %collective-permute-start.4 = (bf16[8,48,768]{2,1,0:T(8,128)(2,1)}, bf16[8,48,768]{2,1,0:T(8,128)(2,1)}, u32[]{:S(2)}, u32[]{:S(2)}) collective-permute-start(bf16[8,48,768]{2,1,0:T(8,128)(2,1)} %constant_dynamic-update-slice_fusion.refs_4_), channel_id=1, source_target_pairs={{0,16},{16,0},{1,17},{17,1},{2,18},{18,2},{3,19},{19,3},{4,20},{20... | collective-permute-start | bytes 1769480 | tf_op jit(solution)/shard_map/ppermute | solution.py:479
  56.4 11.1 %collective-permute-start.9 = (bf16[8,48,768]{2,1,0:T(8,128)(2,1)S(1)}, bf16[8,48,768]{2,1,0:T(8,128)(2,1)S(1)}, u32[]{:S(2)}, u32[]{:S(2)}) collective-permute-start(bf16[8,48,768]{2,1,0:T(8,128)(2,1)S(1)} %constant_dynamic-update-slice_fusion.5.refs_6_), channel_id=1, source_target_pairs={{0,1},{1,0},{2,3},{3,2},{4,5},{5,4},{6,7},{7,6},{8,9},{9,8},{10,11... | collective-permute-start | bytes 1769480 | tf_op jit(solution)/shard_map/ppermute | solution.py:475
  56.5 11.0 %collective-permute-start.7 = (bf16[8,48,768]{2,1,0:T(8,128)(2,1)}, bf16[8,48,768]{2,1,0:T(8,128)(2,1)S(1)}, u32[]{:S(2)}, u32[]{:S(2)}) collective-permute-start(bf16[8,48,768]{2,1,0:T(8,128)(2,1)} %constant_dynamic-update-slice_fusion.refs_4_), channel_id=1, source_target_pairs={{0,1},{1,0},{2,3},{3,2},{4,5},{5,4},{6,7},{7,6},{8,9},{9,8},{10,11... | collective-permute-start | bytes 1769480 | tf_op jit(solution)/shard_map/ppermute | solution.py:475
  66.1 2.2 collective-permute-start.10
  67.3 2.2 collective-permute-start.8
  69.5 17.3 %collective-permute-start.14 = (bf16[4,2,48,768]{3,2,1,0:T(8,128)(2,1)S(1)}, bf16[4,2,48,768]{3,2,1,0:T(8,128)(2,1)S(1)}, u32[]{:S(2)}, u32[]{:S(2)}) collective-permute-start(bf16[4,2,48,768]{3,2,1,0:T(8,128)(2,1)S(1)} %get-tuple-element.188.refs_0_), channel_id=1, source_target_pairs={{0,2},{1,3},{2,0},{3,1},{4,6},{5,7},{6,4},{7,5},{8,10},{9,11},{10,... | collective-permute-start | bytes 1769480 | tf_op jit(solution)/shard_map/ppermute | solution.py:475
  70.8 16.0 %collective-permute-start.15 = (bf16[4,2,48,768]{3,2,1,0:T(8,128)(2,1)S(1)}, bf16[4,2,48,768]{3,2,1,0:T(8,128)(2,1)S(1)}, u32[]{:S(2)}, u32[]{:S(2)}) collective-permute-start(bf16[4,2,48,768]{3,2,1,0:T(8,128)(2,1)S(1)} %get-tuple-element.189.refs_2_), channel_id=1, source_target_pairs={{0,16},{16,0},{1,17},{17,1},{2,18},{18,2},{3,19},{19,3},{4,20},{20... | collective-permute-start | bytes 1769480 | tf_op jit(solution)/shard_map/ppermute | solution.py:479
  74.7 141.7 %copy-start.8 = (s32[10]{0:T(128)}, s32[10]{0:T(128)S(1)}, u32[]{:S(2)}) copy-start(s32[10]{0:T(128)S(1)} %stack.57.refs_0_.scal) | copy-start | bytes 124
  87.0 18.6 %copy-start.14 = (bf16[8,2,48,768]{3,2,1,0:T(8,128)(2,1)}, bf16[8,2,48,768]{3,2,1,0:T(8,128)(2,1)S(1)}, u32[]{:S(2)}) copy-start(bf16[8,2,48,768]{3,2,1,0:T(8,128)(2,1)S(1)} %get-tuple-element.201.refs_5_) | copy-start | bytes 3538948
  87.0 30.1 %copy-start.13 = (bf16[8,2,48,768]{3,2,1,0:T(8,128)(2,1)}, bf16[8,2,48,768]{3,2,1,0:T(8,128)(2,1)S(1)}, u32[]{:S(2)}) copy-start(bf16[8,2,48,768]{3,2,1,0:T(8,128)(2,1)S(1)} %get-tuple-element.200.refs_3_) | copy-start | bytes 3538948
  87.0 38.8 %collective-permute-start.20 = (bf16[8,2,48,768]{3,2,1,0:T(8,128)(2,1)S(1)}, bf16[8,2,48,768]{3,2,1,0:T(8,128)(2,1)S(1)}, u32[]{:S(2)}, u32[]{:S(2)}) collective-permute-start(bf16[8,2,48,768]{3,2,1,0:T(8,128)(2,1)S(1)} %get-tuple-element.201.refs_5_), channel_id=1, source_target_pairs={{0,1},{1,0},{2,3},{3,2},{4,5},{5,4},{6,7},{7,6},{8,9},{9,8},{10,11... | collective-permute-start | bytes 3538952 | tf_op jit(solution)/shard_map/ppermute | solution.py:475
  87.1 29.4 %collective-permute-start.17 = (bf16[8,2,48,768]{3,2,1,0:T(8,128)(2,1)S(1)}, bf16[8,2,48,768]{3,2,1,0:T(8,128)(2,1)S(1)}, u32[]{:S(2)}, u32[]{:S(2)}) collective-permute-start(bf16[8,2,48,768]{3,2,1,0:T(8,128)(2,1)S(1)} %get-tuple-element.201.refs_5_), channel_id=1, source_target_pairs={{0,2},{1,3},{2,0},{3,1},{4,6},{5,7},{6,4},{7,5},{8,10},{9,11},{10,... | collective-permute-start | bytes 3538952 | tf_op jit(solution)/shard_map/ppermute | solution.py:475
  88.4 28.0 %collective-permute-start.16 = (bf16[8,2,48,768]{3,2,1,0:T(8,128)(2,1)S(1)}, bf16[8,2,48,768]{3,2,1,0:T(8,128)(2,1)S(1)}, u32[]{:S(2)}, u32[]{:S(2)}) collective-permute-start(bf16[8,2,48,768]{3,2,1,0:T(8,128)(2,1)S(1)} %get-tuple-element.200.refs_3_), channel_id=1, source_target_pairs={{0,16},{16,0},{1,17},{17,1},{2,18},{18,2},{3,19},{19,3},{4,20},{20... | collective-permute-start | bytes 3538952 | tf_op jit(solution)/shard_map/ppermute | solution.py:479
  88.9 28.2 %copy-start.10 = (bf16[2,512,768]{2,1,0:T(8,128)(2,1)S(1)}, bf16[2,512,768]{2,1,0:T(8,128)(2,1)}, u32[]{:S(2)}) copy-start(bf16[2,512,768]{2,1,0:T(8,128)(2,1)} %param.12) | copy-start | bytes 4718596
  105.6 19.7 %copy-start.15 = (bf16[1024,768]{1,0:T(8,128)(2,1)}, bf16[1024,768]{1,0:T(8,128)(2,1)S(1)}, u32[]{:S(2)}) copy-start(bf16[1024,768]{1,0:T(8,128)(2,1)S(1)} %get-tuple-element.205.dk) | copy-start | bytes 4718596
  116.5 9.9 %collective-permute-start.19 = (bf16[8,2,48,768]{3,2,1,0:T(8,128)(2,1)S(1)}, bf16[8,2,48,768]{3,2,1,0:T(8,128)(2,1)S(1)}, u32[]{:S(2)}, u32[]{:S(2)}) collective-permute-start(bf16[8,2,48,768]{3,2,1,0:T(8,128)(2,1)S(1)} %collective-permute-done.16.refs_4_), channel_id=1, source_target_pairs={{0,1},{1,0},{2,3},{3,2},{4,5},{5,4},{6,7},{7,6},{8,9},{9,8},{10,11... | collective-permute-start | bytes 3538952 | tf_op jit(solution)/shard_map/ppermute | solution.py:475
  116.6 9.8 %collective-permute-start.21 = (bf16[8,2,48,768]{3,2,1,0:T(8,128)(2,1)S(1)}, bf16[8,2,48,768]{3,2,1,0:T(8,128)(2,1)S(1)}, u32[]{:S(2)}, u32[]{:S(2)}) collective-permute-start(bf16[8,2,48,768]{3,2,1,0:T(8,128)(2,1)S(1)} %collective-permute-done.17.refs_6_), channel_id=1, source_target_pairs={{0,1},{1,0},{2,3},{3,2},{4,5},{5,4},{6,7},{7,6},{8,9},{9,8},{10,11... | collective-permute-start | bytes 3538952 | tf_op jit(solution)/shard_map/ppermute | solution.py:475
  117.1 9.3 %collective-permute-start.18 = (bf16[8,2,48,768]{3,2,1,0:T(8,128)(2,1)S(1)}, bf16[8,2,48,768]{3,2,1,0:T(8,128)(2,1)S(1)}, u32[]{:S(2)}, u32[]{:S(2)}) collective-permute-start(bf16[8,2,48,768]{3,2,1,0:T(8,128)(2,1)S(1)} %get-tuple-element.200.refs_3_), channel_id=1, source_target_pairs={{0,1},{1,0},{2,3},{3,2},{4,5},{5,4},{6,7},{7,6},{8,9},{9,8},{10,11... | collective-permute-start | bytes 3538952 | tf_op jit(solution)/shard_map/ppermute | solution.py:475
  125.3 17.5 %collective-permute-start.23 = (bf16[2,8,48,768]{3,2,1,0:T(8,128)(2,1)}, bf16[2,8,48,768]{3,2,1,0:T(8,128)(2,1)S(1)}, u32[]{:S(2)}, u32[]{:S(2)}) collective-permute-start(bf16[2,8,48,768]{3,2,1,0:T(8,128)(2,1)} %get-tuple-element.209), channel_id=1, source_target_pairs={{0,1},{1,0},{2,3},{3,2},{4,5},{5,4},{6,7},{7,6},{8,9},{9,8},{10,11... | collective-permute-start | bytes 3538952 | tf_op jit(solution)/shard_map/ppermute | solution.py:475
  125.9 16.9 %collective-permute-start.22 = (bf16[2,8,48,768]{3,2,1,0:T(8,128)(2,1)}, bf16[2,8,48,768]{3,2,1,0:T(8,128)(2,1)S(1)}, u32[]{:S(2)}, u32[]{:S(2)}) collective-permute-start(bf16[2,8,48,768]{3,2,1,0:T(8,128)(2,1)} %get-tuple-element.210), channel_id=1, source_target_pairs={{0,1},{1,0},{2,3},{3,2},{4,5},{5,4},{6,7},{7,6},{8,9},{9,8},{10,11... | collective-permute-start | bytes 3538952 | tf_op jit(solution)/shard_map/ppermute | solution.py:475
  144.5 15.7 %collective-permute-start.24 = (bf16[8,48,768]{2,1,0:T(8,128)(2,1)S(1)}, bf16[8,48,768]{2,1,0:T(8,128)(2,1)S(1)}, u32[]{:S(2)}, u32[]{:S(2)}) collective-permute-start(bf16[8,48,768]{2,1,0:T(8,128)(2,1)S(1)} %get-tuple-element.225), channel_id=1, source_target_pairs={{0,16},{16,0},{1,17},{17,1},{2,18},{18,2},{3,19},{19,3},{4,20},{20... | collective-permute-start | bytes 1769480 | tf_op jit(solution)/shard_map/ppermute | solution.py:479
  145.0 15.4 %collective-permute-start.25 = (bf16[8,48,768]{2,1,0:T(8,128)(2,1)S(1)}, bf16[8,48,768]{2,1,0:T(8,128)(2,1)S(1)}, u32[]{:S(2)}, u32[]{:S(2)}) collective-permute-start(bf16[8,48,768]{2,1,0:T(8,128)(2,1)S(1)} %get-tuple-element.226), channel_id=1, source_target_pairs={{0,2},{1,3},{2,0},{3,1},{4,6},{5,7},{6,4},{7,5},{8,10},{9,11},{10,... | collective-permute-start | bytes 1769480 | tf_op jit(solution)/shard_map/ppermute | solution.py:475
  162.1 10.7 %collective-permute-start.28 = (bf16[2,8,48,768]{3,2,1,0:T(8,128)(2,1)S(1)}, bf16[2,8,48,768]{3,2,1,0:T(8,128)(2,1)S(1)}, u32[]{:S(2)}, u32[]{:S(2)}) collective-permute-start(bf16[2,8,48,768]{3,2,1,0:T(8,128)(2,1)S(1)} %copy-done.26), channel_id=1, source_target_pairs={{0,1},{1,0},{2,3},{3,2},{4,5},{5,4},{6,7},{7,6},{8,9},{9,8},{10,11... | collective-permute-start | bytes 3538952 | tf_op jit(solution)/shard_map/ppermute | solution.py:475
  162.4 10.4 %collective-permute-start.29 = (bf16[2,8,48,768]{3,2,1,0:T(8,128)(2,1)S(1)}, bf16[2,8,48,768]{3,2,1,0:T(8,128)(2,1)S(1)}, u32[]{:S(2)}, u32[]{:S(2)}) collective-permute-start(bf16[2,8,48,768]{3,2,1,0:T(8,128)(2,1)S(1)} %copy-done.24), channel_id=1, source_target_pairs={{0,1},{1,0},{2,3},{3,2},{4,5},{5,4},{6,7},{7,6},{8,9},{9,8},{10,11... | collective-permute-start | bytes 3538952 | tf_op jit(solution)/shard_map/ppermute | solution.py:475
  162.6 9.8 %collective-permute-start.26 = (bf16[4,48,768]{2,1,0:T(8,128)(2,1)S(1)}, bf16[4,48,768]{2,1,0:T(8,128)(2,1)S(1)}, u32[]{:S(2)}, u32[]{:S(2)}) collective-permute-start(bf16[4,48,768]{2,1,0:T(8,128)(2,1)S(1)} %get-tuple-element.239), channel_id=1, source_target_pairs={{0,2},{1,3},{2,0},{3,1},{4,6},{5,7},{6,4},{7,5},{8,10},{9,11},{10,... | collective-permute-start | bytes 884744 | tf_op jit(solution)/shard_map/ppermute | solution.py:475
  163.9 8.9 %collective-permute-start.27 = (bf16[4,48,768]{2,1,0:T(8,128)(2,1)S(1)}, bf16[4,48,768]{2,1,0:T(8,128)(2,1)S(1)}, u32[]{:S(2)}, u32[]{:S(2)}) collective-permute-start(bf16[4,48,768]{2,1,0:T(8,128)(2,1)S(1)} %get-tuple-element.240), channel_id=1, source_target_pairs={{0,16},{16,0},{1,17},{17,1},{2,18},{18,2},{3,19},{19,3},{4,20},{20... | collective-permute-start | bytes 884744 | tf_op jit(solution)/shard_map/ppermute | solution.py:479
  172.4 17.6 %copy-start.6 = (f32[8,768]{1,0:T(8,128)}, f32[8,768]{1,0:T(8,128)S(1)}, u32[]{:S(2)}) copy-start(f32[8,768]{1,0:T(8,128)S(1)} %get-tuple-element.323) | copy-start | bytes 73732
  174.7 15.5 %collective-permute-start.33 = (bf16[8,48,768]{2,1,0:T(8,128)(2,1)S(1)}, bf16[8,48,768]{2,1,0:T(8,128)(2,1)S(1)}, u32[]{:S(2)}, u32[]{:S(2)}) collective-permute-start(bf16[8,48,768]{2,1,0:T(8,128)(2,1)S(1)} %get-tuple-element.257), channel_id=1, source_target_pairs={{0,16},{16,0},{1,17},{17,1},{2,18},{18,2},{3,19},{19,3},{4,20},{20... | collective-permute-start | bytes 1769480 | tf_op jit(solution)/shard_map/ppermute | solution.py:479
  175.8 14.4 %collective-permute-start.34 = (bf16[8,48,768]{2,1,0:T(8,128)(2,1)S(1)}, bf16[8,48,768]{2,1,0:T(8,128)(2,1)S(1)}, u32[]{:S(2)}, u32[]{:S(2)}) collective-permute-start(bf16[8,48,768]{2,1,0:T(8,128)(2,1)S(1)} %get-tuple-element.258), channel_id=1, source_target_pairs={{0,2},{1,3},{2,0},{3,1},{4,6},{5,7},{6,4},{7,5},{8,10},{9,11},{10,... | collective-permute-start | bytes 1769480 | tf_op jit(solution)/shard_map/ppermute | solution.py:475
  177.1 12.9 %collective-permute-start.30 = (bf16[2,48,768]{2,1,0:T(8,128)(2,1)S(1)}, bf16[2,48,768]{2,1,0:T(8,128)(2,1)S(1)}, u32[]{:S(2)}, u32[]{:S(2)}) collective-permute-start(bf16[2,48,768]{2,1,0:T(8,128)(2,1)S(1)} %get-tuple-element.254), channel_id=1, source_target_pairs={{0,4},{1,5},{2,6},{3,7},{4,0},{5,1},{6,2},{7,3},{8,12},{9,13},{10,... | collective-permute-start | bytes 442376 | tf_op jit(solution)/shard_map/ppermute | solution.py:475
  177.1 13.2 %collective-permute-start.31 = (bf16[2,48,768]{2,1,0:T(8,128)(2,1)S(1)}, bf16[2,48,768]{2,1,0:T(8,128)(2,1)S(1)}, u32[]{:S(2)}, u32[]{:S(2)}) collective-permute-start(bf16[2,48,768]{2,1,0:T(8,128)(2,1)S(1)} %get-tuple-element.255), channel_id=1, source_target_pairs={{0,8},{1,9},{2,10},{3,11},{4,12},{5,13},{6,14},{7,15},{8,0},{9,1},... | collective-permute-start | bytes 442376 | tf_op jit(solution)/shard_map/ppermute | solution.py:475
  178.7 11.5 %collective-permute-start.32 = (bf16[2,48,768]{2,1,0:T(8,128)(2,1)S(1)}, bf16[2,48,768]{2,1,0:T(8,128)(2,1)S(1)}, u32[]{:S(2)}, u32[]{:S(2)}) collective-permute-start(bf16[2,48,768]{2,1,0:T(8,128)(2,1)S(1)} %get-tuple-element.256), channel_id=1, source_target_pairs={{0,12},{1,13},{2,14},{3,15},{4,8},{5,9},{6,10},{7,11},{8,4},{9,5},... | collective-permute-start | bytes 442376 | tf_op jit(solution)/shard_map/ppermute | solution.py:475
  191.9 15.5 %copy-start = (bf16[2,48,768]{2,1,0:T(8,128)(2,1)}, bf16[2,48,768]{2,1,0:T(8,128)(2,1)S(1)}, u32[]{:S(2)}) copy-start(bf16[2,48,768]{2,1,0:T(8,128)(2,1)S(1)} %get-tuple-element.303.a_mine) | copy-start | bytes 442372
  191.9 15.5 %collective-permute-start.37 = (bf16[2,8,48,768]{3,2,1,0:T(8,128)(2,1)}, bf16[2,8,48,768]{3,2,1,0:T(8,128)(2,1)S(1)}, u32[]{:S(2)}, u32[]{:S(2)}) collective-permute-start(bf16[2,8,48,768]{3,2,1,0:T(8,128)(2,1)} %get-tuple-element.276), channel_id=1, source_target_pairs={{0,1},{1,0},{2,3},{3,2},{4,5},{5,4},{6,7},{7,6},{8,9},{9,8},{10,11... | collective-permute-start | bytes 3538952 | tf_op jit(solution)/shard_map/ppermute | solution.py:475
  192.0 15.5 %collective-permute-start.38 = (bf16[2,8,48,768]{3,2,1,0:T(8,128)(2,1)}, bf16[2,8,48,768]{3,2,1,0:T(8,128)(2,1)S(1)}, u32[]{:S(2)}, u32[]{:S(2)}) collective-permute-start(bf16[2,8,48,768]{3,2,1,0:T(8,128)(2,1)} %get-tuple-element.277), channel_id=1, source_target_pairs={{0,1},{1,0},{2,3},{3,2},{4,5},{5,4},{6,7},{7,6},{8,9},{9,8},{10,11... | collective-permute-start | bytes 3538952 | tf_op jit(solution)/shard_map/ppermute | solution.py:475
  192.5 14.9 %collective-permute-start.39 = (bf16[2,48,768]{2,1,0:T(8,128)(2,1)S(1)}, bf16[2,48,768]{2,1,0:T(8,128)(2,1)S(1)}, u32[]{:S(2)}, u32[]{:S(2)}) collective-permute-start(bf16[2,48,768]{2,1,0:T(8,128)(2,1)S(1)} %get-tuple-element.303.a_mine), channel_id=1, source_target_pairs={{0,16},{16,0},{1,17},{17,1},{2,18},{18,2},{3,19},{19,3},{4,20},{20... | collective-permute-start | bytes 442376 | tf_op jit(solution)/shard_map/ppermute | solution.py:479
  193.7 13.8 %collective-permute-start.35 = (bf16[4,48,768]{2,1,0:T(8,128)(2,1)S(1)}, bf16[4,48,768]{2,1,0:T(8,128)(2,1)S(1)}, u32[]{:S(2)}, u32[]{:S(2)}) collective-permute-start(bf16[4,48,768]{2,1,0:T(8,128)(2,1)S(1)} %get-tuple-element.274), channel_id=1, source_target_pairs={{0,2},{1,3},{2,0},{3,1},{4,6},{5,7},{6,4},{7,5},{8,10},{9,11},{10,... | collective-permute-start | bytes 884744 | tf_op jit(solution)/shard_map/ppermute | solution.py:475
  194.6 12.8 %collective-permute-start.36 = (bf16[4,48,768]{2,1,0:T(8,128)(2,1)S(1)}, bf16[4,48,768]{2,1,0:T(8,128)(2,1)S(1)}, u32[]{:S(2)}, u32[]{:S(2)}) collective-permute-start(bf16[4,48,768]{2,1,0:T(8,128)(2,1)S(1)} %get-tuple-element.275), channel_id=1, source_target_pairs={{0,16},{16,0},{1,17},{17,1},{2,18},{18,2},{3,19},{19,3},{4,20},{20... | collective-permute-start | bytes 884744 | tf_op jit(solution)/shard_map/ppermute | solution.py:479
  209.5 17.0 %collective-permute-start.40 = (bf16[8,48,768]{2,1,0:T(8,128)(2,1)S(1)}, bf16[8,48,768]{2,1,0:T(8,128)(2,1)S(1)}, u32[]{:S(2)}, u32[]{:S(2)}) collective-permute-start(bf16[8,48,768]{2,1,0:T(8,128)(2,1)S(1)} %get-tuple-element.295), channel_id=1, source_target_pairs={{0,16},{16,0},{1,17},{17,1},{2,18},{18,2},{3,19},{19,3},{4,20},{20... | collective-permute-start | bytes 1769480 | tf_op jit(solution)/shard_map/ppermute | solution.py:479
  210.7 15.8 %collective-permute-start.41 = (bf16[8,48,768]{2,1,0:T(8,128)(2,1)S(1)}, bf16[8,48,768]{2,1,0:T(8,128)(2,1)S(1)}, u32[]{:S(2)}, u32[]{:S(2)}) collective-permute-start(bf16[8,48,768]{2,1,0:T(8,128)(2,1)S(1)} %get-tuple-element.296), channel_id=1, source_target_pairs={{0,2},{1,3},{2,0},{3,1},{4,6},{5,7},{6,4},{7,5},{8,10},{9,11},{10,... | collective-permute-start | bytes 1769480 | tf_op jit(solution)/shard_map/ppermute | solution.py:475
  211.8 12.6 %collective-permute-start.42 = (bf16[2,48,768]{2,1,0:T(8,128)(2,1)S(1)}, bf16[2,48,768]{2,1,0:T(8,128)(2,1)S(1)}, u32[]{:S(2)}, u32[]{:S(2)}) collective-permute-start(bf16[2,48,768]{2,1,0:T(8,128)(2,1)S(1)} %get-tuple-element.297), channel_id=1, source_target_pairs={{0,4},{1,5},{2,6},{3,7},{4,0},{5,1},{6,2},{7,3},{8,12},{9,13},{10,... | collective-permute-start | bytes 442376 | tf_op jit(solution)/shard_map/ppermute | solution.py:475
  214.0 12.5 %collective-permute-start.43 = (bf16[2,48,768]{2,1,0:T(8,128)(2,1)S(1)}, bf16[2,48,768]{2,1,0:T(8,128)(2,1)S(1)}, u32[]{:S(2)}, u32[]{:S(2)}) collective-permute-start(bf16[2,48,768]{2,1,0:T(8,128)(2,1)S(1)} %get-tuple-element.298), channel_id=1, source_target_pairs={{0,8},{1,9},{2,10},{3,11},{4,12},{5,13},{6,14},{7,15},{8,0},{9,1},... | collective-permute-start | bytes 442376 | tf_op jit(solution)/shard_map/ppermute | solution.py:475
  214.0 12.5 %collective-permute-start.44 = (bf16[2,48,768]{2,1,0:T(8,128)(2,1)S(1)}, bf16[2,48,768]{2,1,0:T(8,128)(2,1)S(1)}, u32[]{:S(2)}, u32[]{:S(2)}) collective-permute-start(bf16[2,48,768]{2,1,0:T(8,128)(2,1)S(1)} %get-tuple-element.299), channel_id=1, source_target_pairs={{0,12},{1,13},{2,14},{3,15},{4,8},{5,9},{6,10},{7,11},{8,4},{9,5},... | collective-permute-start | bytes 442376 | tf_op jit(solution)/shard_map/ppermute | solution.py:475
  228.7 20.0 %collective-permute-start.45 = (bf16[4,48,768]{2,1,0:T(8,128)(2,1)}, bf16[4,48,768]{2,1,0:T(8,128)(2,1)S(1)}, u32[]{:S(2)}, u32[]{:S(2)}) collective-permute-start(bf16[4,48,768]{2,1,0:T(8,128)(2,1)} %get-tuple-element.316), channel_id=1, source_target_pairs={{0,2},{1,3},{2,0},{3,1},{4,6},{5,7},{6,4},{7,5},{8,10},{9,11},{10,... | collective-permute-start | bytes 884744 | tf_op jit(solution)/shard_map/ppermute | solution.py:475
  229.5 19.2 %collective-permute-start.46 = (bf16[4,48,768]{2,1,0:T(8,128)(2,1)}, bf16[4,48,768]{2,1,0:T(8,128)(2,1)S(1)}, u32[]{:S(2)}, u32[]{:S(2)}) collective-permute-start(bf16[4,48,768]{2,1,0:T(8,128)(2,1)} %get-tuple-element.317), channel_id=1, source_target_pairs={{0,16},{16,0},{1,17},{17,1},{2,18},{18,2},{3,19},{19,3},{4,20},{20... | collective-permute-start | bytes 884744 | tf_op jit(solution)/shard_map/ppermute | solution.py:479
  250.4 16.4 %copy-start.4 = (bf16[2,48,768]{2,1,0:T(8,128)(2,1)}, bf16[2,48,768]{2,1,0:T(8,128)(2,1)S(1)}, u32[]{:S(2)}) copy-start(bf16[2,48,768]{2,1,0:T(8,128)(2,1)S(1)} %get-tuple-element.327.d_mine) | copy-start | bytes 442372
  250.4 10.5 %collective-permute-start.48 = (bf16[2,48,768]{2,1,0:T(8,128)(2,1)S(1)}, bf16[2,48,768]{2,1,0:T(8,128)(2,1)S(1)}, u32[]{:S(2)}, u32[]{:S(2)}) collective-permute-start(bf16[2,48,768]{2,1,0:T(8,128)(2,1)S(1)} %get-tuple-element.329), channel_id=1, source_target_pairs={{0,4},{1,5},{2,6},{3,7},{4,0},{5,1},{6,2},{7,3},{8,12},{9,13},{10,... | collective-permute-start | bytes 442376 | tf_op jit(solution)/shard_map/ppermute | solution.py:475
  250.9 14.0 %collective-permute-start.49 = (bf16[2,48,768]{2,1,0:T(8,128)(2,1)S(1)}, bf16[2,48,768]{2,1,0:T(8,128)(2,1)S(1)}, u32[]{:S(2)}, u32[]{:S(2)}) collective-permute-start(bf16[2,48,768]{2,1,0:T(8,128)(2,1)S(1)} %get-tuple-element.330), channel_id=1, source_target_pairs={{0,8},{1,9},{2,10},{3,11},{4,12},{5,13},{6,14},{7,15},{8,0},{9,1},... | collective-permute-start | bytes 442376 | tf_op jit(solution)/shard_map/ppermute | solution.py:475
  251.5 13.3 %collective-permute-start.50 = (bf16[2,48,768]{2,1,0:T(8,128)(2,1)S(1)}, bf16[2,48,768]{2,1,0:T(8,128)(2,1)S(1)}, u32[]{:S(2)}, u32[]{:S(2)}) collective-permute-start(bf16[2,48,768]{2,1,0:T(8,128)(2,1)S(1)} %get-tuple-element.331), channel_id=1, source_target_pairs={{0,12},{1,13},{2,14},{3,15},{4,8},{5,9},{6,10},{7,11},{8,4},{9,5},... | collective-permute-start | bytes 442376 | tf_op jit(solution)/shard_map/ppermute | solution.py:475
  254.8 3.6 %collective-permute-start.52 = (f32[384]{0:T(512)S(1)}, f32[384]{0:T(512)S(1)}, u32[]{:S(2)}, u32[]{:S(2)}) collective-permute-start(f32[384]{0:T(512)S(1)} %reduce_sum.9), channel_id=1, source_target_pairs={{0,16},{16,0},{1,17},{17,1},{2,18},{18,2},{3,19},{19,3},{4,20},{20... | collective-permute-start | bytes 4616 | tf_op jit(solution)/shard_map/ppermute | solution.py:479
  259.7 7.1 %collective-permute-start.47 = (bf16[2,48,768]{2,1,0:T(8,128)(2,1)S(1)}, bf16[2,48,768]{2,1,0:T(8,128)(2,1)S(1)}, u32[]{:S(2)}, u32[]{:S(2)}) collective-permute-start(bf16[2,48,768]{2,1,0:T(8,128)(2,1)S(1)} %get-tuple-element.327.d_mine), channel_id=1, source_target_pairs={{0,16},{16,0},{1,17},{17,1},{2,18},{18,2},{3,19},{19,3},{4,20},{20... | collective-permute-start | bytes 442376 | tf_op jit(solution)/shard_map/ppermute | solution.py:479
  264.9 5.2 %collective-permute-start.51 = (bf16[2,48,768]{2,1,0:T(8,128)(2,1)S(1)}, bf16[2,48,768]{2,1,0:T(8,128)(2,1)S(1)}, u32[]{:S(2)}, u32[]{:S(2)}) collective-permute-start(bf16[2,48,768]{2,1,0:T(8,128)(2,1)S(1)} %sums_8.1.u_mine), channel_id=1, source_target_pairs={{0,16},{16,0},{1,17},{17,1},{2,18},{18,2},{3,19},{19,3},{4,20},{20... | collective-permute-start | bytes 442376 | tf_op jit(solution)/shard_map/ppermute | solution.py:479
  (22 other events, 69.0 us)

commit v3 on v2

--- a/solution.py
+++ b/solution.py
@@ -172,7 +172,7 @@
     scal, x_ref, cot_ref, vec_ref = refs[:4]
     xn, q, k, v, da, w = refs[4 + n_w : 10 + n_w]
     (sem,) = refs[10 + n_w :]
-    load(scal, refs[4 : 4 + n_w], w, sem, (0, 1, 2, 3))
+    load(scal, refs[4 : 4 + n_w], w, sem)
     tokens = x_ref.shape[0]
 
     def norm(i):
@@ -185,14 +185,24 @@
     def ready(i):
         whole_wait(w.at[i], sem.at[i])()
 
-    ready(0)
-    q[...] = (dot_nn(xn[...], w[0]) + vec_ref[1:2, :]).astype(BF16) * jnp.asarray(0.125, BF16)
-    ready(1)
-    k[...] = dot_nn(xn[...], w[1]).astype(BF16)
-    ready(2)
-    v[...] = (dot_nn(xn[...], w[2]) + vec_ref[2:3, :]).astype(BF16)
-    ready(3)
-    da[...] = dot_nt(cot_ref[...], w[3]).astype(BF16)
+    def each(fn):
+        loop(tokens // 512, lambda i: fn(rows_of(i, 512)))
+
+    def queries(r):
+        q[r, :] = (dot_nn(xn[r, :], w[0]) + vec_ref[1:2, :]).astype(BF16) * jnp.asarray(0.125, BF16)
+
+    def keys(r):
+        k[r, :] = dot_nn(xn[r, :], w[1]).astype(BF16)
+
+    def values(r):
+        v[r, :] = (dot_nn(xn[r, :], w[2]) + vec_ref[2:3, :]).astype(BF16)
+
+    def attended(r):
+        da[r, :] = dot_nt(cot_ref[r, :], w[3]).astype(BF16)
+
+    for i, fn in enumerate((queries, keys, values, attended)):
+        ready(i)
+        each(fn)
 
 
 def project_call(scal, x, cot, vec, weights, load):
@@ -209,15 +219,13 @@
     )
 
 
-def core_kernel(scal, q, k, v, da, o, dq, dk, dv):
-    tokens, width = q.shape
-    pairs = width // 128
+def core_kernel(b, scal, q, k, v, da, *refs):
+    o, d = refs[-2:]
+    refs = (q, k, v, da, o, d.at[0], d.at[1], d.at[2])
+    whole = scal[8 + b] == 0
 
     def pair(i):
-        b = i // pairs
-        cols = pl.ds(pl.multiple_of(i % pairs * 128, 128), 128)
-        refs = (q, k, v, da, o, dq, dk, dv)
-        whole = scal[8 + b] == 0
+        cols = pl.ds(pl.multiple_of(i * 128, 128), 128)
 
         @pl.when(whole)
         def _():
@@ -227,32 +235,46 @@
         def _():
             attend(refs, b * 512, cols, SMALL)
 
-    loop(tokens // 512 * pairs, pair)
-
-
-def core_call(scal, q, k, v, da):
-    return call(core_kernel, "core", (scal, q, k, v, da), [], [kept(q.shape)] * 4, [], [], 20 << 30)
-
-
-def attn_grad_kernel(store, scal, xn, o, dq, dk, dv, cot, sums, *refs):
+    loop(q.shape[1] // 128, pair)
+
+
+def core_call(b, scal, q, k, v, da, *before):
+    return call(
+        functools.partial(core_kernel, b),
+        "core",
+        (scal, q, k, v, da, *before),
+        [],
+        [kept(q.shape), kept((3, *q.shape))],
+        [],
+        [],
+        10 << 30,
+        alias={5 + i: i for i in range(len(before))},
+    )
+
+
+def attn_grad_kernel(store, scal, xn, o, d, cot, sums, *refs):
     *g_refs, g, sem = refs
     tokens, width = xn.shape
-    for b, (lhs, rhs) in enumerate(((xn, dq), (xn, dk), (xn, dv), (o, cot))):
-        g[b] = dot_tn(lhs[...], rhs[...]).astype(BF16)
+
+    def grad(b):
+        g[b] = dot_tn(xn[...], d[b]).astype(BF16)
+
+    loop(3, grad)
+    g[3] = dot_tn(o[...], cot[...]).astype(BF16)
     done = store(scal, g, g_refs, sem)
     ones = jnp.ones((8, tokens), BF16)
-    sums[0:1, :] = dot_nn(ones, dq[...])[0:1]
-    sums[1:2, :] = dot_nn(ones, dv[...])[0:1]
+    sums[0:1, :] = dot_nn(ones, d[0])[0:1]
+    sums[1:2, :] = dot_nn(ones, d[2])[0:1]
     sums[2:3, :] = dot_nn(ones, cot[...])[0:1]
     done()
 
 
-def attn_grad_call(scal, xn, o, dq, dk, dv, cot, store, g_shapes):
+def attn_grad_call(scal, xn, o, d, cot, store, g_shapes):
     tokens, width = xn.shape
     return call(
         functools.partial(attn_grad_kernel, store),
         "attn_grad",
-        (scal, xn, o, dq, dk, dv, cot),
+        (scal, xn, o, d, cot),
         [],
         [kept((8, width), F32)],
         g_shapes,
@@ -276,58 +298,54 @@
     whole_wait(w.at[tile_of(t, width), :], sem.at[t])()
 
 
-def up_kernel(load_u, load_d, n_u, n_d, *refs):
+def up_kernel(load, first, count, n_p, *refs):
     scal, xn, bias = refs[:3]
-    act, gp, wu, wd = refs[3 + n_u + n_d : 7 + n_u + n_d]
-    even, odd, sem_u, sem_d = refs[7 + n_u + n_d :]
+    even, odd, sem = refs[-3:]
     tokens, width = xn.shape
-    load_u(scal, refs[3 : 3 + n_u], wu, sem_u)
-    load_d(scal, refs[3 + n_u : 3 + n_u + n_d] or refs[3 : 3 + n_u], wd, sem_d)
-    tiles = bias.shape[0]
+    if n_p:
+        act, gp, w = refs[-6:-3]
+        load(scal, refs[3 : 3 + n_p], w, sem)
+        for t in range(bias.shape[0]):
+            whole_wait(w.at[t], sem.at[t])()
+    else:
+        act, gp = refs[-5:-3]
+        w = refs[5]
     rows = even.shape[0]
     per = tokens // rows
 
     def product(i):
-        t = i // per
-        return dot_nn(xn[rows_of(i % per, rows), :], wu[tile_of(t, width), :])
+        return dot_nn(xn[rows_of(i % per, rows), :], w[first + i // per])
 
     def finish(i, u):
-        t, r = i // per, rows_of(i % per, rows)
+        t, r = first + i // per, rows_of(i % per, rows)
         a, gr = gelu_parts(u + bias[pl.ds(t, 1), :])
         act[t, r, :] = a.astype(BF16)
         gp[t, r, :] = gr.astype(BF16)
 
-    for t in range(tiles):
-        wait_tile(wu, sem_u, t, width)
     even[...] = product(0)
 
     def step(i):
         odd[...] = product(2 * i + 1)
         finish(2 * i, even[...])
-        even[...] = product(2 * i + 2)
+        even[...] = product(jnp.minimum(2 * i + 2, count * per - 1))
         finish(2 * i + 1, odd[...])
 
-    last = tiles * per - 1
-    loop(last // 2, step)
-    odd[...] = product(last)
-    finish(last - 1, even[...])
-    finish(last, odd[...])
-    for t in range(tiles):
-        wait_tile(wd, sem_d, t, width)
-
-
-def up_call(scal, xn, bias, up_w, down_w, load_u, load_d):
+    loop(count * per // 2, step)
+
+
+def up_call(first, count, scal, xn, bias, before, pieces, load):
     tokens, width = xn.shape
     tiles = bias.shape[0]
     return call(
-        functools.partial(up_kernel, load_u, load_d, len(up_w), len(down_w)),
+        functools.partial(up_kernel, load, first, count, len(pieces)),
         "up",
-        (scal, xn, bias),
-        [*up_w, *down_w],
-        [kept((tiles, tokens, width))] * 2 + [kept((tiles * width, width))] * 2,
-        [],
-        [pltpu.VMEM((256, width), F32)] * 2 + [pltpu.SemaphoreType.DMA((tiles,)), pltpu.SemaphoreType.DMA((tiles,))],
-        2 * tiles * tokens * width * width,
+        (scal, xn, bias, *before),
+        pieces,
+        [kept((tiles, tokens, width))] * 2 + [kept((tiles, width, width))] * (1 if pieces else 0),
+        [],
+        [pltpu.VMEM((256, width), F32)] * 2 + [pltpu.SemaphoreType.DMA((tiles,))],
+        2 * count * tokens * width * width,
+        alias={3: 0, 4: 1} if before else None,
     )
 
 
@@ -356,11 +374,15 @@
     )
 
 
-def dpre_kernel(scal, cot, gp, w, dpre, sums):
+def dpre_kernel(load, n_p, *refs):
+    scal, cot, gp = refs[:3]
+    dpre, sums, w, sem = refs[3 + n_p :]
     tiles, tokens, width = gp.shape
+    load(scal, refs[3 : 3 + n_p], w, sem)
     ones = jnp.ones((8, tokens), BF16)
 
     def down(t):
+        wait_tile(w, sem, t, width)
         dpre[t] = (dot_nt(cot[...], w[tile_of(t, width), :]) * gp[t].astype(F32)).astype(BF16)
 
     loop(tiles, down)
@@ -368,16 +390,16 @@
         sums[t : t + 1, :] = dot_nn(ones, dpre[t])[0:1]
 
 
-def dpre_call(scal, cot, gp, w):
+def dpre_call(scal, cot, gp, pieces, load):
     tiles, tokens, width = gp.shape
     return call(
-        dpre_kernel,
+        functools.partial(dpre_kernel, load, len(pieces)),
         "dpre",
-        (scal, cot, gp, w),
-        [],
-        [kept(gp.shape), kept((8, width), F32)],
-        [],
-        [],
+        (scal, cot, gp),
+        pieces,
+        [kept(gp.shape), kept((8, width), F32), kept((tiles * width, width))],
+        [],
+        [pltpu.SemaphoreType.DMA((tiles,))],
         2 * tiles * tokens * width * width,
         alias={2: 0},
     )
@@ -408,15 +430,15 @@
     )
 
 
-def input_grad_kernel(scal, x, cot, dq, dk, dv, dpre, vec, wa, wu, sums, dx_ref, dx, sem):
+def input_grad_kernel(scal, x, cot, d, dpre, vec, wa, wu, sums, dx_ref, dx, sem):
     tiles, tokens, width = dpre.shape
     sums[...] = jnp.zeros_like(sums)
 
     def step(i):
         r = rows_of(i, 256)
-        dnr = dot_nt(dq[r, :], wa[0]) + dot_nt(dk[r, :], wa[1]) + dot_nt(dv[r, :], wa[2])
+        dnr = dot_nt(d[0, r, :], wa[0]) + dot_nt(d[1, r, :], wa[1]) + dot_nt(d[2, r, :], wa[2])
         for t in range(tiles):
-            dnr += dot_nt(dpre[t, r, :], wu[tile_of(t, width), :])
+            dnr += dot_nt(dpre[t, r, :], wu[t])
         standard, inv = norm_rows(x[r, :])
         sums[0:1, :] += jnp.sum(dnr * standard, axis=0, keepdims=True)
         gs = dnr * vec[0:1, :]
@@ -428,12 +450,12 @@
     whole_wait(dx_ref, sem)()
 
 
-def input_grad_call(scal, x, cot, dq, dk, dv, dpre, vec, wa, wu):
+def input_grad_call(scal, x, cot, d, dpre, vec, wa, wu):
     tiles, tokens, width = dpre.shape
     return call(
         input_grad_kernel,
         "input_grad",
-        (scal, x, cot, dq, dk, dv, dpre, vec, wa, wu),
+        (scal, x, cot, d, dpre, vec, wa, wu),
         [],
         [kept((8, width), F32)],
         [sds((tokens // 512, 512, width))],
@@ -500,17 +522,26 @@
     return [swap(value, k << 2) for k in (1, 2, 3)]
 
 
-def gather_stack(half, got):
-    got = [half] + got
-    return [jnp.stack([t[i] for t in got]) for i in range(2)]
-
-
-def gather_xy(za, zb):
-    return swap(za, 2), swap_y(zb)
-
-
-def total(*parts):
-    return sum(v.astype(F32) for v in parts)
+def gather_first(za, zb):
+    return swap(za, 2), swap_y(zb), swap_y(za), swap(zb, 2)
+
+
+def gather_second(xa, yb):
+    return swap_y(xa), swap(yb, 2)
+
+
+def pieces_of(za, zb, first, second):
+    xa, yb, ya, xb = first
+    return [za, xa, ya, second[0], zb, xb, yb, second[1]]
+
+
+def join_job(values):
+    def fn(held, near, outs):
+        size = near[0].shape[0]
+        for i, v in enumerate(near):
+            outs[0][i * size : (i + 1) * size] = v[...]
+
+    return fn, [], values, [kept((len(values) * values[0].shape[0], *values[0].shape[1:]))]
 
 
 def mix(name, jobs):
@@ -562,15 +593,51 @@
     return sum(v.astype(F32) for v in parts)
 
 
-def join_job(pairs):
+def stack_job(values):
     def fn(held, near, outs):
-        for i, out in enumerate(outs):
-            size = near[2 * i].shape[0]
-            out[:size] = near[2 * i][...]
-            out[size:] = near[2 * i + 1][...]
-
-    near = [v for pair in pairs for v in pair]
-    return fn, [], near, [kept((2 * a.shape[0], *a.shape[1:])) for a, _ in pairs]
+        for k, v in enumerate(near):
+            for i in range(2):
+                outs[i][k] = v[i]
+
+    return fn, [], list(values), [kept((len(values), *values[0].shape[1:]))] * 2
+
+
+def vector_job(sums_a, sums_d, sums_x, wide, rows):
+    width = sums_a.shape[1]
+
+    def spread(rows_in, per):
+        flat = jnp.concatenate([rows_in[w * per // width][None] for w in range(wide)])
+        col = lax.broadcasted_iota(jnp.int32, (wide, width), 1)
+        own = lax.broadcasted_iota(jnp.int32, (wide, width), 0) * per % width
+        flat = jnp.where((col >= own) & (col < own + per), flat, 0.0)
+        pick = lax.broadcasted_iota(jnp.int32, (width, per), 0) % per
+        pick = (pick == lax.broadcasted_iota(jnp.int32, (width, per), 1)).astype(F32)
+        return lax.dot_general(
+            flat, pick, (((1,), (0,)), ((), ())), precision=lax.Precision.HIGHEST, preferred_element_type=F32
+        )
+
+    def fn(held, near, outs):
+        a, d, x = near
+        tiles = 4
+        at = 0
+        outs[0][...] = jnp.zeros_like(outs[0])
+        for got in (
+            spread([x[0]], rows),
+            spread([a[0], a[1]], 2 * rows),
+            spread([d[t] for t in range(tiles)], tiles * rows),
+            spread([a[2]], rows),
+        ):
+            outs[0][:, 0, at : at + got.shape[1]] = got
+            at += got.shape[1]
+
+    return fn, [], [sums_a, sums_d, sums_x], [kept((wide, 8, 8 * rows), F32)]
+
+
+def vector_sum_job(value):
+    def fn(held, near, outs):
+        outs[0][...] = jnp.sum(near[0][...], axis=0)
+
+    return fn, [], [value], [kept(value.shape[1:], F32)]
 
 
 def sum1_job(keep1, got1):
@@ -648,17 +715,26 @@
     return pltpu.make_async_copy(ref, ref, sem).wait
 
 
-def load_attn(scal, refs, w, sem, blocks):
+def piece(refs, at, core, k, alone):
+    if core == 0:
+        return refs[at].at[k]
+    if at in alone:
+        return refs[9 + alone.index(at)].at[k]
+    return refs[8].at[(at - sum(i < at for i in alone)) * 4 + k]
+
+
+def load_columns(scal, refs, w, sem):
+    rows = w.shape[1] // 16
+
     def start(own):
-        for block in blocks:
+        for block in range(4):
             for core in range(2):
-                for part, i, slot, half, side, k in slots():
+                for part, _, _, half, side, k in slots():
                     if (own ^ half) * 2 + part != block:
                         continue
-                    src = refs[core * 4 + part * 2 + i]
-                    rows = src.shape[1]
-                    at = pl.multiple_of(device_of(scal, k, side, core) * rows, 16)
-                    pltpu.make_async_copy(src.at[slot], w.at[block, pl.ds(at, rows), :], sem.at[block]).start()
+                    src = piece(refs, part * 4 + half * 2 + side, core, k, (3, 7)).at[pl.ds(0, rows), :]
+                    dst = w.at[block, rows_at(device_of(scal, k, side, core) * rows, rows), :]
+                    pltpu.make_async_copy(src, dst, sem.at[block]).start()
 
     @pl.when(scal[0] == 0)
     def _():
@@ -673,20 +749,19 @@
     def load(scal, refs, w, sem):
         def start(rel):
             for core in range(2):
-                for part, i, slot, half, side, k in slots():
+                for part, _, _, half, side, k in slots():
                     if half != rel:
                         continue
-                    src = refs[core * 4 + part * 2 + i]
-                    per, rows, width = src.shape[1:]
+                    src = piece(refs, part * 4 + half * 2 + side, core, k, (0, 4))
+                    per, rows, width = src.shape
                     dev = device_of(scal, k, side, core)
                     for b in range(per):
                         block = part * per + b
                         if which == 0:
-                            at, tile = block * width + dev * rows, block
+                            dst, tile = w.at[block, rows_at(dev * rows, rows), :], block
                         else:
-                            at, tile = (dev * 2 * per + block) * rows, scal[1] ^ k
-                        dst = w.at[pl.ds(pl.multiple_of(at, 16), rows), :]
-                        pltpu.make_async_copy(src.at[slot, b], dst, sem.at[tile]).start()
+                            dst, tile = w.at[rows_at((dev * 2 * per + block) * rows, rows), :], scal[1] ^ k
+                        pltpu.make_async_copy(src.at[b], dst, sem.at[tile]).start()
 
         @pl.when(scal[0] == which)
         def _():
@@ -697,6 +772,53 @@
             start(1)
 
     return load
+
+
+def vectors_kernel(rows, scal, *refs):
+    pieces, (vec, b_mlp, buf, sem) = refs[:3], refs[3:]
+    width = vec.shape[1]
+    for core in range(2):
+        for side in range(2):
+            for k in range(4):
+                src = pieces[side].at[k] if core == 0 else pieces[2].at[side * 4 + k]
+                src = src.at[pl.ds(rows, 8), :]
+                pltpu.make_async_copy(src, buf.at[device_of(scal, k, side, core)], sem).start()
+    whole_wait(buf, sem)()
+    values = buf[:, 0, :].astype(F32)
+    devices = values.shape[0]
+
+    def line(at, per):
+        pick = lax.broadcasted_iota(jnp.int32, (per, width), 1) % per
+        pick = (pick == lax.broadcasted_iota(jnp.int32, (per, width), 0)).astype(BF16)
+        flat = dot_nn(values[:, at : at + per].astype(BF16), pick)
+        dev = lax.broadcasted_iota(jnp.int32, flat.shape, 0)
+        col = lax.broadcasted_iota(jnp.int32, flat.shape, 1)
+        count = devices * per // width
+        share = devices // count
+        keep = col // per == dev % share
+        return [
+            jnp.sum(jnp.where(keep & (dev // share == i), flat, 0.0), axis=0, keepdims=True) for i in range(count)
+        ]
+
+    lines = line(0, rows) + line(rows, 2 * rows) + line(7 * rows, rows)
+    vec[...] = jnp.zeros_like(vec)
+    for i, v in enumerate(lines):
+        vec[i : i + 1, :] = v
+    for i, v in enumerate(line(3 * rows, 4 * rows)):
+        b_mlp[i : i + 1, :] = v
+
+
+def vectors_call(scal, pieces, rows):
+    width = pieces[0].shape[2]
+    return pl.pallas_call(
+        functools.partial(vectors_kernel, rows),
+        name="vectors",
+        out_shape=[kept((8, width), F32), kept((4, width), F32)],
+        in_specs=[SMEM] + [HBM] * 3,
+        out_specs=[VMEM] * 2,
+        scratch_shapes=[pltpu.VMEM((16, 8, width), BF16), pltpu.SemaphoreType.DMA],
+        compiler_params=pltpu.CompilerParams(vmem_limit_bytes=8 << 20),
+    )(scal, *[pltpu.with_memory_space_constraint(v, pltpu.HBM) for v in pieces])
 
 
 def store_with(source):
@@ -729,18 +851,16 @@
     return g.at[rows_at((dev * 4 + half * 2 + part) * rows, rows), :]
 
 
-def load_whole_attn(scal, refs, w, sem, blocks):
-    for i in blocks:
-        pltpu.make_async_copy(refs[i], w.at[i], sem.at[i]).start()
-
-
-def load_whole_mlp(scal, refs, w, sem):
+def load_whole_blocks(scal, refs, w, sem):
+    for i, r in enumerate(refs):
+        pltpu.make_async_copy(r, w.at[i], sem.at[i]).start()
+
+
+def load_whole_rows(scal, refs, w, sem):
     width = w.shape[1]
-    for i, r in enumerate(refs):
-        for t in range(r.shape[0] // width):
-            at = i + t
-            src = r.at[pl.ds(t * width, width), :]
-            pltpu.make_async_copy(src, w.at[pl.ds(at * width, width), :], sem.at[at]).start()
+    for t in range(w.shape[0] // width):
+        r = tile_of(t, width)
+        pltpu.make_async_copy(refs[0].at[r, :], w.at[r, :], sem.at[t]).start()
 
 
 def store_whole(scal, g, refs, sem):
@@ -804,14 +924,17 @@
         down_w = [lax.all_gather(w_mlp, "wide", axis=0, tiled=True)]
         vec, b_mlp = vectors(lax.all_gather(vec_own, "wide", axis=0))
         square = [sds((width, width))]
-        xn, q, k, v, da, wa = project_call(scal, x, cot, vec, attn_w, load_whole_attn)
-        o, dq, dk, dv = core_call(scal, q, k, v, da)
-        sums_a, *g_attn = attn_grad_call(scal, xn, o, dq, dk, dv, cot, store_whole, square * 4)
-        act, gp, wu, wd = up_call(scal, xn, b_mlp, up_w, down_w, load_whole_mlp, load_whole_mlp)
+        xn, q, k, v, da, wa = project_call(scal, x, cot, vec, attn_w, load_whole_blocks)
+        o, d = core_call(0, scal, q, k, v, da)
+        for b in range(1, last.shape[0]):
+            o, d = core_call(b, scal, q, k, v, da, o, d)
+        sums_a, *g_attn = attn_grad_call(scal, xn, o, d, cot, store_whole, square * 4)
+        act, gp, wu = up_call(0, tiles // 2, scal, xn, b_mlp, (), up_w, load_whole_blocks)
+        act, gp = up_call(tiles // 2, tiles - tiles // 2, scal, xn, b_mlp, (act, gp, wu), [], None)
         g_down = down_grad_call(scal, act, cot, store_whole, [sds((tiles * width, width))])
-        dpre, sums_d = dpre_call(scal, cot, gp, wd)
+        dpre, sums_d, wd = dpre_call(scal, cot, gp, down_w, load_whole_rows)
         g_up = up_grad_call(scal, xn, dpre, store_whole, square * tiles)
-        sums_x, d_x = input_grad_call(scal, x, cot, dq, dk, dv, dpre, vec, wa, wu)
+        sums_x, d_x = input_grad_call(scal, x, cot, d, dpre, vec, wa, wu)
         out = out_call(scal, x, o, act, vec, wa, wd)
 
         def reduce(g):
@@ -824,58 +947,64 @@
         vg = reduce(vector_grads(sums_a, sums_d, sums_x))[0]
     else:
         col = lambda i: w_joined[:, i * width : (i + 1) * width]
-        half = jnp.stack([jnp.where(n == 0, col(0), col(2)), jnp.where(n == 0, col(1), w_out)])
+        pair = lambda f: jnp.stack([jnp.where(n == 0, f(0), f(2)), jnp.where(n == 0, f(1), f(3))])
+        half = pair(lambda i: col(i) if i < 3 else w_out)
+        v_rows = jnp.pad(vec_own, (0, width - vec_own.shape[0]))
+        half = jnp.concatenate([half, jnp.broadcast_to(v_rows, (2, 8, width))], axis=1)
         got = gather_z(half)
-        v_own = behind(vec_own, half)
-        v_all = lax.all_to_all(jnp.broadcast_to(v_own, (wide, *v_own.shape)), "wide", 0, 0, tiled=True)
-        w_up, v_all = lax.optimization_barrier((behind(w_joined, half), v_all))
-        cols = jnp.stack([w_up[:, (3 + t) * width : (4 + t) * width] for t in range(tiles)])
-        c_half = jnp.where(n == 0, cols, w_mlp.reshape(tiles, rows, width))
-        c_half = c_half.reshape(2, tiles // 2, rows, width)
-        c_got = gather_z(c_half)
-        za, zb = gather_stack(half, got)
-        xa, yb = gather_xy(za, zb)
-        vec, b_mlp = vectors(v_all)
-        a0, b0 = jnp.concatenate([za, xa]), jnp.concatenate([zb, yb])
-        a1, b1 = swap_y(a0), swap(b0, 2)
-        a0s, b0s = swap(a0, 1), swap(b0, 1)
-        attn_w = [a0, a1, b0, b1, a0s, swap(a1, 1), b0s, swap(b1, 1)]
-
-        cza, czb = gather_stack(c_half, c_got)
-        xp, attn_w, vec, b_mlp, cza, czb = lax.optimization_barrier((x, attn_w, vec, b_mlp, cza, czb))
-        cxa, cyb = gather_xy(cza, czb)
-        xn, q, k, v, da, wa = project_call(scal, xp, cot, vec, attn_w, load_attn)
-
-        cxa, cyb = behind((cxa, cyb), q)
-        ((ca0, cb0),) = mix("join", [join_job([(cza, cxa), (czb, cyb)])])
-        q, ca0, cb0 = lax.optimization_barrier((q, ca0, cb0))
-        ca1, cb1 = swap_y(ca0), swap(cb0, 2)
-        ca0s, cb0s = swap(ca0, 1), swap(cb0, 1)
-        o, dq, dk, dv = core_call(scal, q, k, v, da)
-
-        ca1, cb1 = behind((ca1, cb1), dq)
-        dq, ca1, cb1 = lax.optimization_barrier((dq, ca1, cb1))
-        ca1s, cb1s = swap(ca1, 1), swap(cb1, 1)
+        za, zb = [jnp.stack([t[i] for t in (half, *got)]) for i in range(2)]
+        c_half = jnp.stack([jnp.where(n == 0, col(3 + t), w_mlp[t * rows : (t + 1) * rows]) for t in range(tiles)])
+        c_half = behind(c_half.reshape(2, tiles // 2, rows, width), za, zb)
+        first = gather_first(za, zb)
+        c2 = swap(c_half, 8)
+        first, c2, c_half = lax.optimization_barrier((first, c2, c_half))
+        second = gather_second(*first[:2])
+        own = pieces_of(za, zb, first, second)
+        ((joined,),) = mix("join_a", [join_job([own[i] for i in (0, 1, 2, 4, 5, 6)])])
+        joined, c1, c3 = swap(joined, 1), swap(c_half, 4), swap(c_half, 12)
+        second, joined, c1, c3 = lax.optimization_barrier((second, joined, c1, c3))
+        own = pieces_of(za, zb, first, second)
+        attn_w = [*own, joined, swap(second[0], 1), swap(second[1], 1)]
+        cza, czb = [jnp.stack([t[i] for t in (c_half, c1, c2, c3)]) for i in range(2)]
+        x_p, attn_w, cza, czb = lax.optimization_barrier((x, attn_w, cza, czb))
+        vec, b_mlp = vectors_call(scal, [attn_w[0], attn_w[1], attn_w[8]], rows)
+        c_first = gather_first(cza, czb)
+        xn, q, k, v, da, wa = project_call(scal, x_p, cot, vec, attn_w, load_columns)
+        part = core_call(0, scal, q, k, v, da)
+
+        part, c_first = lax.optimization_barrier((part, c_first))
+        c_second = gather_second(*c_first[:2])
+        czs = [swap(cza, 1), swap(czb, 1)]
+        o, d = core_call(1, scal, q, k, v, da, *part)
+
+        d, c_second, czs = lax.optimization_barrier((d, c_second, czs))
+        c_own = pieces_of(cza, czb, c_first, c_second)
+        ((c_joined,),) = mix("join_c", [join_job([t for t in c_own if t is not cza and t is not czb])])
+        d, c_joined = lax.optimization_barrier((d, c_joined))
+        c_other = swap(c_joined, 1)
         attn_shapes = [sds((2, 8, rows, width))] * 4
-        sums_a, *ga = attn_grad_call(scal, xn, o, dq, dk, dv, cot, store_with(attn_source), attn_shapes)
-        mlp_w = [ca0, ca1, cb0, cb1, ca0s, *behind([ca1s, cb0s, cb1s], sums_a)]
-
+        sums_a, *ga = attn_grad_call(scal, xn, o, d, cot, store_with(attn_source), attn_shapes)
+
+        c_other, ga = behind((c_other, ga), sums_a)
+        xn_u, ga, c_own, c_other = lax.optimization_barrier((xn, ga, c_own, c_other))
         a_got1, a_got0 = swap(ga[3], 1), swap(ga[2], 1)
-        xn_u = behind(xn, ga)
-        act, gp, wu, wd = up_call(scal, xn_u, b_mlp, mlp_w, [], load_half(0), load_half(1))
+        half_tiles = tiles // 2
+        c_all = [*c_own, c_other, *czs]
+        act, gp, wu = up_call(0, half_tiles, scal, xn_u, b_mlp, (), c_all, load_half(0))
 
         a_got1, a_got0 = behind((a_got1, a_got0), gp)
         ((sa, sb),) = mix("sums_1", [sum1_job(ga[1], a_got1)])
-        act_g, sa, sb = lax.optimization_barrier((act, sa, sb))
+        act, sa, sb = lax.optimization_barrier((act, sa, sb))
         a_xy = swap_y(sa), swap(sb, 2)
-        gd = down_grad_call(scal, act_g, cot, store_with(down_source), attn_shapes)
+        act, gp = up_call(half_tiles, half_tiles, scal, xn_u, b_mlp, (act, gp, wu), [], None)
+        gd = down_grad_call(scal, act, cot, store_with(down_source), attn_shapes)
 
         a_xy = behind(a_xy, gd)
         ((sa, sb),) = mix("sums_2", [sum2_job(ga[0], a_got0, a_xy)])
         gp, sa, sb, gd = lax.optimization_barrier((gp, sa, sb, gd))
         a_yx = swap(sa, 2), swap_y(sb)
         d_got1, d_got0 = swap(gd[3], 1), swap(gd[2], 1)
-        dpre, sums_d = dpre_call(scal, cot, gp, wd)
+        dpre, sums_d, wd = dpre_call(scal, cot, gp, c_all, load_half(1))
 
         a_yx, d_got1, d_got0 = behind((a_yx, d_got1, d_got0), dpre)
         a_t, (sa, sb) = mix("sums_3", [sum3_job(ga[0], a_got0, a_xy, a_yx), sum1_job(gd[1], d_got1)])
@@ -890,28 +1019,35 @@
         u_got1, u_got0 = swap(gu[3], 1), swap(gu[2], 1)
         d_yx = swap(sa, 2), swap_y(sb)
         a_other = swap_y(a_sum)
-        sums_x, d_x = input_grad_call(scal, x_i, cot, dq, dk, dv, dpre, vec, wa, wu)
+        sums_x, d_x = input_grad_call(scal, x_i, cot, d, dpre, vec, wa, wu)
 
         d_yx, u_got1, u_got0, a_other = behind((d_yx, u_got1, u_got0, a_other), d_x)
-        (sa, sb), d_t = mix("sums_5", [sum1_job(gu[1], u_got1), sum3_job(gd[0], d_got0, d_xy, d_yx)])
-        x_o, sa, sb, d_t, sums_x = lax.optimization_barrier((x, sa, sb, d_t, sums_x))
+        (sa, sb), d_t, (v_grad,) = mix(
+            "sums_5",
+            [
+                sum1_job(gu[1], u_got1),
+                sum3_job(gd[0], d_got0, d_xy, d_yx),
+                vector_job(sums_a, sums_d, sums_x, wide, rows),
+            ],
+        )
+        x_o, sa, sb, d_t = lax.optimization_barrier((x, sa, sb, d_t))
         u_xy = swap_y(sa), swap(sb, 2)
         d_z = [swap(d_t[k], k << 2) for k in (1, 2, 3)]
         out = out_call(scal, x_o, o, act, vec, wa, wd)
 
-        late = (u_xy, d_z, a_sum, a_other, sums_a, sums_d, sums_x)
-        u_xy, d_z, a_sum, a_other, sums_a, sums_d, sums_x = behind(late, out)
-        ((sa, sb),) = mix("sums_6", [sum2_job(gu[0], u_got0, u_xy)])
+        u_xy, d_z, v_grad = behind((u_xy, d_z, v_grad), out)
+        (sa, sb), (d_sum,) = mix("sums_6", [sum2_job(gu[0], u_got0, u_xy), sum4_job(d_t[0], d_z)])
+        sa, sb, d_sum, v_grad = lax.optimization_barrier((sa, sb, d_sum, v_grad))
         u_yx = swap(sa, 2), swap_y(sb)
-        sums_a, sums_d, sums_x, d_z = behind((sums_a, sums_d, sums_x, d_z), sa, sb)
-        v_sum = lax.all_to_all(vector_grads(sums_a, sums_d, sums_x), "wide", 0, 0, tiled=True)
-        v_sum = jnp.sum(v_sum, axis=0)
-        (d_sum,), u_t = mix(
-            "sums_7", [sum4_job(d_t[0], behind(d_z, v_sum)), sum3_job(gu[0], u_got0, u_xy, u_yx)]
+        d_other = swap_y(d_sum)
+        v_got = lax.all_to_all(v_grad.reshape(wide * 8, 8 * rows), "wide", 0, 0, tiled=True)
+        u_t, (v_sum,) = mix(
+            "sums_7",
+            [sum3_job(gu[0], u_got0, u_xy, u_yx), vector_sum_job(v_got.reshape(wide, 8, 8 * rows))],
         )
+        v_other = swap_y(v_sum)
         u_z = [swap(u_t[k], k << 2) for k in (1, 2, 3)]
-        d_other = swap_y(d_sum)
-        vg = v_sum + swap_y(v_sum)
+        vg = (v_sum + v_other)[0]
         ((u_sum,),) = mix("sums_8", [sum4_job(u_t[0], u_z)])
         u_other = swap_y(u_sum)
         grad_joined, grad_out, grad_mlp = place_call(

time: 276 us -> 267 us (0.967)
  local copies, waits for them, and re-layouts: 23.4 us -> 10.8 us
  blocking collectives: 11 us -> 0 us
  Pallas kernels: 107 us -> 116 us
  waiting for transfers between devices: 66.7 us -> 72.5 us
  starting transfers between devices: 59.8 us -> 64.3 us
  other arithmetic: 5.19 us -> 2.36 us
    ppermute x39, waiting for transfers between devices: 36.6 us -> 65.4 us  [swap(): return lax.ppermute(value, 'wide', [(i, i ^ mask) for i in range(16)])]
    ppermute x14 -> x16, waiting for transfers between devices: 28.1 us -> 7.03 us  [swap_y(): return lax.ppermute(value, 'narrow', [(0, 1), (1, 0)])]
    all_to_all x1 -> x0, blocking collectives: 11 us -> none  [body(): lax.all_to_all(vector_grads(sums_a, sums_d, sums_x), 'wide', 0, 0, tiled=...]
    unnamed x67 -> x66, local copies, waits for them, and re-layouts: 9.2 us -> 5.2 us
    slice x14 -> x6, local copies, waits for them, and re-layouts: 5.1 us -> 1.12 us  [the longest x2 1.07 us: body(): t[i]]
    pallas_call x9 -> x10, Pallas kernels: 12.8 us -> 16.4 us  [mix(): pl.pallas_call(kernel, name=name, out_shape=outs, in_specs=[VMEM] * len(n...]
    ppermute x39, starting transfers between devices: 37.7 us -> 41.2 us  [swap(): return lax.ppermute(value, 'wide', [(i, i ^ mask) for i in range(16)])]
    ppermute x14 -> x16, starting transfers between devices: 14.7 us -> 17.8 us  [swap_y(): return lax.ppermute(value, 'narrow', [(0, 1), (1, 0)])]
  transfers between devices with their start and end apart: 54 -> 56, of which waited for: 18 -> 16; matrix products, arithmetic and copies ran while one was open for 6% -> 2% of each run, Pallas kernels for 34% -> 36%
where the time goes in v3:
time: 267 us
  Pallas kernels  116 us (43%)
  waiting for transfers between devices  72.5 us (27%)
  starting transfers between devices  64.3 us (24%)
  local copies, waits for them, and re-layouts  10.8 us (4%)
    pallas_call x11, Pallas kernels, call(): pl.pallas_call(kernel, name=name, out_shape=list(outs) + list(g_shapes),...  95.4 us
    ppermute x39, waiting for transfers between devices, swap(): return lax.ppermute(value, 'wide', [(i, i ^ mask) for i in range(16)])  65.4 us
    ppermute x39, starting transfers between devices, swap(): return lax.ppermute(value, 'wide', [(i, i ^ mask) for i in range(16)])  41.2 us
    ppermute x16, starting transfers between devices, swap_y(): return lax.ppermute(value, 'narrow', [(0, 1), (1, 0)])  17.8 us
    pallas_call x10, Pallas kernels, mix(): pl.pallas_call(kernel, name=name, out_shape=outs, in_specs=[VMEM] * len(n...  16.4 us
    ppermute x16, waiting for transfers between devices, swap_y(): return lax.ppermute(value, 'narrow', [(0, 1), (1, 0)])  7.03 us
  transfers between devices with their start and end apart: 56, of which 16 were waited for; matrix products, arithmetic and copies ran while one was open for 2% of the time, Pallas kernels for 36%

profile of v3, /device:TPU:0, one launch (start us, length us, event | category | flops | bytes accessed | tf_op | source)
XLA Modules:
  0.0 267.1 jit_solution(7600973693270517641)
XLA Ops:
  1.4 1.3 select_bitcast_fusion.3
  2.7 5.1 %collective-permute-start.2 = (bf16[2,56,768]{2,1,0:T(8,128)(2,1)S(1)}, bf16[2,56,768]{2,1,0:T(8,128)(2,1)S(1)}, u32[]{:S(2)}, u32[]{:S(2)}) collective-permute-start(bf16[2,56,768]{2,1,0:T(8,128)(2,1)S(1)} %pad_maximum_fusion.5), channel_id=1, source_target_pairs={{0,12},{1,13},{2,14},{3,15},{4,8},{5,9},{6,10},{7,11},{8,4},{9,5},... | collective-permute-start | bytes 516104 | tf_op jit(solution)/shard_map/ppermute | solution.py:497
  8.5 4.6 %collective-permute-done.2 = bf16[2,56,768]{2,1,0:T(8,128)(2,1)S(1)} collective-permute-done((bf16[2,56,768]{2,1,0:T(8,128)(2,1)S(1)}, bf16[2,56,768]{2,1,0:T(8,128)(2,1)S(1)}, u32[]{:S(2)}, u32[]{:S(2)}) %collective-permute-start.2) | collective-permute-done | bytes 172064 | tf_op jit(solution)/shard_map/ppermute | solution.py:497
  13.2 9.3 %collective-permute-done.1 = bf16[2,56,768]{2,1,0:T(8,128)(2,1)S(1)} collective-permute-done((bf16[2,56,768]{2,1,0:T(8,128)(2,1)S(1)}, bf16[2,56,768]{2,1,0:T(8,128)(2,1)S(1)}, u32[]{:S(2)}, u32[]{:S(2)}) %collective-permute-start.1) | collective-permute-done | bytes 172064 | tf_op jit(solution)/shard_map/ppermute | solution.py:497
  22.6 1.6 collective-permute-start.5
  24.2 1.5 collective-permute-start.3
  26.9 13.8 %collective-permute-done.7 = bf16[2,2,48,768]{3,2,1,0:T(8,128)(2,1)S(1)} collective-permute-done((bf16[2,2,48,768]{3,2,1,0:T(8,128)(2,1)S(1)}, bf16[2,2,48,768]{3,2,1,0:T(8,128)(2,1)S(1)}, u32[]{:S(2)}, u32[]{:S(2)}) %collective-permute-start.7) | collective-permute-done | bytes 294944 | tf_op jit(solution)/shard_map/ppermute | solution.py:497
  41.4 1.2 join_a.1
  42.8 1.6 collective-permute-start.12
  44.4 1.5 collective-permute-start.8
  46.0 1.5 collective-permute-start.9
  47.5 1.4 fusion.15
  48.8 1.3 stack.55.scal.refs_0_
  51.2 3.3 %collective-permute-done.12 = bf16[2,2,48,768]{3,2,1,0:T(8,128)(2,1)S(1)} collective-permute-done((bf16[2,2,48,768]{3,2,1,0:T(8,128)(2,1)S(1)}, bf16[2,2,48,768]{3,2,1,0:T(8,128)(2,1)S(1)}, u32[]{:S(2)}, u32[]{:S(2)}) %collective-permute-start.12) | collective-permute-done | bytes 294944 | tf_op jit(solution)/shard_map/ppermute | solution.py:497
  54.5 5.3 %collective-permute-done.11 = bf16[2,2,48,768]{3,2,1,0:T(8,128)(2,1)S(1)} collective-permute-done((bf16[2,2,48,768]{3,2,1,0:T(8,128)(2,1)S(1)}, bf16[2,2,48,768]{3,2,1,0:T(8,128)(2,1)S(1)}, u32[]{:S(2)}, u32[]{:S(2)}) %collective-permute-start.11) | collective-permute-done | bytes 294944 | tf_op jit(solution)/shard_map/ppermute | solution.py:497
  60.7 1.1 collective-permute-done.13.refs_13_
  62.4 1.6 collective-permute-start.17
  63.9 1.5 collective-permute-start.15
  66.5 1.8 vectors.1
  68.3 8.5 %project.1 = (bf16[1024,768]{1,0:T(8,128)(2,1)S(1)}, bf16[1024,768]{1,0:T(8,128)(2,1)S(1)}, bf16[1024,768]{1,0:T(8,128)(2,1)S(1)}, bf16[1024,768]{1,0:T(8,128)(2...) custom-call(s32[10]{0:T(128)S(1)} %stack.55.scal.refs_0_, bf16[1024,768]{1,0:T(8,128)(2,1)S(1)} %bitcast.33, ...), custom_call_target="tpu_custom_call" | custom-call | flops 4831838208 | bytes 1048576 | tf_op jit(solution)/shard_map/project/pallas_call | solution.py:139
  76.8 8.3 %core.2 = (bf16[1024,768]{1,0:T(8,128)(2,1)S(1)}, bf16[3,1024,768]{2,1,0:T(8,128)(2,1)S(1)}) custom-call(s32[10]{0:T(128)S(1)} %stack.55.scal.refs_0_, bf16[1024,768]{1,0:T(8,128)(2,1)S(1)} %get-tuple-element.219.q, bf16[1024,768]{1,0:T(8,128)(2,1)S(1)} %get-tuple-element.220.k, bf16[1024,768]{1,0:T(8,128)(2,1)S(1)} %get-tuple-element.221.v, ...), custom_call_target="tpu_custom_call" | custom-call | flops 10737418240 | bytes 1048576 | tf_op jit(solution)/shard_map/core/pallas_call | solution.py:139
  85.2 6.7 %collective-permute-done.18.refs_3_.refs_8_ = bf16[4,2,48,768]{3,2,1,0:T(8,128)(2,1)S(1)} collective-permute-done((bf16[4,2,48,768]{3,2,1,0:T(8,128)(2,1)S(1)}, bf16[4,2,48,768]{3,2,1,0:T(8,128)(2,1)S(1)}, u32[]{:S(2)}, u32[]{:S(2)}) %collective-permute-start.18) | collective-permute-done | bytes 589856 | tf_op jit(solution)/shard_map/ppermute | solution.py:497
  92.5 1.5 collective-permute-start.20
  93.9 8.3 %core.3 = (bf16[1024,768]{1,0:T(8,128)(2,1)S(1)}, bf16[3,1024,768]{2,1,0:T(8,128)(2,1)S(1)}) custom-call(s32[10]{0:T(128)S(1)} %stack.55.scal.refs_0_, bf16[1024,768]{1,0:T(8,128)(2,1)S(1)} %get-tuple-element.219.q, bf16[1024,768]{1,0:T(8,128)(2,1)S(1)} %get-tuple-element.220.k, ...), custom_call_target="tpu_custom_call", output_to_operand_aliasing={{0}: (5, {}), {1}: (6, {})} | custom-call | flops 10737418240 | bytes 1048576 | tf_op jit(solution)/shard_map/core/pallas_call | solution.py:139
  102.3 4.1 %collective-permute-done.19.refs_2_.refs_6_ = bf16[4,2,48,768]{3,2,1,0:T(8,128)(2,1)S(1)} collective-permute-done((bf16[4,2,48,768]{3,2,1,0:T(8,128)(2,1)S(1)}, bf16[4,2,48,768]{3,2,1,0:T(8,128)(2,1)S(1)}, u32[]{:S(2)}, u32[]{:S(2)}) %collective-permute-start.19) | collective-permute-done | bytes 589856 | tf_op jit(solution)/shard_map/ppermute | solution.py:501
  107.5 9.0 %attn_grad.1 = (f32[8,768]{1,0:T(8,128)S(1)}, bf16[2,8,48,768]{3,2,1,0:T(8,128)(2,1)}, bf16[2,8,48,768]{3,2,1,0:T(8,128)(2,1)}, bf16[2,8,48,768]{3,2,1,0:T(8,128)(2,1)}, bf16[2,8,48,768]{3,2,1,0:T(8,128)(2,1)}) custom-call(s32[10]{0:T(128)S(1)} %stack.55.scal.refs_0_, bf16[1024,768]{1,0:T(8,128)(2,1)S(1)} %get-tuple-element.250.xn.refs_1_, ...), custom_call_target="tpu_custom_call" | custom-call | flops 4831838208 | bytes 1048576 | tf_op jit(solution)/shard_map/attn_grad/pallas_call | solution.py:139
  117.2 1.2 copy-done.19
  118.4 8.4 %up.2 = (bf16[4,1024,768]{2,1,0:T(8,128)(2,1)S(1)}, bf16[4,1024,768]{2,1,0:T(8,128)(2,1)S(1)}, bf16[4,768,768]{2,1,0:T(8,128)(2,1)S(1)}) custom-call(s32[10]{0:T(128)S(1)} %stack.55.scal.refs_0_, bf16[1024,768]{1,0:T(8,128)(2,1)S(1)} %get-tuple-element.250.xn.refs_1_, f32[4,768]{1,0:T(4,128)S(1)} %get-tuple-element.251.refs_2_, ...), custom_call_target="tpu_custom_call" | custom-call | flops 2415919104 | bytes 1048576 | tf_op jit(solution)/shard_map/up/pallas_call | solution.py:139
  126.8 1.6 sums_1.1
  128.4 1.6 collective-permute-start.26
  130.0 5.2 %collective-permute-start.27 = (bf16[8,48,768]{2,1,0:T(8,128)(2,1)S(1)}, bf16[8,48,768]{2,1,0:T(8,128)(2,1)S(1)}, u32[]{:S(2)}, u32[]{:S(2)}) collective-permute-start(bf16[8,48,768]{2,1,0:T(8,128)(2,1)S(1)} %get-tuple-element.276), channel_id=1, source_target_pairs={{0,2},{1,3},{2,0},{3,1},{4,6},{5,7},{6,4},{7,5},{8,10},{9,11},{10,... | collective-permute-start | bytes 1769480 | tf_op jit(solution)/shard_map/ppermute | solution.py:497
  135.2 6.0 %up.3 = (bf16[4,1024,768]{2,1,0:T(8,128)(2,1)S(1)}, bf16[4,1024,768]{2,1,0:T(8,128)(2,1)S(1)}) custom-call(s32[10]{0:T(128)S(1)} %stack.55.scal.refs_0_, bf16[1024,768]{1,0:T(8,128)(2,1)S(1)} %get-tuple-element.250.xn.refs_1_, f32[4,768]{1,0:T(4,128)S(1)} %get-tuple-element.251.refs_2_, ...), custom_call_target="tpu_custom_call", output_to_operand_aliasing={{0}: (3, {}), {1}: (4, {})} | custom-call | flops 2415919104 | bytes 1048576 | tf_op jit(solution)/shard_map/up/pallas_call | solution.py:139
  141.2 8.5 %down_grad.1 = (bf16[2,8,48,768]{3,2,1,0:T(8,128)(2,1)}, bf16[2,8,48,768]{3,2,1,0:T(8,128)(2,1)}, bf16[2,8,48,768]{3,2,1,0:T(8,128)(2,1)}, bf16[2,8,48,768]{3,2,1,0:T(8,128)(2,1)}) custom-call(s32[10]{0:T(128)S(1)} %stack.55.scal.refs_0_, bf16[4,1024,768]{2,1,0:T(8,128)(2,1)S(1)} %get-tuple-element.277.act, bf16[1024,768]{1,0:T(8,128)(2,1)S(1)} %bitcast.30), custom_call_target="tpu_custom_call" | custom-call | flops 4831838208 | bytes 1048576 | tf_op jit(solution)/shard_map/down_grad/pallas_call | solution.py:139
  149.7 1.6 sums_2.1
  152.0 9.9 %dpre.1 = (bf16[4,1024,768]{2,1,0:T(8,128)(2,1)S(1)}, f32[8,768]{1,0:T(8,128)S(1)}, bf16[3072,768]{1,0:T(8,128)(2,1)S(1)}) custom-call(s32[10]{0:T(128)S(1)} %stack.55.scal.refs_0_, bf16[1024,768]{1,0:T(8,128)(2,1)S(1)} %bitcast.31, bf16[4,1024,768]{2,1,0:T(8,128)(2,1)S(1)} %get-tuple-element.287.refs_2_, ...), custom_call_target="tpu_custom_call", output_to_operand_aliasing={{0}: (2, {})} | custom-call | flops 4831838208 | bytes 1048576 | tf_op jit(solution)/shard_map/dpre/pallas_call | solution.py:139
  162.0 2.1 sums_3.1
  164.1 2.0 collective-permute-start.35
  166.1 2.0 collective-permute-start.36
  168.1 2.9 %collective-permute-start.33 = (bf16[2,48,768]{2,1,0:T(8,128)(2,1)S(1)}, bf16[2,48,768]{2,1,0:T(8,128)(2,1)S(1)}, u32[]{:S(2)}, u32[]{:S(2)}) collective-permute-start(bf16[2,48,768]{2,1,0:T(8,128)(2,1)S(1)} %get-tuple-element.305), channel_id=1, source_target_pairs={{0,8},{1,9},{2,10},{3,11},{4,12},{5,13},{6,14},{7,15},{8,0},{9,1},... | collective-permute-start | bytes 442376 | tf_op jit(solution)/shard_map/ppermute | solution.py:497
  171.0 1.5 collective-permute-start.34
  172.5 8.4 %up_grad.1 = (bf16[2,8,48,768]{3,2,1,0:T(8,128)(2,1)}, bf16[2,8,48,768]{3,2,1,0:T(8,128)(2,1)}, bf16[2,8,48,768]{3,2,1,0:T(8,128)(2,1)}, bf16[2,8,48,768]{3,2,1,0:T(8,128)(2,1)}) custom-call(s32[10]{0:T(128)S(1)} %stack.55.scal.refs_0_, bf16[1024,768]{1,0:T(8,128)(2,1)S(1)} %get-tuple-element.250.xn.refs_1_, bf16[4,1024,768]{2,1,0:T(8,128)(2,1)S(1)} %get-tuple-element.309.dpre), custom_call_target="tpu_custom_call" | custom-call | flops 4831838208 | bytes 1048576 | tf_op jit(solution)/shard_map/up_grad/pallas_call | solution.py:139
  181.8 1.6 sums_4.1
  184.4 1.5 collective-permute-start.37
  185.9 1.7 collective-permute-start.38
  187.6 11.8 %input_grad.1 = (f32[8,768]{1,0:T(8,128)S(1)}, bf16[2,512,768]{2,1,0:T(8,128)(2,1)}) custom-call(s32[10]{0:T(128)S(1)} %stack.55.scal.refs_0_, bf16[1024,768]{1,0:T(8,128)(2,1)S(1)} %bitcast.34, bf16[1024,768]{1,0:T(8,128)(2,1)S(1)} %bitcast.32, bf16[3,1024,768]{2,1,0:T(8,128)(2,1)S(1)} %bitcast.37, bf16[4,1024,768]{2,1,0:T(8,128)(2,1)S(1)} %get-tuple-element.309.dpre, ...), custom_call_target="tpu_custom_call" | custom-call | flops 8455716864 | bytes 1048576 | tf_op jit(solution)/shard_map/input_grad/pallas_call | solution.py:139
  199.4 4.1 %sums_5.1 = (bf16[8,48,768]{2,1,0:T(8,128)(2,1)S(1)}, bf16[8,48,768]{2,1,0:T(8,128)(2,1)S(1)}, bf16[2,48,768]{2,1,0:T(8,128)(2,1)S(1)}, bf16[2,48,768]{2,1,0:T(8...) custom-call(bf16[2,8,48,768]{3,2,1,0:T(8,128)(2,1)S(1)} %collective-permute-, ...), custom_call_target="tpu_custom_call" | custom-call | flops 1048576 | bytes 1048576 | tf_op jit(solution)/shard_map/sums_5/pallas_call | solution.py:571
  204.5 2.2 collective-permute-start.44
  207.7 1.3 collective-permute-start.46
  209.0 8.2 %out.1 = bf16[2,512,768]{2,1,0:T(8,128)(2,1)} custom-call(s32[10]{0:T(128)S(1)} %stack.55.scal.refs_0_, bf16[1024,768]{1,0:T(8,128)(2,1)S(1)} %bitcast.35, bf16[1024,768]{1,0:T(8,128)(2,1)S(1)} %get-tuple-element.238.o, bf16[4,1024,768]{2,1,0:T(8,128)(2,1)S(1)} %get-tuple-element.277.act, f32[8,768]{1,0:T(8,128)S(1)} %get-tuple-element.209.refs_3_.vec, ...), custom_call_target="tpu_custom_call" | custom-call | flops 6039797760 | bytes 1048576 | tf_op jit(solution)/shard_map/out/pallas_call | solution.py:139
  217.2 2.5 collective-permute-done.45.refs_5_
  219.8 2.2 sums_6.1
  223.4 5.3 %all-to-all-start = ((f32[16,8,384]{2,1,0:T(8,128)}), f32[16,8,384]{2,1,0:T(8,128)S(1)}, u32[]{:S(2)}, u32[]{:S(2)}) async-start(f32[16,8,384]{2,1,0:T(8,128)} %get-tuple-element.368), calls=%async_computation | async-start | bytes 393216 | tf_op jit(solution)/shard_map/all_to_all | solution.py:1043
  228.7 1.9 collective-permute-start.48
  230.6 1.7 collective-permute-start.49
  232.3 8.0 %collective-permute-done.48.refs_3_ = bf16[4,48,768]{2,1,0:T(8,128)(2,1)S(1)} collective-permute-done((bf16[4,48,768]{2,1,0:T(8,128)(2,1)}, bf16[4,48,768]{2,1,0:T(8,128)(2,1)S(1)}, u32[]{:S(2)}, u32[]{:S(2)}) %collective-permute-start.48) | collective-permute-done | bytes 294944 | tf_op jit(solution)/shard_map/ppermute | solution.py:497
  240.2 1.7 sums_7.1
  241.9 1.7 collective-permute-start.54
  244.0 1.5 collective-permute-start.50
  245.5 2.3 collective-permute-start.51
  249.6 1.3 collective-permute-done.50.refs_1_
  250.9 7.9 %collective-permute-done.51.refs_2_ = bf16[2,48,768]{2,1,0:T(8,128)(2,1)S(1)} collective-permute-done((bf16[2,48,768]{2,1,0:T(8,128)(2,1)S(1)}, bf16[2,48,768]{2,1,0:T(8,128)(2,1)S(1)}, u32[]{:S(2)}, u32[]{:S(2)}) %collective-permute-start.51) | collective-permute-done | bytes 147488 | tf_op jit(solution)/shard_map/ppermute | solution.py:497
  258.9 1.7 collective-permute-start.53
  261.2 2.9 %collective-permute-done.53.u_other = bf16[2,48,768]{2,1,0:T(8,128)(2,1)S(1)} collective-permute-done((bf16[2,48,768]{2,1,0:T(8,128)(2,1)S(1)}, bf16[2,48,768]{2,1,0:T(8,128)(2,1)S(1)}, u32[]{:S(2)}, u32[]{:S(2)}) %collective-permute-start.53) | collective-permute-done | bytes 147488 | tf_op jit(solution)/shard_map/ppermute | solution.py:501
  265.1 2.0 place.1
  (160 shorter events, 19.1 us)
Async XLA Ops:
  2.7 10.4 %collective-permute-start.2 = (bf16[2,56,768]{2,1,0:T(8,128)(2,1)S(1)}, bf16[2,56,768]{2,1,0:T(8,128)(2,1)S(1)}, u32[]{:S(2)}, u32[]{:S(2)}) collective-permute-start(bf16[2,56,768]{2,1,0:T(8,128)(2,1)S(1)} %pad_maximum_fusion.5), channel_id=1, source_target_pairs={{0,12},{1,13},{2,14},{3,15},{4,8},{5,9},{6,10},{7,11},{8,4},{9,5},... | collective-permute-start | bytes 516104 | tf_op jit(solution)/shard_map/ppermute | solution.py:497
  7.9 14.6 %collective-permute-start.1 = (bf16[2,56,768]{2,1,0:T(8,128)(2,1)S(1)}, bf16[2,56,768]{2,1,0:T(8,128)(2,1)S(1)}, u32[]{:S(2)}, u32[]{:S(2)}) collective-permute-start(bf16[2,56,768]{2,1,0:T(8,128)(2,1)S(1)} %pad_maximum_fusion.5), channel_id=1, source_target_pairs={{0,8},{1,9},{2,10},{3,11},{4,12},{5,13},{6,14},{7,15},{8,0},{9,1},... | collective-permute-start | bytes 516104 | tf_op jit(solution)/shard_map/ppermute | solution.py:497
  7.9 14.6 %collective-permute-start = (bf16[2,56,768]{2,1,0:T(8,128)(2,1)S(1)}, bf16[2,56,768]{2,1,0:T(8,128)(2,1)S(1)}, u32[]{:S(2)}, u32[]{:S(2)}) collective-permute-start(bf16[2,56,768]{2,1,0:T(8,128)(2,1)S(1)} %pad_maximum_fusion.5), channel_id=1, source_target_pairs={{0,4},{1,5},{2,6},{3,7},{4,0},{5,1},{6,2},{7,3},{8,12},{9,13},{10,... | collective-permute-start | bytes 516104 | tf_op jit(solution)/shard_map/ppermute | solution.py:497
  22.6 20.1 %copy-start = (bf16[4,56,768]{2,1,0:T(8,128)(2,1)}, bf16[4,56,768]{2,1,0:T(8,128)(2,1)S(1)}, u32[]{:S(2)}) copy-start(bf16[4,56,768]{2,1,0:T(8,128)(2,1)S(1)} %pad_maximum_fusion.2.refs_0_.refs_4_) | copy-start | bytes 1032196
  22.6 18.2 %collective-permute-start.5 = (bf16[4,56,768]{2,1,0:T(8,128)(2,1)S(1)}, bf16[4,56,768]{2,1,0:T(8,128)(2,1)S(1)}, u32[]{:S(2)}, u32[]{:S(2)}) collective-permute-start(bf16[4,56,768]{2,1,0:T(8,128)(2,1)S(1)} %pad_maximum_fusion.2.refs_0_.refs_4_), channel_id=1, source_target_pairs={{0,16},{16,0},{1,17},{17,1},{2,18},{18,2},{3,19},{19,3},{4,20},{20... | collective-permute-start | bytes 1032200 | tf_op jit(solution)/shard_map/ppermute | solution.py:501
  24.2 16.6 %collective-permute-start.3 = (bf16[4,56,768]{2,1,0:T(8,128)(2,1)S(1)}, bf16[4,56,768]{2,1,0:T(8,128)(2,1)S(1)}, u32[]{:S(2)}, u32[]{:S(2)}) collective-permute-start(bf16[4,56,768]{2,1,0:T(8,128)(2,1)S(1)} %pad_maximum_fusion.2.refs_0_.refs_4_), channel_id=1, source_target_pairs={{0,2},{1,3},{2,0},{3,1},{4,6},{5,7},{6,4},{7,5},{8,10},{9,11},{10,... | collective-permute-start | bytes 1032200 | tf_op jit(solution)/shard_map/ppermute | solution.py:497
  25.7 17.0 %copy-start.8 = (bf16[4,56,768]{2,1,0:T(8,128)(2,1)}, bf16[4,56,768]{2,1,0:T(8,128)(2,1)S(1)}, u32[]{:S(2)}) copy-start(bf16[4,56,768]{2,1,0:T(8,128)(2,1)S(1)} %pad_maximum_fusion.3.refs_3_.refs_8_) | copy-start | bytes 1032196
  25.7 15.0 %collective-permute-start.6 = (bf16[4,56,768]{2,1,0:T(8,128)(2,1)S(1)}, bf16[4,56,768]{2,1,0:T(8,128)(2,1)S(1)}, u32[]{:S(2)}, u32[]{:S(2)}) collective-permute-start(bf16[4,56,768]{2,1,0:T(8,128)(2,1)S(1)} %pad_maximum_fusion.3.refs_3_.refs_8_), channel_id=1, source_target_pairs={{0,2},{1,3},{2,0},{3,1},{4,6},{5,7},{6,4},{7,5},{8,10},{9,11},{10,... | collective-permute-start | bytes 1032200 | tf_op jit(solution)/shard_map/ppermute | solution.py:497
  26.3 15.1 %collective-permute-start.4 = (bf16[4,56,768]{2,1,0:T(8,128)(2,1)S(1)}, bf16[4,56,768]{2,1,0:T(8,128)(2,1)}, u32[]{:S(2)}, u32[]{:S(2)}) collective-permute-start(bf16[4,56,768]{2,1,0:T(8,128)(2,1)S(1)} %pad_maximum_fusion.3.refs_3_.refs_8_), channel_id=1, source_target_pairs={{0,16},{16,0},{1,17},{17,1},{2,18},{18,2},{3,19},{19,3},{4,20},{20... | collective-permute-start | bytes 1032200 | tf_op jit(solution)/shard_map/ppermute | solution.py:501
  26.8 13.9 %collective-permute-start.7 = (bf16[2,2,48,768]{3,2,1,0:T(8,128)(2,1)S(1)}, bf16[2,2,48,768]{3,2,1,0:T(8,128)(2,1)S(1)}, u32[]{:S(2)}, u32[]{:S(2)}) collective-permute-start(bf16[2,2,48,768]{3,2,1,0:T(8,128)(2,1)S(1)} %bitcast.38), channel_id=1, source_target_pairs={{0,8},{1,9},{2,10},{3,11},{4,12},{5,13},{6,14},{7,15},{8,0},{9,1},... | collective-permute-start | bytes 884744 | tf_op jit(solution)/shard_map/ppermute | solution.py:497
  42.7 17.1 %collective-permute-start.10 = (bf16[24,56,768]{2,1,0:T(8,128)(2,1)S(1)}, bf16[24,56,768]{2,1,0:T(8,128)(2,1)}, u32[]{:S(2)}, u32[]{:S(2)}) collective-permute-start(bf16[24,56,768]{2,1,0:T(8,128)(2,1)S(1)} %join_a.1), channel_id=1, source_target_pairs={{0,1},{1,0},{2,3},{3,2},{4,5},{5,4},{6,7},{7,6},{8,9},{9,8},{10,11... | collective-permute-start | bytes 6193160 | tf_op jit(solution)/shard_map/ppermute | solution.py:497
  42.8 11.7 %collective-permute-start.12 = (bf16[2,2,48,768]{3,2,1,0:T(8,128)(2,1)S(1)}, bf16[2,2,48,768]{3,2,1,0:T(8,128)(2,1)S(1)}, u32[]{:S(2)}, u32[]{:S(2)}) collective-permute-start(bf16[2,2,48,768]{3,2,1,0:T(8,128)(2,1)S(1)} %bitcast.39), channel_id=1, source_target_pairs={{0,12},{1,13},{2,14},{3,15},{4,8},{5,9},{6,10},{7,11},{8,4},{9,5},... | collective-permute-start | bytes 884744 | tf_op jit(solution)/shard_map/ppermute | solution.py:497
  44.4 15.4 %collective-permute-start.11 = (bf16[2,2,48,768]{3,2,1,0:T(8,128)(2,1)S(1)}, bf16[2,2,48,768]{3,2,1,0:T(8,128)(2,1)S(1)}, u32[]{:S(2)}, u32[]{:S(2)}) collective-permute-start(bf16[2,2,48,768]{3,2,1,0:T(8,128)(2,1)S(1)} %bitcast.40), channel_id=1, source_target_pairs={{0,4},{1,5},{2,6},{3,7},{4,0},{5,1},{6,2},{7,3},{8,12},{9,13},{10,... | collective-permute-start | bytes 884744 | tf_op jit(solution)/shard_map/ppermute | solution.py:497
  44.4 15.4 %collective-permute-start.8 = (bf16[4,56,768]{2,1,0:T(8,128)(2,1)S(1)}, bf16[4,56,768]{2,1,0:T(8,128)(2,1)}, u32[]{:S(2)}, u32[]{:S(2)}) collective-permute-start(bf16[4,56,768]{2,1,0:T(8,128)(2,1)S(1)} %collective-permute-done.3.refs_1_.refs_5_), channel_id=1, source_target_pairs={{0,16},{16,0},{1,17},{17,1},{2,18},{18,2},{3,19},{19,3},{4,20},{20... | collective-permute-start | bytes 1032200 | tf_op jit(solution)/shard_map/ppermute | solution.py:501
  46.0 13.9 %collective-permute-start.9 = (bf16[4,56,768]{2,1,0:T(8,128)(2,1)}, bf16[4,56,768]{2,1,0:T(8,128)(2,1)}, u32[]{:S(2)}, u32[]{:S(2)}) collective-permute-start(bf16[4,56,768]{2,1,0:T(8,128)(2,1)} %collective-permute-done.4.refs_5_.refs_10_), channel_id=1, source_target_pairs={{0,2},{1,3},{2,0},{3,1},{4,6},{5,7},{6,4},{7,5},{8,10},{9,11},{10,... | collective-permute-start | bytes 1032200 | tf_op jit(solution)/shard_map/ppermute | solution.py:497
  50.2 158.8 %copy-start.14 = (s32[10]{0:T(128)}, s32[10]{0:T(128)S(1)}, u32[]{:S(2)}) copy-start(s32[10]{0:T(128)S(1)} %stack.55.scal.refs_0_) | copy-start | bytes 124
  59.8 1.9 collective-permute-start.13
  59.9 2.3 collective-permute-start.14
  60.5 24.6 %copy-start.20 = (bf16[4,2,48,768]{3,2,1,0:T(8,128)(2,1)}, bf16[4,2,48,768]{3,2,1,0:T(8,128)(2,1)S(1)}, u32[]{:S(2)}) copy-start(bf16[4,2,48,768]{3,2,1,0:T(8,128)(2,1)S(1)} %pad_maximum_fusion.1.refs_7_) | copy-start | bytes 1769476
  62.3 40.0 %collective-permute-start.21 = (bf16[4,2,48,768]{3,2,1,0:T(8,128)(2,1)S(1)}, bf16[4,2,48,768]{3,2,1,0:T(8,128)(2,1)S(1)}, u32[]{:S(2)}, u32[]{:S(2)}) collective-permute-start(bf16[4,2,48,768]{3,2,1,0:T(8,128)(2,1)S(1)} %pad_maximum_fusion.refs_3_), channel_id=1, source_target_pairs={{0,1},{1,0},{2,3},{3,2},{4,5},{5,4},{6,7},{7,6},{8,9},{9,8},{10,11... | collective-permute-start | bytes 1769480 | tf_op jit(solution)/shard_map/ppermute | solution.py:497
  62.4 22.7 %collective-permute-start.17 = (bf16[4,2,48,768]{3,2,1,0:T(8,128)(2,1)S(1)}, bf16[4,2,48,768]{3,2,1,0:T(8,128)(2,1)S(1)}, u32[]{:S(2)}, u32[]{:S(2)}) collective-permute-start(bf16[4,2,48,768]{3,2,1,0:T(8,128)(2,1)S(1)} %pad_maximum_fusion.refs_3_), channel_id=1, source_target_pairs={{0,16},{16,0},{1,17},{17,1},{2,18},{18,2},{3,19},{19,3},{4,20},{20... | collective-permute-start | bytes 1769480 | tf_op jit(solution)/shard_map/ppermute | solution.py:501
  63.9 21.3 %collective-permute-start.15 = (bf16[4,2,48,768]{3,2,1,0:T(8,128)(2,1)S(1)}, bf16[4,2,48,768]{3,2,1,0:T(8,128)(2,1)S(1)}, u32[]{:S(2)}, u32[]{:S(2)}) collective-permute-start(bf16[4,2,48,768]{3,2,1,0:T(8,128)(2,1)S(1)} %pad_maximum_fusion.refs_3_), channel_id=1, source_target_pairs={{0,2},{1,3},{2,0},{3,1},{4,6},{5,7},{6,4},{7,5},{8,10},{9,11},{10,... | collective-permute-start | bytes 1769480 | tf_op jit(solution)/shard_map/ppermute | solution.py:497
  65.4 26.5 %collective-permute-start.18 = (bf16[4,2,48,768]{3,2,1,0:T(8,128)(2,1)S(1)}, bf16[4,2,48,768]{3,2,1,0:T(8,128)(2,1)S(1)}, u32[]{:S(2)}, u32[]{:S(2)}) collective-permute-start(bf16[4,2,48,768]{3,2,1,0:T(8,128)(2,1)S(1)} %pad_maximum_fusion.1.refs_7_), channel_id=1, source_target_pairs={{0,2},{1,3},{2,0},{3,1},{4,6},{5,7},{6,4},{7,5},{8,10},{9,11},{10,... | collective-permute-start | bytes 1769480 | tf_op jit(solution)/shard_map/ppermute | solution.py:497
  66.0 25.9 %collective-permute-start.16 = (bf16[4,2,48,768]{3,2,1,0:T(8,128)(2,1)S(1)}, bf16[4,2,48,768]{3,2,1,0:T(8,128)(2,1)S(1)}, u32[]{:S(2)}, u32[]{:S(2)}) collective-permute-start(bf16[4,2,48,768]{3,2,1,0:T(8,128)(2,1)S(1)} %pad_maximum_fusion.1.refs_7_), channel_id=1, source_target_pairs={{0,16},{16,0},{1,17},{17,1},{2,18},{18,2},{3,19},{19,3},{4,20},{20... | collective-permute-start | bytes 1769480 | tf_op jit(solution)/shard_map/ppermute | solution.py:501
  85.1 21.6 %copy-start.1 = (bf16[4,2,48,768]{3,2,1,0:T(8,128)(2,1)}, bf16[4,2,48,768]{3,2,1,0:T(8,128)(2,1)S(1)}, u32[]{:S(2)}) copy-start(bf16[4,2,48,768]{3,2,1,0:T(8,128)(2,1)S(1)} %collective-permute-done.17.refs_1_.refs_5_) | copy-start | bytes 1769476
  85.1 17.2 %collective-permute-start.22 = (bf16[4,2,48,768]{3,2,1,0:T(8,128)(2,1)S(1)}, bf16[4,2,48,768]{3,2,1,0:T(8,128)(2,1)S(1)}, u32[]{:S(2)}, u32[]{:S(2)}) collective-permute-start(bf16[4,2,48,768]{3,2,1,0:T(8,128)(2,1)S(1)} %pad_maximum_fusion.1.refs_7_), channel_id=1, source_target_pairs={{0,1},{1,0},{2,3},{3,2},{4,5},{5,4},{6,7},{7,6},{8,9},{9,8},{10,11... | collective-permute-start | bytes 1769480 | tf_op jit(solution)/shard_map/ppermute | solution.py:497
  85.2 21.5 %copy-start.2 = (bf16[4,2,48,768]{3,2,1,0:T(8,128)(2,1)}, bf16[4,2,48,768]{3,2,1,0:T(8,128)(2,1)S(1)}, u32[]{:S(2)}) copy-start(bf16[4,2,48,768]{3,2,1,0:T(8,128)(2,1)S(1)} %collective-permute-done.15.refs_0_.refs_4_) | copy-start | bytes 1769476
  91.9 14.5 %collective-permute-start.19 = (bf16[4,2,48,768]{3,2,1,0:T(8,128)(2,1)S(1)}, bf16[4,2,48,768]{3,2,1,0:T(8,128)(2,1)S(1)}, u32[]{:S(2)}, u32[]{:S(2)}) collective-permute-start(bf16[4,2,48,768]{3,2,1,0:T(8,128)(2,1)S(1)} %collective-permute-done.15.refs_0_.refs_4_), channel_id=1, source_target_pairs={{0,16},{16,0},{1,17},{17,1},{2,18},{18,2},{3,19},{19,3},{4,20},{20... | collective-permute-start | bytes 1769480 | tf_op jit(solution)/shard_map/ppermute | solution.py:501
  92.5 14.2 %collective-permute-start.20 = (bf16[4,2,48,768]{3,2,1,0:T(8,128)(2,1)S(1)}, bf16[4,2,48,768]{3,2,1,0:T(8,128)(2,1)S(1)}, u32[]{:S(2)}, u32[]{:S(2)}) collective-permute-start(bf16[4,2,48,768]{3,2,1,0:T(8,128)(2,1)S(1)} %collective-permute-done.16.refs_4_.refs_9_), channel_id=1, source_target_pairs={{0,2},{1,3},{2,0},{3,1},{4,6},{5,7},{6,4},{7,5},{8,10},{9,11},{10,... | collective-permute-start | bytes 1769480 | tf_op jit(solution)/shard_map/ppermute | solution.py:497
  107.5 9.0 %collective-permute-start.23 = (bf16[24,2,48,768]{3,2,1,0:T(8,128)(2,1)S(1)}, bf16[24,2,48,768]{3,2,1,0:T(8,128)(2,1)S(1)}, u32[]{:S(2)}, u32[]{:S(2)}) collective-permute-start(bf16[24,2,48,768]{3,2,1,0:T(8,128)(2,1)S(1)} %join_c.1), channel_id=1, source_target_pairs={{0,1},{1,0},{2,3},{3,2},{4,5},{5,4},{6,7},{7,6},{8,9},{9,8},{10,11... | collective-permute-start | bytes 10616840 | tf_op jit(solution)/shard_map/ppermute | solution.py:497
  116.6 10.2 %collective-permute-start.24 = (bf16[2,8,48,768]{3,2,1,0:T(8,128)(2,1)}, bf16[2,8,48,768]{3,2,1,0:T(8,128)(2,1)S(1)}, u32[]{:S(2)}, u32[]{:S(2)}) collective-permute-start(bf16[2,8,48,768]{3,2,1,0:T(8,128)(2,1)} %get-tuple-element.264), channel_id=1, source_target_pairs={{0,1},{1,0},{2,3},{3,2},{4,5},{5,4},{6,7},{7,6},{8,9},{9,8},{10,11... | collective-permute-start | bytes 3538952 | tf_op jit(solution)/shard_map/ppermute | solution.py:497
  117.2 9.7 %collective-permute-start.25 = (bf16[2,8,48,768]{3,2,1,0:T(8,128)(2,1)}, bf16[2,8,48,768]{3,2,1,0:T(8,128)(2,1)S(1)}, u32[]{:S(2)}, u32[]{:S(2)}) collective-permute-start(bf16[2,8,48,768]{3,2,1,0:T(8,128)(2,1)} %get-tuple-element.265), channel_id=1, source_target_pairs={{0,1},{1,0},{2,3},{3,2},{4,5},{5,4},{6,7},{7,6},{8,9},{9,8},{10,11... | collective-permute-start | bytes 3538952 | tf_op jit(solution)/shard_map/ppermute | solution.py:497
  128.4 21.3 %collective-permute-start.26 = (bf16[8,48,768]{2,1,0:T(8,128)(2,1)S(1)}, bf16[8,48,768]{2,1,0:T(8,128)(2,1)S(1)}, u32[]{:S(2)}, u32[]{:S(2)}) collective-permute-start(bf16[8,48,768]{2,1,0:T(8,128)(2,1)S(1)} %get-tuple-element.275), channel_id=1, source_target_pairs={{0,16},{16,0},{1,17},{17,1},{2,18},{18,2},{3,19},{19,3},{4,20},{20... | collective-permute-start | bytes 1769480 | tf_op jit(solution)/shard_map/ppermute | solution.py:501
  130.0 19.7 %collective-permute-start.27 = (bf16[8,48,768]{2,1,0:T(8,128)(2,1)S(1)}, bf16[8,48,768]{2,1,0:T(8,128)(2,1)S(1)}, u32[]{:S(2)}, u32[]{:S(2)}) collective-permute-start(bf16[8,48,768]{2,1,0:T(8,128)(2,1)S(1)} %get-tuple-element.276), channel_id=1, source_target_pairs={{0,2},{1,3},{2,0},{3,1},{4,6},{5,7},{6,4},{7,5},{8,10},{9,11},{10,... | collective-permute-start | bytes 1769480 | tf_op jit(solution)/shard_map/ppermute | solution.py:497
  151.4 10.6 %collective-permute-start.30 = (bf16[2,8,48,768]{3,2,1,0:T(8,128)(2,1)S(1)}, bf16[2,8,48,768]{3,2,1,0:T(8,128)(2,1)S(1)}, u32[]{:S(2)}, u32[]{:S(2)}) collective-permute-start(bf16[2,8,48,768]{3,2,1,0:T(8,128)(2,1)S(1)} %copy-done.28), channel_id=1, source_target_pairs={{0,1},{1,0},{2,3},{3,2},{4,5},{5,4},{6,7},{7,6},{8,9},{9,8},{10,11... | collective-permute-start | bytes 3538952 | tf_op jit(solution)/shard_map/ppermute | solution.py:497
  151.7 10.3 %collective-permute-start.31 = (bf16[2,8,48,768]{3,2,1,0:T(8,128)(2,1)S(1)}, bf16[2,8,48,768]{3,2,1,0:T(8,128)(2,1)S(1)}, u32[]{:S(2)}, u32[]{:S(2)}) collective-permute-start(bf16[2,8,48,768]{3,2,1,0:T(8,128)(2,1)S(1)} %copy-done.27), channel_id=1, source_target_pairs={{0,1},{1,0},{2,3},{3,2},{4,5},{5,4},{6,7},{7,6},{8,9},{9,8},{10,11... | collective-permute-start | bytes 3538952 | tf_op jit(solution)/shard_map/ppermute | solution.py:497
  151.9 10.0 %collective-permute-start.28 = (bf16[4,48,768]{2,1,0:T(8,128)(2,1)S(1)}, bf16[4,48,768]{2,1,0:T(8,128)(2,1)S(1)}, u32[]{:S(2)}, u32[]{:S(2)}) collective-permute-start(bf16[4,48,768]{2,1,0:T(8,128)(2,1)S(1)} %get-tuple-element.289), channel_id=1, source_target_pairs={{0,2},{1,3},{2,0},{3,1},{4,6},{5,7},{6,4},{7,5},{8,10},{9,11},{10,... | collective-permute-start | bytes 884744 | tf_op jit(solution)/shard_map/ppermute | solution.py:497
  151.9 10.0 %collective-permute-start.29 = (bf16[4,48,768]{2,1,0:T(8,128)(2,1)S(1)}, bf16[4,48,768]{2,1,0:T(8,128)(2,1)S(1)}, u32[]{:S(2)}, u32[]{:S(2)}) collective-permute-start(bf16[4,48,768]{2,1,0:T(8,128)(2,1)S(1)} %get-tuple-element.290), channel_id=1, source_target_pairs={{0,16},{16,0},{1,17},{17,1},{2,18},{18,2},{3,19},{19,3},{4,20},{20... | collective-permute-start | bytes 884744 | tf_op jit(solution)/shard_map/ppermute | solution.py:501
  162.0 25.6 %slice-start = ((s8[4718592]{0:T(1024)(128)(4,1)}), s8[4194304]{0:T(1024)(128)(4,1)S(1)}, s32[]{:S(2)}) async-start(s8[4718592]{0:T(1024)(128)(4,1)} %bitcast.36), calls=%async_computation.1 | async-start | bytes 8388608
  164.1 23.5 %slice-start.1 = ((s8[4718592]{0:T(1024)(128)(4,1)}), s8[524288]{0:T(1024)(128)(4,1)S(1)}, s32[]{:S(2)}) async-start(s8[4718592]{0:T(1024)(128)(4,1)} %bitcast.36), calls=%async_computation.2 | async-start | bytes 1048576
  164.1 17.7 %collective-permute-start.35 = (bf16[8,48,768]{2,1,0:T(8,128)(2,1)S(1)}, bf16[8,48,768]{2,1,0:T(8,128)(2,1)S(1)}, u32[]{:S(2)}, u32[]{:S(2)}) collective-permute-start(bf16[8,48,768]{2,1,0:T(8,128)(2,1)S(1)} %get-tuple-element.307), channel_id=1, source_target_pairs={{0,16},{16,0},{1,17},{17,1},{2,18},{18,2},{3,19},{19,3},{4,20},{20... | collective-permute-start | bytes 1769480 | tf_op jit(solution)/shard_map/ppermute | solution.py:501
  166.1 15.7 %collective-permute-start.36 = (bf16[8,48,768]{2,1,0:T(8,128)(2,1)S(1)}, bf16[8,48,768]{2,1,0:T(8,128)(2,1)S(1)}, u32[]{:S(2)}, u32[]{:S(2)}) collective-permute-start(bf16[8,48,768]{2,1,0:T(8,128)(2,1)S(1)} %get-tuple-element.308), channel_id=1, source_target_pairs={{0,2},{1,3},{2,0},{3,1},{4,6},{5,7},{6,4},{7,5},{8,10},{9,11},{10,... | collective-permute-start | bytes 1769480 | tf_op jit(solution)/shard_map/ppermute | solution.py:497
  168.1 12.8 %collective-permute-start.32 = (bf16[2,48,768]{2,1,0:T(8,128)(2,1)S(1)}, bf16[2,48,768]{2,1,0:T(8,128)(2,1)S(1)}, u32[]{:S(2)}, u32[]{:S(2)}) collective-permute-start(bf16[2,48,768]{2,1,0:T(8,128)(2,1)S(1)} %get-tuple-element.304), channel_id=1, source_target_pairs={{0,4},{1,5},{2,6},{3,7},{4,0},{5,1},{6,2},{7,3},{8,12},{9,13},{10,... | collective-permute-start | bytes 442376 | tf_op jit(solution)/shard_map/ppermute | solution.py:497
  168.1 13.7 %collective-permute-start.33 = (bf16[2,48,768]{2,1,0:T(8,128)(2,1)S(1)}, bf16[2,48,768]{2,1,0:T(8,128)(2,1)S(1)}, u32[]{:S(2)}, u32[]{:S(2)}) collective-permute-start(bf16[2,48,768]{2,1,0:T(8,128)(2,1)S(1)} %get-tuple-element.305), channel_id=1, source_target_pairs={{0,8},{1,9},{2,10},{3,11},{4,12},{5,13},{6,14},{7,15},{8,0},{9,1},... | collective-permute-start | bytes 442376 | tf_op jit(solution)/shard_map/ppermute | solution.py:497
  171.0 10.8 %collective-permute-start.34 = (bf16[2,48,768]{2,1,0:T(8,128)(2,1)S(1)}, bf16[2,48,768]{2,1,0:T(8,128)(2,1)S(1)}, u32[]{:S(2)}, u32[]{:S(2)}) collective-permute-start(bf16[2,48,768]{2,1,0:T(8,128)(2,1)S(1)} %get-tuple-element.306), channel_id=1, source_target_pairs={{0,12},{1,13},{2,14},{3,15},{4,8},{5,9},{6,10},{7,11},{8,4},{9,5},... | collective-permute-start | bytes 442376 | tf_op jit(solution)/shard_map/ppermute | solution.py:497
  183.5 15.9 %collective-permute-start.39 = (bf16[2,8,48,768]{3,2,1,0:T(8,128)(2,1)S(1)}, bf16[2,8,48,768]{3,2,1,0:T(8,128)(2,1)S(1)}, u32[]{:S(2)}, u32[]{:S(2)}) collective-permute-start(bf16[2,8,48,768]{3,2,1,0:T(8,128)(2,1)S(1)} %copy-done.26), channel_id=1, source_target_pairs={{0,1},{1,0},{2,3},{3,2},{4,5},{5,4},{6,7},{7,6},{8,9},{9,8},{10,11... | collective-permute-start | bytes 3538952 | tf_op jit(solution)/shard_map/ppermute | solution.py:497
  183.8 15.6 %collective-permute-start.40 = (bf16[2,8,48,768]{3,2,1,0:T(8,128)(2,1)S(1)}, bf16[2,8,48,768]{3,2,1,0:T(8,128)(2,1)S(1)}, u32[]{:S(2)}, u32[]{:S(2)}) collective-permute-start(bf16[2,8,48,768]{3,2,1,0:T(8,128)(2,1)S(1)} %copy-done.25), channel_id=1, source_target_pairs={{0,1},{1,0},{2,3},{3,2},{4,5},{5,4},{6,7},{7,6},{8,9},{9,8},{10,11... | collective-permute-start | bytes 3538952 | tf_op jit(solution)/shard_map/ppermute | solution.py:497
  184.1 15.3 %collective-permute-start.41 = (bf16[2,48,768]{2,1,0:T(8,128)(2,1)S(1)}, bf16[2,48,768]{2,1,0:T(8,128)(2,1)S(1)}, u32[]{:S(2)}, u32[]{:S(2)}) collective-permute-start(bf16[2,48,768]{2,1,0:T(8,128)(2,1)S(1)} %get-tuple-element.328.a_mine), channel_id=1, source_target_pairs={{0,16},{16,0},{1,17},{17,1},{2,18},{18,2},{3,19},{19,3},{4,20},{20... | collective-permute-start | bytes 442376 | tf_op jit(solution)/shard_map/ppermute | solution.py:501
  184.4 14.9 %collective-permute-start.37 = (bf16[4,48,768]{2,1,0:T(8,128)(2,1)S(1)}, bf16[4,48,768]{2,1,0:T(8,128)(2,1)S(1)}, u32[]{:S(2)}, u32[]{:S(2)}) collective-permute-start(bf16[4,48,768]{2,1,0:T(8,128)(2,1)S(1)} %get-tuple-element.324), channel_id=1, source_target_pairs={{0,2},{1,3},{2,0},{3,1},{4,6},{5,7},{6,4},{7,5},{8,10},{9,11},{10,... | collective-permute-start | bytes 884744 | tf_op jit(solution)/shard_map/ppermute | solution.py:497
  185.9 13.5 %collective-permute-start.38 = (bf16[4,48,768]{2,1,0:T(8,128)(2,1)S(1)}, bf16[4,48,768]{2,1,0:T(8,128)(2,1)S(1)}, u32[]{:S(2)}, u32[]{:S(2)}) collective-permute-start(bf16[4,48,768]{2,1,0:T(8,128)(2,1)S(1)} %get-tuple-element.325), channel_id=1, source_target_pairs={{0,16},{16,0},{1,17},{17,1},{2,18},{18,2},{3,19},{19,3},{4,20},{20... | collective-permute-start | bytes 884744 | tf_op jit(solution)/shard_map/ppermute | solution.py:501
  203.5 16.3 %collective-permute-start.42 = (bf16[8,48,768]{2,1,0:T(8,128)(2,1)S(1)}, bf16[8,48,768]{2,1,0:T(8,128)(2,1)S(1)}, u32[]{:S(2)}, u32[]{:S(2)}) collective-permute-start(bf16[8,48,768]{2,1,0:T(8,128)(2,1)S(1)} %get-tuple-element.348), channel_id=1, source_target_pairs={{0,16},{16,0},{1,17},{17,1},{2,18},{18,2},{3,19},{19,3},{4,20},{20... | collective-permute-start | bytes 1769480 | tf_op jit(solution)/shard_map/ppermute | solution.py:501
  203.9 15.8 %collective-permute-start.43 = (bf16[8,48,768]{2,1,0:T(8,128)(2,1)S(1)}, bf16[8,48,768]{2,1,0:T(8,128)(2,1)S(1)}, u32[]{:S(2)}, u32[]{:S(2)}) collective-permute-start(bf16[8,48,768]{2,1,0:T(8,128)(2,1)S(1)} %get-tuple-element.349), channel_id=1, source_target_pairs={{0,2},{1,3},{2,0},{3,1},{4,6},{5,7},{6,4},{7,5},{8,10},{9,11},{10,... | collective-permute-start | bytes 1769480 | tf_op jit(solution)/shard_map/ppermute | solution.py:497
  204.5 12.7 %collective-permute-start.44 = (bf16[2,48,768]{2,1,0:T(8,128)(2,1)S(1)}, bf16[2,48,768]{2,1,0:T(8,128)(2,1)S(1)}, u32[]{:S(2)}, u32[]{:S(2)}) collective-permute-start(bf16[2,48,768]{2,1,0:T(8,128)(2,1)S(1)} %get-tuple-element.350), channel_id=1, source_target_pairs={{0,4},{1,5},{2,6},{3,7},{4,0},{5,1},{6,2},{7,3},{8,12},{9,13},{10,... | collective-permute-start | bytes 442376 | tf_op jit(solution)/shard_map/ppermute | solution.py:497
  206.6 13.1 %collective-permute-start.45 = (bf16[2,48,768]{2,1,0:T(8,128)(2,1)S(1)}, bf16[2,48,768]{2,1,0:T(8,128)(2,1)S(1)}, u32[]{:S(2)}, u32[]{:S(2)}) collective-permute-start(bf16[2,48,768]{2,1,0:T(8,128)(2,1)S(1)} %get-tuple-element.351), channel_id=1, source_target_pairs={{0,8},{1,9},{2,10},{3,11},{4,12},{5,13},{6,14},{7,15},{8,0},{9,1},... | collective-permute-start | bytes 442376 | tf_op jit(solution)/shard_map/ppermute | solution.py:497
  207.7 12.0 %collective-permute-start.46 = (bf16[2,48,768]{2,1,0:T(8,128)(2,1)S(1)}, bf16[2,48,768]{2,1,0:T(8,128)(2,1)S(1)}, u32[]{:S(2)}, u32[]{:S(2)}) collective-permute-start(bf16[2,48,768]{2,1,0:T(8,128)(2,1)S(1)} %get-tuple-element.352), channel_id=1, source_target_pairs={{0,12},{1,13},{2,14},{3,15},{4,8},{5,9},{6,10},{7,11},{8,4},{9,5},... | collective-permute-start | bytes 442376 | tf_op jit(solution)/shard_map/ppermute | solution.py:497
  223.4 16.9 %all-to-all-start = ((f32[16,8,384]{2,1,0:T(8,128)}), f32[16,8,384]{2,1,0:T(8,128)S(1)}, u32[]{:S(2)}, u32[]{:S(2)}) async-start(f32[16,8,384]{2,1,0:T(8,128)} %get-tuple-element.368), calls=%async_computation | async-start | bytes 393216 | tf_op jit(solution)/shard_map/all_to_all | solution.py:1043
  228.7 11.6 %collective-permute-start.48 = (bf16[4,48,768]{2,1,0:T(8,128)(2,1)}, bf16[4,48,768]{2,1,0:T(8,128)(2,1)S(1)}, u32[]{:S(2)}, u32[]{:S(2)}) collective-permute-start(bf16[4,48,768]{2,1,0:T(8,128)(2,1)} %get-tuple-element.366), channel_id=1, source_target_pairs={{0,2},{1,3},{2,0},{3,1},{4,6},{5,7},{6,4},{7,5},{8,10},{9,11},{10,... | collective-permute-start | bytes 884744 | tf_op jit(solution)/shard_map/ppermute | solution.py:497
  230.6 9.6 %collective-permute-start.49 = (bf16[4,48,768]{2,1,0:T(8,128)(2,1)}, bf16[4,48,768]{2,1,0:T(8,128)(2,1)S(1)}, u32[]{:S(2)}, u32[]{:S(2)}) collective-permute-start(bf16[4,48,768]{2,1,0:T(8,128)(2,1)} %copy-done.17), channel_id=1, source_target_pairs={{0,16},{16,0},{1,17},{17,1},{2,18},{18,2},{3,19},{19,3},{4,20},{20... | collective-permute-start | bytes 884744 | tf_op jit(solution)/shard_map/ppermute | solution.py:501
  241.9 6.5 %collective-permute-start.54 = (f32[8,384]{1,0:T(8,128)S(1)}, f32[8,384]{1,0:T(8,128)S(1)}, u32[]{:S(2)}, u32[]{:S(2)}) collective-permute-start(f32[8,384]{1,0:T(8,128)S(1)} %get-tuple-element.376), channel_id=1, source_target_pairs={{0,16},{16,0},{1,17},{17,1},{2,18},{18,2},{3,19},{19,3},{4,20},{20... | collective-permute-start | bytes 36872 | tf_op jit(solution)/shard_map/ppermute | solution.py:501
  243.6 17.6 %collective-permute-start.47 = (bf16[2,48,768]{2,1,0:T(8,128)(2,1)S(1)}, bf16[2,48,768]{2,1,0:T(8,128)(2,1)S(1)}, u32[]{:S(2)}, u32[]{:S(2)}) collective-permute-start(bf16[2,48,768]{2,1,0:T(8,128)(2,1)S(1)} %copy-done.12), channel_id=1, source_target_pairs={{0,16},{16,0},{1,17},{17,1},{2,18},{18,2},{3,19},{19,3},{4,20},{20... | collective-permute-start | bytes 442376 | tf_op jit(solution)/shard_map/ppermute | solution.py:501
  244.0 6.9 %collective-permute-start.50 = (bf16[2,48,768]{2,1,0:T(8,128)(2,1)S(1)}, bf16[2,48,768]{2,1,0:T(8,128)(2,1)S(1)}, u32[]{:S(2)}, u32[]{:S(2)}) collective-permute-start(bf16[2,48,768]{2,1,0:T(8,128)(2,1)S(1)} %get-tuple-element.370), channel_id=1, source_target_pairs={{0,4},{1,5},{2,6},{3,7},{4,0},{5,1},{6,2},{7,3},{8,12},{9,13},{10,... | collective-permute-start | bytes 442376 | tf_op jit(solution)/shard_map/ppermute | solution.py:497
  245.5 13.4 %collective-permute-start.51 = (bf16[2,48,768]{2,1,0:T(8,128)(2,1)S(1)}, bf16[2,48,768]{2,1,0:T(8,128)(2,1)S(1)}, u32[]{:S(2)}, u32[]{:S(2)}) collective-permute-start(bf16[2,48,768]{2,1,0:T(8,128)(2,1)S(1)} %get-tuple-element.371), channel_id=1, source_target_pairs={{0,8},{1,9},{2,10},{3,11},{4,12},{5,13},{6,14},{7,15},{8,0},{9,1},... | collective-permute-start | bytes 442376 | tf_op jit(solution)/shard_map/ppermute | solution.py:497
  247.8 11.0 %collective-permute-start.52 = (bf16[2,48,768]{2,1,0:T(8,128)(2,1)S(1)}, bf16[2,48,768]{2,1,0:T(8,128)(2,1)S(1)}, u32[]{:S(2)}, u32[]{:S(2)}) collective-permute-start(bf16[2,48,768]{2,1,0:T(8,128)(2,1)S(1)} %get-tuple-element.372), channel_id=1, source_target_pairs={{0,12},{1,13},{2,14},{3,15},{4,8},{5,9},{6,10},{7,11},{8,4},{9,5},... | collective-permute-start | bytes 442376 | tf_op jit(solution)/shard_map/ppermute | solution.py:497
  258.9 5.2 %collective-permute-start.53 = (bf16[2,48,768]{2,1,0:T(8,128)(2,1)S(1)}, bf16[2,48,768]{2,1,0:T(8,128)(2,1)S(1)}, u32[]{:S(2)}, u32[]{:S(2)}) collective-permute-start(bf16[2,48,768]{2,1,0:T(8,128)(2,1)S(1)} %sums_8.1.u_mine), channel_id=1, source_target_pairs={{0,16},{16,0},{1,17},{17,1},{2,18},{18,2},{3,19},{19,3},{4,20},{20... | collective-permute-start | bytes 442376 | tf_op jit(solution)/shard_map/ppermute | solution.py:501
  (25 other events, 112.2 us)

commit v4 on v3

--- a/solution.py
+++ b/solution.py
@@ -305,7 +305,7 @@
     if n_p:
         act, gp, w = refs[-6:-3]
         load(scal, refs[3 : 3 + n_p], w, sem)
-        for t in range(bias.shape[0]):
+        for t in range(count):
             whole_wait(w.at[t], sem.at[t])()
     else:
         act, gp = refs[-5:-3]
@@ -331,6 +331,9 @@
         finish(2 * i + 1, odd[...])
 
     loop(count * per // 2, step)
+    if n_p:
+        for t in range(count, bias.shape[0]):
+            whole_wait(w.at[t], sem.at[t])()
 
 
 def up_call(first, count, scal, xn, bias, before, pieces, load):
@@ -349,40 +352,44 @@
     )
 
 
-def down_grad_kernel(store, scal, act, cot, *refs):
-    *g_refs, g, sem = refs
+def down_grad_kernel(load, store, n_p, scal, act, cot, *refs):
+    w, *g_refs, g, wsem, sem = refs[n_p:]
     tiles, tokens, width = act.shape
+    load(scal, refs[:n_p], w, wsem)
 
     def grad(t):
         g[tile_of(t, width), :] = dot_tn(act[t], cot[...]).astype(BF16)
 
     loop(tiles, grad)
-    store(scal, g, g_refs, sem)()
-
-
-def down_grad_call(scal, act, cot, store, g_shapes):
+    done = store(scal, g, g_refs, sem)
+    for t in range(tiles):
+        wait_tile(w, wsem, t, width)
+    done()
+
+
+def down_grad_call(scal, act, cot, pieces, load, store, g_shapes):
     tiles, tokens, width = act.shape
     return call(
-        functools.partial(down_grad_kernel, store),
+        functools.partial(down_grad_kernel, load, store, len(pieces)),
         "down_grad",
         (scal, act, cot),
-        [],
-        [],
+        pieces,
+        [kept((tiles * width, width))],
         g_shapes,
-        [pltpu.VMEM((tiles * width, width), BF16), pltpu.SemaphoreType.DMA((len(g_shapes),))],
+        [
+            pltpu.VMEM((tiles * width, width), BF16),
+            pltpu.SemaphoreType.DMA((tiles,)),
+            pltpu.SemaphoreType.DMA((len(g_shapes),)),
+        ],
         2 * tiles * tokens * width * width,
     )
 
 
-def dpre_kernel(load, n_p, *refs):
-    scal, cot, gp = refs[:3]
-    dpre, sums, w, sem = refs[3 + n_p :]
+def dpre_kernel(scal, cot, gp, w, dpre, sums):
     tiles, tokens, width = gp.shape
-    load(scal, refs[3 : 3 + n_p], w, sem)
     ones = jnp.ones((8, tokens), BF16)
 
     def down(t):
-        wait_tile(w, sem, t, width)
         dpre[t] = (dot_nt(cot[...], w[tile_of(t, width), :]) * gp[t].astype(F32)).astype(BF16)
 
     loop(tiles, down)
@@ -390,16 +397,16 @@
         sums[t : t + 1, :] = dot_nn(ones, dpre[t])[0:1]
 
 
-def dpre_call(scal, cot, gp, pieces, load):
+def dpre_call(scal, cot, gp, w):
     tiles, tokens, width = gp.shape
     return call(
-        functools.partial(dpre_kernel, load, len(pieces)),
+        dpre_kernel,
         "dpre",
-        (scal, cot, gp),
-        pieces,
-        [kept(gp.shape), kept((8, width), F32), kept((tiles * width, width))],
-        [],
-        [pltpu.SemaphoreType.DMA((tiles,))],
+        (scal, cot, gp, w),
+        [],
+        [kept(gp.shape), kept((8, width), F32)],
+        [],
+        [],
         2 * tiles * tokens * width * width,
         alias={2: 0},
     )
@@ -544,12 +551,14 @@
     return fn, [], values, [kept((len(values) * values[0].shape[0], *values[0].shape[1:]))]
 
 
-def mix(name, jobs):
+def mix(name, jobs, scal=None):
+    extra = [] if scal is None else [scal]
     held = [v for job in jobs for v in job[1]]
     near = [v for job in jobs for v in job[2]]
     outs = [o for job in jobs for o in job[3]]
 
     def kernel(*refs):
+        last, refs = refs[: len(extra)], refs[len(extra) :]
         at = len(near) + len(held)
         scratch = refs[at + len(outs) :]
         copies = [
@@ -563,7 +572,7 @@
                 copies[h + i].wait()
             fn(
                 scratch[h : h + len(job_h)],
-                refs[n : n + len(job_n)],
+                (*refs[n : n + len(job_n)], *last),
                 refs[at + o : at + o + len(job_o)],
             )
             h, n, o = h + len(job_h), n + len(job_n), o + len(job_o)
@@ -572,13 +581,14 @@
         kernel,
         name=name,
         out_shape=outs,
-        in_specs=[VMEM] * len(near) + [HBM] * len(held),
+        in_specs=[SMEM] * len(extra) + [VMEM] * len(near) + [HBM] * len(held),
         out_specs=[VMEM] * len(outs),
         scratch_shapes=[pltpu.VMEM(v.shape, v.dtype) for v in held]
         + [pltpu.SemaphoreType.DMA((max(len(held), 1),))],
         compiler_params=pltpu.CompilerParams(vmem_limit_bytes=8 << 20),
         cost_estimate=pl.CostEstimate(flops=1 << 20, bytes_accessed=1 << 20, transcendentals=0),
     )(
+        *extra,
         *[pltpu.with_memory_space_constraint(v, pltpu.VMEM) for v in near],
         *[pltpu.with_memory_space_constraint(v, pltpu.HBM) for v in held],
     )
@@ -611,33 +621,52 @@
         own = lax.broadcasted_iota(jnp.int32, (wide, width), 0) * per % width
         flat = jnp.where((col >= own) & (col < own + per), flat, 0.0)
         pick = lax.broadcasted_iota(jnp.int32, (width, per), 0) % per
-        pick = (pick == lax.broadcasted_iota(jnp.int32, (width, per), 1)).astype(F32)
-        return lax.dot_general(
-            flat, pick, (((1,), (0,)), ((), ())), precision=lax.Precision.HIGHEST, preferred_element_type=F32
-        )
+        pick = (pick == lax.broadcasted_iota(jnp.int32, (width, per), 1)).astype(BF16)
+        got = jnp.zeros((wide, per), F32)
+        for _ in range(3):
+            high = flat.astype(BF16)
+            flat = flat - high.astype(F32)
+            got += dot_nn(high, pick)
+        return got
 
     def fn(held, near, outs):
-        a, d, x = near
+        a, d, x, scal = near
         tiles = 4
         at = 0
-        outs[0][...] = jnp.zeros_like(outs[0])
         for got in (
             spread([x[0]], rows),
             spread([a[0], a[1]], 2 * rows),
             spread([d[t] for t in range(tiles)], tiles * rows),
             spread([a[2]], rows),
         ):
-            outs[0][:, 0, at : at + got.shape[1]] = got
+            outs[4][:, at : at + got.shape[1]] = got
             at += got.shape[1]
-
-    return fn, [], [sums_a, sums_d, sums_x], [kept((wide, 8, 8 * rows), F32)]
-
-
-def vector_sum_job(value):
+        for side in range(2):
+            for core in range(2):
+                out = outs[side * 2 + core]
+                out[...] = jnp.zeros_like(out)
+                for z in range(wide // 4):
+                    dev = (z * 2 + (scal[2] ^ side)) * 2 + (scal[3] ^ core)
+                    out[z : z + 1, :] = outs[4][pl.ds(dev, 1), :]
+
+    return fn, [], [sums_a, sums_d, sums_x], [kept((8, 8 * rows), F32)] * 4 + [kept((wide, 8 * rows), F32)]
+
+
+def add_job(values):
     def fn(held, near, outs):
-        outs[0][...] = jnp.sum(near[0][...], axis=0)
-
-    return fn, [], [value], [kept(value.shape[1:], F32)]
+        outs[0][...] = sum(near[i][...] for i in range(len(values)))
+
+    return fn, [], list(values), [kept(values[0].shape, F32)]
+
+
+def vector_z_job(mine, other):
+    def fn(held, near, outs):
+        outs[4][...] = near[0][...] + near[1][...]
+        for k in range(4):
+            outs[k][...] = jnp.zeros_like(outs[k])
+            outs[k][0:1, :] = outs[4][pl.ds(near[2][1] ^ k, 1), :]
+
+    return fn, [], [mine, other], [kept(mine.shape, F32)] * 5
 
 
 def sum1_job(keep1, got1):
@@ -671,33 +700,41 @@
 
 def sum4_job(own, got):
     def fn(held, near, outs):
-        outs[0][...] = total(*[v[...] for v in near]).astype(BF16)
+        outs[0][...] = total(*[near[i][...] for i in range(1 + len(got))]).astype(BF16)
 
     return fn, [], [own, *got], [kept(own.shape)]
 
 
-def place_kernel(scal, a_mine, a_other, d_mine, d_other, u_mine, u_other, joined, out, down):
+def place_kernel(scal, a_mine, a_other, d_mine, d_other, u_mine, joined_ref, out, down, joined, sem):
     _, rows, width = a_mine.shape
 
     def place(half, a, d, u):
         for p in range(2):
             block = half * 2 + p
             down[pl.ds(block * rows, rows), :] = d[p].astype(F32)
-            joined[:, (3 + block) * width : (4 + block) * width] = u[p].astype(F32)
+            if u is not None:
+                joined[3 + p] = u[p].astype(F32)
+                send(joined.at[3 + p], 3 + block)
             if block < 3:
-                joined[:, block * width : (block + 1) * width] = a[p].astype(F32)
+                joined[block] = a[p].astype(F32)
+                send(joined.at[block], block)
             else:
                 out[...] = a[p].astype(F32)
+
+    def send(src, block):
+        pltpu.make_async_copy(src, joined_ref.at[:, block * width : (block + 1) * width], sem).start()
 
     @pl.when(scal[0] == 0)
     def _():
         place(0, a_mine, d_mine, u_mine)
-        place(1, a_other, d_other, u_other)
+        place(1, a_other, d_other, None)
 
     @pl.when(scal[0] != 0)
     def _():
         place(1, a_mine, d_mine, u_mine)
-        place(0, a_other, d_other, u_other)
+        place(0, a_other, d_other, None)
+
+    whole_wait(joined, sem)()
 
 
 def place_call(scal, parts):
@@ -706,9 +743,31 @@
         place_kernel,
         name="place",
         out_shape=[sds((rows, 7 * width), F32), sds((rows, width), F32), sds((4 * rows, width), F32)],
-        in_specs=[SMEM] + [VMEM] * 6,
-        out_specs=[VMEM] * 3,
+        in_specs=[SMEM] + [VMEM] * 5,
+        out_specs=[HBM, VMEM, VMEM],
+        scratch_shapes=[pltpu.VMEM((5, rows, width), F32), pltpu.SemaphoreType.DMA],
     )(scal, *[pltpu.with_memory_space_constraint(v, pltpu.VMEM) for v in parts])
+
+
+def place_last_kernel(scal, placed, other, joined_ref, wide, sem):
+    _, rows, width = other.shape
+    for p in range(2):
+        wide[p] = other[p].astype(F32)
+        at = pl.multiple_of((3 + (1 - scal[0]) * 2 + p) * width, 128)
+        pltpu.make_async_copy(wide.at[p], joined_ref.at[:, pl.ds(at, width)], sem).start()
+    whole_wait(wide, sem)()
+
+
+def place_last_call(scal, placed, other):
+    return pl.pallas_call(
+        place_last_kernel,
+        name="place_last",
+        out_shape=sds(placed.shape, F32),
+        in_specs=[SMEM, HBM, VMEM],
+        out_specs=HBM,
+        scratch_shapes=[pltpu.VMEM(other.shape, F32), pltpu.SemaphoreType.DMA],
+        input_output_aliases={1: 0},
+    )(scal, placed, pltpu.with_memory_space_constraint(other, pltpu.VMEM))
 
 
 def whole_wait(ref, sem):
@@ -931,8 +990,10 @@
         sums_a, *g_attn = attn_grad_call(scal, xn, o, d, cot, store_whole, square * 4)
         act, gp, wu = up_call(0, tiles // 2, scal, xn, b_mlp, (), up_w, load_whole_blocks)
         act, gp = up_call(tiles // 2, tiles - tiles // 2, scal, xn, b_mlp, (act, gp, wu), [], None)
-        g_down = down_grad_call(scal, act, cot, store_whole, [sds((tiles * width, width))])
-        dpre, sums_d, wd = dpre_call(scal, cot, gp, down_w, load_whole_rows)
+        wd, *g_down = down_grad_call(
+            scal, act, cot, down_w, load_whole_rows, store_whole, [sds((tiles * width, width))]
+        )
+        dpre, sums_d = dpre_call(scal, cot, gp, wd)
         g_up = up_grad_call(scal, xn, dpre, store_whole, square * tiles)
         sums_x, d_x = input_grad_call(scal, x, cot, d, dpre, vec, wa, wu)
         out = out_call(scal, x, o, act, vec, wa, wd)
@@ -963,11 +1024,11 @@
         ((joined,),) = mix("join_a", [join_job([own[i] for i in (0, 1, 2, 4, 5, 6)])])
         joined, c1, c3 = swap(joined, 1), swap(c_half, 4), swap(c_half, 12)
         second, joined, c1, c3 = lax.optimization_barrier((second, joined, c1, c3))
+        vec, b_mlp = vectors_call(scal, [za, first[0], joined], rows)
         own = pieces_of(za, zb, first, second)
         attn_w = [*own, joined, swap(second[0], 1), swap(second[1], 1)]
         cza, czb = [jnp.stack([t[i] for t in (c_half, c1, c2, c3)]) for i in range(2)]
-        x_p, attn_w, cza, czb = lax.optimization_barrier((x, attn_w, cza, czb))
-        vec, b_mlp = vectors_call(scal, [attn_w[0], attn_w[1], attn_w[8]], rows)
+        x_p, attn_w, cza, czb, vec, b_mlp = lax.optimization_barrier((x, attn_w, cza, czb, vec, b_mlp))
         c_first = gather_first(cza, czb)
         xn, q, k, v, da, wa = project_call(scal, x_p, cot, vec, attn_w, load_columns)
         part = core_call(0, scal, q, k, v, da)
@@ -997,14 +1058,16 @@
         act, sa, sb = lax.optimization_barrier((act, sa, sb))
         a_xy = swap_y(sa), swap(sb, 2)
         act, gp = up_call(half_tiles, half_tiles, scal, xn_u, b_mlp, (act, gp, wu), [], None)
-        gd = down_grad_call(scal, act, cot, store_with(down_source), attn_shapes)
+        wd, *gd = down_grad_call(
+            scal, act, cot, c_all, load_half(1), store_with(down_source), attn_shapes
+        )
 
         a_xy = behind(a_xy, gd)
         ((sa, sb),) = mix("sums_2", [sum2_job(ga[0], a_got0, a_xy)])
         gp, sa, sb, gd = lax.optimization_barrier((gp, sa, sb, gd))
         a_yx = swap(sa, 2), swap_y(sb)
         d_got1, d_got0 = swap(gd[3], 1), swap(gd[2], 1)
-        dpre, sums_d, wd = dpre_call(scal, cot, gp, c_all, load_half(1))
+        dpre, sums_d = dpre_call(scal, cot, gp, wd)
 
         a_yx, d_got1, d_got0 = behind((a_yx, d_got1, d_got0), dpre)
         a_t, (sa, sb) = mix("sums_3", [sum3_job(ga[0], a_got0, a_xy, a_yx), sum1_job(gd[1], d_got1)])
@@ -1022,37 +1085,35 @@
         sums_x, d_x = input_grad_call(scal, x_i, cot, d, dpre, vec, wa, wu)
 
         d_yx, u_got1, u_got0, a_other = behind((d_yx, u_got1, u_got0, a_other), d_x)
-        (sa, sb), d_t, (v_grad,) = mix(
+        (sa, sb), d_t, (*v_part, _) = mix(
             "sums_5",
             [
                 sum1_job(gu[1], u_got1),
                 sum3_job(gd[0], d_got0, d_xy, d_yx),
                 vector_job(sums_a, sums_d, sums_x, wide, rows),
             ],
+            scal,
         )
         x_o, sa, sb, d_t = lax.optimization_barrier((x, sa, sb, d_t))
         u_xy = swap_y(sa), swap(sb, 2)
         d_z = [swap(d_t[k], k << 2) for k in (1, 2, 3)]
         out = out_call(scal, x_o, o, act, vec, wa, wd)
 
-        u_xy, d_z, v_grad = behind((u_xy, d_z, v_grad), out)
+        u_xy, d_z, v_part = behind((u_xy, d_z, v_part), out)
         (sa, sb), (d_sum,) = mix("sums_6", [sum2_job(gu[0], u_got0, u_xy), sum4_job(d_t[0], d_z)])
-        sa, sb, d_sum, v_grad = lax.optimization_barrier((sa, sb, d_sum, v_grad))
+        sa, sb, d_sum, v_part = lax.optimization_barrier((sa, sb, d_sum, v_part))
         u_yx = swap(sa, 2), swap_y(sb)
-        d_other = swap_y(d_sum)
-        v_got = lax.all_to_all(v_grad.reshape(wide * 8, 8 * rows), "wide", 0, 0, tiled=True)
-        u_t, (v_sum,) = mix(
-            "sums_7",
-            [sum3_job(gu[0], u_got0, u_xy, u_yx), vector_sum_job(v_got.reshape(wide, 8, 8 * rows))],
-        )
-        v_other = swap_y(v_sum)
+        v_got = [swap(v_part[i], i) for i in (1, 2, 3)]
+        u_t, (v_sum,) = mix("sums_7", [sum3_job(gu[0], u_got0, u_xy, u_yx), add_job([v_part[0], *v_got])])
+        u_t, v_sum, d_sum = lax.optimization_barrier((u_t, v_sum, d_sum))
         u_z = [swap(u_t[k], k << 2) for k in (1, 2, 3)]
-        vg = (v_sum + v_other)[0]
-        ((u_sum,),) = mix("sums_8", [sum4_job(u_t[0], u_z)])
+        v_other, d_other = swap_y(v_sum), swap_y(d_sum)
+        (u_sum,), (*v_z, _) = mix("sums_8", [sum4_job(u_t[0], u_z), vector_z_job(v_sum, v_other)], scal)
         u_other = swap_y(u_sum)
-        grad_joined, grad_out, grad_mlp = place_call(
-            scal, [a_sum, a_other, d_sum, d_other, u_sum, u_other]
-        )
+        vg = sum([v_z[0], *[swap(v_z[k], k << 2) for k in (1, 2, 3)]])[0]
+        d_other = behind(d_other, u_sum)
+        placed, grad_out, grad_mlp = place_call(scal, [a_sum, a_other, d_sum, d_other, u_sum])
+        grad_joined = place_last_call(scal, placed, behind(u_other, grad_out))
     b_at = 3 * rows
     return (
         out.reshape(tokens.shape),

time: 267 us -> 261 us (0.978)
  waiting for transfers between devices: 72.5 us -> 63 us
    ppermute x39 -> x45, waiting for transfers between devices: 65.4 us -> 54.8 us  [swap(): return lax.ppermute(value, 'wide', [(i, i ^ mask) for i in range(16)])]
    ppermute x39 -> x45, starting transfers between devices: 41.2 us -> 48.4 us  [swap(): return lax.ppermute(value, 'wide', [(i, i ^ mask) for i in range(16)])]
    all_to_all x1 -> x0, starting transfers between devices: 5.29 us -> none  [body(): lax.all_to_all(v_grad.reshape(wide * 8, 8 * rows), 'wide', 0, 0, tiled=True)]
    pallas_call x10 -> x11, Pallas kernels: 16.4 us -> 18.4 us  [the longest x10 17 us: mix(): pl.pallas_call(kernel, name=name, out_shape=outs, in_specs=[SMEM] * len(e...]
    unnamed x66 -> x64, local copies, waits for them, and re-layouts: 5.2 us -> 6.81 us
  transfers between devices with their start and end apart: 56 -> 61, of which waited for: 16 -> 15; matrix products, arithmetic and copies ran while one was open for 2% -> 3% of each run, Pallas kernels for 36% -> 38%
where the time goes in v4:
time: 261 us; the launch traced here: 260 us
  Pallas kernels  116 us (44%)
  starting transfers between devices  64.1 us (25%)
  waiting for transfers between devices  63 us (24%)
  local copies, waits for them, and re-layouts  12.5 us (5%)
  other arithmetic  3.08 us (1%)
    pallas_call x11, Pallas kernels, call(): pl.pallas_call(kernel, name=name, out_shape=list(outs) + list(g_shapes),...  93.2 us
    ppermute x45, waiting for transfers between devices, swap(): return lax.ppermute(value, 'wide', [(i, i ^ mask) for i in range(16)])  54.8 us
    ppermute x45, starting transfers between devices, swap(): return lax.ppermute(value, 'wide', [(i, i ^ mask) for i in range(16)])  48.4 us
    pallas_call x10, Pallas kernels, mix(): pl.pallas_call(kernel, name=name, out_shape=outs, in_specs=[SMEM] * len(e...  17 us
    ppermute x16, starting transfers between devices, swap_y(): return lax.ppermute(value, 'narrow', [(0, 1), (1, 0)])  15.8 us
    ppermute x16, waiting for transfers between devices, swap_y(): return lax.ppermute(value, 'narrow', [(0, 1), (1, 0)])  8.17 us
    unnamed x64, local copies, waits for them, and re-layouts  6.81 us
  transfers between devices with their start and end apart: 61, of which 15 were waited for; matrix products, arithmetic and copies ran while one was open for 3% of the time, Pallas kernels for 38%

profile of v4, /device:TPU:0, one launch (start us, length us, event | category | flops | bytes accessed | tf_op | source)
XLA Modules:
  0.0 260.3 jit_solution(11981292494050850919)
XLA Ops:
  1.4 1.3 select_bitcast_fusion.3
  2.7 5.1 %collective-permute-start.2 = (bf16[2,56,768]{2,1,0:T(8,128)(2,1)S(1)}, bf16[2,56,768]{2,1,0:T(8,128)(2,1)S(1)}, u32[]{:S(2)}, u32[]{:S(2)}) collective-permute-start(bf16[2,56,768]{2,1,0:T(8,128)(2,1)S(1)} %pad_maximum_fusion.5), channel_id=1, source_target_pairs={{0,12},{1,13},{2,14},{3,15},{4,8},{5,9},{6,10},{7,11},{8,4},{9,5},... | collective-permute-start | bytes 516104 | tf_op jit(solution)/shard_map/ppermute | solution.py:504
  8.5 4.6 %collective-permute-done.2 = bf16[2,56,768]{2,1,0:T(8,128)(2,1)S(1)} collective-permute-done((bf16[2,56,768]{2,1,0:T(8,128)(2,1)S(1)}, bf16[2,56,768]{2,1,0:T(8,128)(2,1)S(1)}, u32[]{:S(2)}, u32[]{:S(2)}) %collective-permute-start.2) | collective-permute-done | bytes 172064 | tf_op jit(solution)/shard_map/ppermute | solution.py:504
  13.2 9.3 %collective-permute-done.1 = bf16[2,56,768]{2,1,0:T(8,128)(2,1)S(1)} collective-permute-done((bf16[2,56,768]{2,1,0:T(8,128)(2,1)S(1)}, bf16[2,56,768]{2,1,0:T(8,128)(2,1)S(1)}, u32[]{:S(2)}, u32[]{:S(2)}) %collective-permute-start.1) | collective-permute-done | bytes 172064 | tf_op jit(solution)/shard_map/ppermute | solution.py:504
  22.6 1.6 collective-permute-start.5
  24.2 1.5 collective-permute-start.3
  27.6 14.0 %collective-permute-done.7 = bf16[2,2,48,768]{3,2,1,0:T(8,128)(2,1)S(1)} collective-permute-done((bf16[2,2,48,768]{3,2,1,0:T(8,128)(2,1)}, bf16[2,2,48,768]{3,2,1,0:T(8,128)(2,1)S(1)}, u32[]{:S(2)}, u32[]{:S(2)}) %collective-permute-start.7) | collective-permute-done | bytes 294944 | tf_op jit(solution)/shard_map/ppermute | solution.py:504
  41.6 1.4 join_a.1
  43.1 1.6 collective-permute-start.12
  44.7 1.5 collective-permute-start.9
  46.2 1.5 collective-permute-start.8
  47.8 1.4 fusion.15
  49.1 1.4 stack.55.scal.refs_0_
  51.6 3.5 %collective-permute-done.12 = bf16[2,2,48,768]{3,2,1,0:T(8,128)(2,1)S(1)} collective-permute-done((bf16[2,2,48,768]{3,2,1,0:T(8,128)(2,1)}, bf16[2,2,48,768]{3,2,1,0:T(8,128)(2,1)S(1)}, u32[]{:S(2)}, u32[]{:S(2)}) %collective-permute-start.12) | collective-permute-done | bytes 294944 | tf_op jit(solution)/shard_map/ppermute | solution.py:504
  55.1 5.3 %collective-permute-done.11 = bf16[2,2,48,768]{3,2,1,0:T(8,128)(2,1)S(1)} collective-permute-done((bf16[2,2,48,768]{3,2,1,0:T(8,128)(2,1)}, bf16[2,2,48,768]{3,2,1,0:T(8,128)(2,1)S(1)}, u32[]{:S(2)}, u32[]{:S(2)}) %collective-permute-start.11) | collective-permute-done | bytes 294944 | tf_op jit(solution)/shard_map/ppermute | solution.py:504
  61.0 1.8 vectors.1
  63.1 1.5 collective-permute-start.17
  64.7 1.5 collective-permute-start.15
  67.2 8.5 %project.1 = (bf16[1024,768]{1,0:T(8,128)(2,1)S(1)}, bf16[1024,768]{1,0:T(8,128)(2,1)S(1)}, bf16[1024,768]{1,0:T(8,128)(2,1)S(1)}, bf16[1024,768]{1,0:T(8,128)(2...) custom-call(s32[10]{0:T(128)S(1)} %stack.55.scal.refs_0_, bf16[1024,768]{1,0:T(8,128)(2,1)S(1)} %bitcast.33, ...), custom_call_target="tpu_custom_call" | custom-call | flops 4831838208 | bytes 1048576 | tf_op jit(solution)/shard_map/project/pallas_call | solution.py:139
  75.7 2.2 copy-done.14
  77.9 8.3 %core.2 = (bf16[1024,768]{1,0:T(8,128)(2,1)S(1)}, bf16[3,1024,768]{2,1,0:T(8,128)(2,1)S(1)}) custom-call(s32[10]{0:T(128)S(1)} %stack.55.scal.refs_0_, bf16[1024,768]{1,0:T(8,128)(2,1)S(1)} %get-tuple-element.245.q, bf16[1024,768]{1,0:T(8,128)(2,1)S(1)} %get-tuple-element.246.k, bf16[1024,768]{1,0:T(8,128)(2,1)S(1)} %get-tuple-element.247.v, ...), custom_call_target="tpu_custom_call" | custom-call | flops 10737418240 | bytes 1048576 | tf_op jit(solution)/shard_map/core/pallas_call | solution.py:139
  86.4 6.4 %collective-permute-done.18.refs_3_.refs_8_.refs_5_ = bf16[4,2,48,768]{3,2,1,0:T(8,128)(2,1)S(1)} collective-permute-done((bf16[4,2,48,768]{3,2,1,0:T(8,128)(2,1)S(1)}, bf16[4,2,48,768]{3,2,1,0:T(8,128)(2,1)S(1)}, u32[]{:S(2)}, u32[]{:S(2)}) %collective-permute-start.18) | collective-permute-done | bytes 589856 | tf_op jit(solution)/shard_map/ppermute | solution.py:504
  93.3 1.5 collective-permute-start.20
  94.8 8.3 %core.3 = (bf16[1024,768]{1,0:T(8,128)(2,1)S(1)}, bf16[3,1024,768]{2,1,0:T(8,128)(2,1)S(1)}) custom-call(s32[10]{0:T(128)S(1)} %stack.55.scal.refs_0_, bf16[1024,768]{1,0:T(8,128)(2,1)S(1)} %get-tuple-element.245.q, bf16[1024,768]{1,0:T(8,128)(2,1)S(1)} %get-tuple-element.246.k, ...), custom_call_target="tpu_custom_call", output_to_operand_aliasing={{0}: (5, {}), {1}: (6, {})} | custom-call | flops 10737418240 | bytes 1048576 | tf_op jit(solution)/shard_map/core/pallas_call | solution.py:139
  103.2 4.2 %collective-permute-done.19.refs_2_.refs_6_.refs_3_ = bf16[4,2,48,768]{3,2,1,0:T(8,128)(2,1)S(1)} collective-permute-done((bf16[4,2,48,768]{3,2,1,0:T(8,128)(2,1)S(1)}, bf16[4,2,48,768]{3,2,1,0:T(8,128)(2,1)S(1)}, u32[]{:S(2)}, u32[]{:S(2)}) %collective-permute-start.19) | collective-permute-done | bytes 589856 | tf_op jit(solution)/shard_map/ppermute | solution.py:508
  108.5 9.0 %attn_grad.1 = (f32[8,768]{1,0:T(8,128)S(1)}, bf16[2,8,48,768]{3,2,1,0:T(8,128)(2,1)}, bf16[2,8,48,768]{3,2,1,0:T(8,128)(2,1)}, bf16[2,8,48,768]{3,2,1,0:T(8,128)(2,1)}, bf16[2,8,48,768]{3,2,1,0:T(8,128)(2,1)}) custom-call(s32[10]{0:T(128)S(1)} %stack.55.scal.refs_0_, bf16[1024,768]{1,0:T(8,128)(2,1)S(1)} %get-tuple-element.276.xn.refs_1_, ...), custom_call_target="tpu_custom_call" | custom-call | flops 4831838208 | bytes 1048576 | tf_op jit(solution)/shard_map/attn_grad/pallas_call | solution.py:139
  119.4 8.1 %up.2 = (bf16[4,1024,768]{2,1,0:T(8,128)(2,1)S(1)}, bf16[4,1024,768]{2,1,0:T(8,128)(2,1)S(1)}, bf16[4,768,768]{2,1,0:T(8,128)(2,1)S(1)}) custom-call(s32[10]{0:T(128)S(1)} %stack.55.scal.refs_0_, bf16[1024,768]{1,0:T(8,128)(2,1)S(1)} %get-tuple-element.276.xn.refs_1_, f32[4,768]{1,0:T(4,128)S(1)} %get-tuple-element.277.refs_2_, ...), custom_call_target="tpu_custom_call" | custom-call | flops 2415919104 | bytes 1048576 | tf_op jit(solution)/shard_map/up/pallas_call | solution.py:139
  127.5 1.6 sums_1.1
  129.0 1.6 collective-permute-start.26
  130.6 1.5 collective-permute-start.27
  132.1 6.0 %up.3 = (bf16[4,1024,768]{2,1,0:T(8,128)(2,1)S(1)}, bf16[4,1024,768]{2,1,0:T(8,128)(2,1)S(1)}) custom-call(s32[10]{0:T(128)S(1)} %stack.55.scal.refs_0_, bf16[1024,768]{1,0:T(8,128)(2,1)S(1)} %get-tuple-element.276.xn.refs_1_, f32[4,768]{1,0:T(4,128)S(1)} %get-tuple-element.277.refs_2_, ...), custom_call_target="tpu_custom_call", output_to_operand_aliasing={{0}: (3, {}), {1}: (4, {})} | custom-call | flops 2415919104 | bytes 1048576 | tf_op jit(solution)/shard_map/up/pallas_call | solution.py:139
  138.1 8.7 %down_grad.1 = (bf16[3072,768]{1,0:T(8,128)(2,1)S(1)}, bf16[2,8,48,768]{3,2,1,0:T(8,128)(2,1)}, bf16[2,8,48,768]{3,2,1,0:T(8,128)(2,1)}, bf16[2,8,48,768]{3,2,1,0:T(8,128)(2,1)}, bf16[2,8,48,768]{3,2,1,0:T(8,128)(2,1)}) custom-call(s32[10]{0:T(128)S(1)} %stack.55.scal.refs_0_, bf16[4,1024,768]{2,1,0:T(8,128)(2,1)S(1)} %get-tuple-element.303.act, ...), custom_call_target="tpu_custom_call" | custom-call | flops 4831838208 | bytes 1048576 | tf_op jit(solution)/shard_map/down_grad/pallas_call | solution.py:139
  146.9 1.6 sums_2.1
  150.3 7.5 %dpre.1 = (bf16[4,1024,768]{2,1,0:T(8,128)(2,1)S(1)}, f32[8,768]{1,0:T(8,128)S(1)}) custom-call(s32[10]{0:T(128)S(1)} %stack.55.scal.refs_0_, bf16[1024,768]{1,0:T(8,128)(2,1)S(1)} %bitcast.31, bf16[4,1024,768]{2,1,0:T(8,128)(2,1)S(1)} %get-tuple-element.313.gp, bf16[3072,768]{1,0:T(8,128)(2,1)S(1)} %get-tuple-element.314.w.wd), custom_call_target="tpu_custom_call", output_to_operand_aliasing={{0}: (2, {})} | custom-call | flops 4831838208 | bytes 1048576 | tf_op jit(solution)/shard_map/dpre/pallas_call | solution.py:139
  158.7 2.1 sums_3.1
  161.5 1.3 collective-permute-start.36
  162.9 3.0 %collective-permute-start.32 = (bf16[2,48,768]{2,1,0:T(8,128)(2,1)S(1)}, bf16[2,48,768]{2,1,0:T(8,128)(2,1)S(1)}, u32[]{:S(2)}, u32[]{:S(2)}) collective-permute-start(bf16[2,48,768]{2,1,0:T(8,128)(2,1)S(1)} %get-tuple-element.331), channel_id=1, source_target_pairs={{0,4},{1,5},{2,6},{3,7},{4,0},{5,1},{6,2},{7,3},{8,12},{9,13},{10,... | collective-permute-start | bytes 442376 | tf_op jit(solution)/shard_map/ppermute | solution.py:504
  165.9 2.6 %collective-permute-start.33 = (bf16[2,48,768]{2,1,0:T(8,128)(2,1)S(1)}, bf16[2,48,768]{2,1,0:T(8,128)(2,1)S(1)}, u32[]{:S(2)}, u32[]{:S(2)}) collective-permute-start(bf16[2,48,768]{2,1,0:T(8,128)(2,1)S(1)} %get-tuple-element.332), channel_id=1, source_target_pairs={{0,8},{1,9},{2,10},{3,11},{4,12},{5,13},{6,14},{7,15},{8,0},{9,1},... | collective-permute-start | bytes 442376 | tf_op jit(solution)/shard_map/ppermute | solution.py:504
  168.5 1.5 collective-permute-start.34
  169.9 8.5 %up_grad.1 = (bf16[2,8,48,768]{3,2,1,0:T(8,128)(2,1)}, bf16[2,8,48,768]{3,2,1,0:T(8,128)(2,1)}, bf16[2,8,48,768]{3,2,1,0:T(8,128)(2,1)}, bf16[2,8,48,768]{3,2,1,0:T(8,128)(2,1)}) custom-call(s32[10]{0:T(128)S(1)} %stack.55.scal.refs_0_, bf16[1024,768]{1,0:T(8,128)(2,1)S(1)} %get-tuple-element.276.xn.refs_1_, bf16[4,1024,768]{2,1,0:T(8,128)(2,1)S(1)} %get-tuple-element.336.dpre), custom_call_target="tpu_custom_call" | custom-call | flops 4831838208 | bytes 1048576 | tf_op jit(solution)/shard_map/up_grad/pallas_call | solution.py:139
  179.6 1.6 sums_4.1
  183.2 1.5 collective-permute-start.38
  184.7 11.8 %input_grad.1 = (f32[8,768]{1,0:T(8,128)S(1)}, bf16[2,512,768]{2,1,0:T(8,128)(2,1)}) custom-call(s32[10]{0:T(128)S(1)} %stack.55.scal.refs_0_, bf16[1024,768]{1,0:T(8,128)(2,1)S(1)} %bitcast.34, bf16[1024,768]{1,0:T(8,128)(2,1)S(1)} %bitcast.32, bf16[3,1024,768]{2,1,0:T(8,128)(2,1)S(1)} %bitcast.39, bf16[4,1024,768]{2,1,0:T(8,128)(2,1)S(1)} %get-tuple-element.336.dpre, ...), custom_call_target="tpu_custom_call" | custom-call | flops 8455716864 | bytes 1048576 | tf_op jit(solution)/shard_map/input_grad/pallas_call | solution.py:139
  196.6 4.1 %sums_5.1 = (bf16[8,48,768]{2,1,0:T(8,128)(2,1)S(1)}, bf16[8,48,768]{2,1,0:T(8,128)(2,1)S(1)}, bf16[2,48,768]{2,1,0:T(8,128)(2,1)S(1)}, bf16[2,48,768]{2,1,0:T(8...) custom-call(s32[10]{0:T(128)S(1)} %stack.55.scal.refs_0_, ...), custom_call_target="tpu_custom_call" | custom-call | flops 1048576 | bytes 1048576 | tf_op jit(solution)/shard_map/sums_5/pallas_call | solution.py:580
  202.3 2.8 %collective-permute-start.44 = (bf16[2,48,768]{2,1,0:T(8,128)(2,1)S(1)}, bf16[2,48,768]{2,1,0:T(8,128)(2,1)S(1)}, u32[]{:S(2)}, u32[]{:S(2)}) collective-permute-start(bf16[2,48,768]{2,1,0:T(8,128)(2,1)S(1)} %get-tuple-element.376), channel_id=1, source_target_pairs={{0,4},{1,5},{2,6},{3,7},{4,0},{5,1},{6,2},{7,3},{8,12},{9,13},{10,... | collective-permute-start | bytes 442376 | tf_op jit(solution)/shard_map/ppermute | solution.py:504
  205.1 1.9 collective-permute-start.45
  207.0 1.5 collective-permute-start.46
  208.4 2.3 copy-done.15
  210.8 8.4 %out.1 = bf16[2,512,768]{2,1,0:T(8,128)(2,1)} custom-call(s32[10]{0:T(128)S(1)} %stack.55.scal.refs_0_, bf16[1024,768]{1,0:T(8,128)(2,1)S(1)} %bitcast.35, bf16[1024,768]{1,0:T(8,128)(2,1)S(1)} %get-tuple-element.264.o, bf16[4,1024,768]{2,1,0:T(8,128)(2,1)S(1)} %get-tuple-element.303.act, f32[8,768]{1,0:T(8,128)S(1)} %get-tuple-element.232.refs_3_.vec, ...), custom_call_target="tpu_custom_call" | custom-call | flops 6039797760 | bytes 1048576 | tf_op jit(solution)/shard_map/out/pallas_call | solution.py:139
  219.3 1.6 sums_6.1
  222.3 1.4 collective-permute-start.50
  224.2 4.3 %collective-permute-done.50.refs_7_ = f32[8,384]{1,0:T(8,128)S(1)} collective-permute-done((f32[8,384]{1,0:T(8,128)S(1)}, f32[8,384]{1,0:T(8,128)S(1)}, u32[]{:S(2)}, u32[]{:S(2)}) %collective-permute-start.50) | collective-permute-done | bytes 12320 | tf_op jit(solution)/shard_map/ppermute | solution.py:504
  228.5 1.6 sums_7.1
  230.1 1.5 collective-permute-start.53
  231.6 1.9 collective-permute-start.54
  233.5 1.4 collective-permute-start.55
  234.9 1.3 collective-permute-start.52
  236.9 3.5 %collective-permute-done.56.refs_6_ = f32[8,384]{1,0:T(8,128)S(1)} collective-permute-done((f32[8,384]{1,0:T(8,128)S(1)}, f32[8,384]{1,0:T(8,128)S(1)}, u32[]{:S(2)}, u32[]{:S(2)}) %collective-permute-start.56) | collective-permute-done | bytes 12320 | tf_op jit(solution)/shard_map/ppermute | solution.py:508
  240.5 5.0 %collective-permute-done.54.refs_3_ = bf16[2,48,768]{2,1,0:T(8,128)(2,1)S(1)} collective-permute-done((bf16[2,48,768]{2,1,0:T(8,128)(2,1)S(1)}, bf16[2,48,768]{2,1,0:T(8,128)(2,1)S(1)}, u32[]{:S(2)}, u32[]{:S(2)}) %collective-permute-start.54) | collective-permute-done | bytes 147488 | tf_op jit(solution)/shard_map/ppermute | solution.py:504
  246.8 2.7 %collective-permute-start.58 = (f32[8,384]{1,0:T(8,128)S(1)}, f32[8,384]{1,0:T(8,128)S(1)}, u32[]{:S(2)}, u32[]{:S(2)}) collective-permute-start(f32[8,384]{1,0:T(8,128)S(1)} %get-tuple-element.422), channel_id=1, source_target_pairs={{0,4},{1,5},{2,6},{3,7},{4,0},{5,1},{6,2},{7,3},{8,12},{9,13},{10,... | collective-permute-start | bytes 36872 | tf_op jit(solution)/shard_map/ppermute | solution.py:504
  249.5 1.9 collective-permute-start.59
  251.4 1.4 collective-permute-start.60
  254.0 2.4 place.1
  258.7 1.4 place_last.1
  (170 shorter events, 25.6 us)
Async XLA Ops:
  2.7 10.4 %collective-permute-start.2 = (bf16[2,56,768]{2,1,0:T(8,128)(2,1)S(1)}, bf16[2,56,768]{2,1,0:T(8,128)(2,1)S(1)}, u32[]{:S(2)}, u32[]{:S(2)}) collective-permute-start(bf16[2,56,768]{2,1,0:T(8,128)(2,1)S(1)} %pad_maximum_fusion.5), channel_id=1, source_target_pairs={{0,12},{1,13},{2,14},{3,15},{4,8},{5,9},{6,10},{7,11},{8,4},{9,5},... | collective-permute-start | bytes 516104 | tf_op jit(solution)/shard_map/ppermute | solution.py:504
  7.9 14.6 %collective-permute-start.1 = (bf16[2,56,768]{2,1,0:T(8,128)(2,1)S(1)}, bf16[2,56,768]{2,1,0:T(8,128)(2,1)S(1)}, u32[]{:S(2)}, u32[]{:S(2)}) collective-permute-start(bf16[2,56,768]{2,1,0:T(8,128)(2,1)S(1)} %pad_maximum_fusion.5), channel_id=1, source_target_pairs={{0,8},{1,9},{2,10},{3,11},{4,12},{5,13},{6,14},{7,15},{8,0},{9,1},... | collective-permute-start | bytes 516104 | tf_op jit(solution)/shard_map/ppermute | solution.py:504
  7.9 14.6 %collective-permute-start = (bf16[2,56,768]{2,1,0:T(8,128)(2,1)S(1)}, bf16[2,56,768]{2,1,0:T(8,128)(2,1)S(1)}, u32[]{:S(2)}, u32[]{:S(2)}) collective-permute-start(bf16[2,56,768]{2,1,0:T(8,128)(2,1)S(1)} %pad_maximum_fusion.5), channel_id=1, source_target_pairs={{0,4},{1,5},{2,6},{3,7},{4,0},{5,1},{6,2},{7,3},{8,12},{9,13},{10,... | collective-permute-start | bytes 516104 | tf_op jit(solution)/shard_map/ppermute | solution.py:504
  22.6 19.0 %collective-permute-start.5 = (bf16[4,56,768]{2,1,0:T(8,128)(2,1)S(1)}, bf16[4,56,768]{2,1,0:T(8,128)(2,1)S(1)}, u32[]{:S(2)}, u32[]{:S(2)}) collective-permute-start(bf16[4,56,768]{2,1,0:T(8,128)(2,1)S(1)} %pad_maximum_fusion.2.refs_0_.refs_4_), channel_id=1, source_target_pairs={{0,16},{16,0},{1,17},{17,1},{2,18},{18,2},{3,19},{19,3},{4,20},{20... | collective-permute-start | bytes 1032200 | tf_op jit(solution)/shard_map/ppermute | solution.py:508
  24.2 17.4 %collective-permute-start.3 = (bf16[4,56,768]{2,1,0:T(8,128)(2,1)S(1)}, bf16[4,56,768]{2,1,0:T(8,128)(2,1)S(1)}, u32[]{:S(2)}, u32[]{:S(2)}) collective-permute-start(bf16[4,56,768]{2,1,0:T(8,128)(2,1)S(1)} %pad_maximum_fusion.2.refs_0_.refs_4_), channel_id=1, source_target_pairs={{0,2},{1,3},{2,0},{3,1},{4,6},{5,7},{6,4},{7,5},{8,10},{9,11},{10,... | collective-permute-start | bytes 1032200 | tf_op jit(solution)/shard_map/ppermute | solution.py:504
  25.7 15.9 %collective-permute-start.6 = (bf16[4,56,768]{2,1,0:T(8,128)(2,1)S(1)}, bf16[4,56,768]{2,1,0:T(8,128)(2,1)S(1)}, u32[]{:S(2)}, u32[]{:S(2)}) collective-permute-start(bf16[4,56,768]{2,1,0:T(8,128)(2,1)S(1)} %pad_maximum_fusion.3.refs_3_.refs_8_), channel_id=1, source_target_pairs={{0,2},{1,3},{2,0},{3,1},{4,6},{5,7},{6,4},{7,5},{8,10},{9,11},{10,... | collective-permute-start | bytes 1032200 | tf_op jit(solution)/shard_map/ppermute | solution.py:504
  26.3 15.3 %collective-permute-start.4 = (bf16[4,56,768]{2,1,0:T(8,128)(2,1)S(1)}, bf16[4,56,768]{2,1,0:T(8,128)(2,1)}, u32[]{:S(2)}, u32[]{:S(2)}) collective-permute-start(bf16[4,56,768]{2,1,0:T(8,128)(2,1)S(1)} %pad_maximum_fusion.3.refs_3_.refs_8_), channel_id=1, source_target_pairs={{0,16},{16,0},{1,17},{17,1},{2,18},{18,2},{3,19},{19,3},{4,20},{20... | collective-permute-start | bytes 1032200 | tf_op jit(solution)/shard_map/ppermute | solution.py:508
  27.6 14.0 %collective-permute-start.7 = (bf16[2,2,48,768]{3,2,1,0:T(8,128)(2,1)}, bf16[2,2,48,768]{3,2,1,0:T(8,128)(2,1)S(1)}, u32[]{:S(2)}, u32[]{:S(2)}) collective-permute-start(bf16[2,2,48,768]{3,2,1,0:T(8,128)(2,1)} %bitcast.14), channel_id=1, source_target_pairs={{0,8},{1,9},{2,10},{3,11},{4,12},{5,13},{6,14},{7,15},{8,0},{9,1},... | collective-permute-start | bytes 884744 | tf_op jit(solution)/shard_map/ppermute | solution.py:504
  43.1 17.3 %collective-permute-start.10 = (bf16[24,56,768]{2,1,0:T(8,128)(2,1)S(1)}, bf16[24,56,768]{2,1,0:T(8,128)(2,1)}, u32[]{:S(2)}, u32[]{:S(2)}) collective-permute-start(bf16[24,56,768]{2,1,0:T(8,128)(2,1)S(1)} %join_a.1), channel_id=1, source_target_pairs={{0,1},{1,0},{2,3},{3,2},{4,5},{5,4},{6,7},{7,6},{8,9},{9,8},{10,11... | collective-permute-start | bytes 6193160 | tf_op jit(solution)/shard_map/ppermute | solution.py:504
  43.1 11.9 %collective-permute-start.12 = (bf16[2,2,48,768]{3,2,1,0:T(8,128)(2,1)}, bf16[2,2,48,768]{3,2,1,0:T(8,128)(2,1)S(1)}, u32[]{:S(2)}, u32[]{:S(2)}) collective-permute-start(bf16[2,2,48,768]{3,2,1,0:T(8,128)(2,1)} %bitcast.14), channel_id=1, source_target_pairs={{0,12},{1,13},{2,14},{3,15},{4,8},{5,9},{6,10},{7,11},{8,4},{9,5},... | collective-permute-start | bytes 884744 | tf_op jit(solution)/shard_map/ppermute | solution.py:504
  44.7 15.6 %collective-permute-start.11 = (bf16[2,2,48,768]{3,2,1,0:T(8,128)(2,1)}, bf16[2,2,48,768]{3,2,1,0:T(8,128)(2,1)S(1)}, u32[]{:S(2)}, u32[]{:S(2)}) collective-permute-start(bf16[2,2,48,768]{3,2,1,0:T(8,128)(2,1)} %bitcast.14), channel_id=1, source_target_pairs={{0,4},{1,5},{2,6},{3,7},{4,0},{5,1},{6,2},{7,3},{8,12},{9,13},{10,... | collective-permute-start | bytes 884744 | tf_op jit(solution)/shard_map/ppermute | solution.py:504
  44.7 15.6 %collective-permute-start.9 = (bf16[4,56,768]{2,1,0:T(8,128)(2,1)}, bf16[4,56,768]{2,1,0:T(8,128)(2,1)}, u32[]{:S(2)}, u32[]{:S(2)}) collective-permute-start(bf16[4,56,768]{2,1,0:T(8,128)(2,1)} %collective-permute-done.4.refs_5_.refs_10_), channel_id=1, source_target_pairs={{0,2},{1,3},{2,0},{3,1},{4,6},{5,7},{6,4},{7,5},{8,10},{9,11},{10,... | collective-permute-start | bytes 1032200 | tf_op jit(solution)/shard_map/ppermute | solution.py:504
  46.2 14.1 %collective-permute-start.8 = (bf16[4,56,768]{2,1,0:T(8,128)(2,1)S(1)}, bf16[4,56,768]{2,1,0:T(8,128)(2,1)}, u32[]{:S(2)}, u32[]{:S(2)}) collective-permute-start(bf16[4,56,768]{2,1,0:T(8,128)(2,1)S(1)} %collective-permute-done.3.refs_1_.refs_5_), channel_id=1, source_target_pairs={{0,16},{16,0},{1,17},{17,1},{2,18},{18,2},{3,19},{19,3},{4,20},{20... | collective-permute-start | bytes 1032200 | tf_op jit(solution)/shard_map/ppermute | solution.py:508
  50.5 195.0 %copy-start.11 = (s32[10]{0:T(128)}, s32[10]{0:T(128)S(1)}, u32[]{:S(2)}) copy-start(s32[10]{0:T(128)S(1)} %stack.55.scal.refs_0_) | copy-start | bytes 124
  60.4 2.6 %collective-permute-start.13 = (bf16[4,56,768]{2,1,0:T(8,128)(2,1)}, bf16[4,56,768]{2,1,0:T(8,128)(2,1)S(1)}, u32[]{:S(2)}, u32[]{:S(2)}) collective-permute-start(bf16[4,56,768]{2,1,0:T(8,128)(2,1)} %collective-permute-done.8.refs_7_), channel_id=1, source_target_pairs={{0,1},{1,0},{2,3},{3,2},{4,5},{5,4},{6,7},{7,6},{8,9},{9,8},{10,11... | collective-permute-start | bytes 1032200 | tf_op jit(solution)/shard_map/ppermute | solution.py:504
  60.4 2.6 collective-permute-start.14
  63.0 40.1 %collective-permute-start.21 = (bf16[4,2,48,768]{3,2,1,0:T(8,128)(2,1)S(1)}, bf16[4,2,48,768]{3,2,1,0:T(8,128)(2,1)S(1)}, u32[]{:S(2)}, u32[]{:S(2)}) collective-permute-start(bf16[4,2,48,768]{3,2,1,0:T(8,128)(2,1)S(1)} %pad_maximum_fusion.refs_3_.refs_0_), channel_id=1, source_target_pairs={{0,1},{1,0},{2,3},{3,2},{4,5},{5,4},{6,7},{7,6},{8,9},{9,8},{10,11... | collective-permute-start | bytes 1769480 | tf_op jit(solution)/shard_map/ppermute | solution.py:504
  63.1 23.1 %collective-permute-start.17 = (bf16[4,2,48,768]{3,2,1,0:T(8,128)(2,1)S(1)}, bf16[4,2,48,768]{3,2,1,0:T(8,128)(2,1)S(1)}, u32[]{:S(2)}, u32[]{:S(2)}) collective-permute-start(bf16[4,2,48,768]{3,2,1,0:T(8,128)(2,1)S(1)} %pad_maximum_fusion.refs_3_.refs_0_), channel_id=1, source_target_pairs={{0,16},{16,0},{1,17},{17,1},{2,18},{18,2},{3,19},{19,3},{4,20},{20... | collective-permute-start | bytes 1769480 | tf_op jit(solution)/shard_map/ppermute | solution.py:508
  64.7 21.7 %collective-permute-start.15 = (bf16[4,2,48,768]{3,2,1,0:T(8,128)(2,1)S(1)}, bf16[4,2,48,768]{3,2,1,0:T(8,128)(2,1)S(1)}, u32[]{:S(2)}, u32[]{:S(2)}) collective-permute-start(bf16[4,2,48,768]{3,2,1,0:T(8,128)(2,1)S(1)} %pad_maximum_fusion.refs_3_.refs_0_), channel_id=1, source_target_pairs={{0,2},{1,3},{2,0},{3,1},{4,6},{5,7},{6,4},{7,5},{8,10},{9,11},{10,... | collective-permute-start | bytes 1769480 | tf_op jit(solution)/shard_map/ppermute | solution.py:504
  66.2 26.5 %collective-permute-start.18 = (bf16[4,2,48,768]{3,2,1,0:T(8,128)(2,1)S(1)}, bf16[4,2,48,768]{3,2,1,0:T(8,128)(2,1)S(1)}, u32[]{:S(2)}, u32[]{:S(2)}) collective-permute-start(bf16[4,2,48,768]{3,2,1,0:T(8,128)(2,1)S(1)} %pad_maximum_fusion.1.refs_7_.refs_4_), channel_id=1, source_target_pairs={{0,2},{1,3},{2,0},{3,1},{4,6},{5,7},{6,4},{7,5},{8,10},{9,11},{10,... | collective-permute-start | bytes 1769480 | tf_op jit(solution)/shard_map/ppermute | solution.py:504
  66.7 26.0 %collective-permute-start.16 = (bf16[4,2,48,768]{3,2,1,0:T(8,128)(2,1)S(1)}, bf16[4,2,48,768]{3,2,1,0:T(8,128)(2,1)S(1)}, u32[]{:S(2)}, u32[]{:S(2)}) collective-permute-start(bf16[4,2,48,768]{3,2,1,0:T(8,128)(2,1)S(1)} %pad_maximum_fusion.1.refs_7_.refs_4_), channel_id=1, source_target_pairs={{0,16},{16,0},{1,17},{17,1},{2,18},{18,2},{3,19},{19,3},{4,20},{20... | collective-permute-start | bytes 1769480 | tf_op jit(solution)/shard_map/ppermute | solution.py:508
  86.3 16.9 %collective-permute-start.22 = (bf16[4,2,48,768]{3,2,1,0:T(8,128)(2,1)S(1)}, bf16[4,2,48,768]{3,2,1,0:T(8,128)(2,1)S(1)}, u32[]{:S(2)}, u32[]{:S(2)}) collective-permute-start(bf16[4,2,48,768]{3,2,1,0:T(8,128)(2,1)S(1)} %pad_maximum_fusion.1.refs_7_.refs_4_), channel_id=1, source_target_pairs={{0,1},{1,0},{2,3},{3,2},{4,5},{5,4},{6,7},{7,6},{8,9},{9,8},{10,11... | collective-permute-start | bytes 1769480 | tf_op jit(solution)/shard_map/ppermute | solution.py:504
  92.7 14.6 %collective-permute-start.19 = (bf16[4,2,48,768]{3,2,1,0:T(8,128)(2,1)S(1)}, bf16[4,2,48,768]{3,2,1,0:T(8,128)(2,1)S(1)}, u32[]{:S(2)}, u32[]{:S(2)}) collective-permute-start(bf16[4,2,48,768]{3,2,1,0:T(8,128)(2,1)S(1)} %collective-permute-done.15.refs_0_.refs_4_.refs_1_), channel_id=1, source_target_pairs={{0,16},{16,0},{1,17},{17,1},{2,18},{18,2},{3,19},{19,3},{4,20},{20... | collective-permute-start | bytes 1769480 | tf_op jit(solution)/shard_map/ppermute | solution.py:508
  93.3 14.3 %collective-permute-start.20 = (bf16[4,2,48,768]{3,2,1,0:T(8,128)(2,1)S(1)}, bf16[4,2,48,768]{3,2,1,0:T(8,128)(2,1)S(1)}, u32[]{:S(2)}, u32[]{:S(2)}) collective-permute-start(bf16[4,2,48,768]{3,2,1,0:T(8,128)(2,1)S(1)} %collective-permute-done.16.refs_4_.refs_9_.refs_6_), channel_id=1, source_target_pairs={{0,2},{1,3},{2,0},{3,1},{4,6},{5,7},{6,4},{7,5},{8,10},{9,11},{10,... | collective-permute-start | bytes 1769480 | tf_op jit(solution)/shard_map/ppermute | solution.py:504
  108.5 9.0 %collective-permute-start.23 = (bf16[24,2,48,768]{3,2,1,0:T(8,128)(2,1)S(1)}, bf16[24,2,48,768]{3,2,1,0:T(8,128)(2,1)S(1)}, u32[]{:S(2)}, u32[]{:S(2)}) collective-permute-start(bf16[24,2,48,768]{3,2,1,0:T(8,128)(2,1)S(1)} %join_c.1), channel_id=1, source_target_pairs={{0,1},{1,0},{2,3},{3,2},{4,5},{5,4},{6,7},{7,6},{8,9},{9,8},{10,11... | collective-permute-start | bytes 10616840 | tf_op jit(solution)/shard_map/ppermute | solution.py:504
  117.5 9.9 %collective-permute-start.24 = (bf16[2,8,48,768]{3,2,1,0:T(8,128)(2,1)}, bf16[2,8,48,768]{3,2,1,0:T(8,128)(2,1)S(1)}, u32[]{:S(2)}, u32[]{:S(2)}) collective-permute-start(bf16[2,8,48,768]{3,2,1,0:T(8,128)(2,1)} %get-tuple-element.290), channel_id=1, source_target_pairs={{0,1},{1,0},{2,3},{3,2},{4,5},{5,4},{6,7},{7,6},{8,9},{9,8},{10,11... | collective-permute-start | bytes 3538952 | tf_op jit(solution)/shard_map/ppermute | solution.py:504
  118.1 9.4 %collective-permute-start.25 = (bf16[2,8,48,768]{3,2,1,0:T(8,128)(2,1)}, bf16[2,8,48,768]{3,2,1,0:T(8,128)(2,1)S(1)}, u32[]{:S(2)}, u32[]{:S(2)}) collective-permute-start(bf16[2,8,48,768]{3,2,1,0:T(8,128)(2,1)} %get-tuple-element.291), channel_id=1, source_target_pairs={{0,1},{1,0},{2,3},{3,2},{4,5},{5,4},{6,7},{7,6},{8,9},{9,8},{10,11... | collective-permute-start | bytes 3538952 | tf_op jit(solution)/shard_map/ppermute | solution.py:504
  129.0 17.8 %collective-permute-start.26 = (bf16[8,48,768]{2,1,0:T(8,128)(2,1)S(1)}, bf16[8,48,768]{2,1,0:T(8,128)(2,1)S(1)}, u32[]{:S(2)}, u32[]{:S(2)}) collective-permute-start(bf16[8,48,768]{2,1,0:T(8,128)(2,1)S(1)} %get-tuple-element.301), channel_id=1, source_target_pairs={{0,16},{16,0},{1,17},{17,1},{2,18},{18,2},{3,19},{19,3},{4,20},{20... | collective-permute-start | bytes 1769480 | tf_op jit(solution)/shard_map/ppermute | solution.py:508
  130.6 16.2 %collective-permute-start.27 = (bf16[8,48,768]{2,1,0:T(8,128)(2,1)S(1)}, bf16[8,48,768]{2,1,0:T(8,128)(2,1)S(1)}, u32[]{:S(2)}, u32[]{:S(2)}) collective-permute-start(bf16[8,48,768]{2,1,0:T(8,128)(2,1)S(1)} %get-tuple-element.302), channel_id=1, source_target_pairs={{0,2},{1,3},{2,0},{3,1},{4,6},{5,7},{6,4},{7,5},{8,10},{9,11},{10,... | collective-permute-start | bytes 1769480 | tf_op jit(solution)/shard_map/ppermute | solution.py:504
  148.5 10.1 %collective-permute-start.30 = (bf16[2,8,48,768]{3,2,1,0:T(8,128)(2,1)S(1)}, bf16[2,8,48,768]{3,2,1,0:T(8,128)(2,1)S(1)}, u32[]{:S(2)}, u32[]{:S(2)}) collective-permute-start(bf16[2,8,48,768]{3,2,1,0:T(8,128)(2,1)S(1)} %copy-done.25), channel_id=1, source_target_pairs={{0,1},{1,0},{2,3},{3,2},{4,5},{5,4},{6,7},{7,6},{8,9},{9,8},{10,11... | collective-permute-start | bytes 3538952 | tf_op jit(solution)/shard_map/ppermute | solution.py:504
  148.8 9.8 %collective-permute-start.31 = (bf16[2,8,48,768]{3,2,1,0:T(8,128)(2,1)S(1)}, bf16[2,8,48,768]{3,2,1,0:T(8,128)(2,1)S(1)}, u32[]{:S(2)}, u32[]{:S(2)}) collective-permute-start(bf16[2,8,48,768]{3,2,1,0:T(8,128)(2,1)S(1)} %copy-done.24), channel_id=1, source_target_pairs={{0,1},{1,0},{2,3},{3,2},{4,5},{5,4},{6,7},{7,6},{8,9},{9,8},{10,11... | collective-permute-start | bytes 3538952 | tf_op jit(solution)/shard_map/ppermute | solution.py:504
  149.1 9.1 %collective-permute-start.28 = (bf16[4,48,768]{2,1,0:T(8,128)(2,1)S(1)}, bf16[4,48,768]{2,1,0:T(8,128)(2,1)S(1)}, u32[]{:S(2)}, u32[]{:S(2)}) collective-permute-start(bf16[4,48,768]{2,1,0:T(8,128)(2,1)S(1)} %get-tuple-element.316), channel_id=1, source_target_pairs={{0,2},{1,3},{2,0},{3,1},{4,6},{5,7},{6,4},{7,5},{8,10},{9,11},{10,... | collective-permute-start | bytes 884744 | tf_op jit(solution)/shard_map/ppermute | solution.py:504
  149.8 8.9 %collective-permute-start.29 = (bf16[4,48,768]{2,1,0:T(8,128)(2,1)S(1)}, bf16[4,48,768]{2,1,0:T(8,128)(2,1)S(1)}, u32[]{:S(2)}, u32[]{:S(2)}) collective-permute-start(bf16[4,48,768]{2,1,0:T(8,128)(2,1)S(1)} %get-tuple-element.317), channel_id=1, source_target_pairs={{0,16},{16,0},{1,17},{17,1},{2,18},{18,2},{3,19},{19,3},{4,20},{20... | collective-permute-start | bytes 884744 | tf_op jit(solution)/shard_map/ppermute | solution.py:508
  158.7 26.0 %slice-start = ((s8[4718592]{0:T(1024)(128)(4,1)}), s8[524288]{0:T(1024)(128)(4,1)S(1)}, s32[]{:S(2)}) async-start(s8[4718592]{0:T(1024)(128)(4,1)} %bitcast.36), calls=%async_computation | async-start | bytes 1048576
  158.7 26.0 %slice-start.2 = ((s8[4718592]{0:T(1024)(128)(4,1)}), s8[4194304]{0:T(1024)(128)(4,1)S(1)}, s32[]{:S(2)}) async-start(s8[4718592]{0:T(1024)(128)(4,1)} %bitcast.38), calls=%async_computation.2 | async-start | bytes 8388608
  160.8 18.8 %collective-permute-start.35 = (bf16[8,48,768]{2,1,0:T(8,128)(2,1)S(1)}, bf16[8,48,768]{2,1,0:T(8,128)(2,1)S(1)}, u32[]{:S(2)}, u32[]{:S(2)}) collective-permute-start(bf16[8,48,768]{2,1,0:T(8,128)(2,1)S(1)} %get-tuple-element.334), channel_id=1, source_target_pairs={{0,16},{16,0},{1,17},{17,1},{2,18},{18,2},{3,19},{19,3},{4,20},{20... | collective-permute-start | bytes 1769480 | tf_op jit(solution)/shard_map/ppermute | solution.py:508
  161.5 18.1 %collective-permute-start.36 = (bf16[8,48,768]{2,1,0:T(8,128)(2,1)S(1)}, bf16[8,48,768]{2,1,0:T(8,128)(2,1)S(1)}, u32[]{:S(2)}, u32[]{:S(2)}) collective-permute-start(bf16[8,48,768]{2,1,0:T(8,128)(2,1)S(1)} %get-tuple-element.335), channel_id=1, source_target_pairs={{0,2},{1,3},{2,0},{3,1},{4,6},{5,7},{6,4},{7,5},{8,10},{9,11},{10,... | collective-permute-start | bytes 1769480 | tf_op jit(solution)/shard_map/ppermute | solution.py:504
  162.9 15.5 %collective-permute-start.32 = (bf16[2,48,768]{2,1,0:T(8,128)(2,1)S(1)}, bf16[2,48,768]{2,1,0:T(8,128)(2,1)S(1)}, u32[]{:S(2)}, u32[]{:S(2)}) collective-permute-start(bf16[2,48,768]{2,1,0:T(8,128)(2,1)S(1)} %get-tuple-element.331), channel_id=1, source_target_pairs={{0,4},{1,5},{2,6},{3,7},{4,0},{5,1},{6,2},{7,3},{8,12},{9,13},{10,... | collective-permute-start | bytes 442376 | tf_op jit(solution)/shard_map/ppermute | solution.py:504
  165.9 13.8 %collective-permute-start.33 = (bf16[2,48,768]{2,1,0:T(8,128)(2,1)S(1)}, bf16[2,48,768]{2,1,0:T(8,128)(2,1)S(1)}, u32[]{:S(2)}, u32[]{:S(2)}) collective-permute-start(bf16[2,48,768]{2,1,0:T(8,128)(2,1)S(1)} %get-tuple-element.332), channel_id=1, source_target_pairs={{0,8},{1,9},{2,10},{3,11},{4,12},{5,13},{6,14},{7,15},{8,0},{9,1},... | collective-permute-start | bytes 442376 | tf_op jit(solution)/shard_map/ppermute | solution.py:504
  168.5 11.1 %collective-permute-start.34 = (bf16[2,48,768]{2,1,0:T(8,128)(2,1)S(1)}, bf16[2,48,768]{2,1,0:T(8,128)(2,1)S(1)}, u32[]{:S(2)}, u32[]{:S(2)}) collective-permute-start(bf16[2,48,768]{2,1,0:T(8,128)(2,1)S(1)} %get-tuple-element.333), channel_id=1, source_target_pairs={{0,12},{1,13},{2,14},{3,15},{4,8},{5,9},{6,10},{7,11},{8,4},{9,5},... | collective-permute-start | bytes 442376 | tf_op jit(solution)/shard_map/ppermute | solution.py:504
  181.3 15.3 %collective-permute-start.39 = (bf16[2,8,48,768]{3,2,1,0:T(8,128)(2,1)S(1)}, bf16[2,8,48,768]{3,2,1,0:T(8,128)(2,1)S(1)}, u32[]{:S(2)}, u32[]{:S(2)}) collective-permute-start(bf16[2,8,48,768]{3,2,1,0:T(8,128)(2,1)S(1)} %copy-done.23), channel_id=1, source_target_pairs={{0,1},{1,0},{2,3},{3,2},{4,5},{5,4},{6,7},{7,6},{8,9},{9,8},{10,11... | collective-permute-start | bytes 3538952 | tf_op jit(solution)/shard_map/ppermute | solution.py:504
  181.6 15.0 %collective-permute-start.40 = (bf16[2,8,48,768]{3,2,1,0:T(8,128)(2,1)S(1)}, bf16[2,8,48,768]{3,2,1,0:T(8,128)(2,1)S(1)}, u32[]{:S(2)}, u32[]{:S(2)}) collective-permute-start(bf16[2,8,48,768]{3,2,1,0:T(8,128)(2,1)S(1)} %copy-done.22), channel_id=1, source_target_pairs={{0,1},{1,0},{2,3},{3,2},{4,5},{5,4},{6,7},{7,6},{8,9},{9,8},{10,11... | collective-permute-start | bytes 3538952 | tf_op jit(solution)/shard_map/ppermute | solution.py:504
  181.9 14.7 %collective-permute-start.41 = (bf16[2,48,768]{2,1,0:T(8,128)(2,1)S(1)}, bf16[2,48,768]{2,1,0:T(8,128)(2,1)S(1)}, u32[]{:S(2)}, u32[]{:S(2)}) collective-permute-start(bf16[2,48,768]{2,1,0:T(8,128)(2,1)S(1)} %get-tuple-element.355.a_mine), channel_id=1, source_target_pairs={{0,16},{16,0},{1,17},{17,1},{2,18},{18,2},{3,19},{19,3},{4,20},{20... | collective-permute-start | bytes 442376 | tf_op jit(solution)/shard_map/ppermute | solution.py:508
  182.1 14.4 %collective-permute-start.37 = (bf16[4,48,768]{2,1,0:T(8,128)(2,1)S(1)}, bf16[4,48,768]{2,1,0:T(8,128)(2,1)S(1)}, u32[]{:S(2)}, u32[]{:S(2)}) collective-permute-start(bf16[4,48,768]{2,1,0:T(8,128)(2,1)S(1)} %get-tuple-element.351), channel_id=1, source_target_pairs={{0,2},{1,3},{2,0},{3,1},{4,6},{5,7},{6,4},{7,5},{8,10},{9,11},{10,... | collective-permute-start | bytes 884744 | tf_op jit(solution)/shard_map/ppermute | solution.py:504
  183.2 13.4 %collective-permute-start.38 = (bf16[4,48,768]{2,1,0:T(8,128)(2,1)S(1)}, bf16[4,48,768]{2,1,0:T(8,128)(2,1)S(1)}, u32[]{:S(2)}, u32[]{:S(2)}) collective-permute-start(bf16[4,48,768]{2,1,0:T(8,128)(2,1)S(1)} %get-tuple-element.352), channel_id=1, source_target_pairs={{0,16},{16,0},{1,17},{17,1},{2,18},{18,2},{3,19},{19,3},{4,20},{20... | collective-permute-start | bytes 884744 | tf_op jit(solution)/shard_map/ppermute | solution.py:508
  200.7 18.5 %collective-permute-start.42 = (bf16[8,48,768]{2,1,0:T(8,128)(2,1)S(1)}, bf16[8,48,768]{2,1,0:T(8,128)(2,1)S(1)}, u32[]{:S(2)}, u32[]{:S(2)}) collective-permute-start(bf16[8,48,768]{2,1,0:T(8,128)(2,1)S(1)} %get-tuple-element.374), channel_id=1, source_target_pairs={{0,16},{16,0},{1,17},{17,1},{2,18},{18,2},{3,19},{19,3},{4,20},{20... | collective-permute-start | bytes 1769480 | tf_op jit(solution)/shard_map/ppermute | solution.py:508
  201.3 18.0 %collective-permute-start.43 = (bf16[8,48,768]{2,1,0:T(8,128)(2,1)S(1)}, bf16[8,48,768]{2,1,0:T(8,128)(2,1)S(1)}, u32[]{:S(2)}, u32[]{:S(2)}) collective-permute-start(bf16[8,48,768]{2,1,0:T(8,128)(2,1)S(1)} %get-tuple-element.375), channel_id=1, source_target_pairs={{0,2},{1,3},{2,0},{3,1},{4,6},{5,7},{6,4},{7,5},{8,10},{9,11},{10,... | collective-permute-start | bytes 1769480 | tf_op jit(solution)/shard_map/ppermute | solution.py:504
  202.3 16.9 %collective-permute-start.44 = (bf16[2,48,768]{2,1,0:T(8,128)(2,1)S(1)}, bf16[2,48,768]{2,1,0:T(8,128)(2,1)S(1)}, u32[]{:S(2)}, u32[]{:S(2)}) collective-permute-start(bf16[2,48,768]{2,1,0:T(8,128)(2,1)S(1)} %get-tuple-element.376), channel_id=1, source_target_pairs={{0,4},{1,5},{2,6},{3,7},{4,0},{5,1},{6,2},{7,3},{8,12},{9,13},{10,... | collective-permute-start | bytes 442376 | tf_op jit(solution)/shard_map/ppermute | solution.py:504
  205.1 14.2 %collective-permute-start.45 = (bf16[2,48,768]{2,1,0:T(8,128)(2,1)S(1)}, bf16[2,48,768]{2,1,0:T(8,128)(2,1)S(1)}, u32[]{:S(2)}, u32[]{:S(2)}) collective-permute-start(bf16[2,48,768]{2,1,0:T(8,128)(2,1)S(1)} %get-tuple-element.377), channel_id=1, source_target_pairs={{0,8},{1,9},{2,10},{3,11},{4,12},{5,13},{6,14},{7,15},{8,0},{9,1},... | collective-permute-start | bytes 442376 | tf_op jit(solution)/shard_map/ppermute | solution.py:504
  207.0 12.3 %collective-permute-start.46 = (bf16[2,48,768]{2,1,0:T(8,128)(2,1)S(1)}, bf16[2,48,768]{2,1,0:T(8,128)(2,1)S(1)}, u32[]{:S(2)}, u32[]{:S(2)}) collective-permute-start(bf16[2,48,768]{2,1,0:T(8,128)(2,1)S(1)} %get-tuple-element.378), channel_id=1, source_target_pairs={{0,12},{1,13},{2,14},{3,15},{4,8},{5,9},{6,10},{7,11},{8,4},{9,5},... | collective-permute-start | bytes 442376 | tf_op jit(solution)/shard_map/ppermute | solution.py:504
  220.9 7.7 %collective-permute-start.47 = (bf16[4,48,768]{2,1,0:T(8,128)(2,1)S(1)}, bf16[4,48,768]{2,1,0:T(8,128)(2,1)S(1)}, u32[]{:S(2)}, u32[]{:S(2)}) collective-permute-start(bf16[4,48,768]{2,1,0:T(8,128)(2,1)S(1)} %get-tuple-element.397), channel_id=1, source_target_pairs={{0,2},{1,3},{2,0},{3,1},{4,6},{5,7},{6,4},{7,5},{8,10},{9,11},{10,... | collective-permute-start | bytes 884744 | tf_op jit(solution)/shard_map/ppermute | solution.py:504
  221.2 7.3 %collective-permute-start.48 = (bf16[4,48,768]{2,1,0:T(8,128)(2,1)S(1)}, bf16[4,48,768]{2,1,0:T(8,128)(2,1)S(1)}, u32[]{:S(2)}, u32[]{:S(2)}) collective-permute-start(bf16[4,48,768]{2,1,0:T(8,128)(2,1)S(1)} %get-tuple-element.398), channel_id=1, source_target_pairs={{0,16},{16,0},{1,17},{17,1},{2,18},{18,2},{3,19},{19,3},{4,20},{20... | collective-permute-start | bytes 884744 | tf_op jit(solution)/shard_map/ppermute | solution.py:508
  222.3 1.9 collective-permute-start.49
  222.3 6.2 %collective-permute-start.50 = (f32[8,384]{1,0:T(8,128)S(1)}, f32[8,384]{1,0:T(8,128)S(1)}, u32[]{:S(2)}, u32[]{:S(2)}) collective-permute-start(f32[8,384]{1,0:T(8,128)S(1)} %get-tuple-element.401), channel_id=1, source_target_pairs={{0,2},{1,3},{2,0},{3,1},{4,6},{5,7},{6,4},{7,5},{8,10},{9,11},{10,... | collective-permute-start | bytes 36872 | tf_op jit(solution)/shard_map/ppermute | solution.py:504
  223.7 4.8 %collective-permute-start.51 = (f32[8,384]{1,0:T(8,128)S(1)}, f32[8,384]{1,0:T(8,128)S(1)}, u32[]{:S(2)}, u32[]{:S(2)}) collective-permute-start(f32[8,384]{1,0:T(8,128)S(1)} %get-tuple-element.402), channel_id=1, source_target_pairs={{0,3},{1,2},{2,1},{3,0},{4,7},{5,6},{6,5},{7,4},{8,11},{9,10},{10,... | collective-permute-start | bytes 36872 | tf_op jit(solution)/shard_map/ppermute | solution.py:504
  230.1 10.4 %collective-permute-start.53 = (bf16[2,48,768]{2,1,0:T(8,128)(2,1)S(1)}, bf16[2,48,768]{2,1,0:T(8,128)(2,1)S(1)}, u32[]{:S(2)}, u32[]{:S(2)}) collective-permute-start(bf16[2,48,768]{2,1,0:T(8,128)(2,1)S(1)} %get-tuple-element.411), channel_id=1, source_target_pairs={{0,4},{1,5},{2,6},{3,7},{4,0},{5,1},{6,2},{7,3},{8,12},{9,13},{10,... | collective-permute-start | bytes 442376 | tf_op jit(solution)/shard_map/ppermute | solution.py:504
  231.6 13.9 %collective-permute-start.54 = (bf16[2,48,768]{2,1,0:T(8,128)(2,1)S(1)}, bf16[2,48,768]{2,1,0:T(8,128)(2,1)S(1)}, u32[]{:S(2)}, u32[]{:S(2)}) collective-permute-start(bf16[2,48,768]{2,1,0:T(8,128)(2,1)S(1)} %get-tuple-element.412), channel_id=1, source_target_pairs={{0,8},{1,9},{2,10},{3,11},{4,12},{5,13},{6,14},{7,15},{8,0},{9,1},... | collective-permute-start | bytes 442376 | tf_op jit(solution)/shard_map/ppermute | solution.py:504
  233.5 12.0 %collective-permute-start.55 = (bf16[2,48,768]{2,1,0:T(8,128)(2,1)S(1)}, bf16[2,48,768]{2,1,0:T(8,128)(2,1)S(1)}, u32[]{:S(2)}, u32[]{:S(2)}) collective-permute-start(bf16[2,48,768]{2,1,0:T(8,128)(2,1)S(1)} %get-tuple-element.413), channel_id=1, source_target_pairs={{0,12},{1,13},{2,14},{3,15},{4,8},{5,9},{6,10},{7,11},{8,4},{9,5},... | collective-permute-start | bytes 442376 | tf_op jit(solution)/shard_map/ppermute | solution.py:504
  234.9 19.1 %collective-permute-start.52 = (bf16[2,48,768]{2,1,0:T(8,128)(2,1)S(1)}, bf16[2,48,768]{2,1,0:T(8,128)(2,1)S(1)}, u32[]{:S(2)}, u32[]{:S(2)}) collective-permute-start(bf16[2,48,768]{2,1,0:T(8,128)(2,1)S(1)} %get-tuple-element.409.d_mine), channel_id=1, source_target_pairs={{0,16},{16,0},{1,17},{17,1},{2,18},{18,2},{3,19},{19,3},{4,20},{20... | collective-permute-start | bytes 442376 | tf_op jit(solution)/shard_map/ppermute | solution.py:508
  236.2 4.3 %collective-permute-start.56 = (f32[8,384]{1,0:T(8,128)S(1)}, f32[8,384]{1,0:T(8,128)S(1)}, u32[]{:S(2)}, u32[]{:S(2)}) collective-permute-start(f32[8,384]{1,0:T(8,128)S(1)} %get-tuple-element.414.refs_5_), channel_id=1, source_target_pairs={{0,16},{16,0},{1,17},{17,1},{2,18},{18,2},{3,19},{19,3},{4,20},{20... | collective-permute-start | bytes 36872 | tf_op jit(solution)/shard_map/ppermute | solution.py:508
  246.8 9.7 %collective-permute-start.58 = (f32[8,384]{1,0:T(8,128)S(1)}, f32[8,384]{1,0:T(8,128)S(1)}, u32[]{:S(2)}, u32[]{:S(2)}) collective-permute-start(f32[8,384]{1,0:T(8,128)S(1)} %get-tuple-element.422), channel_id=1, source_target_pairs={{0,4},{1,5},{2,6},{3,7},{4,0},{5,1},{6,2},{7,3},{8,12},{9,13},{10,... | collective-permute-start | bytes 36872 | tf_op jit(solution)/shard_map/ppermute | solution.py:504
  249.5 7.0 %collective-permute-start.59 = (f32[8,384]{1,0:T(8,128)S(1)}, f32[8,384]{1,0:T(8,128)S(1)}, u32[]{:S(2)}, u32[]{:S(2)}) collective-permute-start(f32[8,384]{1,0:T(8,128)S(1)} %get-tuple-element.423), channel_id=1, source_target_pairs={{0,8},{1,9},{2,10},{3,11},{4,12},{5,13},{6,14},{7,15},{8,0},{9,1},... | collective-permute-start | bytes 36872 | tf_op jit(solution)/shard_map/ppermute | solution.py:504
  251.4 5.5 %collective-permute-start.60 = (f32[8,384]{1,0:T(8,128)S(1)}, f32[8,384]{1,0:T(8,128)S(1)}, u32[]{:S(2)}, u32[]{:S(2)}) collective-permute-start(f32[8,384]{1,0:T(8,128)S(1)} %get-tuple-element.424), channel_id=1, source_target_pairs={{0,12},{1,13},{2,14},{3,15},{4,8},{5,9},{6,10},{7,11},{8,4},{9,5},... | collective-permute-start | bytes 36872 | tf_op jit(solution)/shard_map/ppermute | solution.py:504
  252.8 5.9 %collective-permute-start.57 = (bf16[2,48,768]{2,1,0:T(8,128)(2,1)S(1)}, bf16[2,48,768]{2,1,0:T(8,128)(2,1)S(1)}, u32[]{:S(2)}, u32[]{:S(2)}) collective-permute-start(bf16[2,48,768]{2,1,0:T(8,128)(2,1)S(1)} %get-tuple-element.415.u_mine), channel_id=1, source_target_pairs={{0,16},{16,0},{1,17},{17,1},{2,18},{18,2},{3,19},{19,3},{4,20},{20... | collective-permute-start | bytes 442376 | tf_op jit(solution)/shard_map/ppermute | solution.py:508
  (29 other events, 251.1 us)

commit v5 on v4

--- a/solution.py
+++ b/solution.py
@@ -170,8 +170,7 @@
 
 def project_kernel(load, n_w, *refs):
     scal, x_ref, cot_ref, vec_ref = refs[:4]
-    xn, q, k, v, da, w = refs[4 + n_w : 10 + n_w]
-    (sem,) = refs[10 + n_w :]
+    xn, q, k, v, da, w, sem = refs[4 + n_w :]
     load(scal, refs[4 : 4 + n_w], w, sem)
     tokens = x_ref.shape[0]
 
@@ -212,10 +211,11 @@
         "project",
         (scal, x, cot, vec),
         weights,
-        [kept(x.shape)] * 5 + [kept((4, width, width))],
+        [kept(x.shape)] * 5,
         [],
-        [pltpu.SemaphoreType.DMA((4,))],
+        [pltpu.VMEM((4, width, width), BF16), pltpu.SemaphoreType.DMA((4,))],
         8 * tokens * width * width,
+        limit=10,
     )
 
 
@@ -249,6 +249,7 @@
         [],
         10 << 30,
         alias={5 + i: i for i in range(len(before))},
+        limit=8,
     )
 
 
@@ -258,15 +259,14 @@
 
     def grad(b):
         g[b] = dot_tn(xn[...], d[b]).astype(BF16)
+        store(scal, g, g_refs, sem, b)
 
     loop(3, grad)
     g[3] = dot_tn(o[...], cot[...]).astype(BF16)
-    done = store(scal, g, g_refs, sem)
-    ones = jnp.ones((8, tokens), BF16)
-    sums[0:1, :] = dot_nn(ones, d[0])[0:1]
-    sums[1:2, :] = dot_nn(ones, d[2])[0:1]
-    sums[2:3, :] = dot_nn(ones, cot[...])[0:1]
-    done()
+    store(scal, g, g_refs, sem, 3)
+    for i, v in enumerate((d[0], d[2], cot[...])):
+        sums[i : i + 1, :] = jnp.sum(v.astype(F32), axis=0, keepdims=True)
+    stored(g_refs, sem)
 
 
 def attn_grad_call(scal, xn, o, d, cot, store, g_shapes):
@@ -280,6 +280,7 @@
         g_shapes,
         [pltpu.VMEM((4, width, width), BF16), pltpu.SemaphoreType.DMA((len(g_shapes),))],
         8 * tokens * width * width,
+        limit=10,
     )
 
 
@@ -349,6 +350,7 @@
         [pltpu.VMEM((256, width), F32)] * 2 + [pltpu.SemaphoreType.DMA((tiles,))],
         2 * count * tokens * width * width,
         alias={3: 0, 4: 1} if before else None,
+        limit=7,
     )
 
 
@@ -359,12 +361,12 @@
 
     def grad(t):
         g[tile_of(t, width), :] = dot_tn(act[t], cot[...]).astype(BF16)
+        store(scal, g, g_refs, sem, t)
 
     loop(tiles, grad)
-    done = store(scal, g, g_refs, sem)
     for t in range(tiles):
         wait_tile(w, wsem, t, width)
-    done()
+    stored(g_refs, sem)
 
 
 def down_grad_call(scal, act, cot, pieces, load, store, g_shapes):
@@ -382,19 +384,19 @@
             pltpu.SemaphoreType.DMA((len(g_shapes),)),
         ],
         2 * tiles * tokens * width * width,
+        limit=12,
     )
 
 
 def dpre_kernel(scal, cot, gp, w, dpre, sums):
     tiles, tokens, width = gp.shape
-    ones = jnp.ones((8, tokens), BF16)
 
     def down(t):
-        dpre[t] = (dot_nt(cot[...], w[tile_of(t, width), :]) * gp[t].astype(F32)).astype(BF16)
+        d = (dot_nt(cot[...], w[tile_of(t, width), :]) * gp[t].astype(F32)).astype(BF16)
+        dpre[t] = d
+        sums[pl.ds(t, 1), :] = jnp.sum(d.astype(F32), axis=0, keepdims=True)
 
     loop(tiles, down)
-    for t in range(tiles):
-        sums[t : t + 1, :] = dot_nn(ones, dpre[t])[0:1]
 
 
 def dpre_call(scal, cot, gp, w):
@@ -409,31 +411,40 @@
         [],
         2 * tiles * tokens * width * width,
         alias={2: 0},
+        limit=8,
     )
 
 
-def up_grad_kernel(store, scal, xn, dpre, *refs):
-    *g_refs, g, sem = refs
-    tiles, tokens, width = dpre.shape
+def up_grad_kernel(load, store, n_p, scal, xn, dpre, *refs):
+    w, *g_refs, g, wsem, sem = refs[n_p:]
+    load(scal, refs[:n_p], w, wsem)
 
     def grad(t):
         g[t] = dot_tn(xn[...], dpre[t]).astype(BF16)
-
-    loop(tiles, grad)
-    store(scal, g, g_refs, sem)()
-
-
-def up_grad_call(scal, xn, dpre, store, g_shapes):
+        store(scal, g, g_refs, sem, t)
+
+    loop(dpre.shape[0], grad)
+    for i in range(4):
+        whole_wait(w.at[i], wsem.at[i])()
+    stored(g_refs, sem)
+
+
+def up_grad_call(scal, xn, dpre, pieces, load, store, g_shapes):
     tiles, tokens, width = dpre.shape
     return call(
-        functools.partial(up_grad_kernel, store),
+        functools.partial(up_grad_kernel, load, store, len(pieces)),
         "up_grad",
         (scal, xn, dpre),
-        [],
-        [],
+        pieces,
+        [kept((4, width, width))],
         g_shapes,
-        [pltpu.VMEM((tiles, width, width), BF16), pltpu.SemaphoreType.DMA((len(g_shapes),))],
+        [
+            pltpu.VMEM((tiles, width, width), BF16),
+            pltpu.SemaphoreType.DMA((4,)),
+            pltpu.SemaphoreType.DMA((len(g_shapes),)),
+        ],
         2 * tiles * tokens * width * width,
+        limit=10,
     )
 
 
@@ -468,6 +479,7 @@
         [sds((tokens // 512, 512, width))],
         [pltpu.VMEM((tokens, width), BF16), pltpu.SemaphoreType.DMA],
         2 * (tiles + 3) * tokens * width * width,
+        limit=8,
     )
 
 
@@ -496,6 +508,7 @@
         [sds((tokens // 512, 512, width))],
         [pltpu.VMEM((tokens, width), BF16), pltpu.SemaphoreType.DMA],
         2 * (tiles + 1) * tokens * width * width,
+        limit=8,
     )
     return out
 
@@ -551,14 +564,12 @@
     return fn, [], values, [kept((len(values) * values[0].shape[0], *values[0].shape[1:]))]
 
 
-def mix(name, jobs, scal=None):
-    extra = [] if scal is None else [scal]
+def mix(name, jobs):
     held = [v for job in jobs for v in job[1]]
     near = [v for job in jobs for v in job[2]]
     outs = [o for job in jobs for o in job[3]]
 
     def kernel(*refs):
-        last, refs = refs[: len(extra)], refs[len(extra) :]
         at = len(near) + len(held)
         scratch = refs[at + len(outs) :]
         copies = [
@@ -572,7 +583,7 @@
                 copies[h + i].wait()
             fn(
                 scratch[h : h + len(job_h)],
-                (*refs[n : n + len(job_n)], *last),
+                refs[n : n + len(job_n)],
                 refs[at + o : at + o + len(job_o)],
             )
             h, n, o = h + len(job_h), n + len(job_n), o + len(job_o)
@@ -581,14 +592,13 @@
         kernel,
         name=name,
         out_shape=outs,
-        in_specs=[SMEM] * len(extra) + [VMEM] * len(near) + [HBM] * len(held),
+        in_specs=[VMEM] * len(near) + [HBM] * len(held),
         out_specs=[VMEM] * len(outs),
         scratch_shapes=[pltpu.VMEM(v.shape, v.dtype) for v in held]
         + [pltpu.SemaphoreType.DMA((max(len(held), 1),))],
         compiler_params=pltpu.CompilerParams(vmem_limit_bytes=8 << 20),
         cost_estimate=pl.CostEstimate(flops=1 << 20, bytes_accessed=1 << 20, transcendentals=0),
     )(
-        *extra,
         *[pltpu.with_memory_space_constraint(v, pltpu.VMEM) for v in near],
         *[pltpu.with_memory_space_constraint(v, pltpu.HBM) for v in held],
     )
@@ -641,13 +651,10 @@
         ):
             outs[4][:, at : at + got.shape[1]] = got
             at += got.shape[1]
-        for side in range(2):
-            for core in range(2):
-                out = outs[side * 2 + core]
-                out[...] = jnp.zeros_like(out)
-                for z in range(wide // 4):
-                    dev = (z * 2 + (scal[2] ^ side)) * 2 + (scal[3] ^ core)
-                    out[z : z + 1, :] = outs[4][pl.ds(dev, 1), :]
+        for k in range(4):
+            outs[k][...] = jnp.zeros_like(outs[k])
+            for r in range(4):
+                outs[k][r : r + 1, :] = outs[4][pl.ds((scal[1] ^ k) * 4 + r, 1), :]
 
     return fn, [], [sums_a, sums_d, sums_x], [kept((8, 8 * rows), F32)] * 4 + [kept((wide, 8 * rows), F32)]
 
@@ -659,14 +666,15 @@
     return fn, [], list(values), [kept(values[0].shape, F32)]
 
 
-def vector_z_job(mine, other):
+def vector_job(sums_a, sums_d, sums_x):
     def fn(held, near, outs):
-        outs[4][...] = near[0][...] + near[1][...]
-        for k in range(4):
-            outs[k][...] = jnp.zeros_like(outs[k])
-            outs[k][0:1, :] = outs[4][pl.ds(near[2][1] ^ k, 1), :]
-
-    return fn, [], [mine, other], [kept(mine.shape, F32)] * 5
+        a, d, x = near
+        outs[0][0:1, :] = x[0:1, :]
+        outs[0][1:3, :] = a[0:2, :]
+        outs[0][3:7, :] = d[0:4, :]
+        outs[0][7:8, :] = a[2:3, :]
+
+    return fn, [], [sums_a, sums_d, sums_x], [kept(sums_a.shape, F32)]
 
 
 def sum1_job(keep1, got1):
@@ -880,34 +888,52 @@
     )(scal, *[pltpu.with_memory_space_constraint(v, pltpu.HBM) for v in pieces])
 
 
-def store_with(source):
-    def store(scal, g, refs, sem):
-        for core in range(2):
-            for part, i, slot, half, side, k in slots():
-                at = core * 2 + i
-                dst = refs[at]
-                src = source(g, scal[0] ^ half, part, device_of(scal, k, side, core), dst.shape[2], dst.shape[3])
-                pltpu.make_async_copy(src, dst.at[part, slot], sem.at[at]).start()
-
-        def done():
-            for at in range(4):
-                whole_wait(refs[at], sem.at[at])()
-
-        return done
-
-    return store
-
-
 def rows_at(base, rows):
     return pl.ds(pl.multiple_of(base, 16), rows)
 
 
-def attn_source(g, half, part, dev, rows, cols):
-    return g.at[half * 2 + part, rows_at(dev * rows, rows), :]
-
-
-def down_source(g, half, part, dev, rows, cols):
-    return g.at[rows_at((dev * 4 + half * 2 + part) * rows, rows), :]
+def stored(refs, sem):
+    for i, r in enumerate(refs):
+        whole_wait(r, sem.at[i])()
+
+
+def store_block(scal, g, refs, sem, t):
+    half, part = scal[0] ^ (t // 2), t % 2
+    rows = refs[0].shape[2]
+
+    def send(at, core, side, k, slot, p):
+        src = g.at[t, rows_at(device_of(scal, k, side, core) * rows, rows), :]
+        pltpu.make_async_copy(src, refs[at].at[p, slot], sem.at[at]).start()
+
+    for i in range(2):
+
+        @pl.when((part == 0) & (half == i))
+        def _(i=i):
+            for core in range(2):
+                for side in range(2):
+                    for k in range(4):
+                        send(core * 2 + i, core, side, k, side * 4 + k, 0)
+
+    @pl.when(part == 1)
+    def _():
+        for core in range(2):
+            for side in range(2):
+                for k in range(4):
+                    send(core * 2 + side, core, side, k, half * 4 + k, 1)
+
+
+def store_rows(scal, g, refs, sem, t):
+    k = scal[1] ^ t
+    rows = refs[0].shape[2]
+    for core in range(2):
+        for side in range(2):
+            dev = (t * 2 + (scal[2] ^ side)) * 2 + (scal[3] ^ core)
+            for half in range(2):
+                for part in range(2):
+                    i, s = (half, side) if part == 0 else (side, half)
+                    at = core * 2 + i
+                    src = g.at[rows_at((dev * 4 + (scal[0] ^ half) * 2 + part) * rows, rows), :]
+                    pltpu.make_async_copy(src, refs[at].at[part, s * 4 + k], sem.at[at]).start()
 
 
 def load_whole_blocks(scal, refs, w, sem):
@@ -922,19 +948,17 @@
         pltpu.make_async_copy(refs[0].at[r, :], w.at[r, :], sem.at[t]).start()
 
 
-def store_whole(scal, g, refs, sem):
-    if len(refs) == 1:
-        copies = [pltpu.make_async_copy(g, refs[0], sem.at[0])]
-    else:
-        copies = [pltpu.make_async_copy(g.at[i], r, sem.at[i]) for i, r in enumerate(refs)]
-    for cp in copies:
-        cp.start()
-
-    def done():
-        for cp in copies:
-            cp.wait()
-
-    return done
+def store_whole_blocks(scal, g, refs, sem, t):
+    for i, r in enumerate(refs):
+
+        @pl.when(t == i)
+        def _(i=i, r=r):
+            pltpu.make_async_copy(g.at[i], r, sem.at[i]).start()
+
+
+def store_whole_rows(scal, g, refs, sem, t):
+    r = tile_of(t, g.shape[1])
+    pltpu.make_async_copy(g.at[r, :], refs[0].at[r, :], sem.at[0]).start()
 
 
 def body(sizes, tokens, image_ids, cotangent, w_joined, w_out, w_mlp, norm_gain, bias_attn, bias_mlp, bias_out):
@@ -983,18 +1007,18 @@
         down_w = [lax.all_gather(w_mlp, "wide", axis=0, tiled=True)]
         vec, b_mlp = vectors(lax.all_gather(vec_own, "wide", axis=0))
         square = [sds((width, width))]
-        xn, q, k, v, da, wa = project_call(scal, x, cot, vec, attn_w, load_whole_blocks)
+        xn, q, k, v, da = project_call(scal, x, cot, vec, attn_w, load_whole_blocks)
         o, d = core_call(0, scal, q, k, v, da)
         for b in range(1, last.shape[0]):
             o, d = core_call(b, scal, q, k, v, da, o, d)
-        sums_a, *g_attn = attn_grad_call(scal, xn, o, d, cot, store_whole, square * 4)
+        sums_a, *g_attn = attn_grad_call(scal, xn, o, d, cot, store_whole_blocks, square * 4)
         act, gp, wu = up_call(0, tiles // 2, scal, xn, b_mlp, (), up_w, load_whole_blocks)
         act, gp = up_call(tiles // 2, tiles - tiles // 2, scal, xn, b_mlp, (act, gp, wu), [], None)
         wd, *g_down = down_grad_call(
-            scal, act, cot, down_w, load_whole_rows, store_whole, [sds((tiles * width, width))]
+            scal, act, cot, down_w, load_whole_rows, store_whole_rows, [sds((tiles * width, width))]
         )
         dpre, sums_d = dpre_call(scal, cot, gp, wd)
-        g_up = up_grad_call(scal, xn, dpre, store_whole, square * tiles)
+        wa, *g_up = up_grad_call(scal, xn, dpre, attn_w, load_whole_blocks, store_whole_blocks, square * tiles)
         sums_x, d_x = input_grad_call(scal, x, cot, d, dpre, vec, wa, wu)
         out = out_call(scal, x, o, act, vec, wa, wd)
 
@@ -1006,6 +1030,7 @@
         grad_out = reduce(g_attn[3])
         grad_mlp = reduce(g_down[0])
         vg = reduce(vector_grads(sums_a, sums_d, sums_x))[0]
+        vg = jnp.split(vg, [rows, 3 * rows, (3 + tiles) * rows])
     else:
         col = lambda i: w_joined[:, i * width : (i + 1) * width]
         pair = lambda f: jnp.stack([jnp.where(n == 0, f(0), f(2)), jnp.where(n == 0, f(1), f(3))])
@@ -1030,7 +1055,7 @@
         cza, czb = [jnp.stack([t[i] for t in (c_half, c1, c2, c3)]) for i in range(2)]
         x_p, attn_w, cza, czb, vec, b_mlp = lax.optimization_barrier((x, attn_w, cza, czb, vec, b_mlp))
         c_first = gather_first(cza, czb)
-        xn, q, k, v, da, wa = project_call(scal, x_p, cot, vec, attn_w, load_columns)
+        xn, q, k, v, da = project_call(scal, x_p, cot, vec, attn_w, load_columns)
         part = core_call(0, scal, q, k, v, da)
 
         part, c_first = lax.optimization_barrier((part, c_first))
@@ -1044,7 +1069,7 @@
         d, c_joined = lax.optimization_barrier((d, c_joined))
         c_other = swap(c_joined, 1)
         attn_shapes = [sds((2, 8, rows, width))] * 4
-        sums_a, *ga = attn_grad_call(scal, xn, o, d, cot, store_with(attn_source), attn_shapes)
+        sums_a, *ga = attn_grad_call(scal, xn, o, d, cot, store_block, attn_shapes)
 
         c_other, ga = behind((c_other, ga), sums_a)
         xn_u, ga, c_own, c_other = lax.optimization_barrier((xn, ga, c_own, c_other))
@@ -1059,7 +1084,7 @@
         a_xy = swap_y(sa), swap(sb, 2)
         act, gp = up_call(half_tiles, half_tiles, scal, xn_u, b_mlp, (act, gp, wu), [], None)
         wd, *gd = down_grad_call(
-            scal, act, cot, c_all, load_half(1), store_with(down_source), attn_shapes
+            scal, act, cot, c_all, load_half(1), store_rows, attn_shapes
         )
 
         a_xy = behind(a_xy, gd)
@@ -1074,7 +1099,7 @@
         dpre_g, a_t, sa, sb = lax.optimization_barrier((dpre, a_t, sa, sb))
         d_xy = swap_y(sa), swap(sb, 2)
         a_z = [swap(a_t[k], k << 2) for k in (1, 2, 3)]
-        gu = up_grad_call(scal, xn, dpre_g, store_with(attn_source), attn_shapes)
+        wa, *gu = up_grad_call(scal, xn, dpre_g, attn_w, load_columns, store_block, attn_shapes)
 
         a_z, d_xy = behind((a_z, d_xy), gu)
         (a_sum,), (sa, sb) = mix("sums_4", [sum4_job(a_t[0], a_z), sum2_job(gd[0], d_got0, d_xy)])
@@ -1085,47 +1110,37 @@
         sums_x, d_x = input_grad_call(scal, x_i, cot, d, dpre, vec, wa, wu)
 
         d_yx, u_got1, u_got0, a_other = behind((d_yx, u_got1, u_got0, a_other), d_x)
-        (sa, sb), d_t, (*v_part, _) = mix(
+        (sa, sb), d_t, (v_own,) = mix(
             "sums_5",
             [
                 sum1_job(gu[1], u_got1),
                 sum3_job(gd[0], d_got0, d_xy, d_yx),
-                vector_job(sums_a, sums_d, sums_x, wide, rows),
+                vector_job(sums_a, sums_d, sums_x),
             ],
-            scal,
         )
         x_o, sa, sb, d_t = lax.optimization_barrier((x, sa, sb, d_t))
         u_xy = swap_y(sa), swap(sb, 2)
         d_z = [swap(d_t[k], k << 2) for k in (1, 2, 3)]
         out = out_call(scal, x_o, o, act, vec, wa, wd)
 
-        u_xy, d_z, v_part = behind((u_xy, d_z, v_part), out)
+        u_xy, d_z, v_own = behind((u_xy, d_z, v_own), out)
         (sa, sb), (d_sum,) = mix("sums_6", [sum2_job(gu[0], u_got0, u_xy), sum4_job(d_t[0], d_z)])
-        sa, sb, d_sum, v_part = lax.optimization_barrier((sa, sb, d_sum, v_part))
+        sa, sb, d_sum, v_own = lax.optimization_barrier((sa, sb, d_sum, v_own))
         u_yx = swap(sa, 2), swap_y(sb)
-        v_got = [swap(v_part[i], i) for i in (1, 2, 3)]
-        u_t, (v_sum,) = mix("sums_7", [sum3_job(gu[0], u_got0, u_xy, u_yx), add_job([v_part[0], *v_got])])
+        v_got = [swap(v_own, k << 2) for k in (1, 2, 3)]
+        u_t, (v_sum,) = mix("sums_7", [sum3_job(gu[0], u_got0, u_xy, u_yx), add_job([v_own, *v_got])])
         u_t, v_sum, d_sum = lax.optimization_barrier((u_t, v_sum, d_sum))
         u_z = [swap(u_t[k], k << 2) for k in (1, 2, 3)]
         v_other, d_other = swap_y(v_sum), swap_y(d_sum)
-        (u_sum,), (*v_z, _) = mix("sums_8", [sum4_job(u_t[0], u_z), vector_z_job(v_sum, v_other)], scal)
+        (u_sum,), (v_sum,) = mix("sums_8", [sum4_job(u_t[0], u_z), add_job([v_sum, v_other])])
         u_other = swap_y(u_sum)
-        vg = sum([v_z[0], *[swap(v_z[k], k << 2) for k in (1, 2, 3)]])[0]
+        vg = sum([v_sum, *[swap(v_sum, i) for i in (1, 2, 3)]])
+        own = lambda v, per: lax.dynamic_slice(v.reshape(-1), (w * per,), (per,))
+        vg = [own(vg[0], rows), own(vg[1:3], 2 * rows), own(vg[3:7], tiles * rows), own(vg[7], rows)]
         d_other = behind(d_other, u_sum)
         placed, grad_out, grad_mlp = place_call(scal, [a_sum, a_other, d_sum, d_other, u_sum])
         grad_joined = place_last_call(scal, placed, behind(u_other, grad_out))
-    b_at = 3 * rows
-    return (
-        out.reshape(tokens.shape),
-        d_x.reshape(tokens.shape),
-        grad_joined,
-        grad_out,
-        grad_mlp,
-        vg[:rows],
-        vg[rows:b_at],
-        vg[b_at : b_at + tiles * rows],
-        vg[b_at + tiles * rows :],
-    )
+    return (out.reshape(tokens.shape), d_x.reshape(tokens.shape), grad_joined, grad_out, grad_mlp, *vg)
 
 
 def solution(mesh):

time: 261 us -> 250 us (0.958)
  Pallas kernels: 116 us -> 109 us
  local copies, waits for them, and re-layouts: 12.5 us -> 8.49 us
    ppermute x45, waiting for transfers between devices: 54.8 us -> 45.7 us  [swap(): return lax.ppermute(value, 'wide', [(i, i ^ mask) for i in range(16)])]
    ppermute x16, waiting for transfers between devices: 8.17 us -> 14.9 us  [swap_y(): return lax.ppermute(value, 'narrow', [(0, 1), (1, 0)])]
    unnamed x64 -> x56, local copies, waits for them, and re-layouts: 6.81 us -> 2.22 us
    pallas_call x10, Pallas kernels: 17 us -> 13.6 us  [mix(): pl.pallas_call(kernel, name=name, out_shape=outs, in_specs=[VMEM] * len(n...]
    pallas_call x11, Pallas kernels: 93.2 us -> 90 us  [call(): pl.pallas_call(kernel, name=name, out_shape=list(outs) + list(g_shapes),...]
  transfers between devices with their start and end apart: 61 -> 61, of which waited for: 15 -> 16; matrix products, arithmetic and copies ran while one was open for 3% -> 3% of each run, Pallas kernels for 38% -> 38%
where the time goes in v5:
time: 250 us; the launch traced here: 249 us
  Pallas kernels  109 us (44%)
  starting transfers between devices  66.1 us (26%)
  waiting for transfers between devices  60.6 us (24%)
  local copies, waits for them, and re-layouts  8.49 us (3%)
  other arithmetic  3.09 us (1%)
    pallas_call x11, Pallas kernels, call(): pl.pallas_call(kernel, name=name, out_shape=list(outs) + list(g_shapes),...  90 us
    ppermute x45, starting transfers between devices, swap(): return lax.ppermute(value, 'wide', [(i, i ^ mask) for i in range(16)])  50.4 us
    ppermute x45, waiting for transfers between devices, swap(): return lax.ppermute(value, 'wide', [(i, i ^ mask) for i in range(16)])  45.7 us
    ppermute x16, starting transfers between devices, swap_y(): return lax.ppermute(value, 'narrow', [(0, 1), (1, 0)])  15.7 us
    ppermute x16, waiting for transfers between devices, swap_y(): return lax.ppermute(value, 'narrow', [(0, 1), (1, 0)])  14.9 us
    pallas_call x10, Pallas kernels, mix(): pl.pallas_call(kernel, name=name, out_shape=outs, in_specs=[VMEM] * len(n...  13.6 us
  transfers between devices with their start and end apart: 61, of which 16 were waited for; matrix products, arithmetic and copies ran while one was open for 3% of the time, Pallas kernels for 38%

profile of v5, /device:TPU:0, one launch (start us, length us, event | category | flops | bytes accessed | tf_op | source)
XLA Modules:
  0.0 249.2 jit_solution(14891933631421206346)
XLA Ops:
  0.7 1.3 select_bitcast_fusion.3
  2.7 3.1 %collective-permute-start = (bf16[2,56,768]{2,1,0:T(8,128)(2,1)S(1)}, bf16[2,56,768]{2,1,0:T(8,128)(2,1)S(1)}, u32[]{:S(2)}, u32[]{:S(2)}) collective-permute-start(bf16[2,56,768]{2,1,0:T(8,128)(2,1)S(1)} %pad_maximum_fusion.5), channel_id=1, source_target_pairs={{0,4},{1,5},{2,6},{3,7},{4,0},{5,1},{6,2},{7,3},{8,12},{9,13},{10,... | collective-permute-start | bytes 516104 | tf_op jit(solution)/shard_map/ppermute | solution.py:517
  5.8 2.6 %collective-permute-start.1 = (bf16[2,56,768]{2,1,0:T(8,128)(2,1)S(1)}, bf16[2,56,768]{2,1,0:T(8,128)(2,1)S(1)}, u32[]{:S(2)}, u32[]{:S(2)}) collective-permute-start(bf16[2,56,768]{2,1,0:T(8,128)(2,1)S(1)} %pad_maximum_fusion.5), channel_id=1, source_target_pairs={{0,8},{1,9},{2,10},{3,11},{4,12},{5,13},{6,14},{7,15},{8,0},{9,1},... | collective-permute-start | bytes 516104 | tf_op jit(solution)/shard_map/ppermute | solution.py:517
  8.4 4.5 %collective-permute-done = bf16[2,56,768]{2,1,0:T(8,128)(2,1)S(1)} collective-permute-done((bf16[2,56,768]{2,1,0:T(8,128)(2,1)S(1)}, bf16[2,56,768]{2,1,0:T(8,128)(2,1)S(1)}, u32[]{:S(2)}, u32[]{:S(2)}) %collective-permute-start) | collective-permute-done | bytes 172064 | tf_op jit(solution)/shard_map/ppermute | solution.py:517
  12.9 8.5 %collective-permute-done.1 = bf16[2,56,768]{2,1,0:T(8,128)(2,1)S(1)} collective-permute-done((bf16[2,56,768]{2,1,0:T(8,128)(2,1)S(1)}, bf16[2,56,768]{2,1,0:T(8,128)(2,1)S(1)}, u32[]{:S(2)}, u32[]{:S(2)}) %collective-permute-start.1) | collective-permute-done | bytes 172064 | tf_op jit(solution)/shard_map/ppermute | solution.py:517
  21.5 1.6 collective-permute-start.3
  23.1 1.5 collective-permute-start.5
  26.5 3.8 %collective-permute-start.7 = (bf16[2,2,48,768]{3,2,1,0:T(8,128)(2,1)}, bf16[2,2,48,768]{3,2,1,0:T(8,128)(2,1)S(1)}, u32[]{:S(2)}, u32[]{:S(2)}) collective-permute-start(bf16[2,2,48,768]{3,2,1,0:T(8,128)(2,1)} %bitcast.14), channel_id=1, source_target_pairs={{0,8},{1,9},{2,10},{3,11},{4,12},{5,13},{6,14},{7,15},{8,0},{9,1},... | collective-permute-start | bytes 884744 | tf_op jit(solution)/shard_map/ppermute | solution.py:517
  30.3 11.4 %collective-permute-done.7 = bf16[2,2,48,768]{3,2,1,0:T(8,128)(2,1)S(1)} collective-permute-done((bf16[2,2,48,768]{3,2,1,0:T(8,128)(2,1)}, bf16[2,2,48,768]{3,2,1,0:T(8,128)(2,1)S(1)}, u32[]{:S(2)}, u32[]{:S(2)}) %collective-permute-start.7) | collective-permute-done | bytes 294944 | tf_op jit(solution)/shard_map/ppermute | solution.py:517
  41.7 1.4 join_a.1
  43.2 1.6 collective-permute-start.8
  44.9 1.5 collective-permute-start.9
  46.4 1.5 collective-permute-start.12
  47.8 1.3 fusion.16
  49.2 1.4 stack.55.scal.refs_0_
  51.6 10.1 %collective-permute-done.11 = bf16[2,2,48,768]{3,2,1,0:T(8,128)(2,1)S(1)} collective-permute-done((bf16[2,2,48,768]{3,2,1,0:T(8,128)(2,1)}, bf16[2,2,48,768]{3,2,1,0:T(8,128)(2,1)S(1)}, u32[]{:S(2)}, u32[]{:S(2)}) %collective-permute-start.11) | collective-permute-done | bytes 294944 | tf_op jit(solution)/shard_map/ppermute | solution.py:517
  62.3 1.8 vectors.1
  65.9 1.5 collective-permute-start.16
  68.5 8.5 %project.1 = (bf16[1024,768]{1,0:T(8,128)(2,1)S(1)}, bf16[1024,768]{1,0:T(8,128)(2,1)S(1)}, bf16[1024,768]{1,0:T(8,128)(2,1)S(1)}, bf16[1024,768]{1,0:T(8,128)(2,1)S(1)}, bf16[1024,768]{1,0:T(8,128)(2,1)S(1)}) custom-call(s32[10]{0:T(128)S(1)} %stack.55.scal.refs_0_, bf16[1024,768]{1,0:T(8,128)(2,1)S(1)} %bitcast.30, bf16[1024,768]{1,0:T(8,128)(2,1)S(1)} %bitcast.25, ...), custom_call_target="tpu_custom_call" | custom-call | flops 4831838208 | bytes 1048576 | tf_op jit(solution)/shard_map/project/pallas_call | solution.py:139
  77.0 8.4 %core.2 = (bf16[1024,768]{1,0:T(8,128)(2,1)S(1)}, bf16[3,1024,768]{2,1,0:T(8,128)(2,1)S(1)}) custom-call(s32[10]{0:T(128)S(1)} %stack.55.scal.refs_0_, bf16[1024,768]{1,0:T(8,128)(2,1)S(1)} %get-tuple-element.233.q, bf16[1024,768]{1,0:T(8,128)(2,1)S(1)} %get-tuple-element.234.k, bf16[1024,768]{1,0:T(8,128)(2,1)S(1)} %get-tuple-element.235.v, ...), custom_call_target="tpu_custom_call" | custom-call | flops 10737418240 | bytes 1048576 | tf_op jit(solution)/shard_map/core/pallas_call | solution.py:139
  86.0 7.1 %collective-permute-done.16.refs_4_.refs_9_.refs_6_ = bf16[4,2,48,768]{3,2,1,0:T(8,128)(2,1)S(1)} collective-permute-done((bf16[4,2,48,768]{3,2,1,0:T(8,128)(2,1)S(1)}, bf16[4,2,48,768]{3,2,1,0:T(8,128)(2,1)S(1)}, u32[]{:S(2)}, u32[]{:S(2)}) %collective-permute-start.16) | collective-permute-done | bytes 589856 | tf_op jit(solution)/shard_map/ppermute | solution.py:521
  94.7 8.4 %core.3 = (bf16[1024,768]{1,0:T(8,128)(2,1)S(1)}, bf16[3,1024,768]{2,1,0:T(8,128)(2,1)S(1)}) custom-call(s32[10]{0:T(128)S(1)} %stack.55.scal.refs_0_, bf16[1024,768]{1,0:T(8,128)(2,1)S(1)} %get-tuple-element.233.q, bf16[1024,768]{1,0:T(8,128)(2,1)S(1)} %get-tuple-element.234.k, ...), custom_call_target="tpu_custom_call", output_to_operand_aliasing={{0}: (5, {}), {1}: (6, {})} | custom-call | flops 10737418240 | bytes 1048576 | tf_op jit(solution)/shard_map/core/pallas_call | solution.py:139
  103.1 4.2 %collective-permute-done.19.refs_2_.refs_6_.refs_3_ = bf16[4,2,48,768]{3,2,1,0:T(8,128)(2,1)S(1)} collective-permute-done((bf16[4,2,48,768]{3,2,1,0:T(8,128)(2,1)S(1)}, bf16[4,2,48,768]{3,2,1,0:T(8,128)(2,1)S(1)}, u32[]{:S(2)}, u32[]{:S(2)}) %collective-permute-start.19) | collective-permute-done | bytes 589856 | tf_op jit(solution)/shard_map/ppermute | solution.py:521
  108.5 7.8 %attn_grad.1 = (f32[8,768]{1,0:T(8,128)S(1)}, bf16[2,8,48,768]{3,2,1,0:T(8,128)(2,1)}, bf16[2,8,48,768]{3,2,1,0:T(8,128)(2,1)}, bf16[2,8,48,768]{3,2,1,0:T(8,128)(2,1)}, bf16[2,8,48,768]{3,2,1,0:T(8,128)(2,1)}) custom-call(s32[10]{0:T(128)S(1)} %stack.55.scal.refs_0_, bf16[1024,768]{1,0:T(8,128)(2,1)S(1)} %get-tuple-element.264.xn.refs_1_, ...), custom_call_target="tpu_custom_call" | custom-call | flops 4831838208 | bytes 1048576 | tf_op jit(solution)/shard_map/attn_grad/pallas_call | solution.py:139
  117.0 1.2 copy-done.15
  118.1 8.1 %up.2 = (bf16[4,1024,768]{2,1,0:T(8,128)(2,1)S(1)}, bf16[4,1024,768]{2,1,0:T(8,128)(2,1)S(1)}, bf16[4,768,768]{2,1,0:T(8,128)(2,1)S(1)}) custom-call(s32[10]{0:T(128)S(1)} %stack.55.scal.refs_0_, bf16[1024,768]{1,0:T(8,128)(2,1)S(1)} %get-tuple-element.264.xn.refs_1_, f32[4,768]{1,0:T(4,128)S(1)} %get-tuple-element.265.refs_2_, ...), custom_call_target="tpu_custom_call" | custom-call | flops 2415919104 | bytes 1048576 | tf_op jit(solution)/shard_map/up/pallas_call | solution.py:139
  126.3 1.6 sums_1.1
  127.8 1.7 collective-permute-start.26
  129.6 5.3 %collective-permute-start.27 = (bf16[8,48,768]{2,1,0:T(8,128)(2,1)S(1)}, bf16[8,48,768]{2,1,0:T(8,128)(2,1)S(1)}, u32[]{:S(2)}, u32[]{:S(2)}) collective-permute-start(bf16[8,48,768]{2,1,0:T(8,128)(2,1)S(1)} %get-tuple-element.290), channel_id=1, source_target_pairs={{0,2},{1,3},{2,0},{3,1},{4,6},{5,7},{6,4},{7,5},{8,10},{9,11},{10,... | collective-permute-start | bytes 1769480 | tf_op jit(solution)/shard_map/ppermute | solution.py:517
  134.9 6.0 %up.3 = (bf16[4,1024,768]{2,1,0:T(8,128)(2,1)S(1)}, bf16[4,1024,768]{2,1,0:T(8,128)(2,1)S(1)}) custom-call(s32[10]{0:T(128)S(1)} %stack.55.scal.refs_0_, bf16[1024,768]{1,0:T(8,128)(2,1)S(1)} %get-tuple-element.264.xn.refs_1_, f32[4,768]{1,0:T(4,128)S(1)} %get-tuple-element.265.refs_2_, ...), custom_call_target="tpu_custom_call", output_to_operand_aliasing={{0}: (3, {}), {1}: (4, {})} | custom-call | flops 2415919104 | bytes 1048576 | tf_op jit(solution)/shard_map/up/pallas_call | solution.py:139
  141.0 7.6 %down_grad.1 = (bf16[3072,768]{1,0:T(8,128)(2,1)S(1)}, bf16[2,8,48,768]{3,2,1,0:T(8,128)(2,1)}, bf16[2,8,48,768]{3,2,1,0:T(8,128)(2,1)}, bf16[2,8,48,768]{3,2,1,0:T(8,128)(2,1)}, bf16[2,8,48,768]{3,2,1,0:T(8,128)(2,1)}) custom-call(s32[10]{0:T(128)S(1)} %stack.55.scal.refs_0_, bf16[4,1024,768]{2,1,0:T(8,128)(2,1)S(1)} %get-tuple-element.291.act, ...), custom_call_target="tpu_custom_call" | custom-call | flops 4831838208 | bytes 1048576 | tf_op jit(solution)/shard_map/down_grad/pallas_call | solution.py:139
  148.6 1.6 sums_2.1
  151.5 7.1 %dpre.1 = (bf16[4,1024,768]{2,1,0:T(8,128)(2,1)S(1)}, f32[8,768]{1,0:T(8,128)S(1)}) custom-call(s32[10]{0:T(128)S(1)} %stack.55.scal.refs_0_, bf16[1024,768]{1,0:T(8,128)(2,1)S(1)} %bitcast.28, bf16[4,1024,768]{2,1,0:T(8,128)(2,1)S(1)} %get-tuple-element.301.gp, bf16[3072,768]{1,0:T(8,128)(2,1)S(1)} %get-tuple-element.302.w.wd), custom_call_target="tpu_custom_call", output_to_operand_aliasing={{0}: (2, {})} | custom-call | flops 4831838208 | bytes 1048576 | tf_op jit(solution)/shard_map/dpre/pallas_call | solution.py:139
  158.6 1.4 collective-permute-done.28.refs_3_
  160.1 2.0 sums_3.1
  162.5 1.6 collective-permute-start.36
  164.1 1.4 collective-permute-start.33
  165.6 2.9 %collective-permute-start.34 = (bf16[2,48,768]{2,1,0:T(8,128)(2,1)S(1)}, bf16[2,48,768]{2,1,0:T(8,128)(2,1)S(1)}, u32[]{:S(2)}, u32[]{:S(2)}) collective-permute-start(bf16[2,48,768]{2,1,0:T(8,128)(2,1)S(1)} %get-tuple-element.321), channel_id=1, source_target_pairs={{0,12},{1,13},{2,14},{3,15},{4,8},{5,9},{6,10},{7,11},{8,4},{9,5},... | collective-permute-start | bytes 442376 | tf_op jit(solution)/shard_map/ppermute | solution.py:517
  168.5 8.0 %up_grad.1 = (bf16[4,768,768]{2,1,0:T(8,128)(2,1)S(1)}, bf16[2,8,48,768]{3,2,1,0:T(8,128)(2,1)}, bf16[2,8,48,768]{3,2,1,0:T(8,128)(2,1)}, bf16[2,8,48,768]{3,2,1,0:T(8,128)(2,1)}, bf16[2,8,48,768]{3,2,1,0:T(8,128)(2,1)}) custom-call(s32[10]{0:T(128)S(1)} %stack.55.scal.refs_0_, bf16[1024,768]{1,0:T(8,128)(2,1)S(1)} %get-tuple-element.264.xn.refs_1_, ...), custom_call_target="tpu_custom_call" | custom-call | flops 4831838208 | bytes 1048576 | tf_op jit(solution)/shard_map/up_grad/pallas_call | solution.py:139
  176.5 1.2 collective-permute-done.33.refs_2_
  177.8 1.6 sums_4.1
  181.0 1.1 collective-permute-start.38
  183.0 11.9 %input_grad.1 = (f32[8,768]{1,0:T(8,128)S(1)}, bf16[2,512,768]{2,1,0:T(8,128)(2,1)}) custom-call(s32[10]{0:T(128)S(1)} %stack.55.scal.refs_0_, bf16[1024,768]{1,0:T(8,128)(2,1)S(1)} %bitcast.31, bf16[1024,768]{1,0:T(8,128)(2,1)S(1)} %bitcast.29, bf16[3,1024,768]{2,1,0:T(8,128)(2,1)S(1)} %bitcast.34, bf16[4,1024,768]{2,1,0:T(8,128)(2,1)S(1)} %get-tuple-element.324.dpre, ...), custom_call_target="tpu_custom_call" | custom-call | flops 8455716864 | bytes 1048576 | tf_op jit(solution)/shard_map/input_grad/pallas_call | solution.py:139
  195.0 1.9 sums_5.1
  196.9 1.2 collective-permute-start.42
  198.2 1.1 collective-permute-start.43
  199.3 2.1 collective-permute-start.44
  201.4 2.4 collective-permute-start.46
  203.8 8.1 %out.1 = bf16[2,512,768]{2,1,0:T(8,128)(2,1)} custom-call(s32[10]{0:T(128)S(1)} %stack.55.scal.refs_0_, bf16[1024,768]{1,0:T(8,128)(2,1)S(1)} %bitcast.32, bf16[1024,768]{1,0:T(8,128)(2,1)S(1)} %get-tuple-element.252.o, bf16[4,1024,768]{2,1,0:T(8,128)(2,1)S(1)} %get-tuple-element.291.act, f32[8,768]{1,0:T(8,128)S(1)} %get-tuple-element.220.refs_3_.vec, ...), custom_call_target="tpu_custom_call" | custom-call | flops 6039797760 | bytes 1048576 | tf_op jit(solution)/shard_map/out/pallas_call | solution.py:139
  211.9 2.2 collective-permute-done.45.refs_5_
  214.1 1.6 sums_6.1
  217.0 2.6 %collective-permute-start.49 = (f32[8,768]{1,0:T(8,128)S(1)}, f32[8,768]{1,0:T(8,128)S(1)}, u32[]{:S(2)}, u32[]{:S(2)}) collective-permute-start(f32[8,768]{1,0:T(8,128)S(1)} %get-tuple-element.381.refs_5_), channel_id=1, source_target_pairs={{0,4},{1,5},{2,6},{3,7},{4,0},{5,1},{6,2},{7,3},{8,12},{9,13},{10,... | collective-permute-start | bytes 73736 | tf_op jit(solution)/shard_map/ppermute | solution.py:517
  219.6 2.3 collective-permute-start.51
  221.9 2.4 collective-permute-done.50.refs_7_
  225.2 1.6 sums_7.1
  226.8 1.4 collective-permute-start.53
  228.2 1.6 collective-permute-start.54
  229.8 1.5 collective-permute-start.55
  231.3 1.4 collective-permute-start.52
  233.3 3.4 %collective-permute-done.56.refs_5_ = f32[8,768]{1,0:T(8,128)S(1)} collective-permute-done((f32[8,768]{1,0:T(8,128)S(1)}, f32[8,768]{1,0:T(8,128)S(1)}, u32[]{:S(2)}, u32[]{:S(2)}) %collective-permute-start.56) | collective-permute-done | bytes 24608 | tf_op jit(solution)/shard_map/ppermute | solution.py:521
  236.7 2.8 %collective-permute-done.54.refs_2_ = bf16[2,48,768]{2,1,0:T(8,128)(2,1)S(1)} collective-permute-done((bf16[2,48,768]{2,1,0:T(8,128)(2,1)S(1)}, bf16[2,48,768]{2,1,0:T(8,128)(2,1)S(1)}, u32[]{:S(2)}, u32[]{:S(2)}) %collective-permute-start.54) | collective-permute-done | bytes 147488 | tf_op jit(solution)/shard_map/ppermute | solution.py:517
  239.6 1.6 collective-permute-start.59
  242.5 2.4 place.1
  247.6 1.4 place_last.1
  (167 shorter events, 22.4 us)
Async XLA Ops:
  2.7 10.2 %collective-permute-start = (bf16[2,56,768]{2,1,0:T(8,128)(2,1)S(1)}, bf16[2,56,768]{2,1,0:T(8,128)(2,1)S(1)}, u32[]{:S(2)}, u32[]{:S(2)}) collective-permute-start(bf16[2,56,768]{2,1,0:T(8,128)(2,1)S(1)} %pad_maximum_fusion.5), channel_id=1, source_target_pairs={{0,4},{1,5},{2,6},{3,7},{4,0},{5,1},{6,2},{7,3},{8,12},{9,13},{10,... | collective-permute-start | bytes 516104 | tf_op jit(solution)/shard_map/ppermute | solution.py:517
  5.8 15.6 %collective-permute-start.1 = (bf16[2,56,768]{2,1,0:T(8,128)(2,1)S(1)}, bf16[2,56,768]{2,1,0:T(8,128)(2,1)S(1)}, u32[]{:S(2)}, u32[]{:S(2)}) collective-permute-start(bf16[2,56,768]{2,1,0:T(8,128)(2,1)S(1)} %pad_maximum_fusion.5), channel_id=1, source_target_pairs={{0,8},{1,9},{2,10},{3,11},{4,12},{5,13},{6,14},{7,15},{8,0},{9,1},... | collective-permute-start | bytes 516104 | tf_op jit(solution)/shard_map/ppermute | solution.py:517
  8.4 13.0 %collective-permute-start.2 = (bf16[2,56,768]{2,1,0:T(8,128)(2,1)S(1)}, bf16[2,56,768]{2,1,0:T(8,128)(2,1)S(1)}, u32[]{:S(2)}, u32[]{:S(2)}) collective-permute-start(bf16[2,56,768]{2,1,0:T(8,128)(2,1)S(1)} %pad_maximum_fusion.5), channel_id=1, source_target_pairs={{0,12},{1,13},{2,14},{3,15},{4,8},{5,9},{6,10},{7,11},{8,4},{9,5},... | collective-permute-start | bytes 516104 | tf_op jit(solution)/shard_map/ppermute | solution.py:517
  21.5 20.2 %collective-permute-start.3 = (bf16[4,56,768]{2,1,0:T(8,128)(2,1)S(1)}, bf16[4,56,768]{2,1,0:T(8,128)(2,1)S(1)}, u32[]{:S(2)}, u32[]{:S(2)}) collective-permute-start(bf16[4,56,768]{2,1,0:T(8,128)(2,1)S(1)} %pad_maximum_fusion.2.refs_0_.refs_4_), channel_id=1, source_target_pairs={{0,2},{1,3},{2,0},{3,1},{4,6},{5,7},{6,4},{7,5},{8,10},{9,11},{10,... | collective-permute-start | bytes 1032200 | tf_op jit(solution)/shard_map/ppermute | solution.py:517
  23.1 18.6 %collective-permute-start.5 = (bf16[4,56,768]{2,1,0:T(8,128)(2,1)S(1)}, bf16[4,56,768]{2,1,0:T(8,128)(2,1)S(1)}, u32[]{:S(2)}, u32[]{:S(2)}) collective-permute-start(bf16[4,56,768]{2,1,0:T(8,128)(2,1)S(1)} %pad_maximum_fusion.2.refs_0_.refs_4_), channel_id=1, source_target_pairs={{0,16},{16,0},{1,17},{17,1},{2,18},{18,2},{3,19},{19,3},{4,20},{20... | collective-permute-start | bytes 1032200 | tf_op jit(solution)/shard_map/ppermute | solution.py:521
  24.7 17.0 %collective-permute-start.4 = (bf16[4,56,768]{2,1,0:T(8,128)(2,1)S(1)}, bf16[4,56,768]{2,1,0:T(8,128)(2,1)}, u32[]{:S(2)}, u32[]{:S(2)}) collective-permute-start(bf16[4,56,768]{2,1,0:T(8,128)(2,1)S(1)} %pad_maximum_fusion.3.refs_3_.refs_8_.refs_4_), channel_id=1, source_target_pairs={{0,16},{16,0},{1,17},{17,1},{2,18},{18,2},{3,19},{19,3},{4,20},{20... | collective-permute-start | bytes 1032200 | tf_op jit(solution)/shard_map/ppermute | solution.py:521
  25.2 16.5 %collective-permute-start.6 = (bf16[4,56,768]{2,1,0:T(8,128)(2,1)S(1)}, bf16[4,56,768]{2,1,0:T(8,128)(2,1)S(1)}, u32[]{:S(2)}, u32[]{:S(2)}) collective-permute-start(bf16[4,56,768]{2,1,0:T(8,128)(2,1)S(1)} %pad_maximum_fusion.3.refs_3_.refs_8_.refs_4_), channel_id=1, source_target_pairs={{0,2},{1,3},{2,0},{3,1},{4,6},{5,7},{6,4},{7,5},{8,10},{9,11},{10,... | collective-permute-start | bytes 1032200 | tf_op jit(solution)/shard_map/ppermute | solution.py:517
  26.5 15.2 %collective-permute-start.7 = (bf16[2,2,48,768]{3,2,1,0:T(8,128)(2,1)}, bf16[2,2,48,768]{3,2,1,0:T(8,128)(2,1)S(1)}, u32[]{:S(2)}, u32[]{:S(2)}) collective-permute-start(bf16[2,2,48,768]{3,2,1,0:T(8,128)(2,1)} %bitcast.14), channel_id=1, source_target_pairs={{0,8},{1,9},{2,10},{3,11},{4,12},{5,13},{6,14},{7,15},{8,0},{9,1},... | collective-permute-start | bytes 884744 | tf_op jit(solution)/shard_map/ppermute | solution.py:517
  43.2 18.5 %collective-permute-start.10 = (bf16[24,56,768]{2,1,0:T(8,128)(2,1)S(1)}, bf16[24,56,768]{2,1,0:T(8,128)(2,1)}, u32[]{:S(2)}, u32[]{:S(2)}) collective-permute-start(bf16[24,56,768]{2,1,0:T(8,128)(2,1)S(1)} %join_a.1), channel_id=1, source_target_pairs={{0,1},{1,0},{2,3},{3,2},{4,5},{5,4},{6,7},{7,6},{8,9},{9,8},{10,11... | collective-permute-start | bytes 6193160 | tf_op jit(solution)/shard_map/ppermute | solution.py:517
  43.2 18.4 %collective-permute-start.8 = (bf16[4,56,768]{2,1,0:T(8,128)(2,1)S(1)}, bf16[4,56,768]{2,1,0:T(8,128)(2,1)}, u32[]{:S(2)}, u32[]{:S(2)}) collective-permute-start(bf16[4,56,768]{2,1,0:T(8,128)(2,1)S(1)} %collective-permute-done.3.refs_1_.refs_5_), channel_id=1, source_target_pairs={{0,16},{16,0},{1,17},{17,1},{2,18},{18,2},{3,19},{19,3},{4,20},{20... | collective-permute-start | bytes 1032200 | tf_op jit(solution)/shard_map/ppermute | solution.py:521
  44.9 16.8 %collective-permute-start.9 = (bf16[4,56,768]{2,1,0:T(8,128)(2,1)}, bf16[4,56,768]{2,1,0:T(8,128)(2,1)}, u32[]{:S(2)}, u32[]{:S(2)}) collective-permute-start(bf16[4,56,768]{2,1,0:T(8,128)(2,1)} %collective-permute-done.4.refs_5_.refs_10_.refs_6_), channel_id=1, source_target_pairs={{0,2},{1,3},{2,0},{3,1},{4,6},{5,7},{6,4},{7,5},{8,10},{9,11},{10,... | collective-permute-start | bytes 1032200 | tf_op jit(solution)/shard_map/ppermute | solution.py:517
  46.3 15.3 %collective-permute-start.11 = (bf16[2,2,48,768]{3,2,1,0:T(8,128)(2,1)}, bf16[2,2,48,768]{3,2,1,0:T(8,128)(2,1)S(1)}, u32[]{:S(2)}, u32[]{:S(2)}) collective-permute-start(bf16[2,2,48,768]{3,2,1,0:T(8,128)(2,1)} %bitcast.14), channel_id=1, source_target_pairs={{0,4},{1,5},{2,6},{3,7},{4,0},{5,1},{6,2},{7,3},{8,12},{9,13},{10,... | collective-permute-start | bytes 884744 | tf_op jit(solution)/shard_map/ppermute | solution.py:517
  46.4 15.3 %collective-permute-start.12 = (bf16[2,2,48,768]{3,2,1,0:T(8,128)(2,1)}, bf16[2,2,48,768]{3,2,1,0:T(8,128)(2,1)S(1)}, u32[]{:S(2)}, u32[]{:S(2)}) collective-permute-start(bf16[2,2,48,768]{3,2,1,0:T(8,128)(2,1)} %bitcast.14), channel_id=1, source_target_pairs={{0,12},{1,13},{2,14},{3,15},{4,8},{5,9},{6,10},{7,11},{8,4},{9,5},... | collective-permute-start | bytes 884744 | tf_op jit(solution)/shard_map/ppermute | solution.py:517
  50.5 153.3 %copy-start.11 = (s32[10]{0:T(128)}, s32[10]{0:T(128)S(1)}, u32[]{:S(2)}) copy-start(s32[10]{0:T(128)S(1)} %stack.55.scal.refs_0_) | copy-start | bytes 124
  61.7 2.6 %collective-permute-start.13 = (bf16[4,56,768]{2,1,0:T(8,128)(2,1)}, bf16[4,56,768]{2,1,0:T(8,128)(2,1)S(1)}, u32[]{:S(2)}, u32[]{:S(2)}) collective-permute-start(bf16[4,56,768]{2,1,0:T(8,128)(2,1)} %collective-permute-done.8.refs_7_.refs_3_), channel_id=1, source_target_pairs={{0,1},{1,0},{2,3},{3,2},{4,5},{5,4},{6,7},{7,6},{8,9},{9,8},{10,11... | collective-permute-start | bytes 1032200 | tf_op jit(solution)/shard_map/ppermute | solution.py:517
  61.8 2.6 %collective-permute-start.14 = (bf16[4,56,768]{2,1,0:T(8,128)(2,1)}, bf16[4,56,768]{2,1,0:T(8,128)(2,1)S(1)}, u32[]{:S(2)}, u32[]{:S(2)}) collective-permute-start(bf16[4,56,768]{2,1,0:T(8,128)(2,1)} %collective-permute-done.9.refs_11_.refs_7_), channel_id=1, source_target_pairs={{0,1},{1,0},{2,3},{3,2},{4,5},{5,4},{6,7},{7,6},{8,9},{9,8},{10,11... | collective-permute-start | bytes 1032200 | tf_op jit(solution)/shard_map/ppermute | solution.py:517
  64.3 21.1 %collective-permute-start.15 = (bf16[4,2,48,768]{3,2,1,0:T(8,128)(2,1)S(1)}, bf16[4,2,48,768]{3,2,1,0:T(8,128)(2,1)S(1)}, u32[]{:S(2)}, u32[]{:S(2)}) collective-permute-start(bf16[4,2,48,768]{3,2,1,0:T(8,128)(2,1)S(1)} %pad_maximum_fusion.refs_3_.refs_0_), channel_id=1, source_target_pairs={{0,2},{1,3},{2,0},{3,1},{4,6},{5,7},{6,4},{7,5},{8,10},{9,11},{10,... | collective-permute-start | bytes 1769480 | tf_op jit(solution)/shard_map/ppermute | solution.py:517
  65.4 27.7 %collective-permute-start.17 = (bf16[4,2,48,768]{3,2,1,0:T(8,128)(2,1)S(1)}, bf16[4,2,48,768]{3,2,1,0:T(8,128)(2,1)S(1)}, u32[]{:S(2)}, u32[]{:S(2)}) collective-permute-start(bf16[4,2,48,768]{3,2,1,0:T(8,128)(2,1)S(1)} %pad_maximum_fusion.refs_3_.refs_0_), channel_id=1, source_target_pairs={{0,16},{16,0},{1,17},{17,1},{2,18},{18,2},{3,19},{19,3},{4,20},{20... | collective-permute-start | bytes 1769480 | tf_op jit(solution)/shard_map/ppermute | solution.py:521
  65.9 27.2 %collective-permute-start.16 = (bf16[4,2,48,768]{3,2,1,0:T(8,128)(2,1)S(1)}, bf16[4,2,48,768]{3,2,1,0:T(8,128)(2,1)S(1)}, u32[]{:S(2)}, u32[]{:S(2)}) collective-permute-start(bf16[4,2,48,768]{3,2,1,0:T(8,128)(2,1)S(1)} %pad_maximum_fusion.1.refs_7_.refs_4_), channel_id=1, source_target_pairs={{0,16},{16,0},{1,17},{17,1},{2,18},{18,2},{3,19},{19,3},{4,20},{20... | collective-permute-start | bytes 1769480 | tf_op jit(solution)/shard_map/ppermute | solution.py:521
  67.5 25.7 %collective-permute-start.18 = (bf16[4,2,48,768]{3,2,1,0:T(8,128)(2,1)S(1)}, bf16[4,2,48,768]{3,2,1,0:T(8,128)(2,1)S(1)}, u32[]{:S(2)}, u32[]{:S(2)}) collective-permute-start(bf16[4,2,48,768]{3,2,1,0:T(8,128)(2,1)S(1)} %pad_maximum_fusion.1.refs_7_.refs_4_), channel_id=1, source_target_pairs={{0,2},{1,3},{2,0},{3,1},{4,6},{5,7},{6,4},{7,5},{8,10},{9,11},{10,... | collective-permute-start | bytes 1769480 | tf_op jit(solution)/shard_map/ppermute | solution.py:517
  68.5 34.6 %collective-permute-start.21 = (bf16[4,2,48,768]{3,2,1,0:T(8,128)(2,1)S(1)}, bf16[4,2,48,768]{3,2,1,0:T(8,128)(2,1)S(1)}, u32[]{:S(2)}, u32[]{:S(2)}) collective-permute-start(bf16[4,2,48,768]{3,2,1,0:T(8,128)(2,1)S(1)} %pad_maximum_fusion.refs_3_.refs_0_), channel_id=1, source_target_pairs={{0,1},{1,0},{2,3},{3,2},{4,5},{5,4},{6,7},{7,6},{8,9},{9,8},{10,11... | collective-permute-start | bytes 1769480 | tf_op jit(solution)/shard_map/ppermute | solution.py:517
  85.4 22.3 %copy-start.1 = (bf16[4,2,48,768]{3,2,1,0:T(8,128)(2,1)}, bf16[4,2,48,768]{3,2,1,0:T(8,128)(2,1)S(1)}, u32[]{:S(2)}) copy-start(bf16[4,2,48,768]{3,2,1,0:T(8,128)(2,1)S(1)} %collective-permute-done.15.refs_0_.refs_4_.refs_1_) | copy-start | bytes 1769476
  85.4 17.7 %collective-permute-start.22 = (bf16[4,2,48,768]{3,2,1,0:T(8,128)(2,1)S(1)}, bf16[4,2,48,768]{3,2,1,0:T(8,128)(2,1)S(1)}, u32[]{:S(2)}, u32[]{:S(2)}) collective-permute-start(bf16[4,2,48,768]{3,2,1,0:T(8,128)(2,1)S(1)} %pad_maximum_fusion.1.refs_7_.refs_4_), channel_id=1, source_target_pairs={{0,1},{1,0},{2,3},{3,2},{4,5},{5,4},{6,7},{7,6},{8,9},{9,8},{10,11... | collective-permute-start | bytes 1769480 | tf_op jit(solution)/shard_map/ppermute | solution.py:517
  93.1 14.2 %collective-permute-start.19 = (bf16[4,2,48,768]{3,2,1,0:T(8,128)(2,1)S(1)}, bf16[4,2,48,768]{3,2,1,0:T(8,128)(2,1)S(1)}, u32[]{:S(2)}, u32[]{:S(2)}) collective-permute-start(bf16[4,2,48,768]{3,2,1,0:T(8,128)(2,1)S(1)} %collective-permute-done.15.refs_0_.refs_4_.refs_1_), channel_id=1, source_target_pairs={{0,16},{16,0},{1,17},{17,1},{2,18},{18,2},{3,19},{19,3},{4,20},{20... | collective-permute-start | bytes 1769480 | tf_op jit(solution)/shard_map/ppermute | solution.py:521
  93.7 14.0 %collective-permute-start.20 = (bf16[4,2,48,768]{3,2,1,0:T(8,128)(2,1)S(1)}, bf16[4,2,48,768]{3,2,1,0:T(8,128)(2,1)S(1)}, u32[]{:S(2)}, u32[]{:S(2)}) collective-permute-start(bf16[4,2,48,768]{3,2,1,0:T(8,128)(2,1)S(1)} %collective-permute-done.16.refs_4_.refs_9_.refs_6_), channel_id=1, source_target_pairs={{0,2},{1,3},{2,0},{3,1},{4,6},{5,7},{6,4},{7,5},{8,10},{9,11},{10,... | collective-permute-start | bytes 1769480 | tf_op jit(solution)/shard_map/ppermute | solution.py:517
  108.5 7.8 %collective-permute-start.23 = (bf16[24,2,48,768]{3,2,1,0:T(8,128)(2,1)S(1)}, bf16[24,2,48,768]{3,2,1,0:T(8,128)(2,1)S(1)}, u32[]{:S(2)}, u32[]{:S(2)}) collective-permute-start(bf16[24,2,48,768]{3,2,1,0:T(8,128)(2,1)S(1)} %join_c.1), channel_id=1, source_target_pairs={{0,1},{1,0},{2,3},{3,2},{4,5},{5,4},{6,7},{7,6},{8,9},{9,8},{10,11... | collective-permute-start | bytes 10616840 | tf_op jit(solution)/shard_map/ppermute | solution.py:517
  116.3 9.9 %collective-permute-start.24 = (bf16[2,8,48,768]{3,2,1,0:T(8,128)(2,1)}, bf16[2,8,48,768]{3,2,1,0:T(8,128)(2,1)S(1)}, u32[]{:S(2)}, u32[]{:S(2)}) collective-permute-start(bf16[2,8,48,768]{3,2,1,0:T(8,128)(2,1)} %get-tuple-element.278), channel_id=1, source_target_pairs={{0,1},{1,0},{2,3},{3,2},{4,5},{5,4},{6,7},{7,6},{8,9},{9,8},{10,11... | collective-permute-start | bytes 3538952 | tf_op jit(solution)/shard_map/ppermute | solution.py:517
  116.9 9.4 %collective-permute-start.25 = (bf16[2,8,48,768]{3,2,1,0:T(8,128)(2,1)}, bf16[2,8,48,768]{3,2,1,0:T(8,128)(2,1)S(1)}, u32[]{:S(2)}, u32[]{:S(2)}) collective-permute-start(bf16[2,8,48,768]{3,2,1,0:T(8,128)(2,1)} %get-tuple-element.279), channel_id=1, source_target_pairs={{0,1},{1,0},{2,3},{3,2},{4,5},{5,4},{6,7},{7,6},{8,9},{9,8},{10,11... | collective-permute-start | bytes 3538952 | tf_op jit(solution)/shard_map/ppermute | solution.py:517
  127.8 20.7 %collective-permute-start.26 = (bf16[8,48,768]{2,1,0:T(8,128)(2,1)S(1)}, bf16[8,48,768]{2,1,0:T(8,128)(2,1)S(1)}, u32[]{:S(2)}, u32[]{:S(2)}) collective-permute-start(bf16[8,48,768]{2,1,0:T(8,128)(2,1)S(1)} %get-tuple-element.289), channel_id=1, source_target_pairs={{0,16},{16,0},{1,17},{17,1},{2,18},{18,2},{3,19},{19,3},{4,20},{20... | collective-permute-start | bytes 1769480 | tf_op jit(solution)/shard_map/ppermute | solution.py:521
  129.6 19.0 %collective-permute-start.27 = (bf16[8,48,768]{2,1,0:T(8,128)(2,1)S(1)}, bf16[8,48,768]{2,1,0:T(8,128)(2,1)S(1)}, u32[]{:S(2)}, u32[]{:S(2)}) collective-permute-start(bf16[8,48,768]{2,1,0:T(8,128)(2,1)S(1)} %get-tuple-element.290), channel_id=1, source_target_pairs={{0,2},{1,3},{2,0},{3,1},{4,6},{5,7},{6,4},{7,5},{8,10},{9,11},{10,... | collective-permute-start | bytes 1769480 | tf_op jit(solution)/shard_map/ppermute | solution.py:517
  150.3 9.8 %collective-permute-start.30 = (bf16[2,8,48,768]{3,2,1,0:T(8,128)(2,1)S(1)}, bf16[2,8,48,768]{3,2,1,0:T(8,128)(2,1)S(1)}, u32[]{:S(2)}, u32[]{:S(2)}) collective-permute-start(bf16[2,8,48,768]{3,2,1,0:T(8,128)(2,1)S(1)} %copy-done.23), channel_id=1, source_target_pairs={{0,1},{1,0},{2,3},{3,2},{4,5},{5,4},{6,7},{7,6},{8,9},{9,8},{10,11... | collective-permute-start | bytes 3538952 | tf_op jit(solution)/shard_map/ppermute | solution.py:517
  150.6 9.5 %collective-permute-start.31 = (bf16[2,8,48,768]{3,2,1,0:T(8,128)(2,1)S(1)}, bf16[2,8,48,768]{3,2,1,0:T(8,128)(2,1)S(1)}, u32[]{:S(2)}, u32[]{:S(2)}) collective-permute-start(bf16[2,8,48,768]{3,2,1,0:T(8,128)(2,1)S(1)} %copy-done.22), channel_id=1, source_target_pairs={{0,1},{1,0},{2,3},{3,2},{4,5},{5,4},{6,7},{7,6},{8,9},{9,8},{10,11... | collective-permute-start | bytes 3538952 | tf_op jit(solution)/shard_map/ppermute | solution.py:517
  150.9 9.1 %collective-permute-start.28 = (bf16[4,48,768]{2,1,0:T(8,128)(2,1)S(1)}, bf16[4,48,768]{2,1,0:T(8,128)(2,1)S(1)}, u32[]{:S(2)}, u32[]{:S(2)}) collective-permute-start(bf16[4,48,768]{2,1,0:T(8,128)(2,1)S(1)} %get-tuple-element.304), channel_id=1, source_target_pairs={{0,2},{1,3},{2,0},{3,1},{4,6},{5,7},{6,4},{7,5},{8,10},{9,11},{10,... | collective-permute-start | bytes 884744 | tf_op jit(solution)/shard_map/ppermute | solution.py:517
  151.2 8.9 %collective-permute-start.29 = (bf16[4,48,768]{2,1,0:T(8,128)(2,1)S(1)}, bf16[4,48,768]{2,1,0:T(8,128)(2,1)S(1)}, u32[]{:S(2)}, u32[]{:S(2)}) collective-permute-start(bf16[4,48,768]{2,1,0:T(8,128)(2,1)S(1)} %get-tuple-element.305), channel_id=1, source_target_pairs={{0,16},{16,0},{1,17},{17,1},{2,18},{18,2},{3,19},{19,3},{4,20},{20... | collective-permute-start | bytes 884744 | tf_op jit(solution)/shard_map/ppermute | solution.py:521
  160.1 23.0 %slice-start = ((s8[4718592]{0:T(1024)(128)(4,1)}), s8[524288]{0:T(1024)(128)(4,1)S(1)}, s32[]{:S(2)}) async-start(s8[4718592]{0:T(1024)(128)(4,1)} %bitcast.33), calls=%async_computation | async-start | bytes 1048576
  162.1 15.7 %collective-permute-start.35 = (bf16[8,48,768]{2,1,0:T(8,128)(2,1)S(1)}, bf16[8,48,768]{2,1,0:T(8,128)(2,1)S(1)}, u32[]{:S(2)}, u32[]{:S(2)}) collective-permute-start(bf16[8,48,768]{2,1,0:T(8,128)(2,1)S(1)} %get-tuple-element.322), channel_id=1, source_target_pairs={{0,16},{16,0},{1,17},{17,1},{2,18},{18,2},{3,19},{19,3},{4,20},{20... | collective-permute-start | bytes 1769480 | tf_op jit(solution)/shard_map/ppermute | solution.py:521
  162.5 15.3 %collective-permute-start.36 = (bf16[8,48,768]{2,1,0:T(8,128)(2,1)S(1)}, bf16[8,48,768]{2,1,0:T(8,128)(2,1)S(1)}, u32[]{:S(2)}, u32[]{:S(2)}) collective-permute-start(bf16[8,48,768]{2,1,0:T(8,128)(2,1)S(1)} %get-tuple-element.323), channel_id=1, source_target_pairs={{0,2},{1,3},{2,0},{3,1},{4,6},{5,7},{6,4},{7,5},{8,10},{9,11},{10,... | collective-permute-start | bytes 1769480 | tf_op jit(solution)/shard_map/ppermute | solution.py:517
  164.1 12.4 %collective-permute-start.32 = (bf16[2,48,768]{2,1,0:T(8,128)(2,1)S(1)}, bf16[2,48,768]{2,1,0:T(8,128)(2,1)S(1)}, u32[]{:S(2)}, u32[]{:S(2)}) collective-permute-start(bf16[2,48,768]{2,1,0:T(8,128)(2,1)S(1)} %get-tuple-element.319), channel_id=1, source_target_pairs={{0,4},{1,5},{2,6},{3,7},{4,0},{5,1},{6,2},{7,3},{8,12},{9,13},{10,... | collective-permute-start | bytes 442376 | tf_op jit(solution)/shard_map/ppermute | solution.py:517
  164.1 13.6 %collective-permute-start.33 = (bf16[2,48,768]{2,1,0:T(8,128)(2,1)S(1)}, bf16[2,48,768]{2,1,0:T(8,128)(2,1)S(1)}, u32[]{:S(2)}, u32[]{:S(2)}) collective-permute-start(bf16[2,48,768]{2,1,0:T(8,128)(2,1)S(1)} %get-tuple-element.320), channel_id=1, source_target_pairs={{0,8},{1,9},{2,10},{3,11},{4,12},{5,13},{6,14},{7,15},{8,0},{9,1},... | collective-permute-start | bytes 442376 | tf_op jit(solution)/shard_map/ppermute | solution.py:517
  165.6 12.2 %collective-permute-start.34 = (bf16[2,48,768]{2,1,0:T(8,128)(2,1)S(1)}, bf16[2,48,768]{2,1,0:T(8,128)(2,1)S(1)}, u32[]{:S(2)}, u32[]{:S(2)}) collective-permute-start(bf16[2,48,768]{2,1,0:T(8,128)(2,1)S(1)} %get-tuple-element.321), channel_id=1, source_target_pairs={{0,12},{1,13},{2,14},{3,15},{4,8},{5,9},{6,10},{7,11},{8,4},{9,5},... | collective-permute-start | bytes 442376 | tf_op jit(solution)/shard_map/ppermute | solution.py:517
  179.5 15.5 %collective-permute-start.39 = (bf16[2,8,48,768]{3,2,1,0:T(8,128)(2,1)S(1)}, bf16[2,8,48,768]{3,2,1,0:T(8,128)(2,1)S(1)}, u32[]{:S(2)}, u32[]{:S(2)}) collective-permute-start(bf16[2,8,48,768]{3,2,1,0:T(8,128)(2,1)S(1)} %copy-done.21), channel_id=1, source_target_pairs={{0,1},{1,0},{2,3},{3,2},{4,5},{5,4},{6,7},{7,6},{8,9},{9,8},{10,11... | collective-permute-start | bytes 3538952 | tf_op jit(solution)/shard_map/ppermute | solution.py:517
  179.8 15.2 %collective-permute-start.40 = (bf16[2,8,48,768]{3,2,1,0:T(8,128)(2,1)S(1)}, bf16[2,8,48,768]{3,2,1,0:T(8,128)(2,1)S(1)}, u32[]{:S(2)}, u32[]{:S(2)}) collective-permute-start(bf16[2,8,48,768]{3,2,1,0:T(8,128)(2,1)S(1)} %copy-done.20), channel_id=1, source_target_pairs={{0,1},{1,0},{2,3},{3,2},{4,5},{5,4},{6,7},{7,6},{8,9},{9,8},{10,11... | collective-permute-start | bytes 3538952 | tf_op jit(solution)/shard_map/ppermute | solution.py:517
  180.1 14.9 %collective-permute-start.37 = (bf16[4,48,768]{2,1,0:T(8,128)(2,1)S(1)}, bf16[4,48,768]{2,1,0:T(8,128)(2,1)S(1)}, u32[]{:S(2)}, u32[]{:S(2)}) collective-permute-start(bf16[4,48,768]{2,1,0:T(8,128)(2,1)S(1)} %get-tuple-element.339), channel_id=1, source_target_pairs={{0,2},{1,3},{2,0},{3,1},{4,6},{5,7},{6,4},{7,5},{8,10},{9,11},{10,... | collective-permute-start | bytes 884744 | tf_op jit(solution)/shard_map/ppermute | solution.py:517
  181.0 14.0 %collective-permute-start.38 = (bf16[4,48,768]{2,1,0:T(8,128)(2,1)S(1)}, bf16[4,48,768]{2,1,0:T(8,128)(2,1)S(1)}, u32[]{:S(2)}, u32[]{:S(2)}) collective-permute-start(bf16[4,48,768]{2,1,0:T(8,128)(2,1)S(1)} %get-tuple-element.340), channel_id=1, source_target_pairs={{0,16},{16,0},{1,17},{17,1},{2,18},{18,2},{3,19},{19,3},{4,20},{20... | collective-permute-start | bytes 884744 | tf_op jit(solution)/shard_map/ppermute | solution.py:521
  182.1 12.8 %collective-permute-start.41 = (bf16[2,48,768]{2,1,0:T(8,128)(2,1)S(1)}, bf16[2,48,768]{2,1,0:T(8,128)(2,1)S(1)}, u32[]{:S(2)}, u32[]{:S(2)}) collective-permute-start(bf16[2,48,768]{2,1,0:T(8,128)(2,1)S(1)} %get-tuple-element.343.a_mine), channel_id=1, source_target_pairs={{0,16},{16,0},{1,17},{17,1},{2,18},{18,2},{3,19},{19,3},{4,20},{20... | collective-permute-start | bytes 442376 | tf_op jit(solution)/shard_map/ppermute | solution.py:521
  196.9 17.2 %collective-permute-start.42 = (bf16[8,48,768]{2,1,0:T(8,128)(2,1)S(1)}, bf16[8,48,768]{2,1,0:T(8,128)(2,1)S(1)}, u32[]{:S(2)}, u32[]{:S(2)}) collective-permute-start(bf16[8,48,768]{2,1,0:T(8,128)(2,1)S(1)} %get-tuple-element.362), channel_id=1, source_target_pairs={{0,16},{16,0},{1,17},{17,1},{2,18},{18,2},{3,19},{19,3},{4,20},{20... | collective-permute-start | bytes 1769480 | tf_op jit(solution)/shard_map/ppermute | solution.py:521
  198.2 16.0 %collective-permute-start.43 = (bf16[8,48,768]{2,1,0:T(8,128)(2,1)S(1)}, bf16[8,48,768]{2,1,0:T(8,128)(2,1)S(1)}, u32[]{:S(2)}, u32[]{:S(2)}) collective-permute-start(bf16[8,48,768]{2,1,0:T(8,128)(2,1)S(1)} %get-tuple-element.363), channel_id=1, source_target_pairs={{0,2},{1,3},{2,0},{3,1},{4,6},{5,7},{6,4},{7,5},{8,10},{9,11},{10,... | collective-permute-start | bytes 1769480 | tf_op jit(solution)/shard_map/ppermute | solution.py:517
  199.3 12.6 %collective-permute-start.44 = (bf16[2,48,768]{2,1,0:T(8,128)(2,1)S(1)}, bf16[2,48,768]{2,1,0:T(8,128)(2,1)S(1)}, u32[]{:S(2)}, u32[]{:S(2)}) collective-permute-start(bf16[2,48,768]{2,1,0:T(8,128)(2,1)S(1)} %get-tuple-element.364), channel_id=1, source_target_pairs={{0,4},{1,5},{2,6},{3,7},{4,0},{5,1},{6,2},{7,3},{8,12},{9,13},{10,... | collective-permute-start | bytes 442376 | tf_op jit(solution)/shard_map/ppermute | solution.py:517
  201.4 12.7 %collective-permute-start.45 = (bf16[2,48,768]{2,1,0:T(8,128)(2,1)S(1)}, bf16[2,48,768]{2,1,0:T(8,128)(2,1)S(1)}, u32[]{:S(2)}, u32[]{:S(2)}) collective-permute-start(bf16[2,48,768]{2,1,0:T(8,128)(2,1)S(1)} %get-tuple-element.365), channel_id=1, source_target_pairs={{0,8},{1,9},{2,10},{3,11},{4,12},{5,13},{6,14},{7,15},{8,0},{9,1},... | collective-permute-start | bytes 442376 | tf_op jit(solution)/shard_map/ppermute | solution.py:517
  201.4 12.7 %collective-permute-start.46 = (bf16[2,48,768]{2,1,0:T(8,128)(2,1)S(1)}, bf16[2,48,768]{2,1,0:T(8,128)(2,1)S(1)}, u32[]{:S(2)}, u32[]{:S(2)}) collective-permute-start(bf16[2,48,768]{2,1,0:T(8,128)(2,1)S(1)} %get-tuple-element.366), channel_id=1, source_target_pairs={{0,12},{1,13},{2,14},{3,15},{4,8},{5,9},{6,10},{7,11},{8,4},{9,5},... | collective-permute-start | bytes 442376 | tf_op jit(solution)/shard_map/ppermute | solution.py:517
  215.7 9.5 %collective-permute-start.47 = (bf16[4,48,768]{2,1,0:T(8,128)(2,1)S(1)}, bf16[4,48,768]{2,1,0:T(8,128)(2,1)S(1)}, u32[]{:S(2)}, u32[]{:S(2)}) collective-permute-start(bf16[4,48,768]{2,1,0:T(8,128)(2,1)S(1)} %get-tuple-element.379), channel_id=1, source_target_pairs={{0,2},{1,3},{2,0},{3,1},{4,6},{5,7},{6,4},{7,5},{8,10},{9,11},{10,... | collective-permute-start | bytes 884744 | tf_op jit(solution)/shard_map/ppermute | solution.py:517
  216.4 8.8 %collective-permute-start.48 = (bf16[4,48,768]{2,1,0:T(8,128)(2,1)S(1)}, bf16[4,48,768]{2,1,0:T(8,128)(2,1)S(1)}, u32[]{:S(2)}, u32[]{:S(2)}) collective-permute-start(bf16[4,48,768]{2,1,0:T(8,128)(2,1)S(1)} %get-tuple-element.380), channel_id=1, source_target_pairs={{0,16},{16,0},{1,17},{17,1},{2,18},{18,2},{3,19},{19,3},{4,20},{20... | collective-permute-start | bytes 884744 | tf_op jit(solution)/shard_map/ppermute | solution.py:521
  217.0 4.9 %collective-permute-start.49 = (f32[8,768]{1,0:T(8,128)S(1)}, f32[8,768]{1,0:T(8,128)S(1)}, u32[]{:S(2)}, u32[]{:S(2)}) collective-permute-start(f32[8,768]{1,0:T(8,128)S(1)} %get-tuple-element.381.refs_5_), channel_id=1, source_target_pairs={{0,4},{1,5},{2,6},{3,7},{4,0},{5,1},{6,2},{7,3},{8,12},{9,13},{10,... | collective-permute-start | bytes 73736 | tf_op jit(solution)/shard_map/ppermute | solution.py:517
  219.6 4.7 %collective-permute-start.50 = (f32[8,768]{1,0:T(8,128)S(1)}, f32[8,768]{1,0:T(8,128)S(1)}, u32[]{:S(2)}, u32[]{:S(2)}) collective-permute-start(f32[8,768]{1,0:T(8,128)S(1)} %get-tuple-element.381.refs_5_), channel_id=1, source_target_pairs={{0,8},{1,9},{2,10},{3,11},{4,12},{5,13},{6,14},{7,15},{8,0},{9,1},... | collective-permute-start | bytes 73736 | tf_op jit(solution)/shard_map/ppermute | solution.py:517
  219.6 5.6 %collective-permute-start.51 = (f32[8,768]{1,0:T(8,128)S(1)}, f32[8,768]{1,0:T(8,128)S(1)}, u32[]{:S(2)}, u32[]{:S(2)}) collective-permute-start(f32[8,768]{1,0:T(8,128)S(1)} %get-tuple-element.381.refs_5_), channel_id=1, source_target_pairs={{0,12},{1,13},{2,14},{3,15},{4,8},{5,9},{6,10},{7,11},{8,4},{9,5},... | collective-permute-start | bytes 73736 | tf_op jit(solution)/shard_map/ppermute | solution.py:517
  226.8 9.9 %collective-permute-start.53 = (bf16[2,48,768]{2,1,0:T(8,128)(2,1)S(1)}, bf16[2,48,768]{2,1,0:T(8,128)(2,1)S(1)}, u32[]{:S(2)}, u32[]{:S(2)}) collective-permute-start(bf16[2,48,768]{2,1,0:T(8,128)(2,1)S(1)} %get-tuple-element.390), channel_id=1, source_target_pairs={{0,4},{1,5},{2,6},{3,7},{4,0},{5,1},{6,2},{7,3},{8,12},{9,13},{10,... | collective-permute-start | bytes 442376 | tf_op jit(solution)/shard_map/ppermute | solution.py:517
  228.2 11.3 %collective-permute-start.54 = (bf16[2,48,768]{2,1,0:T(8,128)(2,1)S(1)}, bf16[2,48,768]{2,1,0:T(8,128)(2,1)S(1)}, u32[]{:S(2)}, u32[]{:S(2)}) collective-permute-start(bf16[2,48,768]{2,1,0:T(8,128)(2,1)S(1)} %get-tuple-element.391), channel_id=1, source_target_pairs={{0,8},{1,9},{2,10},{3,11},{4,12},{5,13},{6,14},{7,15},{8,0},{9,1},... | collective-permute-start | bytes 442376 | tf_op jit(solution)/shard_map/ppermute | solution.py:517
  229.8 9.7 %collective-permute-start.55 = (bf16[2,48,768]{2,1,0:T(8,128)(2,1)S(1)}, bf16[2,48,768]{2,1,0:T(8,128)(2,1)S(1)}, u32[]{:S(2)}, u32[]{:S(2)}) collective-permute-start(bf16[2,48,768]{2,1,0:T(8,128)(2,1)S(1)} %get-tuple-element.392), channel_id=1, source_target_pairs={{0,12},{1,13},{2,14},{3,15},{4,8},{5,9},{6,10},{7,11},{8,4},{9,5},... | collective-permute-start | bytes 442376 | tf_op jit(solution)/shard_map/ppermute | solution.py:517
  231.3 11.2 %collective-permute-start.52 = (bf16[2,48,768]{2,1,0:T(8,128)(2,1)S(1)}, bf16[2,48,768]{2,1,0:T(8,128)(2,1)S(1)}, u32[]{:S(2)}, u32[]{:S(2)}) collective-permute-start(bf16[2,48,768]{2,1,0:T(8,128)(2,1)S(1)} %get-tuple-element.388.d_mine), channel_id=1, source_target_pairs={{0,16},{16,0},{1,17},{17,1},{2,18},{18,2},{3,19},{19,3},{4,20},{20... | collective-permute-start | bytes 442376 | tf_op jit(solution)/shard_map/ppermute | solution.py:521
  232.7 4.0 %collective-permute-start.56 = (f32[8,768]{1,0:T(8,128)S(1)}, f32[8,768]{1,0:T(8,128)S(1)}, u32[]{:S(2)}, u32[]{:S(2)}) collective-permute-start(f32[8,768]{1,0:T(8,128)S(1)} %get-tuple-element.393.refs_4_), channel_id=1, source_target_pairs={{0,16},{16,0},{1,17},{17,1},{2,18},{18,2},{3,19},{19,3},{4,20},{20... | collective-permute-start | bytes 73736 | tf_op jit(solution)/shard_map/ppermute | solution.py:521
  239.5 5.4 %collective-permute-start.58 = (f32[8,768]{1,0:T(8,128)S(1)}, f32[8,768]{1,0:T(8,128)S(1)}, u32[]{:S(2)}, u32[]{:S(2)}) collective-permute-start(f32[8,768]{1,0:T(8,128)S(1)} %get-tuple-element.400), channel_id=1, source_target_pairs={{0,1},{1,0},{2,3},{3,2},{4,5},{5,4},{6,7},{7,6},{8,9},{9,8},{10,11... | collective-permute-start | bytes 73736 | tf_op jit(solution)/shard_map/ppermute | solution.py:517
  239.6 5.3 %collective-permute-start.59 = (f32[8,768]{1,0:T(8,128)S(1)}, f32[8,768]{1,0:T(8,128)S(1)}, u32[]{:S(2)}, u32[]{:S(2)}) collective-permute-start(f32[8,768]{1,0:T(8,128)S(1)} %get-tuple-element.400), channel_id=1, source_target_pairs={{0,2},{1,3},{2,0},{3,1},{4,6},{5,7},{6,4},{7,5},{8,10},{9,11},{10,... | collective-permute-start | bytes 73736 | tf_op jit(solution)/shard_map/ppermute | solution.py:517
  241.2 3.7 %collective-permute-start.60 = (f32[8,768]{1,0:T(8,128)S(1)}, f32[8,768]{1,0:T(8,128)S(1)}, u32[]{:S(2)}, u32[]{:S(2)}) collective-permute-start(f32[8,768]{1,0:T(8,128)S(1)} %get-tuple-element.400), channel_id=1, source_target_pairs={{0,3},{1,2},{2,1},{3,0},{4,7},{5,6},{6,5},{7,4},{8,11},{9,10},{10,... | collective-permute-start | bytes 73736 | tf_op jit(solution)/shard_map/ppermute | solution.py:517
  241.5 6.1 %collective-permute-start.57 = (bf16[2,48,768]{2,1,0:T(8,128)(2,1)S(1)}, bf16[2,48,768]{2,1,0:T(8,128)(2,1)S(1)}, u32[]{:S(2)}, u32[]{:S(2)}) collective-permute-start(bf16[2,48,768]{2,1,0:T(8,128)(2,1)S(1)} %get-tuple-element.394.u_mine), channel_id=1, source_target_pairs={{0,16},{16,0},{1,17},{17,1},{2,18},{18,2},{3,19},{19,3},{4,20},{20... | collective-permute-start | bytes 442376 | tf_op jit(solution)/shard_map/ppermute | solution.py:521
  (25 other events, 187.9 us)

commit v6 on v5

--- a/solution.py
+++ b/solution.py
@@ -168,10 +168,21 @@
     return pl.ds(pl.multiple_of(i * size, size), size)
 
 
-def project_kernel(load, n_w, *refs):
-    scal, x_ref, cot_ref, vec_ref = refs[:4]
-    xn, q, k, v, da, w, sem = refs[4 + n_w :]
-    load(scal, refs[4 : 4 + n_w], w, sem)
+def project_kernel(load, read, n_w, *refs):
+    n_v = 0 if read else 1
+    scal, x_ref, cot_ref = refs[:3]
+    w_refs = refs[3 + n_v : 3 + n_v + n_w]
+    xn, q, k, v, da, w, *rest = refs[3 + n_v + n_w :]
+    sem = rest[-1]
+    if read:
+        vec_ref, b_mlp, buf, vsem = rest[:4]
+        steps = read(scal, w_refs, vec_ref, b_mlp, buf, vsem)
+        next(steps)
+        load(scal, w_refs, w, sem)
+        next(steps)
+    else:
+        vec_ref = refs[3]
+        load(scal, w_refs, w, sem)
     tokens = x_ref.shape[0]
 
     def norm(i):
@@ -204,23 +215,26 @@
         each(fn)
 
 
-def project_call(scal, x, cot, vec, weights, load):
+def project_call(scal, x, cot, vec, weights, load, read=None):
     tokens, width = x.shape
     return call(
-        functools.partial(project_kernel, load, len(weights)),
+        functools.partial(project_kernel, load, read, len(weights)),
         "project",
-        (scal, x, cot, vec),
+        (scal, x, cot) if read else (scal, x, cot, vec),
         weights,
-        [kept(x.shape)] * 5,
+        [kept(x.shape)] * 5
+        + [kept((4, width, width))]
+        + ([kept((8, width), F32), kept((4, width), F32)] if read else []),
         [],
-        [pltpu.VMEM((4, width, width), BF16), pltpu.SemaphoreType.DMA((4,))],
+        ([pltpu.VMEM((16, 8, width), BF16), pltpu.SemaphoreType.DMA] if read else [])
+        + [pltpu.SemaphoreType.DMA((4,))],
         8 * tokens * width * width,
         limit=10,
     )
 
 
-def core_kernel(b, scal, q, k, v, da, *refs):
-    o, d = refs[-2:]
+def core_kernel(b, scal, q, k, v, da, w, *refs):
+    o, d, dn = refs[-3:]
     refs = (q, k, v, da, o, d.at[0], d.at[1], d.at[2])
     whole = scal[8 + b] == 0
 
@@ -237,18 +251,24 @@
 
     loop(q.shape[1] // 128, pair)
 
-
-def core_call(b, scal, q, k, v, da, *before):
+    def back(i):
+        r = rows_of(b * 2 + i, 256)
+        dn[r, :] = dot_nt(d[0, r, :], w[0]) + dot_nt(d[1, r, :], w[1]) + dot_nt(d[2, r, :], w[2])
+
+    loop(2, back)
+
+
+def core_call(b, scal, q, k, v, da, w, *before):
     return call(
         functools.partial(core_kernel, b),
         "core",
-        (scal, q, k, v, da, *before),
+        (scal, q, k, v, da, w, *before),
         [],
-        [kept(q.shape), kept((3, *q.shape))],
+        [kept(q.shape), kept((3, *q.shape)), kept(q.shape, F32)],
         [],
         [],
         10 << 30,
-        alias={5 + i: i for i in range(len(before))},
+        alias={6 + i: i for i in range(len(before))},
         limit=8,
     )
 
@@ -417,15 +437,14 @@
 
 def up_grad_kernel(load, store, n_p, scal, xn, dpre, *refs):
     w, *g_refs, g, wsem, sem = refs[n_p:]
-    load(scal, refs[:n_p], w, wsem)
+    load(scal, refs[:n_p], w, wsem, (3,))
 
     def grad(t):
         g[t] = dot_tn(xn[...], dpre[t]).astype(BF16)
         store(scal, g, g_refs, sem, t)
 
     loop(dpre.shape[0], grad)
-    for i in range(4):
-        whole_wait(w.at[i], wsem.at[i])()
+    whole_wait(w, wsem.at[3])()
     stored(g_refs, sem)
 
 
@@ -436,7 +455,7 @@
         "up_grad",
         (scal, xn, dpre),
         pieces,
-        [kept((4, width, width))],
+        [kept((1, width, width))],
         g_shapes,
         [
             pltpu.VMEM((tiles, width, width), BF16),
@@ -448,13 +467,13 @@
     )
 
 
-def input_grad_kernel(scal, x, cot, d, dpre, vec, wa, wu, sums, dx_ref, dx, sem):
+def input_grad_kernel(scal, x, cot, dn, dpre, vec, wu, sums, dx_ref, dx, sem):
     tiles, tokens, width = dpre.shape
     sums[...] = jnp.zeros_like(sums)
 
     def step(i):
         r = rows_of(i, 256)
-        dnr = dot_nt(d[0, r, :], wa[0]) + dot_nt(d[1, r, :], wa[1]) + dot_nt(d[2, r, :], wa[2])
+        dnr = dn[r, :]
         for t in range(tiles):
             dnr += dot_nt(dpre[t, r, :], wu[t])
         standard, inv = norm_rows(x[r, :])
@@ -468,12 +487,12 @@
     whole_wait(dx_ref, sem)()
 
 
-def input_grad_call(scal, x, cot, d, dpre, vec, wa, wu):
+def input_grad_call(scal, x, cot, dn, dpre, vec, wu):
     tiles, tokens, width = dpre.shape
     return call(
         input_grad_kernel,
         "input_grad",
-        (scal, x, cot, d, dpre, vec, wa, wu),
+        (scal, x, cot, dn, dpre, vec, wu),
         [],
         [kept((8, width), F32)],
         [sds((tokens // 512, 512, width))],
@@ -483,12 +502,12 @@
     )
 
 
-def out_kernel(scal, x, o, act, vec, wa, wd, out_ref, out, sem):
+def out_kernel(scal, x, o, act, vec, wo, wd, out_ref, out, sem):
     tiles, tokens, width = act.shape
 
     def step(i):
         r = rows_of(i, 256)
-        total = x[r, :].astype(F32) + vec[3:4, :] + dot_nn(o[r, :], wa[3])
+        total = x[r, :].astype(F32) + vec[3:4, :] + dot_nn(o[r, :], wo[0])
         for t in range(tiles):
             total += dot_nn(act[t, r, :], wd[tile_of(t, width), :])
         out[r, :] = total.astype(BF16)
@@ -497,12 +516,12 @@
     whole_wait(out_ref, sem)()
 
 
-def out_call(scal, x, o, act, vec, wa, wd):
+def out_call(scal, x, o, act, vec, wo, wd):
     tiles, tokens, width = act.shape
     (out,) = call(
         out_kernel,
         "out",
-        (scal, x, o, act, vec, wa, wd),
+        (scal, x, o, act, vec, wo, wd),
         [],
         [],
         [sds((tokens // 512, 512, width))],
@@ -559,7 +578,11 @@
     def fn(held, near, outs):
         size = near[0].shape[0]
         for i, v in enumerate(near):
-            outs[0][i * size : (i + 1) * size] = v[...]
+            at = slice(i * size, (i + 1) * size)
+            if v.ndim == 3:
+                outs[0][at, : v.shape[1], :] = v[...]
+            else:
+                outs[0][at] = v[...]
 
     return fn, [], values, [kept((len(values) * values[0].shape[0], *values[0].shape[1:]))]
 
@@ -573,7 +596,8 @@
         at = len(near) + len(held)
         scratch = refs[at + len(outs) :]
         copies = [
-            pltpu.make_async_copy(refs[len(near) + i], scratch[i], scratch[-1].at[i]) for i in range(len(held))
+            pltpu.make_async_copy(refs[len(near) + i].at[:, pl.ds(v[1], v[2])], scratch[i], scratch[-1].at[i])
+            for i, v in enumerate(held)
         ]
         for cp in copies:
             cp.start()
@@ -594,13 +618,13 @@
         out_shape=outs,
         in_specs=[VMEM] * len(near) + [HBM] * len(held),
         out_specs=[VMEM] * len(outs),
-        scratch_shapes=[pltpu.VMEM(v.shape, v.dtype) for v in held]
+        scratch_shapes=[pltpu.VMEM((v.shape[0], size, *v.shape[2:]), v.dtype) for v, _, size in held]
         + [pltpu.SemaphoreType.DMA((max(len(held), 1),))],
         compiler_params=pltpu.CompilerParams(vmem_limit_bytes=8 << 20),
         cost_estimate=pl.CostEstimate(flops=1 << 20, bytes_accessed=1 << 20, transcendentals=0),
     )(
         *[pltpu.with_memory_space_constraint(v, pltpu.VMEM) for v in near],
-        *[pltpu.with_memory_space_constraint(v, pltpu.HBM) for v in held],
+        *[pltpu.with_memory_space_constraint(v[0], pltpu.HBM) for v in held],
     )
     split, at = [], 0
     for job in jobs:
@@ -682,7 +706,7 @@
         for i in range(2):
             outs[i][...] = total(held[0][i], near[0][i]).astype(BF16)
 
-    return fn, [keep1], [got1], [kept(keep1.shape[1:])] * 2
+    return fn, [(keep1, 0, keep1.shape[1])], [got1], [kept(keep1.shape[1:])] * 2
 
 
 def sum2_job(keep0, got0, got):
@@ -690,9 +714,9 @@
 
     def fn(held, near, outs):
         for i in range(2):
-            outs[i][...] = total(held[0][i, half:], near[0][i, half:], near[1 + i][half:]).astype(BF16)
-
-    return fn, [keep0], [got0, *got], [kept((half, *keep0.shape[2:]))] * 2
+            outs[i][...] = total(held[0][i], near[0][i, half:], near[1 + i][half:]).astype(BF16)
+
+    return fn, [(keep0, half, half)], [got0, *got], [kept((half, *keep0.shape[2:]))] * 2
 
 
 def sum3_job(keep0, got0, got, got2):
@@ -703,7 +727,7 @@
             for i in range(2):
                 outs[k][i] = total(held[0][i, k], near[0][i, k], near[1 + i][k], near[3 + i][k]).astype(BF16)
 
-    return fn, [keep0], [got0, *got, *got2], [kept((2, *keep0.shape[2:]))] * half
+    return fn, [(keep0, 0, half)], [got0, *got, *got2], [kept((2, *keep0.shape[2:]))] * half
 
 
 def sum4_job(own, got):
@@ -713,34 +737,29 @@
     return fn, [], [own, *got], [kept(own.shape)]
 
 
-def place_kernel(scal, a_mine, a_other, d_mine, d_other, u_mine, joined_ref, out, down, joined, sem):
+def place_kernel(scal, a_mine, a_other, d_mine, d_other, joined_ref, out, down, joined, sem):
     _, rows, width = a_mine.shape
 
-    def place(half, a, d, u):
+    def place(half, a, d):
         for p in range(2):
             block = half * 2 + p
             down[pl.ds(block * rows, rows), :] = d[p].astype(F32)
-            if u is not None:
-                joined[3 + p] = u[p].astype(F32)
-                send(joined.at[3 + p], 3 + block)
             if block < 3:
                 joined[block] = a[p].astype(F32)
-                send(joined.at[block], block)
+                dst = joined_ref.at[:, block * width : (block + 1) * width]
+                pltpu.make_async_copy(joined.at[block], dst, sem).start()
             else:
                 out[...] = a[p].astype(F32)
 
-    def send(src, block):
-        pltpu.make_async_copy(src, joined_ref.at[:, block * width : (block + 1) * width], sem).start()
-
     @pl.when(scal[0] == 0)
     def _():
-        place(0, a_mine, d_mine, u_mine)
-        place(1, a_other, d_other, None)
+        place(0, a_mine, d_mine)
+        place(1, a_other, d_other)
 
     @pl.when(scal[0] != 0)
     def _():
-        place(1, a_mine, d_mine, u_mine)
-        place(0, a_other, d_other, None)
+        place(1, a_mine, d_mine)
+        place(0, a_other, d_other)
 
     whole_wait(joined, sem)()
 
@@ -751,31 +770,34 @@
         place_kernel,
         name="place",
         out_shape=[sds((rows, 7 * width), F32), sds((rows, width), F32), sds((4 * rows, width), F32)],
-        in_specs=[SMEM] + [VMEM] * 5,
+        in_specs=[SMEM] + [VMEM] * 4,
         out_specs=[HBM, VMEM, VMEM],
-        scratch_shapes=[pltpu.VMEM((5, rows, width), F32), pltpu.SemaphoreType.DMA],
+        scratch_shapes=[pltpu.VMEM((3, rows, width), F32), pltpu.SemaphoreType.DMA],
+        compiler_params=pltpu.CompilerParams(vmem_limit_bytes=8 << 20),
     )(scal, *[pltpu.with_memory_space_constraint(v, pltpu.VMEM) for v in parts])
 
 
-def place_last_kernel(scal, placed, other, joined_ref, wide, sem):
+def place_last_kernel(scal, placed, mine, other, joined_ref, wide, sem):
     _, rows, width = other.shape
-    for p in range(2):
-        wide[p] = other[p].astype(F32)
-        at = pl.multiple_of((3 + (1 - scal[0]) * 2 + p) * width, 128)
-        pltpu.make_async_copy(wide.at[p], joined_ref.at[:, pl.ds(at, width)], sem).start()
+    for i, ref in enumerate((mine, other)):
+        for p in range(2):
+            wide[i * 2 + p] = ref[p].astype(F32)
+            at = pl.multiple_of((3 + (scal[0] ^ i) * 2 + p) * width, 128)
+            pltpu.make_async_copy(wide.at[i * 2 + p], joined_ref.at[:, pl.ds(at, width)], sem).start()
     whole_wait(wide, sem)()
 
 
-def place_last_call(scal, placed, other):
+def place_last_call(scal, placed, mine, other):
     return pl.pallas_call(
         place_last_kernel,
         name="place_last",
         out_shape=sds(placed.shape, F32),
-        in_specs=[SMEM, HBM, VMEM],
+        in_specs=[SMEM, HBM, VMEM, VMEM],
         out_specs=HBM,
-        scratch_shapes=[pltpu.VMEM(other.shape, F32), pltpu.SemaphoreType.DMA],
+        scratch_shapes=[pltpu.VMEM((4, *other.shape[1:]), F32), pltpu.SemaphoreType.DMA],
+        compiler_params=pltpu.CompilerParams(vmem_limit_bytes=8 << 20),
         input_output_aliases={1: 0},
-    )(scal, placed, pltpu.with_memory_space_constraint(other, pltpu.VMEM))
+    )(scal, placed, *[pltpu.with_memory_space_constraint(v, pltpu.VMEM) for v in (mine, other)])
 
 
 def whole_wait(ref, sem):
@@ -790,17 +812,17 @@
     return refs[8].at[(at - sum(i < at for i in alone)) * 4 + k]
 
 
-def load_columns(scal, refs, w, sem):
+def load_columns(scal, refs, w, sem, blocks=(0, 1, 2, 3)):
     rows = w.shape[1] // 16
 
     def start(own):
-        for block in range(4):
+        for block in blocks:
             for core in range(2):
                 for part, _, _, half, side, k in slots():
                     if (own ^ half) * 2 + part != block:
                         continue
                     src = piece(refs, part * 4 + half * 2 + side, core, k, (3, 7)).at[pl.ds(0, rows), :]
-                    dst = w.at[block, rows_at(device_of(scal, k, side, core) * rows, rows), :]
+                    dst = w.at[blocks.index(block), rows_at(device_of(scal, k, side, core) * rows, rows), :]
                     pltpu.make_async_copy(src, dst, sem.at[block]).start()
 
     @pl.when(scal[0] == 0)
@@ -841,15 +863,15 @@
     return load
 
 
-def vectors_kernel(rows, scal, *refs):
-    pieces, (vec, b_mlp, buf, sem) = refs[:3], refs[3:]
+def read_vectors(scal, refs, vec, b_mlp, buf, sem):
     width = vec.shape[1]
+    rows = width // 16
     for core in range(2):
         for side in range(2):
             for k in range(4):
-                src = pieces[side].at[k] if core == 0 else pieces[2].at[side * 4 + k]
-                src = src.at[pl.ds(rows, 8), :]
+                src = piece(refs, side, core, k, (3, 7)).at[pl.ds(rows, 8), :]
                 pltpu.make_async_copy(src, buf.at[device_of(scal, k, side, core)], sem).start()
+    yield
     whole_wait(buf, sem)()
     values = buf[:, 0, :].astype(F32)
     devices = values.shape[0]
@@ -873,19 +895,7 @@
         vec[i : i + 1, :] = v
     for i, v in enumerate(line(3 * rows, 4 * rows)):
         b_mlp[i : i + 1, :] = v
-
-
-def vectors_call(scal, pieces, rows):
-    width = pieces[0].shape[2]
-    return pl.pallas_call(
-        functools.partial(vectors_kernel, rows),
-        name="vectors",
-        out_shape=[kept((8, width), F32), kept((4, width), F32)],
-        in_specs=[SMEM] + [HBM] * 3,
-        out_specs=[VMEM] * 2,
-        scratch_shapes=[pltpu.VMEM((16, 8, width), BF16), pltpu.SemaphoreType.DMA],
-        compiler_params=pltpu.CompilerParams(vmem_limit_bytes=8 << 20),
-    )(scal, *[pltpu.with_memory_space_constraint(v, pltpu.HBM) for v in pieces])
+    yield
 
 
 def rows_at(base, rows):
@@ -936,9 +946,9 @@
                     pltpu.make_async_copy(src, refs[at].at[part, s * 4 + k], sem.at[at]).start()
 
 
-def load_whole_blocks(scal, refs, w, sem):
-    for i, r in enumerate(refs):
-        pltpu.make_async_copy(r, w.at[i], sem.at[i]).start()
+def load_whole_blocks(scal, refs, w, sem, blocks=(0, 1, 2, 3)):
+    for i, b in enumerate(blocks):
+        pltpu.make_async_copy(refs[b], w.at[i], sem.at[b]).start()
 
 
 def load_whole_rows(scal, refs, w, sem):
@@ -1007,10 +1017,11 @@
         down_w = [lax.all_gather(w_mlp, "wide", axis=0, tiled=True)]
         vec, b_mlp = vectors(lax.all_gather(vec_own, "wide", axis=0))
         square = [sds((width, width))]
-        xn, q, k, v, da = project_call(scal, x, cot, vec, attn_w, load_whole_blocks)
-        o, d = core_call(0, scal, q, k, v, da)
+        xn, q, k, v, da, wa = project_call(scal, x, cot, vec, attn_w, load_whole_blocks)
+        part = core_call(0, scal, q, k, v, da, wa)
         for b in range(1, last.shape[0]):
-            o, d = core_call(b, scal, q, k, v, da, o, d)
+            part = core_call(b, scal, q, k, v, da, wa, *part)
+        o, d, dn = part
         sums_a, *g_attn = attn_grad_call(scal, xn, o, d, cot, store_whole_blocks, square * 4)
         act, gp, wu = up_call(0, tiles // 2, scal, xn, b_mlp, (), up_w, load_whole_blocks)
         act, gp = up_call(tiles // 2, tiles - tiles // 2, scal, xn, b_mlp, (act, gp, wu), [], None)
@@ -1018,9 +1029,9 @@
             scal, act, cot, down_w, load_whole_rows, store_whole_rows, [sds((tiles * width, width))]
         )
         dpre, sums_d = dpre_call(scal, cot, gp, wd)
-        wa, *g_up = up_grad_call(scal, xn, dpre, attn_w, load_whole_blocks, store_whole_blocks, square * tiles)
-        sums_x, d_x = input_grad_call(scal, x, cot, d, dpre, vec, wa, wu)
-        out = out_call(scal, x, o, act, vec, wa, wd)
+        wo, *g_up = up_grad_call(scal, xn, dpre, attn_w, load_whole_blocks, store_whole_blocks, square * tiles)
+        sums_x, d_x = input_grad_call(scal, x, cot, dn, dpre, vec, wu)
+        out = out_call(scal, x, o, act, vec, wo, wd)
 
         def reduce(g):
             g = lax.psum_scatter(g.astype(F32), "wide", scatter_dimension=0, tiled=True)
@@ -1034,11 +1045,12 @@
     else:
         col = lambda i: w_joined[:, i * width : (i + 1) * width]
         pair = lambda f: jnp.stack([jnp.where(n == 0, f(0), f(2)), jnp.where(n == 0, f(1), f(3))])
-        half = pair(lambda i: col(i) if i < 3 else w_out)
+        half_a, half_b = [jnp.where(n == 0, f, g) for f, g in ((col(0), col(2)), (col(1), w_out))]
         v_rows = jnp.pad(vec_own, (0, width - vec_own.shape[0]))
-        half = jnp.concatenate([half, jnp.broadcast_to(v_rows, (2, 8, width))], axis=1)
+        half = jnp.concatenate([half_a, jnp.broadcast_to(v_rows, (8, width)), half_b])
         got = gather_z(half)
-        za, zb = [jnp.stack([t[i] for t in (half, *got)]) for i in range(2)]
+        za = jnp.stack([t[: rows + 8] for t in (half, *got)])
+        zb = jnp.stack([t[rows + 8 :] for t in (half, *got)])
         c_half = jnp.stack([jnp.where(n == 0, col(3 + t), w_mlp[t * rows : (t + 1) * rows]) for t in range(tiles)])
         c_half = behind(c_half.reshape(2, tiles // 2, rows, width), za, zb)
         first = gather_first(za, zb)
@@ -1049,19 +1061,18 @@
         ((joined,),) = mix("join_a", [join_job([own[i] for i in (0, 1, 2, 4, 5, 6)])])
         joined, c1, c3 = swap(joined, 1), swap(c_half, 4), swap(c_half, 12)
         second, joined, c1, c3 = lax.optimization_barrier((second, joined, c1, c3))
-        vec, b_mlp = vectors_call(scal, [za, first[0], joined], rows)
         own = pieces_of(za, zb, first, second)
         attn_w = [*own, joined, swap(second[0], 1), swap(second[1], 1)]
         cza, czb = [jnp.stack([t[i] for t in (c_half, c1, c2, c3)]) for i in range(2)]
-        x_p, attn_w, cza, czb, vec, b_mlp = lax.optimization_barrier((x, attn_w, cza, czb, vec, b_mlp))
+        x_p, attn_w, cza, czb = lax.optimization_barrier((x, attn_w, cza, czb))
         c_first = gather_first(cza, czb)
-        xn, q, k, v, da = project_call(scal, x_p, cot, vec, attn_w, load_columns)
-        part = core_call(0, scal, q, k, v, da)
+        xn, q, k, v, da, wa, vec, b_mlp = project_call(scal, x_p, cot, None, attn_w, load_columns, read_vectors)
+        part = core_call(0, scal, q, k, v, da, wa)
 
         part, c_first = lax.optimization_barrier((part, c_first))
         c_second = gather_second(*c_first[:2])
         czs = [swap(cza, 1), swap(czb, 1)]
-        o, d = core_call(1, scal, q, k, v, da, *part)
+        o, d, dn = core_call(1, scal, q, k, v, da, wa, *part)
 
         d, c_second, czs = lax.optimization_barrier((d, c_second, czs))
         c_own = pieces_of(cza, czb, c_first, c_second)
@@ -1099,7 +1110,7 @@
         dpre_g, a_t, sa, sb = lax.optimization_barrier((dpre, a_t, sa, sb))
         d_xy = swap_y(sa), swap(sb, 2)
         a_z = [swap(a_t[k], k << 2) for k in (1, 2, 3)]
-        wa, *gu = up_grad_call(scal, xn, dpre_g, attn_w, load_columns, store_block, attn_shapes)
+        wo, *gu = up_grad_call(scal, xn, dpre_g, attn_w, load_columns, store_block, attn_shapes)
 
         a_z, d_xy = behind((a_z, d_xy), gu)
         (a_sum,), (sa, sb) = mix("sums_4", [sum4_job(a_t[0], a_z), sum2_job(gd[0], d_got0, d_xy)])
@@ -1107,7 +1118,7 @@
         u_got1, u_got0 = swap(gu[3], 1), swap(gu[2], 1)
         d_yx = swap(sa, 2), swap_y(sb)
         a_other = swap_y(a_sum)
-        sums_x, d_x = input_grad_call(scal, x_i, cot, d, dpre, vec, wa, wu)
+        sums_x, d_x = input_grad_call(scal, x_i, cot, dn, dpre, vec, wu)
 
         d_yx, u_got1, u_got0, a_other = behind((d_yx, u_got1, u_got0, a_other), d_x)
         (sa, sb), d_t, (v_own,) = mix(
@@ -1121,7 +1132,7 @@
         x_o, sa, sb, d_t = lax.optimization_barrier((x, sa, sb, d_t))
         u_xy = swap_y(sa), swap(sb, 2)
         d_z = [swap(d_t[k], k << 2) for k in (1, 2, 3)]
-        out = out_call(scal, x_o, o, act, vec, wa, wd)
+        out = out_call(scal, x_o, o, act, vec, wo, wd)
 
         u_xy, d_z, v_own = behind((u_xy, d_z, v_own), out)
         (sa, sb), (d_sum,) = mix("sums_6", [sum2_job(gu[0], u_got0, u_xy), sum4_job(d_t[0], d_z)])
@@ -1132,14 +1143,14 @@
         u_t, v_sum, d_sum = lax.optimization_barrier((u_t, v_sum, d_sum))
         u_z = [swap(u_t[k], k << 2) for k in (1, 2, 3)]
         v_other, d_other = swap_y(v_sum), swap_y(d_sum)
+        placed, grad_out, grad_mlp = place_call(scal, [a_sum, a_other, d_sum, d_other])
+        u_z, placed = lax.optimization_barrier((u_z, placed))
         (u_sum,), (v_sum,) = mix("sums_8", [sum4_job(u_t[0], u_z), add_job([v_sum, v_other])])
         u_other = swap_y(u_sum)
         vg = sum([v_sum, *[swap(v_sum, i) for i in (1, 2, 3)]])
         own = lambda v, per: lax.dynamic_slice(v.reshape(-1), (w * per,), (per,))
         vg = [own(vg[0], rows), own(vg[1:3], 2 * rows), own(vg[3:7], tiles * rows), own(vg[7], rows)]
-        d_other = behind(d_other, u_sum)
-        placed, grad_out, grad_mlp = place_call(scal, [a_sum, a_other, d_sum, d_other, u_sum])
-        grad_joined = place_last_call(scal, placed, behind(u_other, grad_out))
+        grad_joined = place_last_call(scal, placed, u_sum, u_other)
     return (out.reshape(tokens.shape), d_x.reshape(tokens.shape), grad_joined, grad_out, grad_mlp, *vg)
 
 

time: 250 us -> 247 us (0.988)
    ppermute x16, waiting for transfers between devices: 14.9 us -> 7.6 us  [swap_y(): return lax.ppermute(value, 'narrow', [(0, 1), (1, 0)])]
    ppermute x45, waiting for transfers between devices: 45.7 us -> 50.7 us  [swap(): return lax.ppermute(value, 'wide', [(i, i ^ mask) for i in range(16)])]
  transfers between devices with their start and end apart: 61 -> 61, of which waited for: 16 -> 21; matrix products, arithmetic and copies ran while one was open for 3% -> 3% of each run, Pallas kernels for 38% -> 38%
where the time goes in v6:
time: 247 us
  Pallas kernels  108 us (44%)
  starting transfers between devices  66.1 us (27%)
  waiting for transfers between devices  58.3 us (24%)
  local copies, waits for them, and re-layouts  9.77 us (4%)
  other arithmetic  3.09 us (1%)
    pallas_call x11, Pallas kernels, call(): pl.pallas_call(kernel, name=name, out_shape=list(outs) + list(g_shapes),...  91.8 us
    ppermute x45, starting transfers between devices, swap(): return lax.ppermute(value, 'wide', [(i, i ^ mask) for i in range(16)])  51.4 us
    ppermute x45, waiting for transfers between devices, swap(): return lax.ppermute(value, 'wide', [(i, i ^ mask) for i in range(16)])  50.7 us
    ppermute x16, starting transfers between devices, swap_y(): return lax.ppermute(value, 'narrow', [(0, 1), (1, 0)])  14.7 us
    pallas_call x10, Pallas kernels, mix(): pl.pallas_call(kernel, name=name, out_shape=outs, in_specs=[VMEM] * len(n...  12.4 us
    ppermute x16, waiting for transfers between devices, swap_y(): return lax.ppermute(value, 'narrow', [(0, 1), (1, 0)])  7.6 us
  transfers between devices with their start and end apart: 61, of which 21 were waited for; matrix products, arithmetic and copies ran while one was open for 3% of the time, Pallas kernels for 38%

profile of v6, /device:TPU:0, one launch (start us, length us, event | category | flops | bytes accessed | tf_op | source)
XLA Modules:
  0.0 246.6 jit_solution(2399670971399043072)
XLA Ops:
  0.7 1.3 select_bitcast_fusion.3
  2.7 5.1 %collective-permute-start.2 = (bf16[104,768]{1,0:T(8,128)(2,1)S(1)}, bf16[104,768]{1,0:T(8,128)(2,1)S(1)}, u32[]{:S(2)}, u32[]{:S(2)}) collective-permute-start(bf16[104,768]{1,0:T(8,128)(2,1)S(1)} %pad_maximum_fusion.5), channel_id=1, source_target_pairs={{0,12},{1,13},{2,14},{3,15},{4,8},{5,9},{6,10},{7,11},{8,4},{9,5},... | collective-permute-start | bytes 479240 | tf_op jit(solution)/shard_map/ppermute | solution.py:536
  9.3 3.6 %collective-permute-done.2 = bf16[104,768]{1,0:T(8,128)(2,1)S(1)} collective-permute-done((bf16[104,768]{1,0:T(8,128)(2,1)S(1)}, bf16[104,768]{1,0:T(8,128)(2,1)S(1)}, u32[]{:S(2)}, u32[]{:S(2)}) %collective-permute-start.2) | collective-permute-done | bytes 159776 | tf_op jit(solution)/shard_map/ppermute | solution.py:536
  12.9 8.5 %collective-permute-done.1 = bf16[104,768]{1,0:T(8,128)(2,1)S(1)} collective-permute-done((bf16[104,768]{1,0:T(8,128)(2,1)S(1)}, bf16[104,768]{1,0:T(8,128)(2,1)S(1)}, u32[]{:S(2)}, u32[]{:S(2)}) %collective-permute-start.1) | collective-permute-done | bytes 159776 | tf_op jit(solution)/shard_map/ppermute | solution.py:536
  21.5 1.6 collective-permute-start.3
  23.0 1.5 collective-permute-start.5
  25.9 13.6 %collective-permute-done.7 = bf16[2,2,48,768]{3,2,1,0:T(8,128)(2,1)} collective-permute-done((bf16[2,2,48,768]{3,2,1,0:T(8,128)(2,1)}, bf16[2,2,48,768]{3,2,1,0:T(8,128)(2,1)}, u32[]{:S(2)}, u32[]{:S(2)}) %collective-permute-start.7) | collective-permute-done | bytes 294944 | tf_op jit(solution)/shard_map/ppermute | solution.py:536
  39.5 1.3 join_a.1
  41.5 2.2 collective-permute-start.12
  44.2 1.3 fusion.12
  45.6 1.4 stack.70.refs_0_.scal
  46.9 1.2 fusion.7
  48.1 2.6 %collective-permute-done.11 = bf16[2,2,48,768]{3,2,1,0:T(8,128)(2,1)S(1)} collective-permute-done((bf16[2,2,48,768]{3,2,1,0:T(8,128)(2,1)}, bf16[2,2,48,768]{3,2,1,0:T(8,128)(2,1)S(1)}, u32[]{:S(2)}, u32[]{:S(2)}) %collective-permute-start.11) | collective-permute-done | bytes 294944 | tf_op jit(solution)/shard_map/ppermute | solution.py:536
  50.8 7.0 %collective-permute-done.12 = bf16[2,2,48,768]{3,2,1,0:T(8,128)(2,1)} collective-permute-done((bf16[2,2,48,768]{3,2,1,0:T(8,128)(2,1)}, bf16[2,2,48,768]{3,2,1,0:T(8,128)(2,1)}, u32[]{:S(2)}, u32[]{:S(2)}) %collective-permute-start.12) | collective-permute-done | bytes 294944 | tf_op jit(solution)/shard_map/ppermute | solution.py:536
  61.7 1.1 collective-permute-start.16
  62.8 1.5 collective-permute-start.18
  64.3 9.5 %project.1 = (bf16[1024,768]{1,0:T(8,128)(2,1)S(1)}, bf16[1024,768]{1,0:T(8,128)(2,1)S(1)}, bf16[1024,768]{1,0:T(8,128)(2,1)S(1)}, bf16[1024,768]{1,0:T(8,128)(2...) custom-call(s32[10]{0:T(128)S(1)} %stack.70.refs_0_.scal, ...), custom_call_target="tpu_custom_call" | custom-call | flops 4831838208 | bytes 1048576 | tf_op jit(solution)/shard_map/project/pallas_call | solution.py:139
  73.8 10.6 %core.2 = (bf16[1024,768]{1,0:T(8,128)(2,1)S(1)}, bf16[3,1024,768]{2,1,0:T(8,128)(2,1)S(1)}, f32[1024,768]{1,0:T(8,128)S(1)}) custom-call(s32[10]{0:T(128)S(1)} %stack.70.refs_0_.scal, bf16[1024,768]{1,0:T(8,128)(2,1)S(1)} %get-tuple-element.234.q, bf16[1024,768]{1,0:T(8,128)(2,1)S(1)} %get-tuple-element.235.k, bf16[1024,768]{1,0:T(8,128)(2,1)S(1)} %get-tuple-element.236.v, ...), custom_call_target="tpu_custom_call" | custom-call | flops 10737418240 | bytes 1048576 | tf_op jit(solution)/shard_map/core/pallas_call | solution.py:139
  84.5 7.5 %collective-permute-start.22 = (bf16[4,2,48,768]{3,2,1,0:T(8,128)(2,1)S(1)}, bf16[4,2,48,768]{3,2,1,0:T(8,128)(2,1)S(1)}, u32[]{:S(2)}, u32[]{:S(2)}) collective-permute-start(bf16[4,2,48,768]{3,2,1,0:T(8,128)(2,1)S(1)} %pad_maximum_fusion.1.refs_7_.refs_4_), channel_id=1, source_target_pairs={{0,1},{1,0},{2,3},{3,2},{4,5},{5,4},{6,7},{7,6},{8,9},{9,8},{10,11... | collective-permute-start | bytes 1769480 | tf_op jit(solution)/shard_map/ppermute | solution.py:536
  92.3 10.6 %core.3 = (bf16[1024,768]{1,0:T(8,128)(2,1)S(1)}, bf16[3,1024,768]{2,1,0:T(8,128)(2,1)S(1)}, f32[1024,768]{1,0:T(8,128)S(1)}) custom-call(s32[10]{0:T(128)S(1)} %stack.70.refs_0_.scal, bf16[1024,768]{1,0:T(8,128)(2,1)S(1)} %get-tuple-element.234.q, ...), custom_call_target="tpu_custom_call", output_to_operand_aliasing={{0}: (6, {}), {1}: (7, {}), {2}: (8, {})} | custom-call | flops 10737418240 | bytes 1048576 | tf_op jit(solution)/shard_map/core/pallas_call | solution.py:139
  103.0 4.4 %collective-permute-done.19.refs_2_.refs_6_.refs_3_ = bf16[4,2,48,768]{3,2,1,0:T(8,128)(2,1)S(1)} collective-permute-done((bf16[4,2,48,768]{3,2,1,0:T(8,128)(2,1)S(1)}, bf16[4,2,48,768]{3,2,1,0:T(8,128)(2,1)S(1)}, u32[]{:S(2)}, u32[]{:S(2)}) %collective-permute-start.19) | collective-permute-done | bytes 589856 | tf_op jit(solution)/shard_map/ppermute | solution.py:540
  108.5 7.8 %attn_grad.1 = (f32[8,768]{1,0:T(8,128)S(1)}, bf16[2,8,48,768]{3,2,1,0:T(8,128)(2,1)}, bf16[2,8,48,768]{3,2,1,0:T(8,128)(2,1)}, bf16[2,8,48,768]{3,2,1,0:T(8,128)(2,1)}, bf16[2,8,48,768]{3,2,1,0:T(8,128)(2,1)}) custom-call(s32[10]{0:T(128)S(1)} %stack.70.refs_0_.scal, bf16[1024,768]{1,0:T(8,128)(2,1)S(1)} %get-tuple-element.268.xn.refs_1_, ...), custom_call_target="tpu_custom_call" | custom-call | flops 4831838208 | bytes 1048576 | tf_op jit(solution)/shard_map/attn_grad/pallas_call | solution.py:139
  116.9 1.1 copy-done.13
  118.0 8.1 %up.2 = (bf16[4,1024,768]{2,1,0:T(8,128)(2,1)S(1)}, bf16[4,1024,768]{2,1,0:T(8,128)(2,1)S(1)}, bf16[4,768,768]{2,1,0:T(8,128)(2,1)S(1)}) custom-call(s32[10]{0:T(128)S(1)} %stack.70.refs_0_.scal, bf16[1024,768]{1,0:T(8,128)(2,1)S(1)} %get-tuple-element.268.xn.refs_1_, f32[4,768]{1,0:T(4,128)S(1)} %get-tuple-element.269.refs_2_, ...), custom_call_target="tpu_custom_call" | custom-call | flops 2415919104 | bytes 1048576 | tf_op jit(solution)/shard_map/up/pallas_call | solution.py:139
  126.1 1.6 sums_1.1
  127.7 1.6 collective-permute-start.26
  129.8 6.0 %up.3 = (bf16[4,1024,768]{2,1,0:T(8,128)(2,1)S(1)}, bf16[4,1024,768]{2,1,0:T(8,128)(2,1)S(1)}) custom-call(s32[10]{0:T(128)S(1)} %stack.70.refs_0_.scal, bf16[1024,768]{1,0:T(8,128)(2,1)S(1)} %get-tuple-element.268.xn.refs_1_, f32[4,768]{1,0:T(4,128)S(1)} %get-tuple-element.269.refs_2_, ...), custom_call_target="tpu_custom_call", output_to_operand_aliasing={{0}: (3, {}), {1}: (4, {})} | custom-call | flops 2415919104 | bytes 1048576 | tf_op jit(solution)/shard_map/up/pallas_call | solution.py:139
  135.8 7.6 %down_grad.1 = (bf16[3072,768]{1,0:T(8,128)(2,1)S(1)}, bf16[2,8,48,768]{3,2,1,0:T(8,128)(2,1)}, bf16[2,8,48,768]{3,2,1,0:T(8,128)(2,1)}, bf16[2,8,48,768]{3,2,1,0:T(8,128)(2,1)}, bf16[2,8,48,768]{3,2,1,0:T(8,128)(2,1)}) custom-call(s32[10]{0:T(128)S(1)} %stack.70.refs_0_.scal, bf16[4,1024,768]{2,1,0:T(8,128)(2,1)S(1)} %get-tuple-element.295.act, ...), custom_call_target="tpu_custom_call" | custom-call | flops 4831838208 | bytes 1048576 | tf_op jit(solution)/shard_map/down_grad/pallas_call | solution.py:139
  143.5 1.3 collective-permute-done.27.refs_2_
  144.7 1.4 sums_2.1
  147.8 7.1 %dpre.1 = (bf16[4,1024,768]{2,1,0:T(8,128)(2,1)S(1)}, f32[8,768]{1,0:T(8,128)S(1)}) custom-call(s32[10]{0:T(128)S(1)} %stack.70.refs_0_.scal, bf16[1024,768]{1,0:T(8,128)(2,1)S(1)} %bitcast.39, bf16[4,1024,768]{2,1,0:T(8,128)(2,1)S(1)} %get-tuple-element.305.gp, bf16[3072,768]{1,0:T(8,128)(2,1)S(1)} %get-tuple-element.306.w.wd), custom_call_target="tpu_custom_call", output_to_operand_aliasing={{0}: (2, {})} | custom-call | flops 4831838208 | bytes 1048576 | tf_op jit(solution)/shard_map/dpre/pallas_call | solution.py:139
  154.9 1.1 collective-permute-done.28.refs_3_
  156.2 1.7 sums_3.1
  158.5 1.5 collective-permute-start.36
  160.0 3.8 %collective-permute-start.32 = (bf16[2,48,768]{2,1,0:T(8,128)(2,1)S(1)}, bf16[2,48,768]{2,1,0:T(8,128)(2,1)S(1)}, u32[]{:S(2)}, u32[]{:S(2)}) collective-permute-start(bf16[2,48,768]{2,1,0:T(8,128)(2,1)S(1)} %get-tuple-element.323), channel_id=1, source_target_pairs={{0,4},{1,5},{2,6},{3,7},{4,0},{5,1},{6,2},{7,3},{8,12},{9,13},{10,... | collective-permute-start | bytes 442376 | tf_op jit(solution)/shard_map/ppermute | solution.py:536
  163.8 2.4 collective-permute-start.34
  166.1 7.9 %up_grad.1 = (bf16[1,768,768]{2,1,0:T(8,128)(2,1)S(1)}, bf16[2,8,48,768]{3,2,1,0:T(8,128)(2,1)}, bf16[2,8,48,768]{3,2,1,0:T(8,128)(2,1)}, bf16[2,8,48,768]{3,2,1,0:T(8,128)(2,1)}, bf16[2,8,48,768]{3,2,1,0:T(8,128)(2,1)}) custom-call(s32[10]{0:T(128)S(1)} %stack.70.refs_0_.scal, bf16[1024,768]{1,0:T(8,128)(2,1)S(1)} %get-tuple-element.268.xn.refs_1_, ...), custom_call_target="tpu_custom_call" | custom-call | flops 4831838208 | bytes 1048576 | tf_op jit(solution)/shard_map/up_grad/pallas_call | solution.py:139
  174.1 1.3 collective-permute-done.33.refs_2_
  175.4 1.4 sums_4.1
  177.5 1.3 collective-permute-start.37
  178.8 1.2 collective-permute-start.38
  180.8 8.4 %input_grad.1 = (f32[8,768]{1,0:T(8,128)S(1)}, bf16[2,512,768]{2,1,0:T(8,128)(2,1)}) custom-call(s32[10]{0:T(128)S(1)} %stack.70.refs_0_.scal, bf16[1024,768]{1,0:T(8,128)(2,1)S(1)} %bitcast.42, bf16[1024,768]{1,0:T(8,128)(2,1)S(1)} %bitcast.40, f32[1024,768]{1,0:T(8,128)S(1)} %get-tuple-element.349.dn, bf16[4,1024,768]{2,1,0:T(8,128)(2,1)S(1)} %get-tuple-element.328.dpre, ...), custom_call_target="tpu_custom_call" | custom-call | flops 8455716864 | bytes 1048576 | tf_op jit(solution)/shard_map/input_grad/pallas_call | solution.py:139
  189.2 1.6 collective-permute-done.41.a_other
  190.8 1.9 sums_5.1
  192.7 1.3 collective-permute-start.42
  195.0 3.4 %collective-permute-start.44 = (bf16[2,48,768]{2,1,0:T(8,128)(2,1)S(1)}, bf16[2,48,768]{2,1,0:T(8,128)(2,1)S(1)}, u32[]{:S(2)}, u32[]{:S(2)}) collective-permute-start(bf16[2,48,768]{2,1,0:T(8,128)(2,1)S(1)} %get-tuple-element.369), channel_id=1, source_target_pairs={{0,4},{1,5},{2,6},{3,7},{4,0},{5,1},{6,2},{7,3},{8,12},{9,13},{10,... | collective-permute-start | bytes 442376 | tf_op jit(solution)/shard_map/ppermute | solution.py:536
  198.5 2.4 collective-permute-start.46
  200.8 8.2 %out.1 = bf16[2,512,768]{2,1,0:T(8,128)(2,1)} custom-call(s32[10]{0:T(128)S(1)} %stack.70.refs_0_.scal, bf16[1024,768]{1,0:T(8,128)(2,1)S(1)} %bitcast.43, bf16[1024,768]{1,0:T(8,128)(2,1)S(1)} %get-tuple-element.256.o, bf16[4,1024,768]{2,1,0:T(8,128)(2,1)S(1)} %get-tuple-element.295.act, f32[8,768]{1,0:T(8,128)S(1)} %get-tuple-element.350.vec, ...), custom_call_target="tpu_custom_call" | custom-call | flops 6039797760 | bytes 1048576 | tf_op jit(solution)/shard_map/out/pallas_call | solution.py:139
  209.0 1.6 collective-permute-done.45.refs_5_
  210.7 1.4 sums_6.1
  212.0 1.1 collective-permute-start.47
  214.2 2.4 collective-permute-start.49
  216.6 2.4 collective-permute-start.51
  219.0 2.4 collective-permute-done.50.refs_7_
  222.2 1.4 sums_7.1
  223.6 1.3 collective-permute-start.55
  225.4 2.4 collective-permute-start.53
  227.8 1.5 collective-permute-start.54
  230.1 2.2 place.1
  232.9 4.0 %collective-permute-done.53.refs_2_ = bf16[2,48,768]{2,1,0:T(8,128)(2,1)S(1)} collective-permute-done((bf16[2,48,768]{2,1,0:T(8,128)(2,1)S(1)}, bf16[2,48,768]{2,1,0:T(8,128)(2,1)S(1)}, u32[]{:S(2)}, u32[]{:S(2)}) %collective-permute-start.53) | collective-permute-done | bytes 147488 | tf_op jit(solution)/shard_map/ppermute | solution.py:536
  237.8 1.1 collective-permute-start.60
  239.8 1.3 collective-permute-done.59
  243.8 1.3 collective-permute-done.57.other
  245.0 1.4 place_last.1
  (160 shorter events, 24.2 us)
Async XLA Ops:
  2.7 10.2 %collective-permute-start.2 = (bf16[104,768]{1,0:T(8,128)(2,1)S(1)}, bf16[104,768]{1,0:T(8,128)(2,1)S(1)}, u32[]{:S(2)}, u32[]{:S(2)}) collective-permute-start(bf16[104,768]{1,0:T(8,128)(2,1)S(1)} %pad_maximum_fusion.5), channel_id=1, source_target_pairs={{0,12},{1,13},{2,14},{3,15},{4,8},{5,9},{6,10},{7,11},{8,4},{9,5},... | collective-permute-start | bytes 479240 | tf_op jit(solution)/shard_map/ppermute | solution.py:536
  7.9 13.5 %collective-permute-start.1 = (bf16[104,768]{1,0:T(8,128)(2,1)S(1)}, bf16[104,768]{1,0:T(8,128)(2,1)S(1)}, u32[]{:S(2)}, u32[]{:S(2)}) collective-permute-start(bf16[104,768]{1,0:T(8,128)(2,1)S(1)} %pad_maximum_fusion.5), channel_id=1, source_target_pairs={{0,8},{1,9},{2,10},{3,11},{4,12},{5,13},{6,14},{7,15},{8,0},{9,1},... | collective-permute-start | bytes 479240 | tf_op jit(solution)/shard_map/ppermute | solution.py:536
  7.9 13.5 %collective-permute-start = (bf16[104,768]{1,0:T(8,128)(2,1)S(1)}, bf16[104,768]{1,0:T(8,128)(2,1)S(1)}, u32[]{:S(2)}, u32[]{:S(2)}) collective-permute-start(bf16[104,768]{1,0:T(8,128)(2,1)S(1)} %pad_maximum_fusion.5), channel_id=1, source_target_pairs={{0,4},{1,5},{2,6},{3,7},{4,0},{5,1},{6,2},{7,3},{8,12},{9,13},{10,... | collective-permute-start | bytes 479240 | tf_op jit(solution)/shard_map/ppermute | solution.py:536
  21.5 19.3 %copy-start.6 = (bf16[4,56,768]{2,1,0:T(8,128)(2,1)}, bf16[4,56,768]{2,1,0:T(8,128)(2,1)S(1)}, u32[]{:S(2)}) copy-start(bf16[4,56,768]{2,1,0:T(8,128)(2,1)S(1)} %pad_maximum_fusion.2.refs_0_.refs_3_) | copy-start | bytes 1032196
  21.5 18.0 %collective-permute-start.3 = (bf16[4,56,768]{2,1,0:T(8,128)(2,1)S(1)}, bf16[4,56,768]{2,1,0:T(8,128)(2,1)S(1)}, u32[]{:S(2)}, u32[]{:S(2)}) collective-permute-start(bf16[4,56,768]{2,1,0:T(8,128)(2,1)S(1)} %pad_maximum_fusion.2.refs_0_.refs_3_), channel_id=1, source_target_pairs={{0,2},{1,3},{2,0},{3,1},{4,6},{5,7},{6,4},{7,5},{8,10},{9,11},{10,... | collective-permute-start | bytes 1032200 | tf_op jit(solution)/shard_map/ppermute | solution.py:536
  23.0 16.4 %collective-permute-start.5 = (bf16[4,56,768]{2,1,0:T(8,128)(2,1)S(1)}, bf16[4,56,768]{2,1,0:T(8,128)(2,1)S(1)}, u32[]{:S(2)}, u32[]{:S(2)}) collective-permute-start(bf16[4,56,768]{2,1,0:T(8,128)(2,1)S(1)} %pad_maximum_fusion.2.refs_0_.refs_3_), channel_id=1, source_target_pairs={{0,16},{16,0},{1,17},{17,1},{2,18},{18,2},{3,19},{19,3},{4,20},{20... | collective-permute-start | bytes 1032200 | tf_op jit(solution)/shard_map/ppermute | solution.py:540
  24.7 14.8 %collective-permute-start.7 = (bf16[2,2,48,768]{3,2,1,0:T(8,128)(2,1)}, bf16[2,2,48,768]{3,2,1,0:T(8,128)(2,1)}, u32[]{:S(2)}, u32[]{:S(2)}) collective-permute-start(bf16[2,2,48,768]{3,2,1,0:T(8,128)(2,1)} %bitcast.20), channel_id=1, source_target_pairs={{0,8},{1,9},{2,10},{3,11},{4,12},{5,13},{6,14},{7,15},{8,0},{9,1},... | collective-permute-start | bytes 884744 | tf_op jit(solution)/shard_map/ppermute | solution.py:536
  24.8 14.7 %collective-permute-start.4 = (bf16[4,48,768]{2,1,0:T(8,128)(2,1)S(1)}, bf16[4,48,768]{2,1,0:T(8,128)(2,1)}, u32[]{:S(2)}, u32[]{:S(2)}) collective-permute-start(bf16[4,48,768]{2,1,0:T(8,128)(2,1)S(1)} %pad_maximum_fusion.3.refs_3_.refs_7_.refs_4_), channel_id=1, source_target_pairs={{0,16},{16,0},{1,17},{17,1},{2,18},{18,2},{3,19},{19,3},{4,20},{20... | collective-permute-start | bytes 884744 | tf_op jit(solution)/shard_map/ppermute | solution.py:540
  25.3 14.1 %collective-permute-start.6 = (bf16[4,48,768]{2,1,0:T(8,128)(2,1)S(1)}, bf16[4,48,768]{2,1,0:T(8,128)(2,1)S(1)}, u32[]{:S(2)}, u32[]{:S(2)}) collective-permute-start(bf16[4,48,768]{2,1,0:T(8,128)(2,1)S(1)} %pad_maximum_fusion.3.refs_3_.refs_7_.refs_4_), channel_id=1, source_target_pairs={{0,2},{1,3},{2,0},{3,1},{4,6},{5,7},{6,4},{7,5},{8,10},{9,11},{10,... | collective-permute-start | bytes 884744 | tf_op jit(solution)/shard_map/ppermute | solution.py:536
  40.9 16.9 %collective-permute-start.10 = (bf16[24,56,768]{2,1,0:T(8,128)(2,1)S(1)}, bf16[24,56,768]{2,1,0:T(8,128)(2,1)}, u32[]{:S(2)}, u32[]{:S(2)}) collective-permute-start(bf16[24,56,768]{2,1,0:T(8,128)(2,1)S(1)} %join_a.1), channel_id=1, source_target_pairs={{0,1},{1,0},{2,3},{3,2},{4,5},{5,4},{6,7},{7,6},{8,9},{9,8},{10,11... | collective-permute-start | bytes 6193160 | tf_op jit(solution)/shard_map/ppermute | solution.py:536
  40.9 16.8 %collective-permute-start.8 = (bf16[4,56,768]{2,1,0:T(8,128)(2,1)S(1)}, bf16[4,56,768]{2,1,0:T(8,128)(2,1)}, u32[]{:S(2)}, u32[]{:S(2)}) collective-permute-start(bf16[4,56,768]{2,1,0:T(8,128)(2,1)S(1)} %collective-permute-done.3.refs_1_.refs_4_), channel_id=1, source_target_pairs={{0,16},{16,0},{1,17},{17,1},{2,18},{18,2},{3,19},{19,3},{4,20},{20... | collective-permute-start | bytes 1032200 | tf_op jit(solution)/shard_map/ppermute | solution.py:540
  41.5 9.3 %collective-permute-start.11 = (bf16[2,2,48,768]{3,2,1,0:T(8,128)(2,1)}, bf16[2,2,48,768]{3,2,1,0:T(8,128)(2,1)S(1)}, u32[]{:S(2)}, u32[]{:S(2)}) collective-permute-start(bf16[2,2,48,768]{3,2,1,0:T(8,128)(2,1)} %bitcast.20), channel_id=1, source_target_pairs={{0,4},{1,5},{2,6},{3,7},{4,0},{5,1},{6,2},{7,3},{8,12},{9,13},{10,... | collective-permute-start | bytes 884744 | tf_op jit(solution)/shard_map/ppermute | solution.py:536
  41.5 16.3 %collective-permute-start.12 = (bf16[2,2,48,768]{3,2,1,0:T(8,128)(2,1)}, bf16[2,2,48,768]{3,2,1,0:T(8,128)(2,1)}, u32[]{:S(2)}, u32[]{:S(2)}) collective-permute-start(bf16[2,2,48,768]{3,2,1,0:T(8,128)(2,1)} %bitcast.20), channel_id=1, source_target_pairs={{0,12},{1,13},{2,14},{3,15},{4,8},{5,9},{6,10},{7,11},{8,4},{9,5},... | collective-permute-start | bytes 884744 | tf_op jit(solution)/shard_map/ppermute | solution.py:536
  43.7 14.1 %collective-permute-start.9 = (bf16[4,48,768]{2,1,0:T(8,128)(2,1)}, bf16[4,48,768]{2,1,0:T(8,128)(2,1)}, u32[]{:S(2)}, u32[]{:S(2)}) collective-permute-start(bf16[4,48,768]{2,1,0:T(8,128)(2,1)} %collective-permute-done.4.refs_5_.refs_9_.refs_6_), channel_id=1, source_target_pairs={{0,2},{1,3},{2,0},{3,1},{4,6},{5,7},{6,4},{7,5},{8,10},{9,11},{10,... | collective-permute-start | bytes 884744 | tf_op jit(solution)/shard_map/ppermute | solution.py:536
  57.8 2.4 collective-permute-start.13
  57.9 2.3 collective-permute-start.14
  59.5 25.0 %copy-start.14 = (bf16[4,2,48,768]{3,2,1,0:T(8,128)(2,1)}, bf16[4,2,48,768]{3,2,1,0:T(8,128)(2,1)S(1)}, u32[]{:S(2)}) copy-start(bf16[4,2,48,768]{3,2,1,0:T(8,128)(2,1)S(1)} %pad_maximum_fusion.1.refs_7_.refs_4_) | copy-start | bytes 1769476
  60.1 24.3 %collective-permute-start.15 = (bf16[4,2,48,768]{3,2,1,0:T(8,128)(2,1)S(1)}, bf16[4,2,48,768]{3,2,1,0:T(8,128)(2,1)S(1)}, u32[]{:S(2)}, u32[]{:S(2)}) collective-permute-start(bf16[4,2,48,768]{3,2,1,0:T(8,128)(2,1)S(1)} %pad_maximum_fusion.refs_3_.refs_0_), channel_id=1, source_target_pairs={{0,2},{1,3},{2,0},{3,1},{4,6},{5,7},{6,4},{7,5},{8,10},{9,11},{10,... | collective-permute-start | bytes 1769480 | tf_op jit(solution)/shard_map/ppermute | solution.py:536
  60.7 31.3 %collective-permute-start.17 = (bf16[4,2,48,768]{3,2,1,0:T(8,128)(2,1)S(1)}, bf16[4,2,48,768]{3,2,1,0:T(8,128)(2,1)S(1)}, u32[]{:S(2)}, u32[]{:S(2)}) collective-permute-start(bf16[4,2,48,768]{3,2,1,0:T(8,128)(2,1)S(1)} %pad_maximum_fusion.refs_3_.refs_0_), channel_id=1, source_target_pairs={{0,16},{16,0},{1,17},{17,1},{2,18},{18,2},{3,19},{19,3},{4,20},{20... | collective-permute-start | bytes 1769480 | tf_op jit(solution)/shard_map/ppermute | solution.py:540
  61.7 30.4 %collective-permute-start.16 = (bf16[4,2,48,768]{3,2,1,0:T(8,128)(2,1)S(1)}, bf16[4,2,48,768]{3,2,1,0:T(8,128)(2,1)S(1)}, u32[]{:S(2)}, u32[]{:S(2)}) collective-permute-start(bf16[4,2,48,768]{3,2,1,0:T(8,128)(2,1)S(1)} %pad_maximum_fusion.1.refs_7_.refs_4_), channel_id=1, source_target_pairs={{0,16},{16,0},{1,17},{17,1},{2,18},{18,2},{3,19},{19,3},{4,20},{20... | collective-permute-start | bytes 1769480 | tf_op jit(solution)/shard_map/ppermute | solution.py:540
  62.8 29.3 %collective-permute-start.18 = (bf16[4,2,48,768]{3,2,1,0:T(8,128)(2,1)S(1)}, bf16[4,2,48,768]{3,2,1,0:T(8,128)(2,1)S(1)}, u32[]{:S(2)}, u32[]{:S(2)}) collective-permute-start(bf16[4,2,48,768]{3,2,1,0:T(8,128)(2,1)S(1)} %pad_maximum_fusion.1.refs_7_.refs_4_), channel_id=1, source_target_pairs={{0,2},{1,3},{2,0},{3,1},{4,6},{5,7},{6,4},{7,5},{8,10},{9,11},{10,... | collective-permute-start | bytes 1769480 | tf_op jit(solution)/shard_map/ppermute | solution.py:536
  64.3 38.7 %collective-permute-start.21 = (bf16[4,2,48,768]{3,2,1,0:T(8,128)(2,1)S(1)}, bf16[4,2,48,768]{3,2,1,0:T(8,128)(2,1)S(1)}, u32[]{:S(2)}, u32[]{:S(2)}) collective-permute-start(bf16[4,2,48,768]{3,2,1,0:T(8,128)(2,1)S(1)} %pad_maximum_fusion.refs_3_.refs_0_), channel_id=1, source_target_pairs={{0,1},{1,0},{2,3},{3,2},{4,5},{5,4},{6,7},{7,6},{8,9},{9,8},{10,11... | collective-permute-start | bytes 1769480 | tf_op jit(solution)/shard_map/ppermute | solution.py:536
  84.5 23.0 %copy-start = (bf16[4,2,48,768]{3,2,1,0:T(8,128)(2,1)}, bf16[4,2,48,768]{3,2,1,0:T(8,128)(2,1)S(1)}, u32[]{:S(2)}) copy-start(bf16[4,2,48,768]{3,2,1,0:T(8,128)(2,1)S(1)} %collective-permute-done.15.refs_0_.refs_4_.refs_1_) | copy-start | bytes 1769476
  84.5 18.5 %collective-permute-start.22 = (bf16[4,2,48,768]{3,2,1,0:T(8,128)(2,1)S(1)}, bf16[4,2,48,768]{3,2,1,0:T(8,128)(2,1)S(1)}, u32[]{:S(2)}, u32[]{:S(2)}) collective-permute-start(bf16[4,2,48,768]{3,2,1,0:T(8,128)(2,1)S(1)} %pad_maximum_fusion.1.refs_7_.refs_4_), channel_id=1, source_target_pairs={{0,1},{1,0},{2,3},{3,2},{4,5},{5,4},{6,7},{7,6},{8,9},{9,8},{10,11... | collective-permute-start | bytes 1769480 | tf_op jit(solution)/shard_map/ppermute | solution.py:536
  92.1 15.3 %collective-permute-start.19 = (bf16[4,2,48,768]{3,2,1,0:T(8,128)(2,1)S(1)}, bf16[4,2,48,768]{3,2,1,0:T(8,128)(2,1)S(1)}, u32[]{:S(2)}, u32[]{:S(2)}) collective-permute-start(bf16[4,2,48,768]{3,2,1,0:T(8,128)(2,1)S(1)} %collective-permute-done.15.refs_0_.refs_4_.refs_1_), channel_id=1, source_target_pairs={{0,16},{16,0},{1,17},{17,1},{2,18},{18,2},{3,19},{19,3},{4,20},{20... | collective-permute-start | bytes 1769480 | tf_op jit(solution)/shard_map/ppermute | solution.py:540
  92.2 15.3 %collective-permute-start.20 = (bf16[4,2,48,768]{3,2,1,0:T(8,128)(2,1)S(1)}, bf16[4,2,48,768]{3,2,1,0:T(8,128)(2,1)S(1)}, u32[]{:S(2)}, u32[]{:S(2)}) collective-permute-start(bf16[4,2,48,768]{3,2,1,0:T(8,128)(2,1)S(1)} %collective-permute-done.16.refs_4_.refs_9_.refs_6_), channel_id=1, source_target_pairs={{0,2},{1,3},{2,0},{3,1},{4,6},{5,7},{6,4},{7,5},{8,10},{9,11},{10,... | collective-permute-start | bytes 1769480 | tf_op jit(solution)/shard_map/ppermute | solution.py:536
  108.4 7.8 %collective-permute-start.23 = (bf16[24,2,48,768]{3,2,1,0:T(8,128)(2,1)S(1)}, bf16[24,2,48,768]{3,2,1,0:T(8,128)(2,1)S(1)}, u32[]{:S(2)}, u32[]{:S(2)}) collective-permute-start(bf16[24,2,48,768]{3,2,1,0:T(8,128)(2,1)S(1)} %join_c.1), channel_id=1, source_target_pairs={{0,1},{1,0},{2,3},{3,2},{4,5},{5,4},{6,7},{7,6},{8,9},{9,8},{10,11... | collective-permute-start | bytes 10616840 | tf_op jit(solution)/shard_map/ppermute | solution.py:536
  116.2 9.8 %collective-permute-start.24 = (bf16[2,8,48,768]{3,2,1,0:T(8,128)(2,1)}, bf16[2,8,48,768]{3,2,1,0:T(8,128)(2,1)S(1)}, u32[]{:S(2)}, u32[]{:S(2)}) collective-permute-start(bf16[2,8,48,768]{3,2,1,0:T(8,128)(2,1)} %get-tuple-element.282), channel_id=1, source_target_pairs={{0,1},{1,0},{2,3},{3,2},{4,5},{5,4},{6,7},{7,6},{8,9},{9,8},{10,11... | collective-permute-start | bytes 3538952 | tf_op jit(solution)/shard_map/ppermute | solution.py:536
  116.8 9.3 %collective-permute-start.25 = (bf16[2,8,48,768]{3,2,1,0:T(8,128)(2,1)}, bf16[2,8,48,768]{3,2,1,0:T(8,128)(2,1)S(1)}, u32[]{:S(2)}, u32[]{:S(2)}) collective-permute-start(bf16[2,8,48,768]{3,2,1,0:T(8,128)(2,1)} %get-tuple-element.283), channel_id=1, source_target_pairs={{0,1},{1,0},{2,3},{3,2},{4,5},{5,4},{6,7},{7,6},{8,9},{9,8},{10,11... | collective-permute-start | bytes 3538952 | tf_op jit(solution)/shard_map/ppermute | solution.py:536
  127.7 15.8 %collective-permute-start.26 = (bf16[8,48,768]{2,1,0:T(8,128)(2,1)S(1)}, bf16[8,48,768]{2,1,0:T(8,128)(2,1)S(1)}, u32[]{:S(2)}, u32[]{:S(2)}) collective-permute-start(bf16[8,48,768]{2,1,0:T(8,128)(2,1)S(1)} %get-tuple-element.293), channel_id=1, source_target_pairs={{0,16},{16,0},{1,17},{17,1},{2,18},{18,2},{3,19},{19,3},{4,20},{20... | collective-permute-start | bytes 1769480 | tf_op jit(solution)/shard_map/ppermute | solution.py:540
  129.3 15.5 %collective-permute-start.27 = (bf16[8,48,768]{2,1,0:T(8,128)(2,1)S(1)}, bf16[8,48,768]{2,1,0:T(8,128)(2,1)S(1)}, u32[]{:S(2)}, u32[]{:S(2)}) collective-permute-start(bf16[8,48,768]{2,1,0:T(8,128)(2,1)S(1)} %get-tuple-element.294), channel_id=1, source_target_pairs={{0,2},{1,3},{2,0},{3,1},{4,6},{5,7},{6,4},{7,5},{8,10},{9,11},{10,... | collective-permute-start | bytes 1769480 | tf_op jit(solution)/shard_map/ppermute | solution.py:536
  146.2 10.0 %collective-permute-start.30 = (bf16[2,8,48,768]{3,2,1,0:T(8,128)(2,1)S(1)}, bf16[2,8,48,768]{3,2,1,0:T(8,128)(2,1)S(1)}, u32[]{:S(2)}, u32[]{:S(2)}) collective-permute-start(bf16[2,8,48,768]{3,2,1,0:T(8,128)(2,1)S(1)} %copy-done.21), channel_id=1, source_target_pairs={{0,1},{1,0},{2,3},{3,2},{4,5},{5,4},{6,7},{7,6},{8,9},{9,8},{10,11... | collective-permute-start | bytes 3538952 | tf_op jit(solution)/shard_map/ppermute | solution.py:536
  146.5 9.7 %collective-permute-start.31 = (bf16[2,8,48,768]{3,2,1,0:T(8,128)(2,1)S(1)}, bf16[2,8,48,768]{3,2,1,0:T(8,128)(2,1)S(1)}, u32[]{:S(2)}, u32[]{:S(2)}) collective-permute-start(bf16[2,8,48,768]{3,2,1,0:T(8,128)(2,1)S(1)} %copy-done.20), channel_id=1, source_target_pairs={{0,1},{1,0},{2,3},{3,2},{4,5},{5,4},{6,7},{7,6},{8,9},{9,8},{10,11... | collective-permute-start | bytes 3538952 | tf_op jit(solution)/shard_map/ppermute | solution.py:536
  146.8 9.2 %collective-permute-start.28 = (bf16[4,48,768]{2,1,0:T(8,128)(2,1)S(1)}, bf16[4,48,768]{2,1,0:T(8,128)(2,1)S(1)}, u32[]{:S(2)}, u32[]{:S(2)}) collective-permute-start(bf16[4,48,768]{2,1,0:T(8,128)(2,1)S(1)} %get-tuple-element.308), channel_id=1, source_target_pairs={{0,2},{1,3},{2,0},{3,1},{4,6},{5,7},{6,4},{7,5},{8,10},{9,11},{10,... | collective-permute-start | bytes 884744 | tf_op jit(solution)/shard_map/ppermute | solution.py:536
  147.3 8.9 %collective-permute-start.29 = (bf16[4,48,768]{2,1,0:T(8,128)(2,1)S(1)}, bf16[4,48,768]{2,1,0:T(8,128)(2,1)S(1)}, u32[]{:S(2)}, u32[]{:S(2)}) collective-permute-start(bf16[4,48,768]{2,1,0:T(8,128)(2,1)S(1)} %get-tuple-element.309), channel_id=1, source_target_pairs={{0,16},{16,0},{1,17},{17,1},{2,18},{18,2},{3,19},{19,3},{4,20},{20... | collective-permute-start | bytes 884744 | tf_op jit(solution)/shard_map/ppermute | solution.py:540
  158.0 17.5 %collective-permute-start.35 = (bf16[8,48,768]{2,1,0:T(8,128)(2,1)S(1)}, bf16[8,48,768]{2,1,0:T(8,128)(2,1)S(1)}, u32[]{:S(2)}, u32[]{:S(2)}) collective-permute-start(bf16[8,48,768]{2,1,0:T(8,128)(2,1)S(1)} %get-tuple-element.326), channel_id=1, source_target_pairs={{0,16},{16,0},{1,17},{17,1},{2,18},{18,2},{3,19},{19,3},{4,20},{20... | collective-permute-start | bytes 1769480 | tf_op jit(solution)/shard_map/ppermute | solution.py:540
  158.5 16.9 %collective-permute-start.36 = (bf16[8,48,768]{2,1,0:T(8,128)(2,1)S(1)}, bf16[8,48,768]{2,1,0:T(8,128)(2,1)S(1)}, u32[]{:S(2)}, u32[]{:S(2)}) collective-permute-start(bf16[8,48,768]{2,1,0:T(8,128)(2,1)S(1)} %get-tuple-element.327), channel_id=1, source_target_pairs={{0,2},{1,3},{2,0},{3,1},{4,6},{5,7},{6,4},{7,5},{8,10},{9,11},{10,... | collective-permute-start | bytes 1769480 | tf_op jit(solution)/shard_map/ppermute | solution.py:536
  160.0 14.0 %collective-permute-start.32 = (bf16[2,48,768]{2,1,0:T(8,128)(2,1)S(1)}, bf16[2,48,768]{2,1,0:T(8,128)(2,1)S(1)}, u32[]{:S(2)}, u32[]{:S(2)}) collective-permute-start(bf16[2,48,768]{2,1,0:T(8,128)(2,1)S(1)} %get-tuple-element.323), channel_id=1, source_target_pairs={{0,4},{1,5},{2,6},{3,7},{4,0},{5,1},{6,2},{7,3},{8,12},{9,13},{10,... | collective-permute-start | bytes 442376 | tf_op jit(solution)/shard_map/ppermute | solution.py:536
  163.8 11.6 %collective-permute-start.33 = (bf16[2,48,768]{2,1,0:T(8,128)(2,1)S(1)}, bf16[2,48,768]{2,1,0:T(8,128)(2,1)S(1)}, u32[]{:S(2)}, u32[]{:S(2)}) collective-permute-start(bf16[2,48,768]{2,1,0:T(8,128)(2,1)S(1)} %get-tuple-element.324), channel_id=1, source_target_pairs={{0,8},{1,9},{2,10},{3,11},{4,12},{5,13},{6,14},{7,15},{8,0},{9,1},... | collective-permute-start | bytes 442376 | tf_op jit(solution)/shard_map/ppermute | solution.py:536
  163.8 11.6 %collective-permute-start.34 = (bf16[2,48,768]{2,1,0:T(8,128)(2,1)S(1)}, bf16[2,48,768]{2,1,0:T(8,128)(2,1)S(1)}, u32[]{:S(2)}, u32[]{:S(2)}) collective-permute-start(bf16[2,48,768]{2,1,0:T(8,128)(2,1)S(1)} %get-tuple-element.325), channel_id=1, source_target_pairs={{0,12},{1,13},{2,14},{3,15},{4,8},{5,9},{6,10},{7,11},{8,4},{9,5},... | collective-permute-start | bytes 442376 | tf_op jit(solution)/shard_map/ppermute | solution.py:536
  176.9 13.9 %collective-permute-start.39 = (bf16[2,8,48,768]{3,2,1,0:T(8,128)(2,1)S(1)}, bf16[2,8,48,768]{3,2,1,0:T(8,128)(2,1)S(1)}, u32[]{:S(2)}, u32[]{:S(2)}) collective-permute-start(bf16[2,8,48,768]{3,2,1,0:T(8,128)(2,1)S(1)} %copy-done.19), channel_id=1, source_target_pairs={{0,1},{1,0},{2,3},{3,2},{4,5},{5,4},{6,7},{7,6},{8,9},{9,8},{10,11... | collective-permute-start | bytes 3538952 | tf_op jit(solution)/shard_map/ppermute | solution.py:536
  177.2 13.6 %collective-permute-start.40 = (bf16[2,8,48,768]{3,2,1,0:T(8,128)(2,1)S(1)}, bf16[2,8,48,768]{3,2,1,0:T(8,128)(2,1)S(1)}, u32[]{:S(2)}, u32[]{:S(2)}) collective-permute-start(bf16[2,8,48,768]{3,2,1,0:T(8,128)(2,1)S(1)} %copy-done.18), channel_id=1, source_target_pairs={{0,1},{1,0},{2,3},{3,2},{4,5},{5,4},{6,7},{7,6},{8,9},{9,8},{10,11... | collective-permute-start | bytes 3538952 | tf_op jit(solution)/shard_map/ppermute | solution.py:536
  177.5 13.3 %collective-permute-start.37 = (bf16[4,48,768]{2,1,0:T(8,128)(2,1)S(1)}, bf16[4,48,768]{2,1,0:T(8,128)(2,1)S(1)}, u32[]{:S(2)}, u32[]{:S(2)}) collective-permute-start(bf16[4,48,768]{2,1,0:T(8,128)(2,1)S(1)} %get-tuple-element.343), channel_id=1, source_target_pairs={{0,2},{1,3},{2,0},{3,1},{4,6},{5,7},{6,4},{7,5},{8,10},{9,11},{10,... | collective-permute-start | bytes 884744 | tf_op jit(solution)/shard_map/ppermute | solution.py:536
  178.8 12.1 %collective-permute-start.38 = (bf16[4,48,768]{2,1,0:T(8,128)(2,1)S(1)}, bf16[4,48,768]{2,1,0:T(8,128)(2,1)S(1)}, u32[]{:S(2)}, u32[]{:S(2)}) collective-permute-start(bf16[4,48,768]{2,1,0:T(8,128)(2,1)S(1)} %get-tuple-element.344), channel_id=1, source_target_pairs={{0,16},{16,0},{1,17},{17,1},{2,18},{18,2},{3,19},{19,3},{4,20},{20... | collective-permute-start | bytes 884744 | tf_op jit(solution)/shard_map/ppermute | solution.py:540
  180.0 10.8 %collective-permute-start.41 = (bf16[2,48,768]{2,1,0:T(8,128)(2,1)S(1)}, bf16[2,48,768]{2,1,0:T(8,128)(2,1)S(1)}, u32[]{:S(2)}, u32[]{:S(2)}) collective-permute-start(bf16[2,48,768]{2,1,0:T(8,128)(2,1)S(1)} %get-tuple-element.347.a_mine), channel_id=1, source_target_pairs={{0,16},{16,0},{1,17},{17,1},{2,18},{18,2},{3,19},{19,3},{4,20},{20... | collective-permute-start | bytes 442376 | tf_op jit(solution)/shard_map/ppermute | solution.py:540
  192.7 18.0 %collective-permute-start.42 = (bf16[8,48,768]{2,1,0:T(8,128)(2,1)S(1)}, bf16[8,48,768]{2,1,0:T(8,128)(2,1)S(1)}, u32[]{:S(2)}, u32[]{:S(2)}) collective-permute-start(bf16[8,48,768]{2,1,0:T(8,128)(2,1)S(1)} %get-tuple-element.367), channel_id=1, source_target_pairs={{0,16},{16,0},{1,17},{17,1},{2,18},{18,2},{3,19},{19,3},{4,20},{20... | collective-permute-start | bytes 1769480 | tf_op jit(solution)/shard_map/ppermute | solution.py:540
  194.0 16.7 %collective-permute-start.43 = (bf16[8,48,768]{2,1,0:T(8,128)(2,1)S(1)}, bf16[8,48,768]{2,1,0:T(8,128)(2,1)S(1)}, u32[]{:S(2)}, u32[]{:S(2)}) collective-permute-start(bf16[8,48,768]{2,1,0:T(8,128)(2,1)S(1)} %get-tuple-element.368), channel_id=1, source_target_pairs={{0,2},{1,3},{2,0},{3,1},{4,6},{5,7},{6,4},{7,5},{8,10},{9,11},{10,... | collective-permute-start | bytes 1769480 | tf_op jit(solution)/shard_map/ppermute | solution.py:536
  195.0 14.0 %collective-permute-start.44 = (bf16[2,48,768]{2,1,0:T(8,128)(2,1)S(1)}, bf16[2,48,768]{2,1,0:T(8,128)(2,1)S(1)}, u32[]{:S(2)}, u32[]{:S(2)}) collective-permute-start(bf16[2,48,768]{2,1,0:T(8,128)(2,1)S(1)} %get-tuple-element.369), channel_id=1, source_target_pairs={{0,4},{1,5},{2,6},{3,7},{4,0},{5,1},{6,2},{7,3},{8,12},{9,13},{10,... | collective-permute-start | bytes 442376 | tf_op jit(solution)/shard_map/ppermute | solution.py:536
  198.5 12.2 %collective-permute-start.45 = (bf16[2,48,768]{2,1,0:T(8,128)(2,1)S(1)}, bf16[2,48,768]{2,1,0:T(8,128)(2,1)S(1)}, u32[]{:S(2)}, u32[]{:S(2)}) collective-permute-start(bf16[2,48,768]{2,1,0:T(8,128)(2,1)S(1)} %get-tuple-element.370), channel_id=1, source_target_pairs={{0,8},{1,9},{2,10},{3,11},{4,12},{5,13},{6,14},{7,15},{8,0},{9,1},... | collective-permute-start | bytes 442376 | tf_op jit(solution)/shard_map/ppermute | solution.py:536
  198.5 12.2 %collective-permute-start.46 = (bf16[2,48,768]{2,1,0:T(8,128)(2,1)S(1)}, bf16[2,48,768]{2,1,0:T(8,128)(2,1)S(1)}, u32[]{:S(2)}, u32[]{:S(2)}) collective-permute-start(bf16[2,48,768]{2,1,0:T(8,128)(2,1)S(1)} %get-tuple-element.371), channel_id=1, source_target_pairs={{0,12},{1,13},{2,14},{3,15},{4,8},{5,9},{6,10},{7,11},{8,4},{9,5},... | collective-permute-start | bytes 442376 | tf_op jit(solution)/shard_map/ppermute | solution.py:536
  212.0 10.2 %collective-permute-start.47 = (bf16[4,48,768]{2,1,0:T(8,128)(2,1)S(1)}, bf16[4,48,768]{2,1,0:T(8,128)(2,1)S(1)}, u32[]{:S(2)}, u32[]{:S(2)}) collective-permute-start(bf16[4,48,768]{2,1,0:T(8,128)(2,1)S(1)} %get-tuple-element.384), channel_id=1, source_target_pairs={{0,2},{1,3},{2,0},{3,1},{4,6},{5,7},{6,4},{7,5},{8,10},{9,11},{10,... | collective-permute-start | bytes 884744 | tf_op jit(solution)/shard_map/ppermute | solution.py:536
  213.2 9.1 %collective-permute-start.48 = (bf16[4,48,768]{2,1,0:T(8,128)(2,1)S(1)}, bf16[4,48,768]{2,1,0:T(8,128)(2,1)S(1)}, u32[]{:S(2)}, u32[]{:S(2)}) collective-permute-start(bf16[4,48,768]{2,1,0:T(8,128)(2,1)S(1)} %get-tuple-element.385), channel_id=1, source_target_pairs={{0,16},{16,0},{1,17},{17,1},{2,18},{18,2},{3,19},{19,3},{4,20},{20... | collective-permute-start | bytes 884744 | tf_op jit(solution)/shard_map/ppermute | solution.py:540
  214.2 4.7 %collective-permute-start.49 = (f32[8,768]{1,0:T(8,128)S(1)}, f32[8,768]{1,0:T(8,128)S(1)}, u32[]{:S(2)}, u32[]{:S(2)}) collective-permute-start(f32[8,768]{1,0:T(8,128)S(1)} %get-tuple-element.386.refs_5_), channel_id=1, source_target_pairs={{0,4},{1,5},{2,6},{3,7},{4,0},{5,1},{6,2},{7,3},{8,12},{9,13},{10,... | collective-permute-start | bytes 73736 | tf_op jit(solution)/shard_map/ppermute | solution.py:536
  216.6 4.7 %collective-permute-start.50 = (f32[8,768]{1,0:T(8,128)S(1)}, f32[8,768]{1,0:T(8,128)S(1)}, u32[]{:S(2)}, u32[]{:S(2)}) collective-permute-start(f32[8,768]{1,0:T(8,128)S(1)} %get-tuple-element.386.refs_5_), channel_id=1, source_target_pairs={{0,8},{1,9},{2,10},{3,11},{4,12},{5,13},{6,14},{7,15},{8,0},{9,1},... | collective-permute-start | bytes 73736 | tf_op jit(solution)/shard_map/ppermute | solution.py:536
  216.6 5.6 %collective-permute-start.51 = (f32[8,768]{1,0:T(8,128)S(1)}, f32[8,768]{1,0:T(8,128)S(1)}, u32[]{:S(2)}, u32[]{:S(2)}) collective-permute-start(f32[8,768]{1,0:T(8,128)S(1)} %get-tuple-element.386.refs_5_), channel_id=1, source_target_pairs={{0,12},{1,13},{2,14},{3,15},{4,8},{5,9},{6,10},{7,11},{8,4},{9,5},... | collective-permute-start | bytes 73736 | tf_op jit(solution)/shard_map/ppermute | solution.py:536
  223.6 6.5 %collective-permute-start.55 = (bf16[2,48,768]{2,1,0:T(8,128)(2,1)S(1)}, bf16[2,48,768]{2,1,0:T(8,128)(2,1)S(1)}, u32[]{:S(2)}, u32[]{:S(2)}) collective-permute-start(bf16[2,48,768]{2,1,0:T(8,128)(2,1)S(1)} %get-tuple-element.397.d_mine), channel_id=1, source_target_pairs={{0,16},{16,0},{1,17},{17,1},{2,18},{18,2},{3,19},{19,3},{4,20},{20... | collective-permute-start | bytes 442376 | tf_op jit(solution)/shard_map/ppermute | solution.py:540
  224.9 8.0 %collective-permute-start.52 = (bf16[2,48,768]{2,1,0:T(8,128)(2,1)S(1)}, bf16[2,48,768]{2,1,0:T(8,128)(2,1)S(1)}, u32[]{:S(2)}, u32[]{:S(2)}) collective-permute-start(bf16[2,48,768]{2,1,0:T(8,128)(2,1)S(1)} %get-tuple-element.393), channel_id=1, source_target_pairs={{0,4},{1,5},{2,6},{3,7},{4,0},{5,1},{6,2},{7,3},{8,12},{9,13},{10,... | collective-permute-start | bytes 442376 | tf_op jit(solution)/shard_map/ppermute | solution.py:536
  225.4 11.4 %collective-permute-start.53 = (bf16[2,48,768]{2,1,0:T(8,128)(2,1)S(1)}, bf16[2,48,768]{2,1,0:T(8,128)(2,1)S(1)}, u32[]{:S(2)}, u32[]{:S(2)}) collective-permute-start(bf16[2,48,768]{2,1,0:T(8,128)(2,1)S(1)} %get-tuple-element.394), channel_id=1, source_target_pairs={{0,8},{1,9},{2,10},{3,11},{4,12},{5,13},{6,14},{7,15},{8,0},{9,1},... | collective-permute-start | bytes 442376 | tf_op jit(solution)/shard_map/ppermute | solution.py:536
  227.8 9.1 %collective-permute-start.54 = (bf16[2,48,768]{2,1,0:T(8,128)(2,1)S(1)}, bf16[2,48,768]{2,1,0:T(8,128)(2,1)S(1)}, u32[]{:S(2)}, u32[]{:S(2)}) collective-permute-start(bf16[2,48,768]{2,1,0:T(8,128)(2,1)S(1)} %get-tuple-element.395), channel_id=1, source_target_pairs={{0,12},{1,13},{2,14},{3,15},{4,8},{5,9},{6,10},{7,11},{8,4},{9,5},... | collective-permute-start | bytes 442376 | tf_op jit(solution)/shard_map/ppermute | solution.py:536
  229.3 7.6 %collective-permute-start.56 = (f32[8,768]{1,0:T(8,128)S(1)}, f32[8,768]{1,0:T(8,128)S(1)}, u32[]{:S(2)}, u32[]{:S(2)}) collective-permute-start(f32[8,768]{1,0:T(8,128)S(1)} %get-tuple-element.404.refs_4_), channel_id=1, source_target_pairs={{0,16},{16,0},{1,17},{17,1},{2,18},{18,2},{3,19},{19,3},{4,20},{20... | collective-permute-start | bytes 73736 | tf_op jit(solution)/shard_map/ppermute | solution.py:540
  237.0 2.8 %collective-permute-start.58 = (f32[8,768]{1,0:T(8,128)S(1)}, f32[8,768]{1,0:T(8,128)S(1)}, u32[]{:S(2)}, u32[]{:S(2)}) collective-permute-start(f32[8,768]{1,0:T(8,128)S(1)} %get-tuple-element.408), channel_id=1, source_target_pairs={{0,1},{1,0},{2,3},{3,2},{4,5},{5,4},{6,7},{7,6},{8,9},{9,8},{10,11... | collective-permute-start | bytes 73736 | tf_op jit(solution)/shard_map/ppermute | solution.py:536
  237.1 4.1 %collective-permute-start.59 = (f32[8,768]{1,0:T(8,128)S(1)}, f32[8,768]{1,0:T(8,128)S(1)}, u32[]{:S(2)}, u32[]{:S(2)}) collective-permute-start(f32[8,768]{1,0:T(8,128)S(1)} %get-tuple-element.408), channel_id=1, source_target_pairs={{0,2},{1,3},{2,0},{3,1},{4,6},{5,7},{6,4},{7,5},{8,10},{9,11},{10,... | collective-permute-start | bytes 73736 | tf_op jit(solution)/shard_map/ppermute | solution.py:536
  237.8 3.5 %collective-permute-start.60 = (f32[8,768]{1,0:T(8,128)S(1)}, f32[8,768]{1,0:T(8,128)S(1)}, u32[]{:S(2)}, u32[]{:S(2)}) collective-permute-start(f32[8,768]{1,0:T(8,128)S(1)} %get-tuple-element.408), channel_id=1, source_target_pairs={{0,3},{1,2},{2,1},{3,0},{4,7},{5,6},{6,5},{7,4},{8,11},{9,10},{10,... | collective-permute-start | bytes 73736 | tf_op jit(solution)/shard_map/ppermute | solution.py:536
  238.9 6.1 %collective-permute-start.57 = (bf16[2,48,768]{2,1,0:T(8,128)(2,1)S(1)}, bf16[2,48,768]{2,1,0:T(8,128)(2,1)S(1)}, u32[]{:S(2)}, u32[]{:S(2)}) collective-permute-start(bf16[2,48,768]{2,1,0:T(8,128)(2,1)S(1)} %get-tuple-element.405.mine), channel_id=1, source_target_pairs={{0,16},{16,0},{1,17},{17,1},{2,18},{18,2},{3,19},{19,3},{4,20},{20... | collective-permute-start | bytes 442376 | tf_op jit(solution)/shard_map/ppermute | solution.py:540
  (21 other events, 141.3 us)

commit v7 on v6

--- a/solution.py
+++ b/solution.py
@@ -777,27 +777,39 @@
     )(scal, *[pltpu.with_memory_space_constraint(v, pltpu.VMEM) for v in parts])
 
 
-def place_last_kernel(scal, placed, mine, other, joined_ref, wide, sem):
+def place_last_kernel(scal, placed, mine, other, v0, v1, v2, v3, joined_ref, gain, b_attn, b_mlp, b_out, wide, sem):
     _, rows, width = other.shape
     for i, ref in enumerate((mine, other)):
         for p in range(2):
             wide[i * 2 + p] = ref[p].astype(F32)
             at = pl.multiple_of((3 + (scal[0] ^ i) * 2 + p) * width, 128)
             pltpu.make_async_copy(wide.at[i * 2 + p], joined_ref.at[:, pl.ds(at, width)], sem).start()
+    total = (v0[...] + v1[...]) + (v2[...] + v3[...])
+    row = lax.broadcasted_iota(jnp.int32, total.shape, 0)
+    dev = (scal[1] * 2 + scal[2]) * 2 + scal[3]
+    for first, out in ((0, gain), (1, b_attn), (3, b_mlp), (7, b_out)):
+        per = out.shape[0]
+        share = width // per
+        line = jnp.sum(jnp.where(row == first + dev // share, total, 0.0), axis=0, keepdims=True)
+        line = jnp.broadcast_to(line, total.shape)
+        line = pltpu.roll(line, (share - dev % share) % share * per, 1)
+        out[...] = line[0, :per]
     whole_wait(wide, sem)()
 
 
-def place_last_call(scal, placed, mine, other):
+def place_last_call(scal, placed, mine, other, vectors):
+    _, rows, width = other.shape
+    near = [pltpu.with_memory_space_constraint(v, pltpu.VMEM) for v in (mine, other, *vectors)]
     return pl.pallas_call(
         place_last_kernel,
         name="place_last",
-        out_shape=sds(placed.shape, F32),
-        in_specs=[SMEM, HBM, VMEM, VMEM],
-        out_specs=HBM,
+        out_shape=[sds(placed.shape, F32)] + [sds((n * rows,), F32) for n in (1, 2, 4, 1)],
+        in_specs=[SMEM, HBM] + [VMEM] * 6,
+        out_specs=[HBM] + [VMEM] * 4,
         scratch_shapes=[pltpu.VMEM((4, *other.shape[1:]), F32), pltpu.SemaphoreType.DMA],
         compiler_params=pltpu.CompilerParams(vmem_limit_bytes=8 << 20),
         input_output_aliases={1: 0},
-    )(scal, placed, *[pltpu.with_memory_space_constraint(v, pltpu.VMEM) for v in (mine, other)])
+    )(scal, placed, *near)
 
 
 def whole_wait(ref, sem):
@@ -1147,10 +1159,8 @@
         u_z, placed = lax.optimization_barrier((u_z, placed))
         (u_sum,), (v_sum,) = mix("sums_8", [sum4_job(u_t[0], u_z), add_job([v_sum, v_other])])
         u_other = swap_y(u_sum)
-        vg = sum([v_sum, *[swap(v_sum, i) for i in (1, 2, 3)]])
-        own = lambda v, per: lax.dynamic_slice(v.reshape(-1), (w * per,), (per,))
-        vg = [own(vg[0], rows), own(vg[1:3], 2 * rows), own(vg[3:7], tiles * rows), own(vg[7], rows)]
-        grad_joined = place_last_call(scal, placed, u_sum, u_other)
+        v_all = [v_sum, *[swap(v_sum, i) for i in (1, 2, 3)]]
+        grad_joined, *vg = place_last_call(scal, placed, u_sum, u_other, v_all)
     return (out.reshape(tokens.shape), d_x.reshape(tokens.shape), grad_joined, grad_out, grad_mlp, *vg)
 
 

time: 247 us -> 243 us (0.984)
  starting transfers between devices: 66.1 us -> 54.6 us
  Pallas kernels: 108 us -> 115 us
    ppermute x45, starting transfers between devices: 51.4 us -> 39.9 us  [swap(): return lax.ppermute(value, 'wide', [(i, i ^ mask) for i in range(16)])]
    pallas_call x11, Pallas kernels: 91.8 us -> 98.7 us  [call(): pl.pallas_call(kernel, name=name, out_shape=list(outs) + list(g_shapes),...]
    ppermute x45, waiting for transfers between devices: 50.7 us -> 54.1 us  [swap(): return lax.ppermute(value, 'wide', [(i, i ^ mask) for i in range(16)])]
  transfers between devices with their start and end apart: 61 -> 61, of which waited for: 21 -> 23; matrix products, arithmetic and copies ran while one was open for 3% -> 2% of each run, Pallas kernels for 38% -> 42%
where the time goes in v7:
time: 243 us; the launch traced here: 242 us
  Pallas kernels  115 us (47%)
  waiting for transfers between devices  60.5 us (25%)
  starting transfers between devices  54.6 us (22%)
  local copies, waits for them, and re-layouts  7.33 us (3%)
  other arithmetic  3.07 us (1%)
    pallas_call x11, Pallas kernels, call(): pl.pallas_call(kernel, name=name, out_shape=list(outs) + list(g_shapes),...  98.7 us
    ppermute x45, waiting for transfers between devices, swap(): return lax.ppermute(value, 'wide', [(i, i ^ mask) for i in range(16)])  54.1 us
    ppermute x45, starting transfers between devices, swap(): return lax.ppermute(value, 'wide', [(i, i ^ mask) for i in range(16)])  39.9 us
    ppermute x16, starting transfers between devices, swap_y(): return lax.ppermute(value, 'narrow', [(0, 1), (1, 0)])  14.7 us
    pallas_call x10, Pallas kernels, mix(): pl.pallas_call(kernel, name=name, out_shape=outs, in_specs=[VMEM] * len(n...  12.4 us
    ppermute x16, waiting for transfers between devices, swap_y(): return lax.ppermute(value, 'narrow', [(0, 1), (1, 0)])  6.46 us
  transfers between devices with their start and end apart: 61, of which 23 were waited for; matrix products, arithmetic and copies ran while one was open for 2% of the time, Pallas kernels for 42%

profile of v7, /device:TPU:0, one launch (start us, length us, event | category | flops | bytes accessed | tf_op | source)
XLA Modules:
  0.0 242.4 jit_solution(8199053245665107318)
XLA Ops:
  1.4 1.3 select_bitcast_fusion.3
  2.7 5.1 %collective-permute-start.2 = (bf16[104,768]{1,0:T(8,128)(2,1)S(1)}, bf16[104,768]{1,0:T(8,128)(2,1)S(1)}, u32[]{:S(2)}, u32[]{:S(2)}) collective-permute-start(bf16[104,768]{1,0:T(8,128)(2,1)S(1)} %pad_maximum_fusion.5), channel_id=1, source_target_pairs={{0,12},{1,13},{2,14},{3,15},{4,8},{5,9},{6,10},{7,11},{8,4},{9,5},... | collective-permute-start | bytes 479240 | tf_op jit(solution)/shard_map/ppermute | solution.py:536
  9.3 3.6 %collective-permute-done.2 = bf16[104,768]{1,0:T(8,128)(2,1)S(1)} collective-permute-done((bf16[104,768]{1,0:T(8,128)(2,1)S(1)}, bf16[104,768]{1,0:T(8,128)(2,1)S(1)}, u32[]{:S(2)}, u32[]{:S(2)}) %collective-permute-start.2) | collective-permute-done | bytes 159776 | tf_op jit(solution)/shard_map/ppermute | solution.py:536
  12.9 8.5 %collective-permute-done.1 = bf16[104,768]{1,0:T(8,128)(2,1)S(1)} collective-permute-done((bf16[104,768]{1,0:T(8,128)(2,1)S(1)}, bf16[104,768]{1,0:T(8,128)(2,1)S(1)}, u32[]{:S(2)}, u32[]{:S(2)}) %collective-permute-start.1) | collective-permute-done | bytes 159776 | tf_op jit(solution)/shard_map/ppermute | solution.py:536
  21.5 1.6 collective-permute-start.5
  23.1 1.5 collective-permute-start.3
  25.8 13.6 %collective-permute-done.7 = bf16[2,2,48,768]{3,2,1,0:T(8,128)(2,1)} collective-permute-done((bf16[2,2,48,768]{3,2,1,0:T(8,128)(2,1)}, bf16[2,2,48,768]{3,2,1,0:T(8,128)(2,1)}, u32[]{:S(2)}, u32[]{:S(2)}) %collective-permute-start.7) | collective-permute-done | bytes 294944 | tf_op jit(solution)/shard_map/ppermute | solution.py:536
  39.5 1.3 join_a.1
  41.5 2.1 collective-permute-start.12
  44.1 1.3 fusion.11
  45.4 1.4 stack.70.refs_0_.scal
  46.8 1.2 fusion.7
  48.0 2.7 %collective-permute-done.9.refs_10_.refs_7_ = bf16[4,48,768]{2,1,0:T(8,128)(2,1)} collective-permute-done((bf16[4,48,768]{2,1,0:T(8,128)(2,1)}, bf16[4,48,768]{2,1,0:T(8,128)(2,1)}, u32[]{:S(2)}, u32[]{:S(2)}) %collective-permute-start.9) | collective-permute-done | bytes 294944 | tf_op jit(solution)/shard_map/ppermute | solution.py:536
  50.7 2.8 %collective-permute-done.12 = bf16[2,2,48,768]{3,2,1,0:T(8,128)(2,1)S(1)} collective-permute-done((bf16[2,2,48,768]{3,2,1,0:T(8,128)(2,1)}, bf16[2,2,48,768]{3,2,1,0:T(8,128)(2,1)S(1)}, u32[]{:S(2)}, u32[]{:S(2)}) %collective-permute-start.12) | collective-permute-done | bytes 294944 | tf_op jit(solution)/shard_map/ppermute | solution.py:536
  53.4 5.6 %collective-permute-done.11 = bf16[2,2,48,768]{3,2,1,0:T(8,128)(2,1)} collective-permute-done((bf16[2,2,48,768]{3,2,1,0:T(8,128)(2,1)}, bf16[2,2,48,768]{3,2,1,0:T(8,128)(2,1)}, u32[]{:S(2)}, u32[]{:S(2)}) %collective-permute-start.11) | collective-permute-done | bytes 294944 | tf_op jit(solution)/shard_map/ppermute | solution.py:536
  62.9 1.1 collective-permute-start.18
  64.0 1.5 collective-permute-start.16
  65.5 9.5 %project.1 = (bf16[1024,768]{1,0:T(8,128)(2,1)S(1)}, bf16[1024,768]{1,0:T(8,128)(2,1)S(1)}, bf16[1024,768]{1,0:T(8,128)(2,1)S(1)}, bf16[1024,768]{1,0:T(8,128)(2...) custom-call(s32[10]{0:T(128)S(1)} %stack.70.refs_0_.scal, ...), custom_call_target="tpu_custom_call" | custom-call | flops 4831838208 | bytes 1048576 | tf_op jit(solution)/shard_map/project/pallas_call | solution.py:139
  75.1 17.6 %core.2 = (bf16[1024,768]{1,0:T(8,128)(2,1)S(1)}, bf16[3,1024,768]{2,1,0:T(8,128)(2,1)S(1)}, f32[1024,768]{1,0:T(8,128)S(1)}) custom-call(s32[10]{0:T(128)S(1)} %stack.70.refs_0_.scal, bf16[1024,768]{1,0:T(8,128)(2,1)S(1)} %get-tuple-element.239.q, bf16[1024,768]{1,0:T(8,128)(2,1)S(1)} %get-tuple-element.240.k, bf16[1024,768]{1,0:T(8,128)(2,1)S(1)} %get-tuple-element.241.v, ...), custom_call_target="tpu_custom_call" | custom-call | flops 10737418240 | bytes 1048576 | tf_op jit(solution)/shard_map/core/pallas_call | solution.py:139
  93.2 10.6 %core.3 = (bf16[1024,768]{1,0:T(8,128)(2,1)S(1)}, bf16[3,1024,768]{2,1,0:T(8,128)(2,1)S(1)}, f32[1024,768]{1,0:T(8,128)S(1)}) custom-call(s32[10]{0:T(128)S(1)} %stack.70.refs_0_.scal, bf16[1024,768]{1,0:T(8,128)(2,1)S(1)} %get-tuple-element.239.q, ...), custom_call_target="tpu_custom_call", output_to_operand_aliasing={{0}: (6, {}), {1}: (7, {}), {2}: (8, {})} | custom-call | flops 10737418240 | bytes 1048576 | tf_op jit(solution)/shard_map/core/pallas_call | solution.py:139
  103.9 4.8 %collective-permute-done.19.refs_2_.refs_6_.refs_3_ = bf16[4,2,48,768]{3,2,1,0:T(8,128)(2,1)S(1)} collective-permute-done((bf16[4,2,48,768]{3,2,1,0:T(8,128)(2,1)S(1)}, bf16[4,2,48,768]{3,2,1,0:T(8,128)(2,1)S(1)}, u32[]{:S(2)}, u32[]{:S(2)}) %collective-permute-start.19) | collective-permute-done | bytes 589856 | tf_op jit(solution)/shard_map/ppermute | solution.py:540
  109.7 7.8 %attn_grad.1 = (f32[8,768]{1,0:T(8,128)S(1)}, bf16[2,8,48,768]{3,2,1,0:T(8,128)(2,1)}, bf16[2,8,48,768]{3,2,1,0:T(8,128)(2,1)}, bf16[2,8,48,768]{3,2,1,0:T(8,128)(2,1)}, bf16[2,8,48,768]{3,2,1,0:T(8,128)(2,1)}) custom-call(s32[10]{0:T(128)S(1)} %stack.70.refs_0_.scal, bf16[1024,768]{1,0:T(8,128)(2,1)S(1)} %get-tuple-element.273.xn.refs_1_, ...), custom_call_target="tpu_custom_call" | custom-call | flops 4831838208 | bytes 1048576 | tf_op jit(solution)/shard_map/attn_grad/pallas_call | solution.py:139
  118.1 1.1 copy-done.13
  119.2 8.1 %up.2 = (bf16[4,1024,768]{2,1,0:T(8,128)(2,1)S(1)}, bf16[4,1024,768]{2,1,0:T(8,128)(2,1)S(1)}, bf16[4,768,768]{2,1,0:T(8,128)(2,1)S(1)}) custom-call(s32[10]{0:T(128)S(1)} %stack.70.refs_0_.scal, bf16[1024,768]{1,0:T(8,128)(2,1)S(1)} %get-tuple-element.273.xn.refs_1_, f32[4,768]{1,0:T(4,128)S(1)} %get-tuple-element.274.refs_2_, ...), custom_call_target="tpu_custom_call" | custom-call | flops 2415919104 | bytes 1048576 | tf_op jit(solution)/shard_map/up/pallas_call | solution.py:139
  127.3 1.6 sums_1.1
  128.9 1.6 collective-permute-start.26
  130.8 6.0 %up.3 = (bf16[4,1024,768]{2,1,0:T(8,128)(2,1)S(1)}, bf16[4,1024,768]{2,1,0:T(8,128)(2,1)S(1)}) custom-call(s32[10]{0:T(128)S(1)} %stack.70.refs_0_.scal, bf16[1024,768]{1,0:T(8,128)(2,1)S(1)} %get-tuple-element.273.xn.refs_1_, f32[4,768]{1,0:T(4,128)S(1)} %get-tuple-element.274.refs_2_, ...), custom_call_target="tpu_custom_call", output_to_operand_aliasing={{0}: (3, {}), {1}: (4, {})} | custom-call | flops 2415919104 | bytes 1048576 | tf_op jit(solution)/shard_map/up/pallas_call | solution.py:139
  136.8 7.6 %down_grad.1 = (bf16[3072,768]{1,0:T(8,128)(2,1)S(1)}, bf16[2,8,48,768]{3,2,1,0:T(8,128)(2,1)}, bf16[2,8,48,768]{3,2,1,0:T(8,128)(2,1)}, bf16[2,8,48,768]{3,2,1,0:T(8,128)(2,1)}, bf16[2,8,48,768]{3,2,1,0:T(8,128)(2,1)}) custom-call(s32[10]{0:T(128)S(1)} %stack.70.refs_0_.scal, bf16[4,1024,768]{2,1,0:T(8,128)(2,1)S(1)} %get-tuple-element.300.act, ...), custom_call_target="tpu_custom_call" | custom-call | flops 4831838208 | bytes 1048576 | tf_op jit(solution)/shard_map/down_grad/pallas_call | solution.py:139
  144.7 1.3 collective-permute-done.27.refs_2_
  146.0 1.4 sums_2.1
  148.8 7.1 %dpre.1 = (bf16[4,1024,768]{2,1,0:T(8,128)(2,1)S(1)}, f32[8,768]{1,0:T(8,128)S(1)}) custom-call(s32[10]{0:T(128)S(1)} %stack.70.refs_0_.scal, bf16[1024,768]{1,0:T(8,128)(2,1)S(1)} %bitcast.35, bf16[4,1024,768]{2,1,0:T(8,128)(2,1)S(1)} %get-tuple-element.310.gp, bf16[3072,768]{1,0:T(8,128)(2,1)S(1)} %get-tuple-element.311.w.wd), custom_call_target="tpu_custom_call", output_to_operand_aliasing={{0}: (2, {})} | custom-call | flops 4831838208 | bytes 1048576 | tf_op jit(solution)/shard_map/dpre/pallas_call | solution.py:139
  155.9 1.3 collective-permute-done.28.refs_3_
  157.2 1.7 sums_3.1
  159.5 1.7 collective-permute-start.36
  161.6 1.8 collective-permute-start.33
  163.4 2.3 collective-permute-start.34
  165.6 7.9 %up_grad.1 = (bf16[1,768,768]{2,1,0:T(8,128)(2,1)S(1)}, bf16[2,8,48,768]{3,2,1,0:T(8,128)(2,1)}, bf16[2,8,48,768]{3,2,1,0:T(8,128)(2,1)}, bf16[2,8,48,768]{3,2,1,0:T(8,128)(2,1)}, bf16[2,8,48,768]{3,2,1,0:T(8,128)(2,1)}) custom-call(s32[10]{0:T(128)S(1)} %stack.70.refs_0_.scal, bf16[1024,768]{1,0:T(8,128)(2,1)S(1)} %get-tuple-element.273.xn.refs_1_, ...), custom_call_target="tpu_custom_call" | custom-call | flops 4831838208 | bytes 1048576 | tf_op jit(solution)/shard_map/up_grad/pallas_call | solution.py:139
  173.6 1.5 collective-permute-done.33.refs_2_
  175.1 1.4 sums_4.1
  177.1 1.2 collective-permute-start.41
  179.7 8.4 %input_grad.1 = (f32[8,768]{1,0:T(8,128)S(1)}, bf16[2,512,768]{2,1,0:T(8,128)(2,1)}) custom-call(s32[10]{0:T(128)S(1)} %stack.70.refs_0_.scal, bf16[1024,768]{1,0:T(8,128)(2,1)S(1)} %bitcast.38, bf16[1024,768]{1,0:T(8,128)(2,1)S(1)} %bitcast.36, f32[1024,768]{1,0:T(8,128)S(1)} %get-tuple-element.354.dn, bf16[4,1024,768]{2,1,0:T(8,128)(2,1)S(1)} %get-tuple-element.333.dpre, ...), custom_call_target="tpu_custom_call" | custom-call | flops 8455716864 | bytes 1048576 | tf_op jit(solution)/shard_map/input_grad/pallas_call | solution.py:139
  188.1 1.3 collective-permute-done.38.refs_5_
  189.5 1.9 sums_5.1
  191.3 1.3 collective-permute-start.42
  193.3 2.2 collective-permute-start.44
  195.5 1.3 collective-permute-start.45
  196.8 1.5 collective-permute-start.46
  198.2 8.2 %out.1 = bf16[2,512,768]{2,1,0:T(8,128)(2,1)} custom-call(s32[10]{0:T(128)S(1)} %stack.70.refs_0_.scal, bf16[1024,768]{1,0:T(8,128)(2,1)S(1)} %bitcast.39, bf16[1024,768]{1,0:T(8,128)(2,1)S(1)} %get-tuple-element.261.o, bf16[4,1024,768]{2,1,0:T(8,128)(2,1)S(1)} %get-tuple-element.300.act, f32[8,768]{1,0:T(8,128)S(1)} %get-tuple-element.355.vec, ...), custom_call_target="tpu_custom_call" | custom-call | flops 6039797760 | bytes 1048576 | tf_op jit(solution)/shard_map/out/pallas_call | solution.py:139
  206.4 2.3 collective-permute-done.45.refs_5_
  208.7 1.4 sums_6.1
  210.1 1.3 collective-permute-start.47
  212.3 2.0 collective-permute-start.51
  214.2 1.6 collective-permute-start.50
  216.6 1.3 collective-permute-done.51.refs_8_
  219.7 1.4 sums_7.1
  221.1 1.3 collective-permute-start.55
  223.3 2.0 collective-permute-start.53
  225.3 1.4 collective-permute-start.54
  227.5 2.2 place.1
  229.7 5.2 %collective-permute-done.53.refs_2_ = bf16[2,48,768]{2,1,0:T(8,128)(2,1)S(1)} collective-permute-done((bf16[2,48,768]{2,1,0:T(8,128)(2,1)S(1)}, bf16[2,48,768]{2,1,0:T(8,128)(2,1)S(1)}, u32[]{:S(2)}, u32[]{:S(2)}) %collective-permute-start.53) | collective-permute-done | bytes 147488 | tf_op jit(solution)/shard_map/ppermute | solution.py:536
  235.0 1.3 collective-permute-start.57
  236.3 1.3 collective-permute-start.59
  238.2 1.5 collective-permute-done.60.v3
  240.2 2.0 place_last.1
  (150 shorter events, 22.6 us)
Async XLA Ops:
  2.7 10.2 %collective-permute-start.2 = (bf16[104,768]{1,0:T(8,128)(2,1)S(1)}, bf16[104,768]{1,0:T(8,128)(2,1)S(1)}, u32[]{:S(2)}, u32[]{:S(2)}) collective-permute-start(bf16[104,768]{1,0:T(8,128)(2,1)S(1)} %pad_maximum_fusion.5), channel_id=1, source_target_pairs={{0,12},{1,13},{2,14},{3,15},{4,8},{5,9},{6,10},{7,11},{8,4},{9,5},... | collective-permute-start | bytes 479240 | tf_op jit(solution)/shard_map/ppermute | solution.py:536
  7.9 13.5 %collective-permute-start.1 = (bf16[104,768]{1,0:T(8,128)(2,1)S(1)}, bf16[104,768]{1,0:T(8,128)(2,1)S(1)}, u32[]{:S(2)}, u32[]{:S(2)}) collective-permute-start(bf16[104,768]{1,0:T(8,128)(2,1)S(1)} %pad_maximum_fusion.5), channel_id=1, source_target_pairs={{0,8},{1,9},{2,10},{3,11},{4,12},{5,13},{6,14},{7,15},{8,0},{9,1},... | collective-permute-start | bytes 479240 | tf_op jit(solution)/shard_map/ppermute | solution.py:536
  7.9 13.5 %collective-permute-start = (bf16[104,768]{1,0:T(8,128)(2,1)S(1)}, bf16[104,768]{1,0:T(8,128)(2,1)S(1)}, u32[]{:S(2)}, u32[]{:S(2)}) collective-permute-start(bf16[104,768]{1,0:T(8,128)(2,1)S(1)} %pad_maximum_fusion.5), channel_id=1, source_target_pairs={{0,4},{1,5},{2,6},{3,7},{4,0},{5,1},{6,2},{7,3},{8,12},{9,13},{10,... | collective-permute-start | bytes 479240 | tf_op jit(solution)/shard_map/ppermute | solution.py:536
  21.5 19.3 %copy-start.6 = (bf16[4,56,768]{2,1,0:T(8,128)(2,1)}, bf16[4,56,768]{2,1,0:T(8,128)(2,1)S(1)}, u32[]{:S(2)}) copy-start(bf16[4,56,768]{2,1,0:T(8,128)(2,1)S(1)} %pad_maximum_fusion.2.refs_0_.refs_3_) | copy-start | bytes 1032196
  21.5 18.0 %collective-permute-start.5 = (bf16[4,56,768]{2,1,0:T(8,128)(2,1)S(1)}, bf16[4,56,768]{2,1,0:T(8,128)(2,1)S(1)}, u32[]{:S(2)}, u32[]{:S(2)}) collective-permute-start(bf16[4,56,768]{2,1,0:T(8,128)(2,1)S(1)} %pad_maximum_fusion.2.refs_0_.refs_3_), channel_id=1, source_target_pairs={{0,16},{16,0},{1,17},{17,1},{2,18},{18,2},{3,19},{19,3},{4,20},{20... | collective-permute-start | bytes 1032200 | tf_op jit(solution)/shard_map/ppermute | solution.py:540
  23.1 16.4 %collective-permute-start.3 = (bf16[4,56,768]{2,1,0:T(8,128)(2,1)S(1)}, bf16[4,56,768]{2,1,0:T(8,128)(2,1)S(1)}, u32[]{:S(2)}, u32[]{:S(2)}) collective-permute-start(bf16[4,56,768]{2,1,0:T(8,128)(2,1)S(1)} %pad_maximum_fusion.2.refs_0_.refs_3_), channel_id=1, source_target_pairs={{0,2},{1,3},{2,0},{3,1},{4,6},{5,7},{6,4},{7,5},{8,10},{9,11},{10,... | collective-permute-start | bytes 1032200 | tf_op jit(solution)/shard_map/ppermute | solution.py:536
  24.7 14.8 %collective-permute-start.7 = (bf16[2,2,48,768]{3,2,1,0:T(8,128)(2,1)}, bf16[2,2,48,768]{3,2,1,0:T(8,128)(2,1)}, u32[]{:S(2)}, u32[]{:S(2)}) collective-permute-start(bf16[2,2,48,768]{3,2,1,0:T(8,128)(2,1)} %bitcast.20), channel_id=1, source_target_pairs={{0,8},{1,9},{2,10},{3,11},{4,12},{5,13},{6,14},{7,15},{8,0},{9,1},... | collective-permute-start | bytes 884744 | tf_op jit(solution)/shard_map/ppermute | solution.py:536
  24.8 14.7 %collective-permute-start.6 = (bf16[4,48,768]{2,1,0:T(8,128)(2,1)S(1)}, bf16[4,48,768]{2,1,0:T(8,128)(2,1)S(1)}, u32[]{:S(2)}, u32[]{:S(2)}) collective-permute-start(bf16[4,48,768]{2,1,0:T(8,128)(2,1)S(1)} %pad_maximum_fusion.3.refs_3_.refs_7_.refs_4_), channel_id=1, source_target_pairs={{0,2},{1,3},{2,0},{3,1},{4,6},{5,7},{6,4},{7,5},{8,10},{9,11},{10,... | collective-permute-start | bytes 884744 | tf_op jit(solution)/shard_map/ppermute | solution.py:536
  25.4 14.1 %collective-permute-start.4 = (bf16[4,48,768]{2,1,0:T(8,128)(2,1)S(1)}, bf16[4,48,768]{2,1,0:T(8,128)(2,1)}, u32[]{:S(2)}, u32[]{:S(2)}) collective-permute-start(bf16[4,48,768]{2,1,0:T(8,128)(2,1)S(1)} %pad_maximum_fusion.3.refs_3_.refs_7_.refs_4_), channel_id=1, source_target_pairs={{0,16},{16,0},{1,17},{17,1},{2,18},{18,2},{3,19},{19,3},{4,20},{20... | collective-permute-start | bytes 884744 | tf_op jit(solution)/shard_map/ppermute | solution.py:540
  40.9 18.2 %collective-permute-start.10 = (bf16[24,56,768]{2,1,0:T(8,128)(2,1)S(1)}, bf16[24,56,768]{2,1,0:T(8,128)(2,1)}, u32[]{:S(2)}, u32[]{:S(2)}) collective-permute-start(bf16[24,56,768]{2,1,0:T(8,128)(2,1)S(1)} %join_a.1), channel_id=1, source_target_pairs={{0,1},{1,0},{2,3},{3,2},{4,5},{5,4},{6,7},{7,6},{8,9},{9,8},{10,11... | collective-permute-start | bytes 6193160 | tf_op jit(solution)/shard_map/ppermute | solution.py:536
  40.9 9.7 %collective-permute-start.9 = (bf16[4,48,768]{2,1,0:T(8,128)(2,1)}, bf16[4,48,768]{2,1,0:T(8,128)(2,1)}, u32[]{:S(2)}, u32[]{:S(2)}) collective-permute-start(bf16[4,48,768]{2,1,0:T(8,128)(2,1)} %collective-permute-done.4.refs_5_.refs_9_.refs_6_), channel_id=1, source_target_pairs={{0,2},{1,3},{2,0},{3,1},{4,6},{5,7},{6,4},{7,5},{8,10},{9,11},{10,... | collective-permute-start | bytes 884744 | tf_op jit(solution)/shard_map/ppermute | solution.py:536
  41.5 11.9 %collective-permute-start.12 = (bf16[2,2,48,768]{3,2,1,0:T(8,128)(2,1)}, bf16[2,2,48,768]{3,2,1,0:T(8,128)(2,1)S(1)}, u32[]{:S(2)}, u32[]{:S(2)}) collective-permute-start(bf16[2,2,48,768]{3,2,1,0:T(8,128)(2,1)} %bitcast.20), channel_id=1, source_target_pairs={{0,12},{1,13},{2,14},{3,15},{4,8},{5,9},{6,10},{7,11},{8,4},{9,5},... | collective-permute-start | bytes 884744 | tf_op jit(solution)/shard_map/ppermute | solution.py:536
  43.6 15.4 %collective-permute-start.11 = (bf16[2,2,48,768]{3,2,1,0:T(8,128)(2,1)}, bf16[2,2,48,768]{3,2,1,0:T(8,128)(2,1)}, u32[]{:S(2)}, u32[]{:S(2)}) collective-permute-start(bf16[2,2,48,768]{3,2,1,0:T(8,128)(2,1)} %bitcast.20), channel_id=1, source_target_pairs={{0,4},{1,5},{2,6},{3,7},{4,0},{5,1},{6,2},{7,3},{8,12},{9,13},{10,... | collective-permute-start | bytes 884744 | tf_op jit(solution)/shard_map/ppermute | solution.py:536
  43.6 15.4 %collective-permute-start.8 = (bf16[4,56,768]{2,1,0:T(8,128)(2,1)S(1)}, bf16[4,56,768]{2,1,0:T(8,128)(2,1)}, u32[]{:S(2)}, u32[]{:S(2)}) collective-permute-start(bf16[4,56,768]{2,1,0:T(8,128)(2,1)S(1)} %collective-permute-done.3.refs_1_.refs_4_), channel_id=1, source_target_pairs={{0,16},{16,0},{1,17},{17,1},{2,18},{18,2},{3,19},{19,3},{4,20},{20... | collective-permute-start | bytes 1032200 | tf_op jit(solution)/shard_map/ppermute | solution.py:540
  48.0 17.6 %copy-start.11 = (bf16[2,512,768]{2,1,0:T(8,128)(2,1)S(1)}, bf16[2,512,768]{2,1,0:T(8,128)(2,1)}, u32[]{:S(2)}) copy-start(bf16[2,512,768]{2,1,0:T(8,128)(2,1)} %param.12) | copy-start | bytes 4718596
  59.0 1.8 collective-permute-start.14
  59.0 2.3 collective-permute-start.13
  60.7 32.1 %copy-start.14 = (bf16[4,2,48,768]{3,2,1,0:T(8,128)(2,1)}, bf16[4,2,48,768]{3,2,1,0:T(8,128)(2,1)S(1)}, u32[]{:S(2)}) copy-start(bf16[4,2,48,768]{3,2,1,0:T(8,128)(2,1)S(1)} %pad_maximum_fusion.1.refs_7_.refs_4_) | copy-start | bytes 1769476
  61.3 42.5 %collective-permute-start.21 = (bf16[4,2,48,768]{3,2,1,0:T(8,128)(2,1)S(1)}, bf16[4,2,48,768]{3,2,1,0:T(8,128)(2,1)S(1)}, u32[]{:S(2)}, u32[]{:S(2)}) collective-permute-start(bf16[4,2,48,768]{3,2,1,0:T(8,128)(2,1)S(1)} %pad_maximum_fusion.refs_3_.refs_0_), channel_id=1, source_target_pairs={{0,1},{1,0},{2,3},{3,2},{4,5},{5,4},{6,7},{7,6},{8,9},{9,8},{10,11... | collective-permute-start | bytes 1769480 | tf_op jit(solution)/shard_map/ppermute | solution.py:536
  61.5 31.2 %collective-permute-start.17 = (bf16[4,2,48,768]{3,2,1,0:T(8,128)(2,1)S(1)}, bf16[4,2,48,768]{3,2,1,0:T(8,128)(2,1)S(1)}, u32[]{:S(2)}, u32[]{:S(2)}) collective-permute-start(bf16[4,2,48,768]{3,2,1,0:T(8,128)(2,1)S(1)} %pad_maximum_fusion.refs_3_.refs_0_), channel_id=1, source_target_pairs={{0,16},{16,0},{1,17},{17,1},{2,18},{18,2},{3,19},{19,3},{4,20},{20... | collective-permute-start | bytes 1769480 | tf_op jit(solution)/shard_map/ppermute | solution.py:540
  62.0 30.9 %collective-permute-start.15 = (bf16[4,2,48,768]{3,2,1,0:T(8,128)(2,1)S(1)}, bf16[4,2,48,768]{3,2,1,0:T(8,128)(2,1)S(1)}, u32[]{:S(2)}, u32[]{:S(2)}) collective-permute-start(bf16[4,2,48,768]{3,2,1,0:T(8,128)(2,1)S(1)} %pad_maximum_fusion.refs_3_.refs_0_), channel_id=1, source_target_pairs={{0,2},{1,3},{2,0},{3,1},{4,6},{5,7},{6,4},{7,5},{8,10},{9,11},{10,... | collective-permute-start | bytes 1769480 | tf_op jit(solution)/shard_map/ppermute | solution.py:536
  62.9 29.9 %collective-permute-start.18 = (bf16[4,2,48,768]{3,2,1,0:T(8,128)(2,1)S(1)}, bf16[4,2,48,768]{3,2,1,0:T(8,128)(2,1)S(1)}, u32[]{:S(2)}, u32[]{:S(2)}) collective-permute-start(bf16[4,2,48,768]{3,2,1,0:T(8,128)(2,1)S(1)} %pad_maximum_fusion.1.refs_7_.refs_4_), channel_id=1, source_target_pairs={{0,2},{1,3},{2,0},{3,1},{4,6},{5,7},{6,4},{7,5},{8,10},{9,11},{10,... | collective-permute-start | bytes 1769480 | tf_op jit(solution)/shard_map/ppermute | solution.py:536
  64.0 28.9 %collective-permute-start.16 = (bf16[4,2,48,768]{3,2,1,0:T(8,128)(2,1)S(1)}, bf16[4,2,48,768]{3,2,1,0:T(8,128)(2,1)S(1)}, u32[]{:S(2)}, u32[]{:S(2)}) collective-permute-start(bf16[4,2,48,768]{3,2,1,0:T(8,128)(2,1)S(1)} %pad_maximum_fusion.1.refs_7_.refs_4_), channel_id=1, source_target_pairs={{0,16},{16,0},{1,17},{17,1},{2,18},{18,2},{3,19},{19,3},{4,20},{20... | collective-permute-start | bytes 1769480 | tf_op jit(solution)/shard_map/ppermute | solution.py:540
  92.7 11.1 %collective-permute-start.22 = (bf16[4,2,48,768]{3,2,1,0:T(8,128)(2,1)S(1)}, bf16[4,2,48,768]{3,2,1,0:T(8,128)(2,1)S(1)}, u32[]{:S(2)}, u32[]{:S(2)}) collective-permute-start(bf16[4,2,48,768]{3,2,1,0:T(8,128)(2,1)S(1)} %pad_maximum_fusion.1.refs_7_.refs_4_), channel_id=1, source_target_pairs={{0,1},{1,0},{2,3},{3,2},{4,5},{5,4},{6,7},{7,6},{8,9},{9,8},{10,11... | collective-permute-start | bytes 1769480 | tf_op jit(solution)/shard_map/ppermute | solution.py:536
  92.9 15.8 %collective-permute-start.19 = (bf16[4,2,48,768]{3,2,1,0:T(8,128)(2,1)S(1)}, bf16[4,2,48,768]{3,2,1,0:T(8,128)(2,1)S(1)}, u32[]{:S(2)}, u32[]{:S(2)}) collective-permute-start(bf16[4,2,48,768]{3,2,1,0:T(8,128)(2,1)S(1)} %collective-permute-done.15.refs_0_.refs_4_.refs_1_), channel_id=1, source_target_pairs={{0,16},{16,0},{1,17},{17,1},{2,18},{18,2},{3,19},{19,3},{4,20},{20... | collective-permute-start | bytes 1769480 | tf_op jit(solution)/shard_map/ppermute | solution.py:540
  93.0 15.8 %collective-permute-start.20 = (bf16[4,2,48,768]{3,2,1,0:T(8,128)(2,1)S(1)}, bf16[4,2,48,768]{3,2,1,0:T(8,128)(2,1)S(1)}, u32[]{:S(2)}, u32[]{:S(2)}) collective-permute-start(bf16[4,2,48,768]{3,2,1,0:T(8,128)(2,1)S(1)} %collective-permute-done.16.refs_4_.refs_9_.refs_6_), channel_id=1, source_target_pairs={{0,2},{1,3},{2,0},{3,1},{4,6},{5,7},{6,4},{7,5},{8,10},{9,11},{10,... | collective-permute-start | bytes 1769480 | tf_op jit(solution)/shard_map/ppermute | solution.py:536
  109.7 7.8 %collective-permute-start.23 = (bf16[24,2,48,768]{3,2,1,0:T(8,128)(2,1)S(1)}, bf16[24,2,48,768]{3,2,1,0:T(8,128)(2,1)S(1)}, u32[]{:S(2)}, u32[]{:S(2)}) collective-permute-start(bf16[24,2,48,768]{3,2,1,0:T(8,128)(2,1)S(1)} %join_c.1), channel_id=1, source_target_pairs={{0,1},{1,0},{2,3},{3,2},{4,5},{5,4},{6,7},{7,6},{8,9},{9,8},{10,11... | collective-permute-start | bytes 10616840 | tf_op jit(solution)/shard_map/ppermute | solution.py:536
  117.5 9.8 %collective-permute-start.24 = (bf16[2,8,48,768]{3,2,1,0:T(8,128)(2,1)}, bf16[2,8,48,768]{3,2,1,0:T(8,128)(2,1)S(1)}, u32[]{:S(2)}, u32[]{:S(2)}) collective-permute-start(bf16[2,8,48,768]{3,2,1,0:T(8,128)(2,1)} %get-tuple-element.287), channel_id=1, source_target_pairs={{0,1},{1,0},{2,3},{3,2},{4,5},{5,4},{6,7},{7,6},{8,9},{9,8},{10,11... | collective-permute-start | bytes 3538952 | tf_op jit(solution)/shard_map/ppermute | solution.py:536
  118.1 9.3 %collective-permute-start.25 = (bf16[2,8,48,768]{3,2,1,0:T(8,128)(2,1)}, bf16[2,8,48,768]{3,2,1,0:T(8,128)(2,1)S(1)}, u32[]{:S(2)}, u32[]{:S(2)}) collective-permute-start(bf16[2,8,48,768]{3,2,1,0:T(8,128)(2,1)} %get-tuple-element.288), channel_id=1, source_target_pairs={{0,1},{1,0},{2,3},{3,2},{4,5},{5,4},{6,7},{7,6},{8,9},{9,8},{10,11... | collective-permute-start | bytes 3538952 | tf_op jit(solution)/shard_map/ppermute | solution.py:536
  128.9 15.8 %collective-permute-start.26 = (bf16[8,48,768]{2,1,0:T(8,128)(2,1)S(1)}, bf16[8,48,768]{2,1,0:T(8,128)(2,1)S(1)}, u32[]{:S(2)}, u32[]{:S(2)}) collective-permute-start(bf16[8,48,768]{2,1,0:T(8,128)(2,1)S(1)} %get-tuple-element.298), channel_id=1, source_target_pairs={{0,16},{16,0},{1,17},{17,1},{2,18},{18,2},{3,19},{19,3},{4,20},{20... | collective-permute-start | bytes 1769480 | tf_op jit(solution)/shard_map/ppermute | solution.py:540
  130.5 15.5 %collective-permute-start.27 = (bf16[8,48,768]{2,1,0:T(8,128)(2,1)S(1)}, bf16[8,48,768]{2,1,0:T(8,128)(2,1)S(1)}, u32[]{:S(2)}, u32[]{:S(2)}) collective-permute-start(bf16[8,48,768]{2,1,0:T(8,128)(2,1)S(1)} %get-tuple-element.299), channel_id=1, source_target_pairs={{0,2},{1,3},{2,0},{3,1},{4,6},{5,7},{6,4},{7,5},{8,10},{9,11},{10,... | collective-permute-start | bytes 1769480 | tf_op jit(solution)/shard_map/ppermute | solution.py:536
  147.4 9.8 %collective-permute-start.30 = (bf16[2,8,48,768]{3,2,1,0:T(8,128)(2,1)S(1)}, bf16[2,8,48,768]{3,2,1,0:T(8,128)(2,1)S(1)}, u32[]{:S(2)}, u32[]{:S(2)}) collective-permute-start(bf16[2,8,48,768]{3,2,1,0:T(8,128)(2,1)S(1)} %copy-done.21), channel_id=1, source_target_pairs={{0,1},{1,0},{2,3},{3,2},{4,5},{5,4},{6,7},{7,6},{8,9},{9,8},{10,11... | collective-permute-start | bytes 3538952 | tf_op jit(solution)/shard_map/ppermute | solution.py:536
  147.8 9.4 %collective-permute-start.31 = (bf16[2,8,48,768]{3,2,1,0:T(8,128)(2,1)S(1)}, bf16[2,8,48,768]{3,2,1,0:T(8,128)(2,1)S(1)}, u32[]{:S(2)}, u32[]{:S(2)}) collective-permute-start(bf16[2,8,48,768]{3,2,1,0:T(8,128)(2,1)S(1)} %copy-done.20), channel_id=1, source_target_pairs={{0,1},{1,0},{2,3},{3,2},{4,5},{5,4},{6,7},{7,6},{8,9},{9,8},{10,11... | collective-permute-start | bytes 3538952 | tf_op jit(solution)/shard_map/ppermute | solution.py:536
  148.0 9.2 %collective-permute-start.28 = (bf16[4,48,768]{2,1,0:T(8,128)(2,1)S(1)}, bf16[4,48,768]{2,1,0:T(8,128)(2,1)S(1)}, u32[]{:S(2)}, u32[]{:S(2)}) collective-permute-start(bf16[4,48,768]{2,1,0:T(8,128)(2,1)S(1)} %get-tuple-element.313), channel_id=1, source_target_pairs={{0,2},{1,3},{2,0},{3,1},{4,6},{5,7},{6,4},{7,5},{8,10},{9,11},{10,... | collective-permute-start | bytes 884744 | tf_op jit(solution)/shard_map/ppermute | solution.py:536
  148.3 8.9 %collective-permute-start.29 = (bf16[4,48,768]{2,1,0:T(8,128)(2,1)S(1)}, bf16[4,48,768]{2,1,0:T(8,128)(2,1)S(1)}, u32[]{:S(2)}, u32[]{:S(2)}) collective-permute-start(bf16[4,48,768]{2,1,0:T(8,128)(2,1)S(1)} %get-tuple-element.314), channel_id=1, source_target_pairs={{0,16},{16,0},{1,17},{17,1},{2,18},{18,2},{3,19},{19,3},{4,20},{20... | collective-permute-start | bytes 884744 | tf_op jit(solution)/shard_map/ppermute | solution.py:540
  159.0 16.1 %collective-permute-start.35 = (bf16[8,48,768]{2,1,0:T(8,128)(2,1)S(1)}, bf16[8,48,768]{2,1,0:T(8,128)(2,1)S(1)}, u32[]{:S(2)}, u32[]{:S(2)}) collective-permute-start(bf16[8,48,768]{2,1,0:T(8,128)(2,1)S(1)} %get-tuple-element.331), channel_id=1, source_target_pairs={{0,16},{16,0},{1,17},{17,1},{2,18},{18,2},{3,19},{19,3},{4,20},{20... | collective-permute-start | bytes 1769480 | tf_op jit(solution)/shard_map/ppermute | solution.py:540
  159.5 15.5 %collective-permute-start.36 = (bf16[8,48,768]{2,1,0:T(8,128)(2,1)S(1)}, bf16[8,48,768]{2,1,0:T(8,128)(2,1)S(1)}, u32[]{:S(2)}, u32[]{:S(2)}) collective-permute-start(bf16[8,48,768]{2,1,0:T(8,128)(2,1)S(1)} %get-tuple-element.332), channel_id=1, source_target_pairs={{0,2},{1,3},{2,0},{3,1},{4,6},{5,7},{6,4},{7,5},{8,10},{9,11},{10,... | collective-permute-start | bytes 1769480 | tf_op jit(solution)/shard_map/ppermute | solution.py:536
  161.3 12.3 %collective-permute-start.32 = (bf16[2,48,768]{2,1,0:T(8,128)(2,1)S(1)}, bf16[2,48,768]{2,1,0:T(8,128)(2,1)S(1)}, u32[]{:S(2)}, u32[]{:S(2)}) collective-permute-start(bf16[2,48,768]{2,1,0:T(8,128)(2,1)S(1)} %get-tuple-element.328), channel_id=1, source_target_pairs={{0,4},{1,5},{2,6},{3,7},{4,0},{5,1},{6,2},{7,3},{8,12},{9,13},{10,... | collective-permute-start | bytes 442376 | tf_op jit(solution)/shard_map/ppermute | solution.py:536
  161.6 13.5 %collective-permute-start.33 = (bf16[2,48,768]{2,1,0:T(8,128)(2,1)S(1)}, bf16[2,48,768]{2,1,0:T(8,128)(2,1)S(1)}, u32[]{:S(2)}, u32[]{:S(2)}) collective-permute-start(bf16[2,48,768]{2,1,0:T(8,128)(2,1)S(1)} %get-tuple-element.329), channel_id=1, source_target_pairs={{0,8},{1,9},{2,10},{3,11},{4,12},{5,13},{6,14},{7,15},{8,0},{9,1},... | collective-permute-start | bytes 442376 | tf_op jit(solution)/shard_map/ppermute | solution.py:536
  163.4 11.7 %collective-permute-start.34 = (bf16[2,48,768]{2,1,0:T(8,128)(2,1)S(1)}, bf16[2,48,768]{2,1,0:T(8,128)(2,1)S(1)}, u32[]{:S(2)}, u32[]{:S(2)}) collective-permute-start(bf16[2,48,768]{2,1,0:T(8,128)(2,1)S(1)} %get-tuple-element.330), channel_id=1, source_target_pairs={{0,12},{1,13},{2,14},{3,15},{4,8},{5,9},{6,10},{7,11},{8,4},{9,5},... | collective-permute-start | bytes 442376 | tf_op jit(solution)/shard_map/ppermute | solution.py:536
  176.6 12.9 %collective-permute-start.39 = (bf16[2,8,48,768]{3,2,1,0:T(8,128)(2,1)S(1)}, bf16[2,8,48,768]{3,2,1,0:T(8,128)(2,1)S(1)}, u32[]{:S(2)}, u32[]{:S(2)}) collective-permute-start(bf16[2,8,48,768]{3,2,1,0:T(8,128)(2,1)S(1)} %copy-done.19), channel_id=1, source_target_pairs={{0,1},{1,0},{2,3},{3,2},{4,5},{5,4},{6,7},{7,6},{8,9},{9,8},{10,11... | collective-permute-start | bytes 3538952 | tf_op jit(solution)/shard_map/ppermute | solution.py:536
  176.9 12.6 %collective-permute-start.40 = (bf16[2,8,48,768]{3,2,1,0:T(8,128)(2,1)S(1)}, bf16[2,8,48,768]{3,2,1,0:T(8,128)(2,1)S(1)}, u32[]{:S(2)}, u32[]{:S(2)}) collective-permute-start(bf16[2,8,48,768]{3,2,1,0:T(8,128)(2,1)S(1)} %copy-done.18), channel_id=1, source_target_pairs={{0,1},{1,0},{2,3},{3,2},{4,5},{5,4},{6,7},{7,6},{8,9},{9,8},{10,11... | collective-permute-start | bytes 3538952 | tf_op jit(solution)/shard_map/ppermute | solution.py:536
  177.1 11.0 %collective-permute-start.41 = (bf16[2,48,768]{2,1,0:T(8,128)(2,1)S(1)}, bf16[2,48,768]{2,1,0:T(8,128)(2,1)S(1)}, u32[]{:S(2)}, u32[]{:S(2)}) collective-permute-start(bf16[2,48,768]{2,1,0:T(8,128)(2,1)S(1)} %get-tuple-element.352.a_mine), channel_id=1, source_target_pairs={{0,16},{16,0},{1,17},{17,1},{2,18},{18,2},{3,19},{19,3},{4,20},{20... | collective-permute-start | bytes 442376 | tf_op jit(solution)/shard_map/ppermute | solution.py:540
  178.3 9.8 %collective-permute-start.37 = (bf16[4,48,768]{2,1,0:T(8,128)(2,1)S(1)}, bf16[4,48,768]{2,1,0:T(8,128)(2,1)S(1)}, u32[]{:S(2)}, u32[]{:S(2)}) collective-permute-start(bf16[4,48,768]{2,1,0:T(8,128)(2,1)S(1)} %get-tuple-element.348), channel_id=1, source_target_pairs={{0,2},{1,3},{2,0},{3,1},{4,6},{5,7},{6,4},{7,5},{8,10},{9,11},{10,... | collective-permute-start | bytes 884744 | tf_op jit(solution)/shard_map/ppermute | solution.py:536
  179.0 10.5 %collective-permute-start.38 = (bf16[4,48,768]{2,1,0:T(8,128)(2,1)S(1)}, bf16[4,48,768]{2,1,0:T(8,128)(2,1)S(1)}, u32[]{:S(2)}, u32[]{:S(2)}) collective-permute-start(bf16[4,48,768]{2,1,0:T(8,128)(2,1)S(1)} %get-tuple-element.349), channel_id=1, source_target_pairs={{0,16},{16,0},{1,17},{17,1},{2,18},{18,2},{3,19},{19,3},{4,20},{20... | collective-permute-start | bytes 884744 | tf_op jit(solution)/shard_map/ppermute | solution.py:540
  191.3 17.4 %collective-permute-start.42 = (bf16[8,48,768]{2,1,0:T(8,128)(2,1)S(1)}, bf16[8,48,768]{2,1,0:T(8,128)(2,1)S(1)}, u32[]{:S(2)}, u32[]{:S(2)}) collective-permute-start(bf16[8,48,768]{2,1,0:T(8,128)(2,1)S(1)} %get-tuple-element.372), channel_id=1, source_target_pairs={{0,16},{16,0},{1,17},{17,1},{2,18},{18,2},{3,19},{19,3},{4,20},{20... | collective-permute-start | bytes 1769480 | tf_op jit(solution)/shard_map/ppermute | solution.py:540
  192.6 16.1 %collective-permute-start.43 = (bf16[8,48,768]{2,1,0:T(8,128)(2,1)S(1)}, bf16[8,48,768]{2,1,0:T(8,128)(2,1)S(1)}, u32[]{:S(2)}, u32[]{:S(2)}) collective-permute-start(bf16[8,48,768]{2,1,0:T(8,128)(2,1)S(1)} %get-tuple-element.373), channel_id=1, source_target_pairs={{0,2},{1,3},{2,0},{3,1},{4,6},{5,7},{6,4},{7,5},{8,10},{9,11},{10,... | collective-permute-start | bytes 1769480 | tf_op jit(solution)/shard_map/ppermute | solution.py:536
  193.3 13.1 %collective-permute-start.44 = (bf16[2,48,768]{2,1,0:T(8,128)(2,1)S(1)}, bf16[2,48,768]{2,1,0:T(8,128)(2,1)S(1)}, u32[]{:S(2)}, u32[]{:S(2)}) collective-permute-start(bf16[2,48,768]{2,1,0:T(8,128)(2,1)S(1)} %get-tuple-element.374), channel_id=1, source_target_pairs={{0,4},{1,5},{2,6},{3,7},{4,0},{5,1},{6,2},{7,3},{8,12},{9,13},{10,... | collective-permute-start | bytes 442376 | tf_op jit(solution)/shard_map/ppermute | solution.py:536
  195.5 13.2 %collective-permute-start.45 = (bf16[2,48,768]{2,1,0:T(8,128)(2,1)S(1)}, bf16[2,48,768]{2,1,0:T(8,128)(2,1)S(1)}, u32[]{:S(2)}, u32[]{:S(2)}) collective-permute-start(bf16[2,48,768]{2,1,0:T(8,128)(2,1)S(1)} %get-tuple-element.375), channel_id=1, source_target_pairs={{0,8},{1,9},{2,10},{3,11},{4,12},{5,13},{6,14},{7,15},{8,0},{9,1},... | collective-permute-start | bytes 442376 | tf_op jit(solution)/shard_map/ppermute | solution.py:536
  196.8 11.9 %collective-permute-start.46 = (bf16[2,48,768]{2,1,0:T(8,128)(2,1)S(1)}, bf16[2,48,768]{2,1,0:T(8,128)(2,1)S(1)}, u32[]{:S(2)}, u32[]{:S(2)}) collective-permute-start(bf16[2,48,768]{2,1,0:T(8,128)(2,1)S(1)} %get-tuple-element.376), channel_id=1, source_target_pairs={{0,12},{1,13},{2,14},{3,15},{4,8},{5,9},{6,10},{7,11},{8,4},{9,5},... | collective-permute-start | bytes 442376 | tf_op jit(solution)/shard_map/ppermute | solution.py:536
  210.1 9.6 %collective-permute-start.47 = (bf16[4,48,768]{2,1,0:T(8,128)(2,1)S(1)}, bf16[4,48,768]{2,1,0:T(8,128)(2,1)S(1)}, u32[]{:S(2)}, u32[]{:S(2)}) collective-permute-start(bf16[4,48,768]{2,1,0:T(8,128)(2,1)S(1)} %get-tuple-element.389), channel_id=1, source_target_pairs={{0,2},{1,3},{2,0},{3,1},{4,6},{5,7},{6,4},{7,5},{8,10},{9,11},{10,... | collective-permute-start | bytes 884744 | tf_op jit(solution)/shard_map/ppermute | solution.py:536
  211.4 8.3 %collective-permute-start.48 = (bf16[4,48,768]{2,1,0:T(8,128)(2,1)S(1)}, bf16[4,48,768]{2,1,0:T(8,128)(2,1)S(1)}, u32[]{:S(2)}, u32[]{:S(2)}) collective-permute-start(bf16[4,48,768]{2,1,0:T(8,128)(2,1)S(1)} %get-tuple-element.390), channel_id=1, source_target_pairs={{0,16},{16,0},{1,17},{17,1},{2,18},{18,2},{3,19},{19,3},{4,20},{20... | collective-permute-start | bytes 884744 | tf_op jit(solution)/shard_map/ppermute | solution.py:540
  212.3 5.7 %collective-permute-start.51 = (f32[8,768]{1,0:T(8,128)S(1)}, f32[8,768]{1,0:T(8,128)S(1)}, u32[]{:S(2)}, u32[]{:S(2)}) collective-permute-start(f32[8,768]{1,0:T(8,128)S(1)} %get-tuple-element.391.refs_5_), channel_id=1, source_target_pairs={{0,12},{1,13},{2,14},{3,15},{4,8},{5,9},{6,10},{7,11},{8,4},{9,5},... | collective-permute-start | bytes 73736 | tf_op jit(solution)/shard_map/ppermute | solution.py:536
  214.2 4.7 %collective-permute-start.50 = (f32[8,768]{1,0:T(8,128)S(1)}, f32[8,768]{1,0:T(8,128)S(1)}, u32[]{:S(2)}, u32[]{:S(2)}) collective-permute-start(f32[8,768]{1,0:T(8,128)S(1)} %get-tuple-element.391.refs_5_), channel_id=1, source_target_pairs={{0,8},{1,9},{2,10},{3,11},{4,12},{5,13},{6,14},{7,15},{8,0},{9,1},... | collective-permute-start | bytes 73736 | tf_op jit(solution)/shard_map/ppermute | solution.py:536
  215.8 3.8 %collective-permute-start.49 = (f32[8,768]{1,0:T(8,128)S(1)}, f32[8,768]{1,0:T(8,128)S(1)}, u32[]{:S(2)}, u32[]{:S(2)}) collective-permute-start(f32[8,768]{1,0:T(8,128)S(1)} %get-tuple-element.391.refs_5_), channel_id=1, source_target_pairs={{0,4},{1,5},{2,6},{3,7},{4,0},{5,1},{6,2},{7,3},{8,12},{9,13},{10,... | collective-permute-start | bytes 73736 | tf_op jit(solution)/shard_map/ppermute | solution.py:536
  221.1 6.5 %collective-permute-start.55 = (bf16[2,48,768]{2,1,0:T(8,128)(2,1)S(1)}, bf16[2,48,768]{2,1,0:T(8,128)(2,1)S(1)}, u32[]{:S(2)}, u32[]{:S(2)}) collective-permute-start(bf16[2,48,768]{2,1,0:T(8,128)(2,1)S(1)} %get-tuple-element.402.d_mine), channel_id=1, source_target_pairs={{0,16},{16,0},{1,17},{17,1},{2,18},{18,2},{3,19},{19,3},{4,20},{20... | collective-permute-start | bytes 442376 | tf_op jit(solution)/shard_map/ppermute | solution.py:540
  222.3 7.4 %collective-permute-start.52 = (bf16[2,48,768]{2,1,0:T(8,128)(2,1)S(1)}, bf16[2,48,768]{2,1,0:T(8,128)(2,1)S(1)}, u32[]{:S(2)}, u32[]{:S(2)}) collective-permute-start(bf16[2,48,768]{2,1,0:T(8,128)(2,1)S(1)} %get-tuple-element.398), channel_id=1, source_target_pairs={{0,4},{1,5},{2,6},{3,7},{4,0},{5,1},{6,2},{7,3},{8,12},{9,13},{10,... | collective-permute-start | bytes 442376 | tf_op jit(solution)/shard_map/ppermute | solution.py:536
  223.3 11.6 %collective-permute-start.53 = (bf16[2,48,768]{2,1,0:T(8,128)(2,1)S(1)}, bf16[2,48,768]{2,1,0:T(8,128)(2,1)S(1)}, u32[]{:S(2)}, u32[]{:S(2)}) collective-permute-start(bf16[2,48,768]{2,1,0:T(8,128)(2,1)S(1)} %get-tuple-element.399), channel_id=1, source_target_pairs={{0,8},{1,9},{2,10},{3,11},{4,12},{5,13},{6,14},{7,15},{8,0},{9,1},... | collective-permute-start | bytes 442376 | tf_op jit(solution)/shard_map/ppermute | solution.py:536
  225.3 9.6 %collective-permute-start.54 = (bf16[2,48,768]{2,1,0:T(8,128)(2,1)S(1)}, bf16[2,48,768]{2,1,0:T(8,128)(2,1)S(1)}, u32[]{:S(2)}, u32[]{:S(2)}) collective-permute-start(bf16[2,48,768]{2,1,0:T(8,128)(2,1)S(1)} %get-tuple-element.400), channel_id=1, source_target_pairs={{0,12},{1,13},{2,14},{3,15},{4,8},{5,9},{6,10},{7,11},{8,4},{9,5},... | collective-permute-start | bytes 442376 | tf_op jit(solution)/shard_map/ppermute | solution.py:536
  226.7 8.2 %collective-permute-start.56 = (f32[8,768]{1,0:T(8,128)S(1)}, f32[8,768]{1,0:T(8,128)S(1)}, u32[]{:S(2)}, u32[]{:S(2)}) collective-permute-start(f32[8,768]{1,0:T(8,128)S(1)} %get-tuple-element.409.refs_4_), channel_id=1, source_target_pairs={{0,16},{16,0},{1,17},{17,1},{2,18},{18,2},{3,19},{19,3},{4,20},{20... | collective-permute-start | bytes 73736 | tf_op jit(solution)/shard_map/ppermute | solution.py:540
  235.0 5.2 %collective-permute-start.57 = (bf16[2,48,768]{2,1,0:T(8,128)(2,1)S(1)}, bf16[2,48,768]{2,1,0:T(8,128)(2,1)S(1)}, u32[]{:S(2)}, u32[]{:S(2)}) collective-permute-start(bf16[2,48,768]{2,1,0:T(8,128)(2,1)S(1)} %get-tuple-element.410.mine), channel_id=1, source_target_pairs={{0,16},{16,0},{1,17},{17,1},{2,18},{18,2},{3,19},{19,3},{4,20},{20... | collective-permute-start | bytes 442376 | tf_op jit(solution)/shard_map/ppermute | solution.py:540
  236.3 3.3 %collective-permute-start.60 = (f32[8,768]{1,0:T(8,128)S(1)}, f32[8,768]{1,0:T(8,128)S(1)}, u32[]{:S(2)}, u32[]{:S(2)}) collective-permute-start(f32[8,768]{1,0:T(8,128)S(1)} %get-tuple-element.411.v0), channel_id=1, source_target_pairs={{0,3},{1,2},{2,1},{3,0},{4,7},{5,6},{6,5},{7,4},{8,11},{9,10},{10,... | collective-permute-start | bytes 73736 | tf_op jit(solution)/shard_map/ppermute | solution.py:536
  236.3 3.9 %collective-permute-start.59 = (f32[8,768]{1,0:T(8,128)S(1)}, f32[8,768]{1,0:T(8,128)S(1)}, u32[]{:S(2)}, u32[]{:S(2)}) collective-permute-start(f32[8,768]{1,0:T(8,128)S(1)} %get-tuple-element.411.v0), channel_id=1, source_target_pairs={{0,2},{1,3},{2,0},{3,1},{4,6},{5,7},{6,4},{7,5},{8,10},{9,11},{10,... | collective-permute-start | bytes 73736 | tf_op jit(solution)/shard_map/ppermute | solution.py:536
  237.6 2.6 %collective-permute-start.58 = (f32[8,768]{1,0:T(8,128)S(1)}, f32[8,768]{1,0:T(8,128)S(1)}, u32[]{:S(2)}, u32[]{:S(2)}) collective-permute-start(f32[8,768]{1,0:T(8,128)S(1)} %get-tuple-element.411.v0), channel_id=1, source_target_pairs={{0,1},{1,0},{2,3},{3,2},{4,5},{5,4},{6,7},{7,6},{8,9},{9,8},{10,11... | collective-permute-start | bytes 73736 | tf_op jit(solution)/shard_map/ppermute | solution.py:536
  (21 other events, 148.0 us)

commit v8 on v7

--- a/solution.py
+++ b/solution.py
@@ -849,20 +849,19 @@
 def load_half(which):
     def load(scal, refs, w, sem):
         def start(rel):
-            for core in range(2):
-                for part, _, _, half, side, k in slots():
-                    if half != rel:
-                        continue
-                    src = piece(refs, part * 4 + half * 2 + side, core, k, (0, 4))
-                    per, rows, width = src.shape
-                    dev = device_of(scal, k, side, core)
-                    for b in range(per):
-                        block = part * per + b
+            for block in range(4):
+                for core in range(2):
+                    for part, _, _, half, side, k in slots():
+                        src = piece(refs, part * 4 + half * 2 + side, core, k, (0, 4))
+                        per, rows, width = src.shape
+                        if half != rel or block // per != part:
+                            continue
+                        dev = device_of(scal, k, side, core)
                         if which == 0:
                             dst, tile = w.at[block, rows_at(dev * rows, rows), :], block
                         else:
                             dst, tile = w.at[rows_at((dev * 2 * per + block) * rows, rows), :], scal[1] ^ k
-                        pltpu.make_async_copy(src.at[b], dst, sem.at[tile]).start()
+                        pltpu.make_async_copy(src.at[block % per], dst, sem.at[tile]).start()
 
         @pl.when(scal[0] == which)
         def _():
@@ -1076,17 +1075,18 @@
         own = pieces_of(za, zb, first, second)
         attn_w = [*own, joined, swap(second[0], 1), swap(second[1], 1)]
         cza, czb = [jnp.stack([t[i] for t in (c_half, c1, c2, c3)]) for i in range(2)]
+        c_xa, c_yb = swap(cza, 2), swap_y(czb)
         x_p, attn_w, cza, czb = lax.optimization_barrier((x, attn_w, cza, czb))
-        c_first = gather_first(cza, czb)
+        c_first = (c_xa, c_yb, swap_y(cza), swap(czb, 2))
         xn, q, k, v, da, wa, vec, b_mlp = project_call(scal, x_p, cot, None, attn_w, load_columns, read_vectors)
         part = core_call(0, scal, q, k, v, da, wa)
 
-        part, c_first = lax.optimization_barrier((part, c_first))
-        c_second = gather_second(*c_first[:2])
-        czs = [swap(cza, 1), swap(czb, 1)]
+        part, c_xa, c_yb, z_a, czb_b = lax.optimization_barrier((part, *c_first[:2], swap(cza, 1), czb))
+        c_second = gather_second(c_xa, c_yb)
+        czs = [z_a, swap(czb_b, 1)]
         o, d, dn = core_call(1, scal, q, k, v, da, wa, *part)
 
-        d, c_second, czs = lax.optimization_barrier((d, c_second, czs))
+        d, c_second, czs, c_first = lax.optimization_barrier((d, c_second, czs, (c_xa, c_yb, *c_first[2:])))
         c_own = pieces_of(cza, czb, c_first, c_second)
         ((c_joined,),) = mix("join_c", [join_job([t for t in c_own if t is not cza and t is not czb])])
         d, c_joined = lax.optimization_barrier((d, c_joined))

time: 243 us -> 245 us (level)
  starting transfers between devices: 54.6 us -> 65.1 us
  Pallas kernels: 115 us -> 108 us
    ppermute x45, starting transfers between devices: 39.9 us -> 48.3 us  [swap(): return lax.ppermute(value, 'wide', [(i, i ^ mask) for i in range(16)])]
    pallas_call x11, Pallas kernels: 98.7 us -> 91.5 us  [call(): pl.pallas_call(kernel, name=name, out_shape=list(outs) + list(g_shapes),...]
  transfers between devices with their start and end apart: 61 -> 61, of which waited for: 23 -> 19; matrix products, arithmetic and copies ran while one was open for 2% -> 2% of each run, Pallas kernels for 42% -> 38%
where the time goes in v8:
time: 245 us; the launch traced here: 244 us
  Pallas kernels  108 us (44%)
  starting transfers between devices  65.1 us (27%)
  waiting for transfers between devices  58.5 us (24%)
  local copies, waits for them, and re-layouts  7.4 us (3%)
  other arithmetic  3.07 us (1%)
    pallas_call x11, Pallas kernels, call(): pl.pallas_call(kernel, name=name, out_shape=list(outs) + list(g_shapes),...  91.5 us
    ppermute x45, waiting for transfers between devices, swap(): return lax.ppermute(value, 'wide', [(i, i ^ mask) for i in range(16)])  52.7 us
    ppermute x45, starting transfers between devices, swap(): return lax.ppermute(value, 'wide', [(i, i ^ mask) for i in range(16)])  48.3 us
    ppermute x16, starting transfers between devices, swap_y(): return lax.ppermute(value, 'narrow', [(0, 1), (1, 0)])  16.9 us
    pallas_call x10, Pallas kernels, mix(): pl.pallas_call(kernel, name=name, out_shape=outs, in_specs=[VMEM] * len(n...  12.4 us
    ppermute x16, waiting for transfers between devices, swap_y(): return lax.ppermute(value, 'narrow', [(0, 1), (1, 0)])  5.81 us
  transfers between devices with their start and end apart: 61, of which 19 were waited for; matrix products, arithmetic and copies ran while one was open for 2% of the time, Pallas kernels for 38%

profile of v8, /device:TPU:0, one launch (start us, length us, event | category | flops | bytes accessed | tf_op | source)
XLA Modules:
  0.0 243.7 jit_solution(16832441332570297723)
XLA Ops:
  1.4 1.3 select_bitcast_fusion.3
  2.7 5.1 %collective-permute-start.2 = (bf16[104,768]{1,0:T(8,128)(2,1)S(1)}, bf16[104,768]{1,0:T(8,128)(2,1)S(1)}, u32[]{:S(2)}, u32[]{:S(2)}) collective-permute-start(bf16[104,768]{1,0:T(8,128)(2,1)S(1)} %pad_maximum_fusion.5), channel_id=1, source_target_pairs={{0,12},{1,13},{2,14},{3,15},{4,8},{5,9},{6,10},{7,11},{8,4},{9,5},... | collective-permute-start | bytes 479240 | tf_op jit(solution)/shard_map/ppermute | solution.py:536
  9.3 3.6 %collective-permute-done.2 = bf16[104,768]{1,0:T(8,128)(2,1)S(1)} collective-permute-done((bf16[104,768]{1,0:T(8,128)(2,1)S(1)}, bf16[104,768]{1,0:T(8,128)(2,1)S(1)}, u32[]{:S(2)}, u32[]{:S(2)}) %collective-permute-start.2) | collective-permute-done | bytes 159776 | tf_op jit(solution)/shard_map/ppermute | solution.py:536
  12.9 8.5 %collective-permute-done.1 = bf16[104,768]{1,0:T(8,128)(2,1)S(1)} collective-permute-done((bf16[104,768]{1,0:T(8,128)(2,1)S(1)}, bf16[104,768]{1,0:T(8,128)(2,1)S(1)}, u32[]{:S(2)}, u32[]{:S(2)}) %collective-permute-start.1) | collective-permute-done | bytes 159776 | tf_op jit(solution)/shard_map/ppermute | solution.py:536
  21.5 1.6 collective-permute-start.5
  23.1 1.5 collective-permute-start.3
  25.8 13.6 %collective-permute-done.7 = bf16[2,2,48,768]{3,2,1,0:T(8,128)(2,1)} collective-permute-done((bf16[2,2,48,768]{3,2,1,0:T(8,128)(2,1)}, bf16[2,2,48,768]{3,2,1,0:T(8,128)(2,1)}, u32[]{:S(2)}, u32[]{:S(2)}) %collective-permute-start.7) | collective-permute-done | bytes 294944 | tf_op jit(solution)/shard_map/ppermute | solution.py:536
  39.5 1.3 join_a.1
  41.5 2.1 collective-permute-start.12
  44.1 1.3 fusion.11
  45.4 1.4 stack.70.refs_0_.scal
  46.8 1.2 fusion.7
  48.0 2.7 %collective-permute-done.9.refs_10_.refs_7_ = bf16[4,48,768]{2,1,0:T(8,128)(2,1)} collective-permute-done((bf16[4,48,768]{2,1,0:T(8,128)(2,1)}, bf16[4,48,768]{2,1,0:T(8,128)(2,1)}, u32[]{:S(2)}, u32[]{:S(2)}) %collective-permute-start.9) | collective-permute-done | bytes 294944 | tf_op jit(solution)/shard_map/ppermute | solution.py:536
  50.7 2.8 %collective-permute-done.12 = bf16[2,2,48,768]{3,2,1,0:T(8,128)(2,1)S(1)} collective-permute-done((bf16[2,2,48,768]{3,2,1,0:T(8,128)(2,1)}, bf16[2,2,48,768]{3,2,1,0:T(8,128)(2,1)S(1)}, u32[]{:S(2)}, u32[]{:S(2)}) %collective-permute-start.12) | collective-permute-done | bytes 294944 | tf_op jit(solution)/shard_map/ppermute | solution.py:536
  53.4 5.6 %collective-permute-done.11 = bf16[2,2,48,768]{3,2,1,0:T(8,128)(2,1)} collective-permute-done((bf16[2,2,48,768]{3,2,1,0:T(8,128)(2,1)}, bf16[2,2,48,768]{3,2,1,0:T(8,128)(2,1)}, u32[]{:S(2)}, u32[]{:S(2)}) %collective-permute-start.11) | collective-permute-done | bytes 294944 | tf_op jit(solution)/shard_map/ppermute | solution.py:536
  60.7 1.0 collective-permute-start.15
  62.4 1.6 collective-permute-start.21
  64.0 1.1 collective-permute-start.22
  65.0 9.5 %project.1 = (bf16[1024,768]{1,0:T(8,128)(2,1)S(1)}, bf16[1024,768]{1,0:T(8,128)(2,1)S(1)}, bf16[1024,768]{1,0:T(8,128)(2,1)S(1)}, bf16[1024,768]{1,0:T(8,128)(2...) custom-call(s32[10]{0:T(128)S(1)} %stack.70.refs_0_.scal, ...), custom_call_target="tpu_custom_call" | custom-call | flops 4831838208 | bytes 1048576 | tf_op jit(solution)/shard_map/project/pallas_call | solution.py:139
  74.6 10.6 %core.2 = (bf16[1024,768]{1,0:T(8,128)(2,1)S(1)}, bf16[3,1024,768]{2,1,0:T(8,128)(2,1)S(1)}, f32[1024,768]{1,0:T(8,128)S(1)}) custom-call(s32[10]{0:T(128)S(1)} %stack.70.refs_0_.scal, bf16[1024,768]{1,0:T(8,128)(2,1)S(1)} %get-tuple-element.243.q, bf16[1024,768]{1,0:T(8,128)(2,1)S(1)} %get-tuple-element.244.k, bf16[1024,768]{1,0:T(8,128)(2,1)S(1)} %get-tuple-element.245.v, ...), custom_call_target="tpu_custom_call" | custom-call | flops 10737418240 | bytes 1048576 | tf_op jit(solution)/shard_map/core/pallas_call | solution.py:139
  87.1 10.6 %core.3 = (bf16[1024,768]{1,0:T(8,128)(2,1)S(1)}, bf16[3,1024,768]{2,1,0:T(8,128)(2,1)S(1)}, f32[1024,768]{1,0:T(8,128)S(1)}) custom-call(s32[10]{0:T(128)S(1)} %stack.70.refs_0_.scal, bf16[1024,768]{1,0:T(8,128)(2,1)S(1)} %get-tuple-element.243.q, ...), custom_call_target="tpu_custom_call", output_to_operand_aliasing={{0}: (6, {}), {1}: (7, {}), {2}: (8, {})} | custom-call | flops 10737418240 | bytes 1048576 | tf_op jit(solution)/shard_map/core/pallas_call | solution.py:139
  97.8 4.4 %collective-permute-done.18.refs_2_.refs_6_.refs_3_ = bf16[4,2,48,768]{3,2,1,0:T(8,128)(2,1)S(1)} collective-permute-done((bf16[4,2,48,768]{3,2,1,0:T(8,128)(2,1)S(1)}, bf16[4,2,48,768]{3,2,1,0:T(8,128)(2,1)S(1)}, u32[]{:S(2)}, u32[]{:S(2)}) %collective-permute-start.18) | collective-permute-done | bytes 589856 | tf_op jit(solution)/shard_map/ppermute | solution.py:540
  103.2 7.8 %attn_grad.1 = (f32[8,768]{1,0:T(8,128)S(1)}, bf16[2,8,48,768]{3,2,1,0:T(8,128)(2,1)}, bf16[2,8,48,768]{3,2,1,0:T(8,128)(2,1)}, bf16[2,8,48,768]{3,2,1,0:T(8,128)(2,1)}, bf16[2,8,48,768]{3,2,1,0:T(8,128)(2,1)}) custom-call(s32[10]{0:T(128)S(1)} %stack.70.refs_0_.scal, bf16[1024,768]{1,0:T(8,128)(2,1)S(1)} %get-tuple-element.281.xn.refs_1_, ...), custom_call_target="tpu_custom_call" | custom-call | flops 4831838208 | bytes 1048576 | tf_op jit(solution)/shard_map/attn_grad/pallas_call | solution.py:139
  111.6 1.1 copy-done.13
  112.8 7.7 %up.2 = (bf16[4,1024,768]{2,1,0:T(8,128)(2,1)S(1)}, bf16[4,1024,768]{2,1,0:T(8,128)(2,1)S(1)}, bf16[4,768,768]{2,1,0:T(8,128)(2,1)S(1)}) custom-call(s32[10]{0:T(128)S(1)} %stack.70.refs_0_.scal, bf16[1024,768]{1,0:T(8,128)(2,1)S(1)} %get-tuple-element.281.xn.refs_1_, f32[4,768]{1,0:T(4,128)S(1)} %get-tuple-element.282.refs_2_, ...), custom_call_target="tpu_custom_call" | custom-call | flops 2415919104 | bytes 1048576 | tf_op jit(solution)/shard_map/up/pallas_call | solution.py:139
  120.5 1.6 sums_1.1
  122.6 1.0 collective-permute-start.27
  123.7 6.0 %up.3 = (bf16[4,1024,768]{2,1,0:T(8,128)(2,1)S(1)}, bf16[4,1024,768]{2,1,0:T(8,128)(2,1)S(1)}) custom-call(s32[10]{0:T(128)S(1)} %stack.70.refs_0_.scal, bf16[1024,768]{1,0:T(8,128)(2,1)S(1)} %get-tuple-element.281.xn.refs_1_, f32[4,768]{1,0:T(4,128)S(1)} %get-tuple-element.282.refs_2_, ...), custom_call_target="tpu_custom_call", output_to_operand_aliasing={{0}: (3, {}), {1}: (4, {})} | custom-call | flops 2415919104 | bytes 1048576 | tf_op jit(solution)/shard_map/up/pallas_call | solution.py:139
  129.7 7.7 %down_grad.1 = (bf16[3072,768]{1,0:T(8,128)(2,1)S(1)}, bf16[2,8,48,768]{3,2,1,0:T(8,128)(2,1)}, bf16[2,8,48,768]{3,2,1,0:T(8,128)(2,1)}, bf16[2,8,48,768]{3,2,1,0:T(8,128)(2,1)}, bf16[2,8,48,768]{3,2,1,0:T(8,128)(2,1)}) custom-call(s32[10]{0:T(128)S(1)} %stack.70.refs_0_.scal, bf16[4,1024,768]{2,1,0:T(8,128)(2,1)S(1)} %get-tuple-element.308.act, ...), custom_call_target="tpu_custom_call" | custom-call | flops 4831838208 | bytes 1048576 | tf_op jit(solution)/shard_map/down_grad/pallas_call | solution.py:139
  138.1 1.4 sums_2.1
  140.1 1.0 collective-permute-start.28
  141.2 1.5 collective-permute-start.29
  142.7 7.1 %dpre.1 = (bf16[4,1024,768]{2,1,0:T(8,128)(2,1)S(1)}, f32[8,768]{1,0:T(8,128)S(1)}) custom-call(s32[10]{0:T(128)S(1)} %stack.70.refs_0_.scal, bf16[1024,768]{1,0:T(8,128)(2,1)S(1)} %bitcast.35, bf16[4,1024,768]{2,1,0:T(8,128)(2,1)S(1)} %get-tuple-element.318.gp, bf16[3072,768]{1,0:T(8,128)(2,1)S(1)} %get-tuple-element.319.w.wd), custom_call_target="tpu_custom_call", output_to_operand_aliasing={{0}: (2, {})} | custom-call | flops 4831838208 | bytes 1048576 | tf_op jit(solution)/shard_map/dpre/pallas_call | solution.py:139
  150.1 1.7 sums_3.1
  151.8 1.6 collective-permute-start.35
  154.4 2.3 collective-permute-start.32
  156.7 8.9 %collective-permute-start.33 = (bf16[2,48,768]{2,1,0:T(8,128)(2,1)S(1)}, bf16[2,48,768]{2,1,0:T(8,128)(2,1)S(1)}, u32[]{:S(2)}, u32[]{:S(2)}) collective-permute-start(bf16[2,48,768]{2,1,0:T(8,128)(2,1)S(1)} %get-tuple-element.337), channel_id=1, source_target_pairs={{0,8},{1,9},{2,10},{3,11},{4,12},{5,13},{6,14},{7,15},{8,0},{9,1},... | collective-permute-start | bytes 442376 | tf_op jit(solution)/shard_map/ppermute | solution.py:536
  165.6 7.9 %up_grad.1 = (bf16[1,768,768]{2,1,0:T(8,128)(2,1)S(1)}, bf16[2,8,48,768]{3,2,1,0:T(8,128)(2,1)}, bf16[2,8,48,768]{3,2,1,0:T(8,128)(2,1)}, bf16[2,8,48,768]{3,2,1,0:T(8,128)(2,1)}, bf16[2,8,48,768]{3,2,1,0:T(8,128)(2,1)}) custom-call(s32[10]{0:T(128)S(1)} %stack.70.refs_0_.scal, bf16[1024,768]{1,0:T(8,128)(2,1)S(1)} %get-tuple-element.281.xn.refs_1_, ...), custom_call_target="tpu_custom_call" | custom-call | flops 4831838208 | bytes 1048576 | tf_op jit(solution)/shard_map/up_grad/pallas_call | solution.py:139
  173.5 2.8 %collective-permute-done.33.refs_2_ = bf16[2,48,768]{2,1,0:T(8,128)(2,1)S(1)} collective-permute-done((bf16[2,48,768]{2,1,0:T(8,128)(2,1)S(1)}, bf16[2,48,768]{2,1,0:T(8,128)(2,1)S(1)}, u32[]{:S(2)}, u32[]{:S(2)}) %collective-permute-start.33) | collective-permute-done | bytes 147488 | tf_op jit(solution)/shard_map/ppermute | solution.py:536
  176.3 1.4 sums_4.1
  178.3 1.2 collective-permute-start.41
  180.4 1.2 collective-permute-start.38
  181.6 8.4 %input_grad.1 = (f32[8,768]{1,0:T(8,128)S(1)}, bf16[2,512,768]{2,1,0:T(8,128)(2,1)}) custom-call(s32[10]{0:T(128)S(1)} %stack.70.refs_0_.scal, bf16[1024,768]{1,0:T(8,128)(2,1)S(1)} %bitcast.38, bf16[1024,768]{1,0:T(8,128)(2,1)S(1)} %bitcast.36, f32[1024,768]{1,0:T(8,128)S(1)} %get-tuple-element.362.dn, bf16[4,1024,768]{2,1,0:T(8,128)(2,1)S(1)} %get-tuple-element.341.dpre, ...), custom_call_target="tpu_custom_call" | custom-call | flops 8455716864 | bytes 1048576 | tf_op jit(solution)/shard_map/input_grad/pallas_call | solution.py:139
  190.7 1.9 sums_5.1
  192.5 1.3 collective-permute-start.42
  194.7 2.1 collective-permute-start.44
  197.8 1.5 collective-permute-start.46
  199.2 8.2 %out.1 = bf16[2,512,768]{2,1,0:T(8,128)(2,1)} custom-call(s32[10]{0:T(128)S(1)} %stack.70.refs_0_.scal, bf16[1024,768]{1,0:T(8,128)(2,1)S(1)} %bitcast.39, bf16[1024,768]{1,0:T(8,128)(2,1)S(1)} %get-tuple-element.269.o, bf16[4,1024,768]{2,1,0:T(8,128)(2,1)S(1)} %get-tuple-element.308.act, f32[8,768]{1,0:T(8,128)S(1)} %get-tuple-element.363.vec, ...), custom_call_target="tpu_custom_call" | custom-call | flops 6039797760 | bytes 1048576 | tf_op jit(solution)/shard_map/out/pallas_call | solution.py:139
  207.4 2.6 %collective-permute-done.45.refs_5_ = bf16[2,48,768]{2,1,0:T(8,128)(2,1)S(1)} collective-permute-done((bf16[2,48,768]{2,1,0:T(8,128)(2,1)S(1)}, bf16[2,48,768]{2,1,0:T(8,128)(2,1)S(1)}, u32[]{:S(2)}, u32[]{:S(2)}) %collective-permute-start.45) | collective-permute-done | bytes 147488 | tf_op jit(solution)/shard_map/ppermute | solution.py:536
  210.0 1.4 sums_6.1
  211.4 1.2 collective-permute-start.47
  213.5 1.9 collective-permute-start.51
  215.4 1.7 collective-permute-start.50
  217.8 1.3 collective-permute-done.51.refs_8_
  220.9 1.4 sums_7.1
  222.3 1.3 collective-permute-start.55
  224.5 2.0 collective-permute-start.53
  226.5 1.4 collective-permute-start.54
  228.7 2.2 place.1
  230.9 5.1 %collective-permute-done.53.refs_2_ = bf16[2,48,768]{2,1,0:T(8,128)(2,1)S(1)} collective-permute-done((bf16[2,48,768]{2,1,0:T(8,128)(2,1)S(1)}, bf16[2,48,768]{2,1,0:T(8,128)(2,1)S(1)}, u32[]{:S(2)}, u32[]{:S(2)}) %collective-permute-start.53) | collective-permute-done | bytes 147488 | tf_op jit(solution)/shard_map/ppermute | solution.py:536
  236.1 1.4 collective-permute-start.57
  238.3 1.0 collective-permute-start.58
  239.3 1.4 collective-permute-done.60.v3
  241.5 2.0 place_last.1
  (150 shorter events, 24.3 us)
Async XLA Ops:
  2.7 10.2 %collective-permute-start.2 = (bf16[104,768]{1,0:T(8,128)(2,1)S(1)}, bf16[104,768]{1,0:T(8,128)(2,1)S(1)}, u32[]{:S(2)}, u32[]{:S(2)}) collective-permute-start(bf16[104,768]{1,0:T(8,128)(2,1)S(1)} %pad_maximum_fusion.5), channel_id=1, source_target_pairs={{0,12},{1,13},{2,14},{3,15},{4,8},{5,9},{6,10},{7,11},{8,4},{9,5},... | collective-permute-start | bytes 479240 | tf_op jit(solution)/shard_map/ppermute | solution.py:536
  7.9 13.5 %collective-permute-start.1 = (bf16[104,768]{1,0:T(8,128)(2,1)S(1)}, bf16[104,768]{1,0:T(8,128)(2,1)S(1)}, u32[]{:S(2)}, u32[]{:S(2)}) collective-permute-start(bf16[104,768]{1,0:T(8,128)(2,1)S(1)} %pad_maximum_fusion.5), channel_id=1, source_target_pairs={{0,8},{1,9},{2,10},{3,11},{4,12},{5,13},{6,14},{7,15},{8,0},{9,1},... | collective-permute-start | bytes 479240 | tf_op jit(solution)/shard_map/ppermute | solution.py:536
  7.9 13.5 %collective-permute-start = (bf16[104,768]{1,0:T(8,128)(2,1)S(1)}, bf16[104,768]{1,0:T(8,128)(2,1)S(1)}, u32[]{:S(2)}, u32[]{:S(2)}) collective-permute-start(bf16[104,768]{1,0:T(8,128)(2,1)S(1)} %pad_maximum_fusion.5), channel_id=1, source_target_pairs={{0,4},{1,5},{2,6},{3,7},{4,0},{5,1},{6,2},{7,3},{8,12},{9,13},{10,... | collective-permute-start | bytes 479240 | tf_op jit(solution)/shard_map/ppermute | solution.py:536
  21.5 19.3 %copy-start.6 = (bf16[4,56,768]{2,1,0:T(8,128)(2,1)}, bf16[4,56,768]{2,1,0:T(8,128)(2,1)S(1)}, u32[]{:S(2)}) copy-start(bf16[4,56,768]{2,1,0:T(8,128)(2,1)S(1)} %pad_maximum_fusion.2.refs_0_.refs_3_) | copy-start | bytes 1032196
  21.5 18.0 %collective-permute-start.5 = (bf16[4,56,768]{2,1,0:T(8,128)(2,1)S(1)}, bf16[4,56,768]{2,1,0:T(8,128)(2,1)S(1)}, u32[]{:S(2)}, u32[]{:S(2)}) collective-permute-start(bf16[4,56,768]{2,1,0:T(8,128)(2,1)S(1)} %pad_maximum_fusion.2.refs_0_.refs_3_), channel_id=1, source_target_pairs={{0,16},{16,0},{1,17},{17,1},{2,18},{18,2},{3,19},{19,3},{4,20},{20... | collective-permute-start | bytes 1032200 | tf_op jit(solution)/shard_map/ppermute | solution.py:540
  23.1 16.4 %collective-permute-start.3 = (bf16[4,56,768]{2,1,0:T(8,128)(2,1)S(1)}, bf16[4,56,768]{2,1,0:T(8,128)(2,1)S(1)}, u32[]{:S(2)}, u32[]{:S(2)}) collective-permute-start(bf16[4,56,768]{2,1,0:T(8,128)(2,1)S(1)} %pad_maximum_fusion.2.refs_0_.refs_3_), channel_id=1, source_target_pairs={{0,2},{1,3},{2,0},{3,1},{4,6},{5,7},{6,4},{7,5},{8,10},{9,11},{10,... | collective-permute-start | bytes 1032200 | tf_op jit(solution)/shard_map/ppermute | solution.py:536
  24.7 14.8 %collective-permute-start.7 = (bf16[2,2,48,768]{3,2,1,0:T(8,128)(2,1)}, bf16[2,2,48,768]{3,2,1,0:T(8,128)(2,1)}, u32[]{:S(2)}, u32[]{:S(2)}) collective-permute-start(bf16[2,2,48,768]{3,2,1,0:T(8,128)(2,1)} %bitcast.20), channel_id=1, source_target_pairs={{0,8},{1,9},{2,10},{3,11},{4,12},{5,13},{6,14},{7,15},{8,0},{9,1},... | collective-permute-start | bytes 884744 | tf_op jit(solution)/shard_map/ppermute | solution.py:536
  24.8 14.7 %collective-permute-start.6 = (bf16[4,48,768]{2,1,0:T(8,128)(2,1)S(1)}, bf16[4,48,768]{2,1,0:T(8,128)(2,1)S(1)}, u32[]{:S(2)}, u32[]{:S(2)}) collective-permute-start(bf16[4,48,768]{2,1,0:T(8,128)(2,1)S(1)} %pad_maximum_fusion.3.refs_3_.refs_7_.refs_4_), channel_id=1, source_target_pairs={{0,2},{1,3},{2,0},{3,1},{4,6},{5,7},{6,4},{7,5},{8,10},{9,11},{10,... | collective-permute-start | bytes 884744 | tf_op jit(solution)/shard_map/ppermute | solution.py:536
  25.4 14.1 %collective-permute-start.4 = (bf16[4,48,768]{2,1,0:T(8,128)(2,1)S(1)}, bf16[4,48,768]{2,1,0:T(8,128)(2,1)}, u32[]{:S(2)}, u32[]{:S(2)}) collective-permute-start(bf16[4,48,768]{2,1,0:T(8,128)(2,1)S(1)} %pad_maximum_fusion.3.refs_3_.refs_7_.refs_4_), channel_id=1, source_target_pairs={{0,16},{16,0},{1,17},{17,1},{2,18},{18,2},{3,19},{19,3},{4,20},{20... | collective-permute-start | bytes 884744 | tf_op jit(solution)/shard_map/ppermute | solution.py:540
  40.9 18.2 %collective-permute-start.10 = (bf16[24,56,768]{2,1,0:T(8,128)(2,1)S(1)}, bf16[24,56,768]{2,1,0:T(8,128)(2,1)}, u32[]{:S(2)}, u32[]{:S(2)}) collective-permute-start(bf16[24,56,768]{2,1,0:T(8,128)(2,1)S(1)} %join_a.1), channel_id=1, source_target_pairs={{0,1},{1,0},{2,3},{3,2},{4,5},{5,4},{6,7},{7,6},{8,9},{9,8},{10,11... | collective-permute-start | bytes 6193160 | tf_op jit(solution)/shard_map/ppermute | solution.py:536
  40.9 9.7 %collective-permute-start.9 = (bf16[4,48,768]{2,1,0:T(8,128)(2,1)}, bf16[4,48,768]{2,1,0:T(8,128)(2,1)}, u32[]{:S(2)}, u32[]{:S(2)}) collective-permute-start(bf16[4,48,768]{2,1,0:T(8,128)(2,1)} %collective-permute-done.4.refs_5_.refs_9_.refs_6_), channel_id=1, source_target_pairs={{0,2},{1,3},{2,0},{3,1},{4,6},{5,7},{6,4},{7,5},{8,10},{9,11},{10,... | collective-permute-start | bytes 884744 | tf_op jit(solution)/shard_map/ppermute | solution.py:536
  41.5 11.9 %collective-permute-start.12 = (bf16[2,2,48,768]{3,2,1,0:T(8,128)(2,1)}, bf16[2,2,48,768]{3,2,1,0:T(8,128)(2,1)S(1)}, u32[]{:S(2)}, u32[]{:S(2)}) collective-permute-start(bf16[2,2,48,768]{3,2,1,0:T(8,128)(2,1)} %bitcast.20), channel_id=1, source_target_pairs={{0,12},{1,13},{2,14},{3,15},{4,8},{5,9},{6,10},{7,11},{8,4},{9,5},... | collective-permute-start | bytes 884744 | tf_op jit(solution)/shard_map/ppermute | solution.py:536
  43.6 15.4 %collective-permute-start.11 = (bf16[2,2,48,768]{3,2,1,0:T(8,128)(2,1)}, bf16[2,2,48,768]{3,2,1,0:T(8,128)(2,1)}, u32[]{:S(2)}, u32[]{:S(2)}) collective-permute-start(bf16[2,2,48,768]{3,2,1,0:T(8,128)(2,1)} %bitcast.20), channel_id=1, source_target_pairs={{0,4},{1,5},{2,6},{3,7},{4,0},{5,1},{6,2},{7,3},{8,12},{9,13},{10,... | collective-permute-start | bytes 884744 | tf_op jit(solution)/shard_map/ppermute | solution.py:536
  43.6 15.4 %collective-permute-start.8 = (bf16[4,56,768]{2,1,0:T(8,128)(2,1)S(1)}, bf16[4,56,768]{2,1,0:T(8,128)(2,1)}, u32[]{:S(2)}, u32[]{:S(2)}) collective-permute-start(bf16[4,56,768]{2,1,0:T(8,128)(2,1)S(1)} %collective-permute-done.3.refs_1_.refs_4_), channel_id=1, source_target_pairs={{0,16},{16,0},{1,17},{17,1},{2,18},{18,2},{3,19},{19,3},{4,20},{20... | collective-permute-start | bytes 1032200 | tf_op jit(solution)/shard_map/ppermute | solution.py:540
  48.0 17.1 %copy-start.11 = (bf16[2,512,768]{2,1,0:T(8,128)(2,1)S(1)}, bf16[2,512,768]{2,1,0:T(8,128)(2,1)}, u32[]{:S(2)}) copy-start(bf16[2,512,768]{2,1,0:T(8,128)(2,1)} %param.12) | copy-start | bytes 4718596
  59.0 3.3 %collective-permute-start.14 = (bf16[4,48,768]{2,1,0:T(8,128)(2,1)}, bf16[4,48,768]{2,1,0:T(8,128)(2,1)S(1)}, u32[]{:S(2)}, u32[]{:S(2)}) collective-permute-start(bf16[4,48,768]{2,1,0:T(8,128)(2,1)} %collective-permute-done.9.refs_10_.refs_7_), channel_id=1, source_target_pairs={{0,1},{1,0},{2,3},{3,2},{4,5},{5,4},{6,7},{7,6},{8,9},{9,8},{10,11... | collective-permute-start | bytes 884744 | tf_op jit(solution)/shard_map/ppermute | solution.py:536
  59.0 3.3 %collective-permute-start.13 = (bf16[4,56,768]{2,1,0:T(8,128)(2,1)}, bf16[4,56,768]{2,1,0:T(8,128)(2,1)S(1)}, u32[]{:S(2)}, u32[]{:S(2)}) collective-permute-start(bf16[4,56,768]{2,1,0:T(8,128)(2,1)} %collective-permute-done.8.refs_6_.refs_3_), channel_id=1, source_target_pairs={{0,1},{1,0},{2,3},{3,2},{4,5},{5,4},{6,7},{7,6},{8,9},{9,8},{10,11... | collective-permute-start | bytes 1032200 | tf_op jit(solution)/shard_map/ppermute | solution.py:536
  60.7 24.6 %collective-permute-start.15 = (bf16[4,2,48,768]{3,2,1,0:T(8,128)(2,1)S(1)}, bf16[4,2,48,768]{3,2,1,0:T(8,128)(2,1)S(1)}, u32[]{:S(2)}, u32[]{:S(2)}) collective-permute-start(bf16[4,2,48,768]{3,2,1,0:T(8,128)(2,1)S(1)} %pad_maximum_fusion.refs_3_.refs_0_), channel_id=1, source_target_pairs={{0,2},{1,3},{2,0},{3,1},{4,6},{5,7},{6,4},{7,5},{8,10},{9,11},{10,... | collective-permute-start | bytes 1769480 | tf_op jit(solution)/shard_map/ppermute | solution.py:536
  61.8 23.5 %copy-start.15 = (bf16[4,2,48,768]{3,2,1,0:T(8,128)(2,1)}, bf16[4,2,48,768]{3,2,1,0:T(8,128)(2,1)S(1)}, u32[]{:S(2)}) copy-start(bf16[4,2,48,768]{3,2,1,0:T(8,128)(2,1)S(1)} %pad_maximum_fusion.1.refs_7_.refs_4_) | copy-start | bytes 1769476
  61.8 23.5 %collective-permute-start.16 = (bf16[4,2,48,768]{3,2,1,0:T(8,128)(2,1)S(1)}, bf16[4,2,48,768]{3,2,1,0:T(8,128)(2,1)S(1)}, u32[]{:S(2)}, u32[]{:S(2)}) collective-permute-start(bf16[4,2,48,768]{3,2,1,0:T(8,128)(2,1)S(1)} %pad_maximum_fusion.1.refs_7_.refs_4_), channel_id=1, source_target_pairs={{0,16},{16,0},{1,17},{17,1},{2,18},{18,2},{3,19},{19,3},{4,20},{20... | collective-permute-start | bytes 1769480 | tf_op jit(solution)/shard_map/ppermute | solution.py:540
  62.4 35.4 %collective-permute-start.21 = (bf16[4,2,48,768]{3,2,1,0:T(8,128)(2,1)S(1)}, bf16[4,2,48,768]{3,2,1,0:T(8,128)(2,1)S(1)}, u32[]{:S(2)}, u32[]{:S(2)}) collective-permute-start(bf16[4,2,48,768]{3,2,1,0:T(8,128)(2,1)S(1)} %pad_maximum_fusion.refs_3_.refs_0_), channel_id=1, source_target_pairs={{0,16},{16,0},{1,17},{17,1},{2,18},{18,2},{3,19},{19,3},{4,20},{20... | collective-permute-start | bytes 1769480 | tf_op jit(solution)/shard_map/ppermute | solution.py:540
  64.0 21.3 %collective-permute-start.17 = (bf16[4,2,48,768]{3,2,1,0:T(8,128)(2,1)S(1)}, bf16[4,2,48,768]{3,2,1,0:T(8,128)(2,1)S(1)}, u32[]{:S(2)}, u32[]{:S(2)}) collective-permute-start(bf16[4,2,48,768]{3,2,1,0:T(8,128)(2,1)S(1)} %pad_maximum_fusion.refs_3_.refs_0_), channel_id=1, source_target_pairs={{0,1},{1,0},{2,3},{3,2},{4,5},{5,4},{6,7},{7,6},{8,9},{9,8},{10,11... | collective-permute-start | bytes 1769480 | tf_op jit(solution)/shard_map/ppermute | solution.py:536
  64.0 33.8 %collective-permute-start.22 = (bf16[4,2,48,768]{3,2,1,0:T(8,128)(2,1)S(1)}, bf16[4,2,48,768]{3,2,1,0:T(8,128)(2,1)S(1)}, u32[]{:S(2)}, u32[]{:S(2)}) collective-permute-start(bf16[4,2,48,768]{3,2,1,0:T(8,128)(2,1)S(1)} %pad_maximum_fusion.1.refs_7_.refs_4_), channel_id=1, source_target_pairs={{0,2},{1,3},{2,0},{3,1},{4,6},{5,7},{6,4},{7,5},{8,10},{9,11},{10,... | collective-permute-start | bytes 1769480 | tf_op jit(solution)/shard_map/ppermute | solution.py:536
  85.3 12.5 %collective-permute-start.20 = (bf16[4,2,48,768]{3,2,1,0:T(8,128)(2,1)S(1)}, bf16[4,2,48,768]{3,2,1,0:T(8,128)(2,1)S(1)}, u32[]{:S(2)}, u32[]{:S(2)}) collective-permute-start(bf16[4,2,48,768]{3,2,1,0:T(8,128)(2,1)S(1)} %pad_maximum_fusion.1.refs_7_.refs_4_), channel_id=1, source_target_pairs={{0,1},{1,0},{2,3},{3,2},{4,5},{5,4},{6,7},{7,6},{8,9},{9,8},{10,11... | collective-permute-start | bytes 1769480 | tf_op jit(solution)/shard_map/ppermute | solution.py:536
  85.6 16.5 %collective-permute-start.18 = (bf16[4,2,48,768]{3,2,1,0:T(8,128)(2,1)S(1)}, bf16[4,2,48,768]{3,2,1,0:T(8,128)(2,1)S(1)}, u32[]{:S(2)}, u32[]{:S(2)}) collective-permute-start(bf16[4,2,48,768]{3,2,1,0:T(8,128)(2,1)S(1)} %collective-permute-done.15.refs_0_.refs_4_.refs_1_), channel_id=1, source_target_pairs={{0,16},{16,0},{1,17},{17,1},{2,18},{18,2},{3,19},{19,3},{4,20},{20... | collective-permute-start | bytes 1769480 | tf_op jit(solution)/shard_map/ppermute | solution.py:540
  86.1 16.1 %collective-permute-start.19 = (bf16[4,2,48,768]{3,2,1,0:T(8,128)(2,1)S(1)}, bf16[4,2,48,768]{3,2,1,0:T(8,128)(2,1)S(1)}, u32[]{:S(2)}, u32[]{:S(2)}) collective-permute-start(bf16[4,2,48,768]{3,2,1,0:T(8,128)(2,1)S(1)} %collective-permute-done.16.refs_4_.refs_9_.refs_6_), channel_id=1, source_target_pairs={{0,2},{1,3},{2,0},{3,1},{4,6},{5,7},{6,4},{7,5},{8,10},{9,11},{10,... | collective-permute-start | bytes 1769480 | tf_op jit(solution)/shard_map/ppermute | solution.py:536
  103.2 7.8 %collective-permute-start.23 = (bf16[24,2,48,768]{3,2,1,0:T(8,128)(2,1)S(1)}, bf16[24,2,48,768]{3,2,1,0:T(8,128)(2,1)S(1)}, u32[]{:S(2)}, u32[]{:S(2)}) collective-permute-start(bf16[24,2,48,768]{3,2,1,0:T(8,128)(2,1)S(1)} %join_c.1), channel_id=1, source_target_pairs={{0,1},{1,0},{2,3},{3,2},{4,5},{5,4},{6,7},{7,6},{8,9},{9,8},{10,11... | collective-permute-start | bytes 10616840 | tf_op jit(solution)/shard_map/ppermute | solution.py:536
  111.0 9.5 %collective-permute-start.24 = (bf16[2,8,48,768]{3,2,1,0:T(8,128)(2,1)}, bf16[2,8,48,768]{3,2,1,0:T(8,128)(2,1)S(1)}, u32[]{:S(2)}, u32[]{:S(2)}) collective-permute-start(bf16[2,8,48,768]{3,2,1,0:T(8,128)(2,1)} %get-tuple-element.295), channel_id=1, source_target_pairs={{0,1},{1,0},{2,3},{3,2},{4,5},{5,4},{6,7},{7,6},{8,9},{9,8},{10,11... | collective-permute-start | bytes 3538952 | tf_op jit(solution)/shard_map/ppermute | solution.py:536
  111.6 8.9 %collective-permute-start.25 = (bf16[2,8,48,768]{3,2,1,0:T(8,128)(2,1)}, bf16[2,8,48,768]{3,2,1,0:T(8,128)(2,1)S(1)}, u32[]{:S(2)}, u32[]{:S(2)}) collective-permute-start(bf16[2,8,48,768]{3,2,1,0:T(8,128)(2,1)} %get-tuple-element.296), channel_id=1, source_target_pairs={{0,1},{1,0},{2,3},{3,2},{4,5},{5,4},{6,7},{7,6},{8,9},{9,8},{10,11... | collective-permute-start | bytes 3538952 | tf_op jit(solution)/shard_map/ppermute | solution.py:536
  122.1 15.8 %collective-permute-start.26 = (bf16[8,48,768]{2,1,0:T(8,128)(2,1)S(1)}, bf16[8,48,768]{2,1,0:T(8,128)(2,1)S(1)}, u32[]{:S(2)}, u32[]{:S(2)}) collective-permute-start(bf16[8,48,768]{2,1,0:T(8,128)(2,1)S(1)} %get-tuple-element.306), channel_id=1, source_target_pairs={{0,16},{16,0},{1,17},{17,1},{2,18},{18,2},{3,19},{19,3},{4,20},{20... | collective-permute-start | bytes 1769480 | tf_op jit(solution)/shard_map/ppermute | solution.py:540
  122.6 15.5 %collective-permute-start.27 = (bf16[8,48,768]{2,1,0:T(8,128)(2,1)S(1)}, bf16[8,48,768]{2,1,0:T(8,128)(2,1)S(1)}, u32[]{:S(2)}, u32[]{:S(2)}) collective-permute-start(bf16[8,48,768]{2,1,0:T(8,128)(2,1)S(1)} %get-tuple-element.307), channel_id=1, source_target_pairs={{0,2},{1,3},{2,0},{3,1},{4,6},{5,7},{6,4},{7,5},{8,10},{9,11},{10,... | collective-permute-start | bytes 1769480 | tf_op jit(solution)/shard_map/ppermute | solution.py:536
  139.6 10.5 %collective-permute-start.30 = (bf16[2,8,48,768]{3,2,1,0:T(8,128)(2,1)S(1)}, bf16[2,8,48,768]{3,2,1,0:T(8,128)(2,1)S(1)}, u32[]{:S(2)}, u32[]{:S(2)}) collective-permute-start(bf16[2,8,48,768]{3,2,1,0:T(8,128)(2,1)S(1)} %copy-done.21), channel_id=1, source_target_pairs={{0,1},{1,0},{2,3},{3,2},{4,5},{5,4},{6,7},{7,6},{8,9},{9,8},{10,11... | collective-permute-start | bytes 3538952 | tf_op jit(solution)/shard_map/ppermute | solution.py:536
  139.9 10.2 %collective-permute-start.31 = (bf16[2,8,48,768]{3,2,1,0:T(8,128)(2,1)S(1)}, bf16[2,8,48,768]{3,2,1,0:T(8,128)(2,1)S(1)}, u32[]{:S(2)}, u32[]{:S(2)}) collective-permute-start(bf16[2,8,48,768]{3,2,1,0:T(8,128)(2,1)S(1)} %copy-done.20), channel_id=1, source_target_pairs={{0,1},{1,0},{2,3},{3,2},{4,5},{5,4},{6,7},{7,6},{8,9},{9,8},{10,11... | collective-permute-start | bytes 3538952 | tf_op jit(solution)/shard_map/ppermute | solution.py:536
  140.1 9.7 %collective-permute-start.28 = (bf16[4,48,768]{2,1,0:T(8,128)(2,1)S(1)}, bf16[4,48,768]{2,1,0:T(8,128)(2,1)S(1)}, u32[]{:S(2)}, u32[]{:S(2)}) collective-permute-start(bf16[4,48,768]{2,1,0:T(8,128)(2,1)S(1)} %get-tuple-element.321), channel_id=1, source_target_pairs={{0,2},{1,3},{2,0},{3,1},{4,6},{5,7},{6,4},{7,5},{8,10},{9,11},{10,... | collective-permute-start | bytes 884744 | tf_op jit(solution)/shard_map/ppermute | solution.py:536
  141.2 8.9 %collective-permute-start.29 = (bf16[4,48,768]{2,1,0:T(8,128)(2,1)S(1)}, bf16[4,48,768]{2,1,0:T(8,128)(2,1)S(1)}, u32[]{:S(2)}, u32[]{:S(2)}) collective-permute-start(bf16[4,48,768]{2,1,0:T(8,128)(2,1)S(1)} %get-tuple-element.322), channel_id=1, source_target_pairs={{0,16},{16,0},{1,17},{17,1},{2,18},{18,2},{3,19},{19,3},{4,20},{20... | collective-permute-start | bytes 884744 | tf_op jit(solution)/shard_map/ppermute | solution.py:540
  151.8 24.4 %collective-permute-start.35 = (bf16[8,48,768]{2,1,0:T(8,128)(2,1)S(1)}, bf16[8,48,768]{2,1,0:T(8,128)(2,1)S(1)}, u32[]{:S(2)}, u32[]{:S(2)}) collective-permute-start(bf16[8,48,768]{2,1,0:T(8,128)(2,1)S(1)} %get-tuple-element.339), channel_id=1, source_target_pairs={{0,16},{16,0},{1,17},{17,1},{2,18},{18,2},{3,19},{19,3},{4,20},{20... | collective-permute-start | bytes 1769480 | tf_op jit(solution)/shard_map/ppermute | solution.py:540
  153.4 22.8 %collective-permute-start.36 = (bf16[8,48,768]{2,1,0:T(8,128)(2,1)S(1)}, bf16[8,48,768]{2,1,0:T(8,128)(2,1)S(1)}, u32[]{:S(2)}, u32[]{:S(2)}) collective-permute-start(bf16[8,48,768]{2,1,0:T(8,128)(2,1)S(1)} %get-tuple-element.340), channel_id=1, source_target_pairs={{0,2},{1,3},{2,0},{3,1},{4,6},{5,7},{6,4},{7,5},{8,10},{9,11},{10,... | collective-permute-start | bytes 1769480 | tf_op jit(solution)/shard_map/ppermute | solution.py:536
  154.4 19.1 %collective-permute-start.32 = (bf16[2,48,768]{2,1,0:T(8,128)(2,1)S(1)}, bf16[2,48,768]{2,1,0:T(8,128)(2,1)S(1)}, u32[]{:S(2)}, u32[]{:S(2)}) collective-permute-start(bf16[2,48,768]{2,1,0:T(8,128)(2,1)S(1)} %get-tuple-element.336), channel_id=1, source_target_pairs={{0,4},{1,5},{2,6},{3,7},{4,0},{5,1},{6,2},{7,3},{8,12},{9,13},{10,... | collective-permute-start | bytes 442376 | tf_op jit(solution)/shard_map/ppermute | solution.py:536
  156.7 19.6 %collective-permute-start.33 = (bf16[2,48,768]{2,1,0:T(8,128)(2,1)S(1)}, bf16[2,48,768]{2,1,0:T(8,128)(2,1)S(1)}, u32[]{:S(2)}, u32[]{:S(2)}) collective-permute-start(bf16[2,48,768]{2,1,0:T(8,128)(2,1)S(1)} %get-tuple-element.337), channel_id=1, source_target_pairs={{0,8},{1,9},{2,10},{3,11},{4,12},{5,13},{6,14},{7,15},{8,0},{9,1},... | collective-permute-start | bytes 442376 | tf_op jit(solution)/shard_map/ppermute | solution.py:536
  165.6 10.7 %collective-permute-start.34 = (bf16[2,48,768]{2,1,0:T(8,128)(2,1)S(1)}, bf16[2,48,768]{2,1,0:T(8,128)(2,1)S(1)}, u32[]{:S(2)}, u32[]{:S(2)}) collective-permute-start(bf16[2,48,768]{2,1,0:T(8,128)(2,1)S(1)} %get-tuple-element.338), channel_id=1, source_target_pairs={{0,12},{1,13},{2,14},{3,15},{4,8},{5,9},{6,10},{7,11},{8,4},{9,5},... | collective-permute-start | bytes 442376 | tf_op jit(solution)/shard_map/ppermute | solution.py:536
  177.8 12.9 %collective-permute-start.39 = (bf16[2,8,48,768]{3,2,1,0:T(8,128)(2,1)S(1)}, bf16[2,8,48,768]{3,2,1,0:T(8,128)(2,1)S(1)}, u32[]{:S(2)}, u32[]{:S(2)}) collective-permute-start(bf16[2,8,48,768]{3,2,1,0:T(8,128)(2,1)S(1)} %copy-done.19), channel_id=1, source_target_pairs={{0,1},{1,0},{2,3},{3,2},{4,5},{5,4},{6,7},{7,6},{8,9},{9,8},{10,11... | collective-permute-start | bytes 3538952 | tf_op jit(solution)/shard_map/ppermute | solution.py:536
  178.1 12.6 %collective-permute-start.40 = (bf16[2,8,48,768]{3,2,1,0:T(8,128)(2,1)S(1)}, bf16[2,8,48,768]{3,2,1,0:T(8,128)(2,1)S(1)}, u32[]{:S(2)}, u32[]{:S(2)}) collective-permute-start(bf16[2,8,48,768]{3,2,1,0:T(8,128)(2,1)S(1)} %copy-done.18), channel_id=1, source_target_pairs={{0,1},{1,0},{2,3},{3,2},{4,5},{5,4},{6,7},{7,6},{8,9},{9,8},{10,11... | collective-permute-start | bytes 3538952 | tf_op jit(solution)/shard_map/ppermute | solution.py:536
  178.3 11.7 %collective-permute-start.41 = (bf16[2,48,768]{2,1,0:T(8,128)(2,1)S(1)}, bf16[2,48,768]{2,1,0:T(8,128)(2,1)S(1)}, u32[]{:S(2)}, u32[]{:S(2)}) collective-permute-start(bf16[2,48,768]{2,1,0:T(8,128)(2,1)S(1)} %get-tuple-element.360.a_mine), channel_id=1, source_target_pairs={{0,16},{16,0},{1,17},{17,1},{2,18},{18,2},{3,19},{19,3},{4,20},{20... | collective-permute-start | bytes 442376 | tf_op jit(solution)/shard_map/ppermute | solution.py:540
  179.5 10.5 %collective-permute-start.37 = (bf16[4,48,768]{2,1,0:T(8,128)(2,1)S(1)}, bf16[4,48,768]{2,1,0:T(8,128)(2,1)S(1)}, u32[]{:S(2)}, u32[]{:S(2)}) collective-permute-start(bf16[4,48,768]{2,1,0:T(8,128)(2,1)S(1)} %get-tuple-element.356), channel_id=1, source_target_pairs={{0,2},{1,3},{2,0},{3,1},{4,6},{5,7},{6,4},{7,5},{8,10},{9,11},{10,... | collective-permute-start | bytes 884744 | tf_op jit(solution)/shard_map/ppermute | solution.py:536
  180.4 10.2 %collective-permute-start.38 = (bf16[4,48,768]{2,1,0:T(8,128)(2,1)S(1)}, bf16[4,48,768]{2,1,0:T(8,128)(2,1)S(1)}, u32[]{:S(2)}, u32[]{:S(2)}) collective-permute-start(bf16[4,48,768]{2,1,0:T(8,128)(2,1)S(1)} %get-tuple-element.357), channel_id=1, source_target_pairs={{0,16},{16,0},{1,17},{17,1},{2,18},{18,2},{3,19},{19,3},{4,20},{20... | collective-permute-start | bytes 884744 | tf_op jit(solution)/shard_map/ppermute | solution.py:540
  192.5 17.5 %collective-permute-start.42 = (bf16[8,48,768]{2,1,0:T(8,128)(2,1)S(1)}, bf16[8,48,768]{2,1,0:T(8,128)(2,1)S(1)}, u32[]{:S(2)}, u32[]{:S(2)}) collective-permute-start(bf16[8,48,768]{2,1,0:T(8,128)(2,1)S(1)} %get-tuple-element.380), channel_id=1, source_target_pairs={{0,16},{16,0},{1,17},{17,1},{2,18},{18,2},{3,19},{19,3},{4,20},{20... | collective-permute-start | bytes 1769480 | tf_op jit(solution)/shard_map/ppermute | solution.py:540
  193.8 16.2 %collective-permute-start.43 = (bf16[8,48,768]{2,1,0:T(8,128)(2,1)S(1)}, bf16[8,48,768]{2,1,0:T(8,128)(2,1)S(1)}, u32[]{:S(2)}, u32[]{:S(2)}) collective-permute-start(bf16[8,48,768]{2,1,0:T(8,128)(2,1)S(1)} %get-tuple-element.381), channel_id=1, source_target_pairs={{0,2},{1,3},{2,0},{3,1},{4,6},{5,7},{6,4},{7,5},{8,10},{9,11},{10,... | collective-permute-start | bytes 1769480 | tf_op jit(solution)/shard_map/ppermute | solution.py:536
  194.7 12.7 %collective-permute-start.44 = (bf16[2,48,768]{2,1,0:T(8,128)(2,1)S(1)}, bf16[2,48,768]{2,1,0:T(8,128)(2,1)S(1)}, u32[]{:S(2)}, u32[]{:S(2)}) collective-permute-start(bf16[2,48,768]{2,1,0:T(8,128)(2,1)S(1)} %get-tuple-element.382), channel_id=1, source_target_pairs={{0,4},{1,5},{2,6},{3,7},{4,0},{5,1},{6,2},{7,3},{8,12},{9,13},{10,... | collective-permute-start | bytes 442376 | tf_op jit(solution)/shard_map/ppermute | solution.py:536
  196.8 13.2 %collective-permute-start.45 = (bf16[2,48,768]{2,1,0:T(8,128)(2,1)S(1)}, bf16[2,48,768]{2,1,0:T(8,128)(2,1)S(1)}, u32[]{:S(2)}, u32[]{:S(2)}) collective-permute-start(bf16[2,48,768]{2,1,0:T(8,128)(2,1)S(1)} %get-tuple-element.383), channel_id=1, source_target_pairs={{0,8},{1,9},{2,10},{3,11},{4,12},{5,13},{6,14},{7,15},{8,0},{9,1},... | collective-permute-start | bytes 442376 | tf_op jit(solution)/shard_map/ppermute | solution.py:536
  197.8 12.3 %collective-permute-start.46 = (bf16[2,48,768]{2,1,0:T(8,128)(2,1)S(1)}, bf16[2,48,768]{2,1,0:T(8,128)(2,1)S(1)}, u32[]{:S(2)}, u32[]{:S(2)}) collective-permute-start(bf16[2,48,768]{2,1,0:T(8,128)(2,1)S(1)} %get-tuple-element.384), channel_id=1, source_target_pairs={{0,12},{1,13},{2,14},{3,15},{4,8},{5,9},{6,10},{7,11},{8,4},{9,5},... | collective-permute-start | bytes 442376 | tf_op jit(solution)/shard_map/ppermute | solution.py:536
  211.4 9.5 %collective-permute-start.47 = (bf16[4,48,768]{2,1,0:T(8,128)(2,1)S(1)}, bf16[4,48,768]{2,1,0:T(8,128)(2,1)S(1)}, u32[]{:S(2)}, u32[]{:S(2)}) collective-permute-start(bf16[4,48,768]{2,1,0:T(8,128)(2,1)S(1)} %get-tuple-element.397), channel_id=1, source_target_pairs={{0,2},{1,3},{2,0},{3,1},{4,6},{5,7},{6,4},{7,5},{8,10},{9,11},{10,... | collective-permute-start | bytes 884744 | tf_op jit(solution)/shard_map/ppermute | solution.py:536
  212.6 8.3 %collective-permute-start.48 = (bf16[4,48,768]{2,1,0:T(8,128)(2,1)S(1)}, bf16[4,48,768]{2,1,0:T(8,128)(2,1)S(1)}, u32[]{:S(2)}, u32[]{:S(2)}) collective-permute-start(bf16[4,48,768]{2,1,0:T(8,128)(2,1)S(1)} %get-tuple-element.398), channel_id=1, source_target_pairs={{0,16},{16,0},{1,17},{17,1},{2,18},{18,2},{3,19},{19,3},{4,20},{20... | collective-permute-start | bytes 884744 | tf_op jit(solution)/shard_map/ppermute | solution.py:540
  213.5 5.7 %collective-permute-start.51 = (f32[8,768]{1,0:T(8,128)S(1)}, f32[8,768]{1,0:T(8,128)S(1)}, u32[]{:S(2)}, u32[]{:S(2)}) collective-permute-start(f32[8,768]{1,0:T(8,128)S(1)} %get-tuple-element.399.refs_5_), channel_id=1, source_target_pairs={{0,12},{1,13},{2,14},{3,15},{4,8},{5,9},{6,10},{7,11},{8,4},{9,5},... | collective-permute-start | bytes 73736 | tf_op jit(solution)/shard_map/ppermute | solution.py:536
  215.4 4.7 %collective-permute-start.50 = (f32[8,768]{1,0:T(8,128)S(1)}, f32[8,768]{1,0:T(8,128)S(1)}, u32[]{:S(2)}, u32[]{:S(2)}) collective-permute-start(f32[8,768]{1,0:T(8,128)S(1)} %get-tuple-element.399.refs_5_), channel_id=1, source_target_pairs={{0,8},{1,9},{2,10},{3,11},{4,12},{5,13},{6,14},{7,15},{8,0},{9,1},... | collective-permute-start | bytes 73736 | tf_op jit(solution)/shard_map/ppermute | solution.py:536
  217.1 3.8 %collective-permute-start.49 = (f32[8,768]{1,0:T(8,128)S(1)}, f32[8,768]{1,0:T(8,128)S(1)}, u32[]{:S(2)}, u32[]{:S(2)}) collective-permute-start(f32[8,768]{1,0:T(8,128)S(1)} %get-tuple-element.399.refs_5_), channel_id=1, source_target_pairs={{0,4},{1,5},{2,6},{3,7},{4,0},{5,1},{6,2},{7,3},{8,12},{9,13},{10,... | collective-permute-start | bytes 73736 | tf_op jit(solution)/shard_map/ppermute | solution.py:536
  222.3 6.5 %collective-permute-start.55 = (bf16[2,48,768]{2,1,0:T(8,128)(2,1)S(1)}, bf16[2,48,768]{2,1,0:T(8,128)(2,1)S(1)}, u32[]{:S(2)}, u32[]{:S(2)}) collective-permute-start(bf16[2,48,768]{2,1,0:T(8,128)(2,1)S(1)} %get-tuple-element.410.d_mine), channel_id=1, source_target_pairs={{0,16},{16,0},{1,17},{17,1},{2,18},{18,2},{3,19},{19,3},{4,20},{20... | collective-permute-start | bytes 442376 | tf_op jit(solution)/shard_map/ppermute | solution.py:540
  223.5 7.4 %collective-permute-start.52 = (bf16[2,48,768]{2,1,0:T(8,128)(2,1)S(1)}, bf16[2,48,768]{2,1,0:T(8,128)(2,1)S(1)}, u32[]{:S(2)}, u32[]{:S(2)}) collective-permute-start(bf16[2,48,768]{2,1,0:T(8,128)(2,1)S(1)} %get-tuple-element.406), channel_id=1, source_target_pairs={{0,4},{1,5},{2,6},{3,7},{4,0},{5,1},{6,2},{7,3},{8,12},{9,13},{10,... | collective-permute-start | bytes 442376 | tf_op jit(solution)/shard_map/ppermute | solution.py:536
  224.5 11.5 %collective-permute-start.53 = (bf16[2,48,768]{2,1,0:T(8,128)(2,1)S(1)}, bf16[2,48,768]{2,1,0:T(8,128)(2,1)S(1)}, u32[]{:S(2)}, u32[]{:S(2)}) collective-permute-start(bf16[2,48,768]{2,1,0:T(8,128)(2,1)S(1)} %get-tuple-element.407), channel_id=1, source_target_pairs={{0,8},{1,9},{2,10},{3,11},{4,12},{5,13},{6,14},{7,15},{8,0},{9,1},... | collective-permute-start | bytes 442376 | tf_op jit(solution)/shard_map/ppermute | solution.py:536
  226.5 9.5 %collective-permute-start.54 = (bf16[2,48,768]{2,1,0:T(8,128)(2,1)S(1)}, bf16[2,48,768]{2,1,0:T(8,128)(2,1)S(1)}, u32[]{:S(2)}, u32[]{:S(2)}) collective-permute-start(bf16[2,48,768]{2,1,0:T(8,128)(2,1)S(1)} %get-tuple-element.408), channel_id=1, source_target_pairs={{0,12},{1,13},{2,14},{3,15},{4,8},{5,9},{6,10},{7,11},{8,4},{9,5},... | collective-permute-start | bytes 442376 | tf_op jit(solution)/shard_map/ppermute | solution.py:536
  227.9 8.1 %collective-permute-start.56 = (f32[8,768]{1,0:T(8,128)S(1)}, f32[8,768]{1,0:T(8,128)S(1)}, u32[]{:S(2)}, u32[]{:S(2)}) collective-permute-start(f32[8,768]{1,0:T(8,128)S(1)} %get-tuple-element.417.refs_4_), channel_id=1, source_target_pairs={{0,16},{16,0},{1,17},{17,1},{2,18},{18,2},{3,19},{19,3},{4,20},{20... | collective-permute-start | bytes 73736 | tf_op jit(solution)/shard_map/ppermute | solution.py:540
  236.1 5.4 %collective-permute-start.57 = (bf16[2,48,768]{2,1,0:T(8,128)(2,1)S(1)}, bf16[2,48,768]{2,1,0:T(8,128)(2,1)S(1)}, u32[]{:S(2)}, u32[]{:S(2)}) collective-permute-start(bf16[2,48,768]{2,1,0:T(8,128)(2,1)S(1)} %get-tuple-element.418.mine), channel_id=1, source_target_pairs={{0,16},{16,0},{1,17},{17,1},{2,18},{18,2},{3,19},{19,3},{4,20},{20... | collective-permute-start | bytes 442376 | tf_op jit(solution)/shard_map/ppermute | solution.py:540
  237.5 3.3 %collective-permute-start.60 = (f32[8,768]{1,0:T(8,128)S(1)}, f32[8,768]{1,0:T(8,128)S(1)}, u32[]{:S(2)}, u32[]{:S(2)}) collective-permute-start(f32[8,768]{1,0:T(8,128)S(1)} %get-tuple-element.419.v0), channel_id=1, source_target_pairs={{0,3},{1,2},{2,1},{3,0},{4,7},{5,6},{6,5},{7,4},{8,11},{9,10},{10,... | collective-permute-start | bytes 73736 | tf_op jit(solution)/shard_map/ppermute | solution.py:536
  237.5 4.0 %collective-permute-start.59 = (f32[8,768]{1,0:T(8,128)S(1)}, f32[8,768]{1,0:T(8,128)S(1)}, u32[]{:S(2)}, u32[]{:S(2)}) collective-permute-start(f32[8,768]{1,0:T(8,128)S(1)} %get-tuple-element.419.v0), channel_id=1, source_target_pairs={{0,2},{1,3},{2,0},{3,1},{4,6},{5,7},{6,4},{7,5},{8,10},{9,11},{10,... | collective-permute-start | bytes 73736 | tf_op jit(solution)/shard_map/ppermute | solution.py:536
  238.3 3.2 %collective-permute-start.58 = (f32[8,768]{1,0:T(8,128)S(1)}, f32[8,768]{1,0:T(8,128)S(1)}, u32[]{:S(2)}, u32[]{:S(2)}) collective-permute-start(f32[8,768]{1,0:T(8,128)S(1)} %get-tuple-element.419.v0), channel_id=1, source_target_pairs={{0,1},{1,0},{2,3},{3,2},{4,5},{5,4},{6,7},{7,6},{8,9},{9,8},{10,11... | collective-permute-start | bytes 73736 | tf_op jit(solution)/shard_map/ppermute | solution.py:536
  (21 other events, 130.0 us)

commit v9 on v8

--- a/solution.py
+++ b/solution.py
@@ -506,13 +506,13 @@
     tiles, tokens, width = act.shape
 
     def step(i):
-        r = rows_of(i, 256)
+        r = rows_of(i, 512)
         total = x[r, :].astype(F32) + vec[3:4, :] + dot_nn(o[r, :], wo[0])
         for t in range(tiles):
             total += dot_nn(act[t, r, :], wd[tile_of(t, width), :])
         out[r, :] = total.astype(BF16)
 
-    loop(tokens // 256, step, lambda i: send_rows(out, out_ref, i, 256, sem))
+    loop(tokens // 512, step, lambda i: send_rows(out, out_ref, i, 512, sem))
     whole_wait(out_ref, sem)()
 
 

time: 245 us -> 244 us (level)
  transfers between devices with their start and end apart: 61 -> 61, of which waited for: 19 -> 20; matrix products, arithmetic and copies ran while one was open for 2% -> 2% of each run, Pallas kernels for 38% -> 38%
where the time goes in v9:
time: 244 us
  Pallas kernels  108 us (44%)
  starting transfers between devices  67.4 us (28%)
  waiting for transfers between devices  56.2 us (23%)
  local copies, waits for them, and re-layouts  7.4 us (3%)
  other arithmetic  3.07 us (1%)
    pallas_call x11, Pallas kernels, call(): pl.pallas_call(kernel, name=name, out_shape=list(outs) + list(g_shapes),...  91.2 us
    ppermute x45, waiting for transfers between devices, swap(): return lax.ppermute(value, 'wide', [(i, i ^ mask) for i in range(16)])  50.4 us
    ppermute x45, starting transfers between devices, swap(): return lax.ppermute(value, 'wide', [(i, i ^ mask) for i in range(16)])  50.4 us
    ppermute x16, starting transfers between devices, swap_y(): return lax.ppermute(value, 'narrow', [(0, 1), (1, 0)])  17 us
    pallas_call x10, Pallas kernels, mix(): pl.pallas_call(kernel, name=name, out_shape=outs, in_specs=[VMEM] * len(n...  12.4 us
    ppermute x16, waiting for transfers between devices, swap_y(): return lax.ppermute(value, 'narrow', [(0, 1), (1, 0)])  5.87 us
  transfers between devices with their start and end apart: 61, of which 20 were waited for; matrix products, arithmetic and copies ran while one was open for 2% of the time, Pallas kernels for 38%

profile of v9, /device:TPU:0, one launch (start us, length us, event | category | flops | bytes accessed | tf_op | source)
XLA Modules:
  0.0 243.5 jit_solution(16309067874238920589)
XLA Ops:
  1.4 1.3 select_bitcast_fusion.3
  2.7 5.1 %collective-permute-start.2 = (bf16[104,768]{1,0:T(8,128)(2,1)S(1)}, bf16[104,768]{1,0:T(8,128)(2,1)S(1)}, u32[]{:S(2)}, u32[]{:S(2)}) collective-permute-start(bf16[104,768]{1,0:T(8,128)(2,1)S(1)} %pad_maximum_fusion.5), channel_id=1, source_target_pairs={{0,12},{1,13},{2,14},{3,15},{4,8},{5,9},{6,10},{7,11},{8,4},{9,5},... | collective-permute-start | bytes 479240 | tf_op jit(solution)/shard_map/ppermute | solution.py:536
  9.3 3.6 %collective-permute-done.2 = bf16[104,768]{1,0:T(8,128)(2,1)S(1)} collective-permute-done((bf16[104,768]{1,0:T(8,128)(2,1)S(1)}, bf16[104,768]{1,0:T(8,128)(2,1)S(1)}, u32[]{:S(2)}, u32[]{:S(2)}) %collective-permute-start.2) | collective-permute-done | bytes 159776 | tf_op jit(solution)/shard_map/ppermute | solution.py:536
  12.9 8.5 %collective-permute-done.1 = bf16[104,768]{1,0:T(8,128)(2,1)S(1)} collective-permute-done((bf16[104,768]{1,0:T(8,128)(2,1)S(1)}, bf16[104,768]{1,0:T(8,128)(2,1)S(1)}, u32[]{:S(2)}, u32[]{:S(2)}) %collective-permute-start.1) | collective-permute-done | bytes 159776 | tf_op jit(solution)/shard_map/ppermute | solution.py:536
  21.5 1.6 collective-permute-start.5
  23.1 1.5 collective-permute-start.3
  25.8 13.6 %collective-permute-done.7 = bf16[2,2,48,768]{3,2,1,0:T(8,128)(2,1)} collective-permute-done((bf16[2,2,48,768]{3,2,1,0:T(8,128)(2,1)}, bf16[2,2,48,768]{3,2,1,0:T(8,128)(2,1)}, u32[]{:S(2)}, u32[]{:S(2)}) %collective-permute-start.7) | collective-permute-done | bytes 294944 | tf_op jit(solution)/shard_map/ppermute | solution.py:536
  39.5 1.3 join_a.1
  41.5 2.1 collective-permute-start.12
  44.1 1.3 fusion.11
  45.4 1.4 stack.70.refs_0_.scal
  46.8 1.2 fusion.7
  48.0 2.7 %collective-permute-done.9.refs_10_.refs_7_ = bf16[4,48,768]{2,1,0:T(8,128)(2,1)} collective-permute-done((bf16[4,48,768]{2,1,0:T(8,128)(2,1)}, bf16[4,48,768]{2,1,0:T(8,128)(2,1)}, u32[]{:S(2)}, u32[]{:S(2)}) %collective-permute-start.9) | collective-permute-done | bytes 294944 | tf_op jit(solution)/shard_map/ppermute | solution.py:536
  50.7 2.8 %collective-permute-done.12 = bf16[2,2,48,768]{3,2,1,0:T(8,128)(2,1)S(1)} collective-permute-done((bf16[2,2,48,768]{3,2,1,0:T(8,128)(2,1)}, bf16[2,2,48,768]{3,2,1,0:T(8,128)(2,1)S(1)}, u32[]{:S(2)}, u32[]{:S(2)}) %collective-permute-start.12) | collective-permute-done | bytes 294944 | tf_op jit(solution)/shard_map/ppermute | solution.py:536
  53.4 5.6 %collective-permute-done.11 = bf16[2,2,48,768]{3,2,1,0:T(8,128)(2,1)} collective-permute-done((bf16[2,2,48,768]{3,2,1,0:T(8,128)(2,1)}, bf16[2,2,48,768]{3,2,1,0:T(8,128)(2,1)}, u32[]{:S(2)}, u32[]{:S(2)}) %collective-permute-start.11) | collective-permute-done | bytes 294944 | tf_op jit(solution)/shard_map/ppermute | solution.py:536
  60.7 1.0 collective-permute-start.15
  62.4 1.6 collective-permute-start.21
  64.0 1.1 collective-permute-start.22
  65.0 9.5 %project.1 = (bf16[1024,768]{1,0:T(8,128)(2,1)S(1)}, bf16[1024,768]{1,0:T(8,128)(2,1)S(1)}, bf16[1024,768]{1,0:T(8,128)(2,1)S(1)}, bf16[1024,768]{1,0:T(8,128)(2...) custom-call(s32[10]{0:T(128)S(1)} %stack.70.refs_0_.scal, ...), custom_call_target="tpu_custom_call" | custom-call | flops 4831838208 | bytes 1048576 | tf_op jit(solution)/shard_map/project/pallas_call | solution.py:139
  74.6 10.6 %core.2 = (bf16[1024,768]{1,0:T(8,128)(2,1)S(1)}, bf16[3,1024,768]{2,1,0:T(8,128)(2,1)S(1)}, f32[1024,768]{1,0:T(8,128)S(1)}) custom-call(s32[10]{0:T(128)S(1)} %stack.70.refs_0_.scal, bf16[1024,768]{1,0:T(8,128)(2,1)S(1)} %get-tuple-element.243.q, bf16[1024,768]{1,0:T(8,128)(2,1)S(1)} %get-tuple-element.244.k, bf16[1024,768]{1,0:T(8,128)(2,1)S(1)} %get-tuple-element.245.v, ...), custom_call_target="tpu_custom_call" | custom-call | flops 10737418240 | bytes 1048576 | tf_op jit(solution)/shard_map/core/pallas_call | solution.py:139
  87.1 10.6 %core.3 = (bf16[1024,768]{1,0:T(8,128)(2,1)S(1)}, bf16[3,1024,768]{2,1,0:T(8,128)(2,1)S(1)}, f32[1024,768]{1,0:T(8,128)S(1)}) custom-call(s32[10]{0:T(128)S(1)} %stack.70.refs_0_.scal, bf16[1024,768]{1,0:T(8,128)(2,1)S(1)} %get-tuple-element.243.q, ...), custom_call_target="tpu_custom_call", output_to_operand_aliasing={{0}: (6, {}), {1}: (7, {}), {2}: (8, {})} | custom-call | flops 10737418240 | bytes 1048576 | tf_op jit(solution)/shard_map/core/pallas_call | solution.py:139
  97.8 4.4 %collective-permute-done.18.refs_2_.refs_6_.refs_3_ = bf16[4,2,48,768]{3,2,1,0:T(8,128)(2,1)S(1)} collective-permute-done((bf16[4,2,48,768]{3,2,1,0:T(8,128)(2,1)S(1)}, bf16[4,2,48,768]{3,2,1,0:T(8,128)(2,1)S(1)}, u32[]{:S(2)}, u32[]{:S(2)}) %collective-permute-start.18) | collective-permute-done | bytes 589856 | tf_op jit(solution)/shard_map/ppermute | solution.py:540
  103.2 7.8 %attn_grad.1 = (f32[8,768]{1,0:T(8,128)S(1)}, bf16[2,8,48,768]{3,2,1,0:T(8,128)(2,1)}, bf16[2,8,48,768]{3,2,1,0:T(8,128)(2,1)}, bf16[2,8,48,768]{3,2,1,0:T(8,128)(2,1)}, bf16[2,8,48,768]{3,2,1,0:T(8,128)(2,1)}) custom-call(s32[10]{0:T(128)S(1)} %stack.70.refs_0_.scal, bf16[1024,768]{1,0:T(8,128)(2,1)S(1)} %get-tuple-element.281.xn.refs_1_, ...), custom_call_target="tpu_custom_call" | custom-call | flops 4831838208 | bytes 1048576 | tf_op jit(solution)/shard_map/attn_grad/pallas_call | solution.py:139
  111.6 1.1 copy-done.13
  112.8 7.7 %up.2 = (bf16[4,1024,768]{2,1,0:T(8,128)(2,1)S(1)}, bf16[4,1024,768]{2,1,0:T(8,128)(2,1)S(1)}, bf16[4,768,768]{2,1,0:T(8,128)(2,1)S(1)}) custom-call(s32[10]{0:T(128)S(1)} %stack.70.refs_0_.scal, bf16[1024,768]{1,0:T(8,128)(2,1)S(1)} %get-tuple-element.281.xn.refs_1_, f32[4,768]{1,0:T(4,128)S(1)} %get-tuple-element.282.refs_2_, ...), custom_call_target="tpu_custom_call" | custom-call | flops 2415919104 | bytes 1048576 | tf_op jit(solution)/shard_map/up/pallas_call | solution.py:139
  120.5 1.6 sums_1.1
  122.6 1.0 collective-permute-start.27
  123.7 6.0 %up.3 = (bf16[4,1024,768]{2,1,0:T(8,128)(2,1)S(1)}, bf16[4,1024,768]{2,1,0:T(8,128)(2,1)S(1)}) custom-call(s32[10]{0:T(128)S(1)} %stack.70.refs_0_.scal, bf16[1024,768]{1,0:T(8,128)(2,1)S(1)} %get-tuple-element.281.xn.refs_1_, f32[4,768]{1,0:T(4,128)S(1)} %get-tuple-element.282.refs_2_, ...), custom_call_target="tpu_custom_call", output_to_operand_aliasing={{0}: (3, {}), {1}: (4, {})} | custom-call | flops 2415919104 | bytes 1048576 | tf_op jit(solution)/shard_map/up/pallas_call | solution.py:139
  129.7 7.7 %down_grad.1 = (bf16[3072,768]{1,0:T(8,128)(2,1)S(1)}, bf16[2,8,48,768]{3,2,1,0:T(8,128)(2,1)}, bf16[2,8,48,768]{3,2,1,0:T(8,128)(2,1)}, bf16[2,8,48,768]{3,2,1,0:T(8,128)(2,1)}, bf16[2,8,48,768]{3,2,1,0:T(8,128)(2,1)}) custom-call(s32[10]{0:T(128)S(1)} %stack.70.refs_0_.scal, bf16[4,1024,768]{2,1,0:T(8,128)(2,1)S(1)} %get-tuple-element.308.act, ...), custom_call_target="tpu_custom_call" | custom-call | flops 4831838208 | bytes 1048576 | tf_op jit(solution)/shard_map/down_grad/pallas_call | solution.py:139
  138.1 1.4 sums_2.1
  140.1 1.0 collective-permute-start.28
  141.2 1.5 collective-permute-start.29
  142.7 7.1 %dpre.1 = (bf16[4,1024,768]{2,1,0:T(8,128)(2,1)S(1)}, f32[8,768]{1,0:T(8,128)S(1)}) custom-call(s32[10]{0:T(128)S(1)} %stack.70.refs_0_.scal, bf16[1024,768]{1,0:T(8,128)(2,1)S(1)} %bitcast.35, bf16[4,1024,768]{2,1,0:T(8,128)(2,1)S(1)} %get-tuple-element.318.gp, bf16[3072,768]{1,0:T(8,128)(2,1)S(1)} %get-tuple-element.319.w.wd), custom_call_target="tpu_custom_call", output_to_operand_aliasing={{0}: (2, {})} | custom-call | flops 4831838208 | bytes 1048576 | tf_op jit(solution)/shard_map/dpre/pallas_call | solution.py:139
  150.1 1.7 sums_3.1
  151.8 1.6 collective-permute-start.35
  154.4 9.3 %collective-permute-start.32 = (bf16[2,48,768]{2,1,0:T(8,128)(2,1)S(1)}, bf16[2,48,768]{2,1,0:T(8,128)(2,1)S(1)}, u32[]{:S(2)}, u32[]{:S(2)}) collective-permute-start(bf16[2,48,768]{2,1,0:T(8,128)(2,1)S(1)} %get-tuple-element.336), channel_id=1, source_target_pairs={{0,4},{1,5},{2,6},{3,7},{4,0},{5,1},{6,2},{7,3},{8,12},{9,13},{10,... | collective-permute-start | bytes 442376 | tf_op jit(solution)/shard_map/ppermute | solution.py:536
  163.7 2.4 collective-permute-start.34
  166.1 7.9 %up_grad.1 = (bf16[1,768,768]{2,1,0:T(8,128)(2,1)S(1)}, bf16[2,8,48,768]{3,2,1,0:T(8,128)(2,1)}, bf16[2,8,48,768]{3,2,1,0:T(8,128)(2,1)}, bf16[2,8,48,768]{3,2,1,0:T(8,128)(2,1)}, bf16[2,8,48,768]{3,2,1,0:T(8,128)(2,1)}) custom-call(s32[10]{0:T(128)S(1)} %stack.70.refs_0_.scal, bf16[1024,768]{1,0:T(8,128)(2,1)S(1)} %get-tuple-element.281.xn.refs_1_, ...), custom_call_target="tpu_custom_call" | custom-call | flops 4831838208 | bytes 1048576 | tf_op jit(solution)/shard_map/up_grad/pallas_call | solution.py:139
  174.0 1.3 collective-permute-done.33.refs_2_
  175.3 1.4 sums_4.1
  177.3 1.2 collective-permute-start.41
  178.5 1.1 collective-permute-start.37
  180.6 8.4 %input_grad.1 = (f32[8,768]{1,0:T(8,128)S(1)}, bf16[2,512,768]{2,1,0:T(8,128)(2,1)}) custom-call(s32[10]{0:T(128)S(1)} %stack.70.refs_0_.scal, bf16[1024,768]{1,0:T(8,128)(2,1)S(1)} %bitcast.38, bf16[1024,768]{1,0:T(8,128)(2,1)S(1)} %bitcast.36, f32[1024,768]{1,0:T(8,128)S(1)} %get-tuple-element.362.dn, bf16[4,1024,768]{2,1,0:T(8,128)(2,1)S(1)} %get-tuple-element.341.dpre, ...), custom_call_target="tpu_custom_call" | custom-call | flops 8455716864 | bytes 1048576 | tf_op jit(solution)/shard_map/input_grad/pallas_call | solution.py:139
  189.7 1.9 sums_5.1
  191.5 1.3 collective-permute-start.42
  192.8 1.1 collective-permute-start.43
  193.9 3.6 %collective-permute-start.44 = (bf16[2,48,768]{2,1,0:T(8,128)(2,1)S(1)}, bf16[2,48,768]{2,1,0:T(8,128)(2,1)S(1)}, u32[]{:S(2)}, u32[]{:S(2)}) collective-permute-start(bf16[2,48,768]{2,1,0:T(8,128)(2,1)S(1)} %get-tuple-element.382), channel_id=1, source_target_pairs={{0,4},{1,5},{2,6},{3,7},{4,0},{5,1},{6,2},{7,3},{8,12},{9,13},{10,... | collective-permute-start | bytes 442376 | tf_op jit(solution)/shard_map/ppermute | solution.py:536
  197.5 2.4 collective-permute-start.46
  199.9 7.9 %out.1 = bf16[2,512,768]{2,1,0:T(8,128)(2,1)} custom-call(s32[10]{0:T(128)S(1)} %stack.70.refs_0_.scal, bf16[1024,768]{1,0:T(8,128)(2,1)S(1)} %bitcast.39, bf16[1024,768]{1,0:T(8,128)(2,1)S(1)} %get-tuple-element.269.o, bf16[4,1024,768]{2,1,0:T(8,128)(2,1)S(1)} %get-tuple-element.308.act, f32[8,768]{1,0:T(8,128)S(1)} %get-tuple-element.363.vec, ...), custom_call_target="tpu_custom_call" | custom-call | flops 6039797760 | bytes 1048576 | tf_op jit(solution)/shard_map/out/pallas_call | solution.py:139
  207.8 2.1 collective-permute-done.45.refs_5_
  209.9 1.4 sums_6.1
  211.3 1.0 collective-permute-start.47
  213.3 1.6 collective-permute-start.51
  215.0 2.3 collective-permute-start.50
  217.7 1.2 collective-permute-done.51.refs_8_
  219.7 1.4 collective-permute-done.49.refs_6_
  221.1 1.4 sums_7.1
  222.5 1.2 collective-permute-start.55
  225.6 2.5 %collective-permute-start.54 = (bf16[2,48,768]{2,1,0:T(8,128)(2,1)S(1)}, bf16[2,48,768]{2,1,0:T(8,128)(2,1)S(1)}, u32[]{:S(2)}, u32[]{:S(2)}) collective-permute-start(bf16[2,48,768]{2,1,0:T(8,128)(2,1)S(1)} %get-tuple-element.408), channel_id=1, source_target_pairs={{0,12},{1,13},{2,14},{3,15},{4,8},{5,9},{6,10},{7,11},{8,4},{9,5},... | collective-permute-start | bytes 442376 | tf_op jit(solution)/shard_map/ppermute | solution.py:536
  229.0 2.2 place.1
  231.6 4.0 %collective-permute-done.53.refs_2_ = bf16[2,48,768]{2,1,0:T(8,128)(2,1)S(1)} collective-permute-done((bf16[2,48,768]{2,1,0:T(8,128)(2,1)S(1)}, bf16[2,48,768]{2,1,0:T(8,128)(2,1)S(1)}, u32[]{:S(2)}, u32[]{:S(2)}) %collective-permute-start.53) | collective-permute-done | bytes 147488 | tf_op jit(solution)/shard_map/ppermute | solution.py:536
  235.7 1.6 collective-permute-start.57
  239.1 1.4 collective-permute-done.60.v3
  241.3 2.0 place_last.1
  (150 shorter events, 23.9 us)
Async XLA Ops:
  2.7 10.2 %collective-permute-start.2 = (bf16[104,768]{1,0:T(8,128)(2,1)S(1)}, bf16[104,768]{1,0:T(8,128)(2,1)S(1)}, u32[]{:S(2)}, u32[]{:S(2)}) collective-permute-start(bf16[104,768]{1,0:T(8,128)(2,1)S(1)} %pad_maximum_fusion.5), channel_id=1, source_target_pairs={{0,12},{1,13},{2,14},{3,15},{4,8},{5,9},{6,10},{7,11},{8,4},{9,5},... | collective-permute-start | bytes 479240 | tf_op jit(solution)/shard_map/ppermute | solution.py:536
  7.9 13.5 %collective-permute-start.1 = (bf16[104,768]{1,0:T(8,128)(2,1)S(1)}, bf16[104,768]{1,0:T(8,128)(2,1)S(1)}, u32[]{:S(2)}, u32[]{:S(2)}) collective-permute-start(bf16[104,768]{1,0:T(8,128)(2,1)S(1)} %pad_maximum_fusion.5), channel_id=1, source_target_pairs={{0,8},{1,9},{2,10},{3,11},{4,12},{5,13},{6,14},{7,15},{8,0},{9,1},... | collective-permute-start | bytes 479240 | tf_op jit(solution)/shard_map/ppermute | solution.py:536
  7.9 13.5 %collective-permute-start = (bf16[104,768]{1,0:T(8,128)(2,1)S(1)}, bf16[104,768]{1,0:T(8,128)(2,1)S(1)}, u32[]{:S(2)}, u32[]{:S(2)}) collective-permute-start(bf16[104,768]{1,0:T(8,128)(2,1)S(1)} %pad_maximum_fusion.5), channel_id=1, source_target_pairs={{0,4},{1,5},{2,6},{3,7},{4,0},{5,1},{6,2},{7,3},{8,12},{9,13},{10,... | collective-permute-start | bytes 479240 | tf_op jit(solution)/shard_map/ppermute | solution.py:536
  21.5 19.3 %copy-start.6 = (bf16[4,56,768]{2,1,0:T(8,128)(2,1)}, bf16[4,56,768]{2,1,0:T(8,128)(2,1)S(1)}, u32[]{:S(2)}) copy-start(bf16[4,56,768]{2,1,0:T(8,128)(2,1)S(1)} %pad_maximum_fusion.2.refs_0_.refs_3_) | copy-start | bytes 1032196
  21.5 18.0 %collective-permute-start.5 = (bf16[4,56,768]{2,1,0:T(8,128)(2,1)S(1)}, bf16[4,56,768]{2,1,0:T(8,128)(2,1)S(1)}, u32[]{:S(2)}, u32[]{:S(2)}) collective-permute-start(bf16[4,56,768]{2,1,0:T(8,128)(2,1)S(1)} %pad_maximum_fusion.2.refs_0_.refs_3_), channel_id=1, source_target_pairs={{0,16},{16,0},{1,17},{17,1},{2,18},{18,2},{3,19},{19,3},{4,20},{20... | collective-permute-start | bytes 1032200 | tf_op jit(solution)/shard_map/ppermute | solution.py:540
  23.1 16.4 %collective-permute-start.3 = (bf16[4,56,768]{2,1,0:T(8,128)(2,1)S(1)}, bf16[4,56,768]{2,1,0:T(8,128)(2,1)S(1)}, u32[]{:S(2)}, u32[]{:S(2)}) collective-permute-start(bf16[4,56,768]{2,1,0:T(8,128)(2,1)S(1)} %pad_maximum_fusion.2.refs_0_.refs_3_), channel_id=1, source_target_pairs={{0,2},{1,3},{2,0},{3,1},{4,6},{5,7},{6,4},{7,5},{8,10},{9,11},{10,... | collective-permute-start | bytes 1032200 | tf_op jit(solution)/shard_map/ppermute | solution.py:536
  24.7 14.8 %collective-permute-start.7 = (bf16[2,2,48,768]{3,2,1,0:T(8,128)(2,1)}, bf16[2,2,48,768]{3,2,1,0:T(8,128)(2,1)}, u32[]{:S(2)}, u32[]{:S(2)}) collective-permute-start(bf16[2,2,48,768]{3,2,1,0:T(8,128)(2,1)} %bitcast.20), channel_id=1, source_target_pairs={{0,8},{1,9},{2,10},{3,11},{4,12},{5,13},{6,14},{7,15},{8,0},{9,1},... | collective-permute-start | bytes 884744 | tf_op jit(solution)/shard_map/ppermute | solution.py:536
  24.8 14.7 %collective-permute-start.6 = (bf16[4,48,768]{2,1,0:T(8,128)(2,1)S(1)}, bf16[4,48,768]{2,1,0:T(8,128)(2,1)S(1)}, u32[]{:S(2)}, u32[]{:S(2)}) collective-permute-start(bf16[4,48,768]{2,1,0:T(8,128)(2,1)S(1)} %pad_maximum_fusion.3.refs_3_.refs_7_.refs_4_), channel_id=1, source_target_pairs={{0,2},{1,3},{2,0},{3,1},{4,6},{5,7},{6,4},{7,5},{8,10},{9,11},{10,... | collective-permute-start | bytes 884744 | tf_op jit(solution)/shard_map/ppermute | solution.py:536
  25.4 14.1 %collective-permute-start.4 = (bf16[4,48,768]{2,1,0:T(8,128)(2,1)S(1)}, bf16[4,48,768]{2,1,0:T(8,128)(2,1)}, u32[]{:S(2)}, u32[]{:S(2)}) collective-permute-start(bf16[4,48,768]{2,1,0:T(8,128)(2,1)S(1)} %pad_maximum_fusion.3.refs_3_.refs_7_.refs_4_), channel_id=1, source_target_pairs={{0,16},{16,0},{1,17},{17,1},{2,18},{18,2},{3,19},{19,3},{4,20},{20... | collective-permute-start | bytes 884744 | tf_op jit(solution)/shard_map/ppermute | solution.py:540
  40.9 18.2 %collective-permute-start.10 = (bf16[24,56,768]{2,1,0:T(8,128)(2,1)S(1)}, bf16[24,56,768]{2,1,0:T(8,128)(2,1)}, u32[]{:S(2)}, u32[]{:S(2)}) collective-permute-start(bf16[24,56,768]{2,1,0:T(8,128)(2,1)S(1)} %join_a.1), channel_id=1, source_target_pairs={{0,1},{1,0},{2,3},{3,2},{4,5},{5,4},{6,7},{7,6},{8,9},{9,8},{10,11... | collective-permute-start | bytes 6193160 | tf_op jit(solution)/shard_map/ppermute | solution.py:536
  40.9 9.7 %collective-permute-start.9 = (bf16[4,48,768]{2,1,0:T(8,128)(2,1)}, bf16[4,48,768]{2,1,0:T(8,128)(2,1)}, u32[]{:S(2)}, u32[]{:S(2)}) collective-permute-start(bf16[4,48,768]{2,1,0:T(8,128)(2,1)} %collective-permute-done.4.refs_5_.refs_9_.refs_6_), channel_id=1, source_target_pairs={{0,2},{1,3},{2,0},{3,1},{4,6},{5,7},{6,4},{7,5},{8,10},{9,11},{10,... | collective-permute-start | bytes 884744 | tf_op jit(solution)/shard_map/ppermute | solution.py:536
  41.5 11.9 %collective-permute-start.12 = (bf16[2,2,48,768]{3,2,1,0:T(8,128)(2,1)}, bf16[2,2,48,768]{3,2,1,0:T(8,128)(2,1)S(1)}, u32[]{:S(2)}, u32[]{:S(2)}) collective-permute-start(bf16[2,2,48,768]{3,2,1,0:T(8,128)(2,1)} %bitcast.20), channel_id=1, source_target_pairs={{0,12},{1,13},{2,14},{3,15},{4,8},{5,9},{6,10},{7,11},{8,4},{9,5},... | collective-permute-start | bytes 884744 | tf_op jit(solution)/shard_map/ppermute | solution.py:536
  43.6 15.4 %collective-permute-start.11 = (bf16[2,2,48,768]{3,2,1,0:T(8,128)(2,1)}, bf16[2,2,48,768]{3,2,1,0:T(8,128)(2,1)}, u32[]{:S(2)}, u32[]{:S(2)}) collective-permute-start(bf16[2,2,48,768]{3,2,1,0:T(8,128)(2,1)} %bitcast.20), channel_id=1, source_target_pairs={{0,4},{1,5},{2,6},{3,7},{4,0},{5,1},{6,2},{7,3},{8,12},{9,13},{10,... | collective-permute-start | bytes 884744 | tf_op jit(solution)/shard_map/ppermute | solution.py:536
  43.6 15.4 %collective-permute-start.8 = (bf16[4,56,768]{2,1,0:T(8,128)(2,1)S(1)}, bf16[4,56,768]{2,1,0:T(8,128)(2,1)}, u32[]{:S(2)}, u32[]{:S(2)}) collective-permute-start(bf16[4,56,768]{2,1,0:T(8,128)(2,1)S(1)} %collective-permute-done.3.refs_1_.refs_4_), channel_id=1, source_target_pairs={{0,16},{16,0},{1,17},{17,1},{2,18},{18,2},{3,19},{19,3},{4,20},{20... | collective-permute-start | bytes 1032200 | tf_op jit(solution)/shard_map/ppermute | solution.py:540
  48.0 17.1 %copy-start.11 = (bf16[2,512,768]{2,1,0:T(8,128)(2,1)S(1)}, bf16[2,512,768]{2,1,0:T(8,128)(2,1)}, u32[]{:S(2)}) copy-start(bf16[2,512,768]{2,1,0:T(8,128)(2,1)} %param.12) | copy-start | bytes 4718596
  59.0 3.3 %collective-permute-start.14 = (bf16[4,48,768]{2,1,0:T(8,128)(2,1)}, bf16[4,48,768]{2,1,0:T(8,128)(2,1)S(1)}, u32[]{:S(2)}, u32[]{:S(2)}) collective-permute-start(bf16[4,48,768]{2,1,0:T(8,128)(2,1)} %collective-permute-done.9.refs_10_.refs_7_), channel_id=1, source_target_pairs={{0,1},{1,0},{2,3},{3,2},{4,5},{5,4},{6,7},{7,6},{8,9},{9,8},{10,11... | collective-permute-start | bytes 884744 | tf_op jit(solution)/shard_map/ppermute | solution.py:536
  59.0 3.3 %collective-permute-start.13 = (bf16[4,56,768]{2,1,0:T(8,128)(2,1)}, bf16[4,56,768]{2,1,0:T(8,128)(2,1)S(1)}, u32[]{:S(2)}, u32[]{:S(2)}) collective-permute-start(bf16[4,56,768]{2,1,0:T(8,128)(2,1)} %collective-permute-done.8.refs_6_.refs_3_), channel_id=1, source_target_pairs={{0,1},{1,0},{2,3},{3,2},{4,5},{5,4},{6,7},{7,6},{8,9},{9,8},{10,11... | collective-permute-start | bytes 1032200 | tf_op jit(solution)/shard_map/ppermute | solution.py:536
  60.7 24.6 %collective-permute-start.15 = (bf16[4,2,48,768]{3,2,1,0:T(8,128)(2,1)S(1)}, bf16[4,2,48,768]{3,2,1,0:T(8,128)(2,1)S(1)}, u32[]{:S(2)}, u32[]{:S(2)}) collective-permute-start(bf16[4,2,48,768]{3,2,1,0:T(8,128)(2,1)S(1)} %pad_maximum_fusion.refs_3_.refs_0_), channel_id=1, source_target_pairs={{0,2},{1,3},{2,0},{3,1},{4,6},{5,7},{6,4},{7,5},{8,10},{9,11},{10,... | collective-permute-start | bytes 1769480 | tf_op jit(solution)/shard_map/ppermute | solution.py:536
  61.8 23.5 %copy-start.15 = (bf16[4,2,48,768]{3,2,1,0:T(8,128)(2,1)}, bf16[4,2,48,768]{3,2,1,0:T(8,128)(2,1)S(1)}, u32[]{:S(2)}) copy-start(bf16[4,2,48,768]{3,2,1,0:T(8,128)(2,1)S(1)} %pad_maximum_fusion.1.refs_7_.refs_4_) | copy-start | bytes 1769476
  61.8 23.5 %collective-permute-start.16 = (bf16[4,2,48,768]{3,2,1,0:T(8,128)(2,1)S(1)}, bf16[4,2,48,768]{3,2,1,0:T(8,128)(2,1)S(1)}, u32[]{:S(2)}, u32[]{:S(2)}) collective-permute-start(bf16[4,2,48,768]{3,2,1,0:T(8,128)(2,1)S(1)} %pad_maximum_fusion.1.refs_7_.refs_4_), channel_id=1, source_target_pairs={{0,16},{16,0},{1,17},{17,1},{2,18},{18,2},{3,19},{19,3},{4,20},{20... | collective-permute-start | bytes 1769480 | tf_op jit(solution)/shard_map/ppermute | solution.py:540
  62.4 35.4 %collective-permute-start.21 = (bf16[4,2,48,768]{3,2,1,0:T(8,128)(2,1)S(1)}, bf16[4,2,48,768]{3,2,1,0:T(8,128)(2,1)S(1)}, u32[]{:S(2)}, u32[]{:S(2)}) collective-permute-start(bf16[4,2,48,768]{3,2,1,0:T(8,128)(2,1)S(1)} %pad_maximum_fusion.refs_3_.refs_0_), channel_id=1, source_target_pairs={{0,16},{16,0},{1,17},{17,1},{2,18},{18,2},{3,19},{19,3},{4,20},{20... | collective-permute-start | bytes 1769480 | tf_op jit(solution)/shard_map/ppermute | solution.py:540
  64.0 21.3 %collective-permute-start.17 = (bf16[4,2,48,768]{3,2,1,0:T(8,128)(2,1)S(1)}, bf16[4,2,48,768]{3,2,1,0:T(8,128)(2,1)S(1)}, u32[]{:S(2)}, u32[]{:S(2)}) collective-permute-start(bf16[4,2,48,768]{3,2,1,0:T(8,128)(2,1)S(1)} %pad_maximum_fusion.refs_3_.refs_0_), channel_id=1, source_target_pairs={{0,1},{1,0},{2,3},{3,2},{4,5},{5,4},{6,7},{7,6},{8,9},{9,8},{10,11... | collective-permute-start | bytes 1769480 | tf_op jit(solution)/shard_map/ppermute | solution.py:536
  64.0 33.8 %collective-permute-start.22 = (bf16[4,2,48,768]{3,2,1,0:T(8,128)(2,1)S(1)}, bf16[4,2,48,768]{3,2,1,0:T(8,128)(2,1)S(1)}, u32[]{:S(2)}, u32[]{:S(2)}) collective-permute-start(bf16[4,2,48,768]{3,2,1,0:T(8,128)(2,1)S(1)} %pad_maximum_fusion.1.refs_7_.refs_4_), channel_id=1, source_target_pairs={{0,2},{1,3},{2,0},{3,1},{4,6},{5,7},{6,4},{7,5},{8,10},{9,11},{10,... | collective-permute-start | bytes 1769480 | tf_op jit(solution)/shard_map/ppermute | solution.py:536
  85.3 12.5 %collective-permute-start.20 = (bf16[4,2,48,768]{3,2,1,0:T(8,128)(2,1)S(1)}, bf16[4,2,48,768]{3,2,1,0:T(8,128)(2,1)S(1)}, u32[]{:S(2)}, u32[]{:S(2)}) collective-permute-start(bf16[4,2,48,768]{3,2,1,0:T(8,128)(2,1)S(1)} %pad_maximum_fusion.1.refs_7_.refs_4_), channel_id=1, source_target_pairs={{0,1},{1,0},{2,3},{3,2},{4,5},{5,4},{6,7},{7,6},{8,9},{9,8},{10,11... | collective-permute-start | bytes 1769480 | tf_op jit(solution)/shard_map/ppermute | solution.py:536
  85.6 16.5 %collective-permute-start.18 = (bf16[4,2,48,768]{3,2,1,0:T(8,128)(2,1)S(1)}, bf16[4,2,48,768]{3,2,1,0:T(8,128)(2,1)S(1)}, u32[]{:S(2)}, u32[]{:S(2)}) collective-permute-start(bf16[4,2,48,768]{3,2,1,0:T(8,128)(2,1)S(1)} %collective-permute-done.15.refs_0_.refs_4_.refs_1_), channel_id=1, source_target_pairs={{0,16},{16,0},{1,17},{17,1},{2,18},{18,2},{3,19},{19,3},{4,20},{20... | collective-permute-start | bytes 1769480 | tf_op jit(solution)/shard_map/ppermute | solution.py:540
  86.1 16.1 %collective-permute-start.19 = (bf16[4,2,48,768]{3,2,1,0:T(8,128)(2,1)S(1)}, bf16[4,2,48,768]{3,2,1,0:T(8,128)(2,1)S(1)}, u32[]{:S(2)}, u32[]{:S(2)}) collective-permute-start(bf16[4,2,48,768]{3,2,1,0:T(8,128)(2,1)S(1)} %collective-permute-done.16.refs_4_.refs_9_.refs_6_), channel_id=1, source_target_pairs={{0,2},{1,3},{2,0},{3,1},{4,6},{5,7},{6,4},{7,5},{8,10},{9,11},{10,... | collective-permute-start | bytes 1769480 | tf_op jit(solution)/shard_map/ppermute | solution.py:536
  103.2 7.8 %collective-permute-start.23 = (bf16[24,2,48,768]{3,2,1,0:T(8,128)(2,1)S(1)}, bf16[24,2,48,768]{3,2,1,0:T(8,128)(2,1)S(1)}, u32[]{:S(2)}, u32[]{:S(2)}) collective-permute-start(bf16[24,2,48,768]{3,2,1,0:T(8,128)(2,1)S(1)} %join_c.1), channel_id=1, source_target_pairs={{0,1},{1,0},{2,3},{3,2},{4,5},{5,4},{6,7},{7,6},{8,9},{9,8},{10,11... | collective-permute-start | bytes 10616840 | tf_op jit(solution)/shard_map/ppermute | solution.py:536
  111.0 9.5 %collective-permute-start.24 = (bf16[2,8,48,768]{3,2,1,0:T(8,128)(2,1)}, bf16[2,8,48,768]{3,2,1,0:T(8,128)(2,1)S(1)}, u32[]{:S(2)}, u32[]{:S(2)}) collective-permute-start(bf16[2,8,48,768]{3,2,1,0:T(8,128)(2,1)} %get-tuple-element.295), channel_id=1, source_target_pairs={{0,1},{1,0},{2,3},{3,2},{4,5},{5,4},{6,7},{7,6},{8,9},{9,8},{10,11... | collective-permute-start | bytes 3538952 | tf_op jit(solution)/shard_map/ppermute | solution.py:536
  111.6 8.9 %collective-permute-start.25 = (bf16[2,8,48,768]{3,2,1,0:T(8,128)(2,1)}, bf16[2,8,48,768]{3,2,1,0:T(8,128)(2,1)S(1)}, u32[]{:S(2)}, u32[]{:S(2)}) collective-permute-start(bf16[2,8,48,768]{3,2,1,0:T(8,128)(2,1)} %get-tuple-element.296), channel_id=1, source_target_pairs={{0,1},{1,0},{2,3},{3,2},{4,5},{5,4},{6,7},{7,6},{8,9},{9,8},{10,11... | collective-permute-start | bytes 3538952 | tf_op jit(solution)/shard_map/ppermute | solution.py:536
  122.1 15.8 %collective-permute-start.26 = (bf16[8,48,768]{2,1,0:T(8,128)(2,1)S(1)}, bf16[8,48,768]{2,1,0:T(8,128)(2,1)S(1)}, u32[]{:S(2)}, u32[]{:S(2)}) collective-permute-start(bf16[8,48,768]{2,1,0:T(8,128)(2,1)S(1)} %get-tuple-element.306), channel_id=1, source_target_pairs={{0,16},{16,0},{1,17},{17,1},{2,18},{18,2},{3,19},{19,3},{4,20},{20... | collective-permute-start | bytes 1769480 | tf_op jit(solution)/shard_map/ppermute | solution.py:540
  122.6 15.5 %collective-permute-start.27 = (bf16[8,48,768]{2,1,0:T(8,128)(2,1)S(1)}, bf16[8,48,768]{2,1,0:T(8,128)(2,1)S(1)}, u32[]{:S(2)}, u32[]{:S(2)}) collective-permute-start(bf16[8,48,768]{2,1,0:T(8,128)(2,1)S(1)} %get-tuple-element.307), channel_id=1, source_target_pairs={{0,2},{1,3},{2,0},{3,1},{4,6},{5,7},{6,4},{7,5},{8,10},{9,11},{10,... | collective-permute-start | bytes 1769480 | tf_op jit(solution)/shard_map/ppermute | solution.py:536
  139.6 10.5 %collective-permute-start.30 = (bf16[2,8,48,768]{3,2,1,0:T(8,128)(2,1)S(1)}, bf16[2,8,48,768]{3,2,1,0:T(8,128)(2,1)S(1)}, u32[]{:S(2)}, u32[]{:S(2)}) collective-permute-start(bf16[2,8,48,768]{3,2,1,0:T(8,128)(2,1)S(1)} %copy-done.21), channel_id=1, source_target_pairs={{0,1},{1,0},{2,3},{3,2},{4,5},{5,4},{6,7},{7,6},{8,9},{9,8},{10,11... | collective-permute-start | bytes 3538952 | tf_op jit(solution)/shard_map/ppermute | solution.py:536
  139.9 10.2 %collective-permute-start.31 = (bf16[2,8,48,768]{3,2,1,0:T(8,128)(2,1)S(1)}, bf16[2,8,48,768]{3,2,1,0:T(8,128)(2,1)S(1)}, u32[]{:S(2)}, u32[]{:S(2)}) collective-permute-start(bf16[2,8,48,768]{3,2,1,0:T(8,128)(2,1)S(1)} %copy-done.20), channel_id=1, source_target_pairs={{0,1},{1,0},{2,3},{3,2},{4,5},{5,4},{6,7},{7,6},{8,9},{9,8},{10,11... | collective-permute-start | bytes 3538952 | tf_op jit(solution)/shard_map/ppermute | solution.py:536
  140.1 9.7 %collective-permute-start.28 = (bf16[4,48,768]{2,1,0:T(8,128)(2,1)S(1)}, bf16[4,48,768]{2,1,0:T(8,128)(2,1)S(1)}, u32[]{:S(2)}, u32[]{:S(2)}) collective-permute-start(bf16[4,48,768]{2,1,0:T(8,128)(2,1)S(1)} %get-tuple-element.321), channel_id=1, source_target_pairs={{0,2},{1,3},{2,0},{3,1},{4,6},{5,7},{6,4},{7,5},{8,10},{9,11},{10,... | collective-permute-start | bytes 884744 | tf_op jit(solution)/shard_map/ppermute | solution.py:536
  141.2 8.9 %collective-permute-start.29 = (bf16[4,48,768]{2,1,0:T(8,128)(2,1)S(1)}, bf16[4,48,768]{2,1,0:T(8,128)(2,1)S(1)}, u32[]{:S(2)}, u32[]{:S(2)}) collective-permute-start(bf16[4,48,768]{2,1,0:T(8,128)(2,1)S(1)} %get-tuple-element.322), channel_id=1, source_target_pairs={{0,16},{16,0},{1,17},{17,1},{2,18},{18,2},{3,19},{19,3},{4,20},{20... | collective-permute-start | bytes 884744 | tf_op jit(solution)/shard_map/ppermute | solution.py:540
  151.8 23.4 %collective-permute-start.35 = (bf16[8,48,768]{2,1,0:T(8,128)(2,1)S(1)}, bf16[8,48,768]{2,1,0:T(8,128)(2,1)S(1)}, u32[]{:S(2)}, u32[]{:S(2)}) collective-permute-start(bf16[8,48,768]{2,1,0:T(8,128)(2,1)S(1)} %get-tuple-element.339), channel_id=1, source_target_pairs={{0,16},{16,0},{1,17},{17,1},{2,18},{18,2},{3,19},{19,3},{4,20},{20... | collective-permute-start | bytes 1769480 | tf_op jit(solution)/shard_map/ppermute | solution.py:540
  153.4 21.8 %collective-permute-start.36 = (bf16[8,48,768]{2,1,0:T(8,128)(2,1)S(1)}, bf16[8,48,768]{2,1,0:T(8,128)(2,1)S(1)}, u32[]{:S(2)}, u32[]{:S(2)}) collective-permute-start(bf16[8,48,768]{2,1,0:T(8,128)(2,1)S(1)} %get-tuple-element.340), channel_id=1, source_target_pairs={{0,2},{1,3},{2,0},{3,1},{4,6},{5,7},{6,4},{7,5},{8,10},{9,11},{10,... | collective-permute-start | bytes 1769480 | tf_op jit(solution)/shard_map/ppermute | solution.py:536
  154.4 19.6 %collective-permute-start.32 = (bf16[2,48,768]{2,1,0:T(8,128)(2,1)S(1)}, bf16[2,48,768]{2,1,0:T(8,128)(2,1)S(1)}, u32[]{:S(2)}, u32[]{:S(2)}) collective-permute-start(bf16[2,48,768]{2,1,0:T(8,128)(2,1)S(1)} %get-tuple-element.336), channel_id=1, source_target_pairs={{0,4},{1,5},{2,6},{3,7},{4,0},{5,1},{6,2},{7,3},{8,12},{9,13},{10,... | collective-permute-start | bytes 442376 | tf_op jit(solution)/shard_map/ppermute | solution.py:536
  163.7 11.5 %collective-permute-start.33 = (bf16[2,48,768]{2,1,0:T(8,128)(2,1)S(1)}, bf16[2,48,768]{2,1,0:T(8,128)(2,1)S(1)}, u32[]{:S(2)}, u32[]{:S(2)}) collective-permute-start(bf16[2,48,768]{2,1,0:T(8,128)(2,1)S(1)} %get-tuple-element.337), channel_id=1, source_target_pairs={{0,8},{1,9},{2,10},{3,11},{4,12},{5,13},{6,14},{7,15},{8,0},{9,1},... | collective-permute-start | bytes 442376 | tf_op jit(solution)/shard_map/ppermute | solution.py:536
  163.7 11.5 %collective-permute-start.34 = (bf16[2,48,768]{2,1,0:T(8,128)(2,1)S(1)}, bf16[2,48,768]{2,1,0:T(8,128)(2,1)S(1)}, u32[]{:S(2)}, u32[]{:S(2)}) collective-permute-start(bf16[2,48,768]{2,1,0:T(8,128)(2,1)S(1)} %get-tuple-element.338), channel_id=1, source_target_pairs={{0,12},{1,13},{2,14},{3,15},{4,8},{5,9},{6,10},{7,11},{8,4},{9,5},... | collective-permute-start | bytes 442376 | tf_op jit(solution)/shard_map/ppermute | solution.py:536
  176.8 12.9 %collective-permute-start.39 = (bf16[2,8,48,768]{3,2,1,0:T(8,128)(2,1)S(1)}, bf16[2,8,48,768]{3,2,1,0:T(8,128)(2,1)S(1)}, u32[]{:S(2)}, u32[]{:S(2)}) collective-permute-start(bf16[2,8,48,768]{3,2,1,0:T(8,128)(2,1)S(1)} %copy-done.19), channel_id=1, source_target_pairs={{0,1},{1,0},{2,3},{3,2},{4,5},{5,4},{6,7},{7,6},{8,9},{9,8},{10,11... | collective-permute-start | bytes 3538952 | tf_op jit(solution)/shard_map/ppermute | solution.py:536
  177.1 12.6 %collective-permute-start.40 = (bf16[2,8,48,768]{3,2,1,0:T(8,128)(2,1)S(1)}, bf16[2,8,48,768]{3,2,1,0:T(8,128)(2,1)S(1)}, u32[]{:S(2)}, u32[]{:S(2)}) collective-permute-start(bf16[2,8,48,768]{3,2,1,0:T(8,128)(2,1)S(1)} %copy-done.18), channel_id=1, source_target_pairs={{0,1},{1,0},{2,3},{3,2},{4,5},{5,4},{6,7},{7,6},{8,9},{9,8},{10,11... | collective-permute-start | bytes 3538952 | tf_op jit(solution)/shard_map/ppermute | solution.py:536
  177.3 11.6 %collective-permute-start.41 = (bf16[2,48,768]{2,1,0:T(8,128)(2,1)S(1)}, bf16[2,48,768]{2,1,0:T(8,128)(2,1)S(1)}, u32[]{:S(2)}, u32[]{:S(2)}) collective-permute-start(bf16[2,48,768]{2,1,0:T(8,128)(2,1)S(1)} %get-tuple-element.360.a_mine), channel_id=1, source_target_pairs={{0,16},{16,0},{1,17},{17,1},{2,18},{18,2},{3,19},{19,3},{4,20},{20... | collective-permute-start | bytes 442376 | tf_op jit(solution)/shard_map/ppermute | solution.py:540
  178.5 10.4 %collective-permute-start.37 = (bf16[4,48,768]{2,1,0:T(8,128)(2,1)S(1)}, bf16[4,48,768]{2,1,0:T(8,128)(2,1)S(1)}, u32[]{:S(2)}, u32[]{:S(2)}) collective-permute-start(bf16[4,48,768]{2,1,0:T(8,128)(2,1)S(1)} %get-tuple-element.356), channel_id=1, source_target_pairs={{0,2},{1,3},{2,0},{3,1},{4,6},{5,7},{6,4},{7,5},{8,10},{9,11},{10,... | collective-permute-start | bytes 884744 | tf_op jit(solution)/shard_map/ppermute | solution.py:536
  179.6 10.1 %collective-permute-start.38 = (bf16[4,48,768]{2,1,0:T(8,128)(2,1)S(1)}, bf16[4,48,768]{2,1,0:T(8,128)(2,1)S(1)}, u32[]{:S(2)}, u32[]{:S(2)}) collective-permute-start(bf16[4,48,768]{2,1,0:T(8,128)(2,1)S(1)} %get-tuple-element.357), channel_id=1, source_target_pairs={{0,16},{16,0},{1,17},{17,1},{2,18},{18,2},{3,19},{19,3},{4,20},{20... | collective-permute-start | bytes 884744 | tf_op jit(solution)/shard_map/ppermute | solution.py:540
  191.5 18.4 %collective-permute-start.42 = (bf16[8,48,768]{2,1,0:T(8,128)(2,1)S(1)}, bf16[8,48,768]{2,1,0:T(8,128)(2,1)S(1)}, u32[]{:S(2)}, u32[]{:S(2)}) collective-permute-start(bf16[8,48,768]{2,1,0:T(8,128)(2,1)S(1)} %get-tuple-element.380), channel_id=1, source_target_pairs={{0,16},{16,0},{1,17},{17,1},{2,18},{18,2},{3,19},{19,3},{4,20},{20... | collective-permute-start | bytes 1769480 | tf_op jit(solution)/shard_map/ppermute | solution.py:540
  192.8 17.1 %collective-permute-start.43 = (bf16[8,48,768]{2,1,0:T(8,128)(2,1)S(1)}, bf16[8,48,768]{2,1,0:T(8,128)(2,1)S(1)}, u32[]{:S(2)}, u32[]{:S(2)}) collective-permute-start(bf16[8,48,768]{2,1,0:T(8,128)(2,1)S(1)} %get-tuple-element.381), channel_id=1, source_target_pairs={{0,2},{1,3},{2,0},{3,1},{4,6},{5,7},{6,4},{7,5},{8,10},{9,11},{10,... | collective-permute-start | bytes 1769480 | tf_op jit(solution)/shard_map/ppermute | solution.py:536
  193.9 13.9 %collective-permute-start.44 = (bf16[2,48,768]{2,1,0:T(8,128)(2,1)S(1)}, bf16[2,48,768]{2,1,0:T(8,128)(2,1)S(1)}, u32[]{:S(2)}, u32[]{:S(2)}) collective-permute-start(bf16[2,48,768]{2,1,0:T(8,128)(2,1)S(1)} %get-tuple-element.382), channel_id=1, source_target_pairs={{0,4},{1,5},{2,6},{3,7},{4,0},{5,1},{6,2},{7,3},{8,12},{9,13},{10,... | collective-permute-start | bytes 442376 | tf_op jit(solution)/shard_map/ppermute | solution.py:536
  197.5 12.4 %collective-permute-start.45 = (bf16[2,48,768]{2,1,0:T(8,128)(2,1)S(1)}, bf16[2,48,768]{2,1,0:T(8,128)(2,1)S(1)}, u32[]{:S(2)}, u32[]{:S(2)}) collective-permute-start(bf16[2,48,768]{2,1,0:T(8,128)(2,1)S(1)} %get-tuple-element.383), channel_id=1, source_target_pairs={{0,8},{1,9},{2,10},{3,11},{4,12},{5,13},{6,14},{7,15},{8,0},{9,1},... | collective-permute-start | bytes 442376 | tf_op jit(solution)/shard_map/ppermute | solution.py:536
  197.5 12.4 %collective-permute-start.46 = (bf16[2,48,768]{2,1,0:T(8,128)(2,1)S(1)}, bf16[2,48,768]{2,1,0:T(8,128)(2,1)S(1)}, u32[]{:S(2)}, u32[]{:S(2)}) collective-permute-start(bf16[2,48,768]{2,1,0:T(8,128)(2,1)S(1)} %get-tuple-element.384), channel_id=1, source_target_pairs={{0,12},{1,13},{2,14},{3,15},{4,8},{5,9},{6,10},{7,11},{8,4},{9,5},... | collective-permute-start | bytes 442376 | tf_op jit(solution)/shard_map/ppermute | solution.py:536
  211.3 9.8 %collective-permute-start.47 = (bf16[4,48,768]{2,1,0:T(8,128)(2,1)S(1)}, bf16[4,48,768]{2,1,0:T(8,128)(2,1)S(1)}, u32[]{:S(2)}, u32[]{:S(2)}) collective-permute-start(bf16[4,48,768]{2,1,0:T(8,128)(2,1)S(1)} %get-tuple-element.397), channel_id=1, source_target_pairs={{0,2},{1,3},{2,0},{3,1},{4,6},{5,7},{6,4},{7,5},{8,10},{9,11},{10,... | collective-permute-start | bytes 884744 | tf_op jit(solution)/shard_map/ppermute | solution.py:536
  212.3 8.8 %collective-permute-start.48 = (bf16[4,48,768]{2,1,0:T(8,128)(2,1)S(1)}, bf16[4,48,768]{2,1,0:T(8,128)(2,1)S(1)}, u32[]{:S(2)}, u32[]{:S(2)}) collective-permute-start(bf16[4,48,768]{2,1,0:T(8,128)(2,1)S(1)} %get-tuple-element.398), channel_id=1, source_target_pairs={{0,16},{16,0},{1,17},{17,1},{2,18},{18,2},{3,19},{19,3},{4,20},{20... | collective-permute-start | bytes 884744 | tf_op jit(solution)/shard_map/ppermute | solution.py:540
  213.3 5.6 %collective-permute-start.51 = (f32[8,768]{1,0:T(8,128)S(1)}, f32[8,768]{1,0:T(8,128)S(1)}, u32[]{:S(2)}, u32[]{:S(2)}) collective-permute-start(f32[8,768]{1,0:T(8,128)S(1)} %get-tuple-element.399.refs_5_), channel_id=1, source_target_pairs={{0,12},{1,13},{2,14},{3,15},{4,8},{5,9},{6,10},{7,11},{8,4},{9,5},... | collective-permute-start | bytes 73736 | tf_op jit(solution)/shard_map/ppermute | solution.py:536
  215.0 4.7 %collective-permute-start.50 = (f32[8,768]{1,0:T(8,128)S(1)}, f32[8,768]{1,0:T(8,128)S(1)}, u32[]{:S(2)}, u32[]{:S(2)}) collective-permute-start(f32[8,768]{1,0:T(8,128)S(1)} %get-tuple-element.399.refs_5_), channel_id=1, source_target_pairs={{0,8},{1,9},{2,10},{3,11},{4,12},{5,13},{6,14},{7,15},{8,0},{9,1},... | collective-permute-start | bytes 73736 | tf_op jit(solution)/shard_map/ppermute | solution.py:536
  217.3 3.8 %collective-permute-start.49 = (f32[8,768]{1,0:T(8,128)S(1)}, f32[8,768]{1,0:T(8,128)S(1)}, u32[]{:S(2)}, u32[]{:S(2)}) collective-permute-start(f32[8,768]{1,0:T(8,128)S(1)} %get-tuple-element.399.refs_5_), channel_id=1, source_target_pairs={{0,4},{1,5},{2,6},{3,7},{4,0},{5,1},{6,2},{7,3},{8,12},{9,13},{10,... | collective-permute-start | bytes 73736 | tf_op jit(solution)/shard_map/ppermute | solution.py:536
  222.5 6.5 %collective-permute-start.55 = (bf16[2,48,768]{2,1,0:T(8,128)(2,1)S(1)}, bf16[2,48,768]{2,1,0:T(8,128)(2,1)S(1)}, u32[]{:S(2)}, u32[]{:S(2)}) collective-permute-start(bf16[2,48,768]{2,1,0:T(8,128)(2,1)S(1)} %get-tuple-element.410.d_mine), channel_id=1, source_target_pairs={{0,16},{16,0},{1,17},{17,1},{2,18},{18,2},{3,19},{19,3},{4,20},{20... | collective-permute-start | bytes 442376 | tf_op jit(solution)/shard_map/ppermute | solution.py:540
  223.7 7.9 %collective-permute-start.52 = (bf16[2,48,768]{2,1,0:T(8,128)(2,1)S(1)}, bf16[2,48,768]{2,1,0:T(8,128)(2,1)S(1)}, u32[]{:S(2)}, u32[]{:S(2)}) collective-permute-start(bf16[2,48,768]{2,1,0:T(8,128)(2,1)S(1)} %get-tuple-element.406), channel_id=1, source_target_pairs={{0,4},{1,5},{2,6},{3,7},{4,0},{5,1},{6,2},{7,3},{8,12},{9,13},{10,... | collective-permute-start | bytes 442376 | tf_op jit(solution)/shard_map/ppermute | solution.py:536
  224.7 10.8 %collective-permute-start.53 = (bf16[2,48,768]{2,1,0:T(8,128)(2,1)S(1)}, bf16[2,48,768]{2,1,0:T(8,128)(2,1)S(1)}, u32[]{:S(2)}, u32[]{:S(2)}) collective-permute-start(bf16[2,48,768]{2,1,0:T(8,128)(2,1)S(1)} %get-tuple-element.407), channel_id=1, source_target_pairs={{0,8},{1,9},{2,10},{3,11},{4,12},{5,13},{6,14},{7,15},{8,0},{9,1},... | collective-permute-start | bytes 442376 | tf_op jit(solution)/shard_map/ppermute | solution.py:536
  225.6 10.0 %collective-permute-start.54 = (bf16[2,48,768]{2,1,0:T(8,128)(2,1)S(1)}, bf16[2,48,768]{2,1,0:T(8,128)(2,1)S(1)}, u32[]{:S(2)}, u32[]{:S(2)}) collective-permute-start(bf16[2,48,768]{2,1,0:T(8,128)(2,1)S(1)} %get-tuple-element.408), channel_id=1, source_target_pairs={{0,12},{1,13},{2,14},{3,15},{4,8},{5,9},{6,10},{7,11},{8,4},{9,5},... | collective-permute-start | bytes 442376 | tf_op jit(solution)/shard_map/ppermute | solution.py:536
  228.1 7.5 %collective-permute-start.56 = (f32[8,768]{1,0:T(8,128)S(1)}, f32[8,768]{1,0:T(8,128)S(1)}, u32[]{:S(2)}, u32[]{:S(2)}) collective-permute-start(f32[8,768]{1,0:T(8,128)S(1)} %get-tuple-element.417.refs_4_), channel_id=1, source_target_pairs={{0,16},{16,0},{1,17},{17,1},{2,18},{18,2},{3,19},{19,3},{4,20},{20... | collective-permute-start | bytes 73736 | tf_op jit(solution)/shard_map/ppermute | solution.py:540
  235.7 5.6 %collective-permute-start.57 = (bf16[2,48,768]{2,1,0:T(8,128)(2,1)S(1)}, bf16[2,48,768]{2,1,0:T(8,128)(2,1)S(1)}, u32[]{:S(2)}, u32[]{:S(2)}) collective-permute-start(bf16[2,48,768]{2,1,0:T(8,128)(2,1)S(1)} %get-tuple-element.418.mine), channel_id=1, source_target_pairs={{0,16},{16,0},{1,17},{17,1},{2,18},{18,2},{3,19},{19,3},{4,20},{20... | collective-permute-start | bytes 442376 | tf_op jit(solution)/shard_map/ppermute | solution.py:540
  237.3 3.3 %collective-permute-start.60 = (f32[8,768]{1,0:T(8,128)S(1)}, f32[8,768]{1,0:T(8,128)S(1)}, u32[]{:S(2)}, u32[]{:S(2)}) collective-permute-start(f32[8,768]{1,0:T(8,128)S(1)} %get-tuple-element.419.v0), channel_id=1, source_target_pairs={{0,3},{1,2},{2,1},{3,0},{4,7},{5,6},{6,5},{7,4},{8,11},{9,10},{10,... | collective-permute-start | bytes 73736 | tf_op jit(solution)/shard_map/ppermute | solution.py:536
  237.3 4.0 %collective-permute-start.59 = (f32[8,768]{1,0:T(8,128)S(1)}, f32[8,768]{1,0:T(8,128)S(1)}, u32[]{:S(2)}, u32[]{:S(2)}) collective-permute-start(f32[8,768]{1,0:T(8,128)S(1)} %get-tuple-element.419.v0), channel_id=1, source_target_pairs={{0,2},{1,3},{2,0},{3,1},{4,6},{5,7},{6,4},{7,5},{8,10},{9,11},{10,... | collective-permute-start | bytes 73736 | tf_op jit(solution)/shard_map/ppermute | solution.py:536
  238.3 3.1 %collective-permute-start.58 = (f32[8,768]{1,0:T(8,128)S(1)}, f32[8,768]{1,0:T(8,128)S(1)}, u32[]{:S(2)}, u32[]{:S(2)}) collective-permute-start(f32[8,768]{1,0:T(8,128)S(1)} %get-tuple-element.419.v0), channel_id=1, source_target_pairs={{0,1},{1,0},{2,3},{3,2},{4,5},{5,4},{6,7},{7,6},{8,9},{9,8},{10,11... | collective-permute-start | bytes 73736 | tf_op jit(solution)/shard_map/ppermute | solution.py:536
  (21 other events, 130.0 us)
